TPU v7x, 256 devices: a whole 4x4x8 slice. The times are simulated.
256 devices in a mesh: sec: 2 (over core), var: 32 (over y, z), trait: 4 (over x).
Axes of the slice: x: 4, y: 4, z: 8, core: 2. Of those that a mesh axis runs over, the one named last changes fastest.
Arguments:
- z_typed: bfloat16 [262144, 512], P(('sec', 'var'), 'trait'), may hold values from -6 to 6
- band_inverse: bfloat16 [2048, 128, 384], P(('sec', 'var')), may hold values from -0.3125 to 0.3125
- ld_untyped: bfloat16 [4096, 128, 512], P(('sec', 'var')), may hold values from -0.375 to 0.375
- trait_mix: bfloat16 [512, 512], replicated, may hold values from -0.25 to 0.25
- win_start: int32 [4096], P(('sec', 'var')), may hold values from 0 to 2047, as said below
- win_count: int32 [4096], P(('sec', 'var')), may hold values from 1 to 4, as said below
Outputs:
- imputed_mixed: bfloat16 [524288, 512], P(('sec', 'var'), 'trait')
Inputs may be any that keep to these rules, and one draw needn't show every extreme that they name: Windows follow chromosome order: within the 64 untyped blocks of one index g of sec+var, win_start never falls, and every window lies in typed blocks g * 32 - 32 to (g + 1) * 32 + 31; the first window of each index starts at its lower end (or at 0) and the last one ends at its upper end (or at the chromosome's end). win_start + win_count never exceeds 2048.
All inputs are finite; a program needn't handle non-finite values.
Results may differ from a plain program's by a relative error of at most 0.0057.
Values may be sent and summed in bfloat16 or wider, within the bound.
No kernel may reach another device: no remote copies, remote signals or barrier semaphores. Data moves between devices by JAX's collectives and lax.ppermute only.
A program may use at most 64 MiB of HBM per device.

v0:
```python
import jax
import jax.numpy as jnp
from jax import lax
from jax.sharding import PartitionSpec as P

BLK = 128
WIN = 4


def padded_2(cells, sides, width):
    for axis, dim in sides:
        count = lax.axis_size(axis)
        ends = count - 1
        head = lax.slice_in_dim(cells, 0, width, axis=dim)
        tail = lax.slice_in_dim(cells, cells.shape[dim] - width, cells.shape[dim], axis=dim)
        cells = jnp.concatenate(
            [
                lax.ppermute(tail, axis, [(i, (i + 1) % count) for i in range(ends)]),
                cells,
                lax.ppermute(head, axis, [((i + 1) % count, i) for i in range(ends)]),
            ],
            axis=dim,
        )
    return cells


def on_device(z_typed, band_inverse, ld_untyped, trait_mix, win_start, win_count):
    trait_cols = z_typed.shape[1]
    typed_blocks = z_typed.shape[0] // BLK
    padded = padded_2(z_typed, ((("sec", "var"), 0),), BLK)
    stacked = jnp.concatenate(
        [
            padded[k * BLK : (k + typed_blocks) * BLK].reshape(typed_blocks, BLK, trait_cols)
            for k in range(3)
        ],
        axis=1,
    )
    whitened = jnp.einsum(
        "bij,bjc->bic", band_inverse, stacked, preferred_element_type=jnp.float32
    ).astype(jnp.bfloat16)
    whitened_rows = whitened.reshape(typed_blocks * BLK, trait_cols)
    column_start = lax.axis_index("trait") * trait_cols
    mix_cols = lax.dynamic_slice_in_dim(trait_mix, column_start, trait_cols, 1)
    mixed_sums = jnp.dot(
        lax.all_gather(whitened_rows, "trait", axis=1, tiled=True),
        mix_cols,
        preferred_element_type=jnp.float32,
    )
    mixed = mixed_sums.astype(jnp.bfloat16).reshape(typed_blocks, BLK, trait_cols)
    window_steps = jnp.arange(WIN, dtype=jnp.int32)
    usable = window_steps[None, :] < win_count[:, None]
    untyped_blocks = win_start.shape[0]
    extended = padded_2(mixed, ((("sec", "var"), 0),), typed_blocks)
    local_first = win_start - lax.axis_index(("sec", "var")) * typed_blocks + typed_blocks
    wanted = jnp.clip(local_first[:, None] + window_steps[None, :], 0, 3 * typed_blocks - 1)
    picked = extended[wanted]
    chosen = jnp.where(usable[:, :, None, None], picked, jnp.zeros_like(picked))
    window_rows = chosen.reshape(untyped_blocks, WIN * BLK, trait_cols)
    imputed = jnp.einsum(
        "uij,ujc->uic", ld_untyped, window_rows, preferred_element_type=jnp.float32
    ).astype(jnp.bfloat16)
    return imputed.reshape(untyped_blocks * BLK, trait_cols)


def solution(mesh):
    in_specs = (
        P(("sec", "var"), "trait"),
        P(("sec", "var"), None, None),
        P(("sec", "var"), None, None),
        P(),
        P(("sec", "var")),
        P(("sec", "var")),
    )
    out_specs = P(("sec", "var"), "trait")
    return jax.shard_map(
        on_device, mesh=mesh, in_specs=in_specs, out_specs=out_specs, check_vma=False
    )
```

profile of v0, /device:TPU:1, one launch (start us, length us, event | category | flops | bytes accessed | tf_op | source)
XLA Modules:
  0.0 149.6 jit_solution(10747132638285355354)
XLA Ops:
  6.5 0.0 copy-start
  6.5 0.0 all-gather.2.cloned.1.call-start
  6.5 0.9 fusion.12
  7.5 4.5 %collective-permute-start = (bf16[128,128]{1,0:T(8,128)(2,1)S(1)}, bf16[128,128]{1,0:T(8,128)(2,1)S(1)}, u32[]{:S(2)}, u32[]{:S(2)}) collective-permute-start(bf16[128,128]{1,0:T(8,128)(2,1)S(1)} %get-tuple-element.7), channel_id=1, source_target_pairs={{0,4},{4,8},{8,12},{12,16},{16,20},{20,24},{24,28},{28,32},{32,36}... | collective-permute-start | bytes 98312 | tf_op jit(solution)/shard_map/ppermute | solution.py:18
  12.0 8.9 %collective-permute-start.1 = (bf16[128,128]{1,0:T(8,128)(2,1)S(1)}, bf16[128,128]{1,0:T(8,128)(2,1)S(1)}, u32[]{:S(2)}, u32[]{:S(2)}) collective-permute-start(bf16[128,128]{1,0:T(8,128)(2,1)S(1)} %get-tuple-element.8), channel_id=1, source_target_pairs={{4,0},{8,4},{12,8},{16,12},{20,16},{24,20},{28,24},{32,28},{36,32}... | collective-permute-start | bytes 98312 | tf_op jit(solution)/shard_map/ppermute | solution.py:20
  20.9 0.0 collective-permute-done
  20.9 1.0 collective-permute-done.1
  21.9 1.7 %pad_maximum_fusion.2 = (bf16[4096,128]{1,0:T(8,128)(2,1)S(1)}, bf16[4096,128]{1,0:T(8,128)(2,1)S(1)}) fusion(bf16[4096,128]{1,0:T(8,128)(2,1)} %param.6, bf16[128,128]{1,0:T(8,128)(2,1)S(1)} %collective-permute-done, bf16[128,128]{1,0:T(8,128)(2,1)S(1)} %collective-permute-done.1), kind=kLoop, calls=%fused_computation.13 | loop fusion | flops 4194304 | bytes 3211264 | tf_op jit(solution)/shard_map/concatenate | solution.py:16
  23.6 0.0 copy-done
  23.6 3.2 %fusion.6 = bf16[32,128,128]{1,2,0:T(8,128)(2,1)} fusion(bf16[32,128,384]{2,1,0:T(8,128)(2,1)S(1)} %copy-done, bf16[32,128,128]{2,1,0:T(8,128)(2,1)S(1)} %bitcast.26, bf16[32,128,128]{2,1,0:T(8,128)(2,1)} %bitcast.24, bf16[32,128,128]{2,1,0:T(8,128)(2,1)S(1)} %bitcast.25), kind=kOutput, calls=%fused_computation.11 | convolution fusion | flops 412614656 | bytes 7340032 | tf_op jit(solution)/shard_map/bij,bjc->bic/dot_general | solution.py:38
  26.8 0.0 copy-start.1
  26.8 0.0 copy-start.2
  26.8 0.0 all-gather.2.cloned.1.call-update
  26.8 52.8 %all-gather.2.cloned.1.call-done = bf16[4096,512]{1,0:T(8,128)(2,1)} async-done(((bf16[4096,128]{1,0:T(8,128)(2,1)}), bf16[4096,512]{1,0:T(8,128)(2,1)}) %all-gather.2.cloned.1.call-update) | async-done | bytes 4194320 | tf_op jit(solution)/shard_map/all_gather | solution.py:45
  79.7 4.4 %convolution_convert_fusion = bf16[4096,128]{1,0:T(8,128)(2,1)} fusion(bf16[4096,512]{1,0:T(8,128)(2,1)} %all-gather.2.cloned.1.call-done, bf16[512,512]{1,0:T(8,128)(2,1)} %param.9, s32[]{:T(128)S(6)} %select_n.18), kind=kOutput, calls=%fused_computation.2 | convolution fusion | flops 537395200 | bytes 5373956 | tf_op jit(solution)/shard_map/dot_general | solution.py:44
  84.1 8.5 %collective-permute-start.3 = (bf16[32,128,128]{2,1,0:T(8,128)(2,1)}, bf16[32,128,128]{2,1,0:T(8,128)(2,1)}, u32[]{:S(2)}, u32[]{:S(2)}) collective-permute-start(bf16[32,128,128]{2,1,0:T(8,128)(2,1)} %bitcast.5), channel_id=1, source_target_pairs={{4,0},{8,4},{12,8},{16,12},{20,16},{24,20},{28,24},{32,28},{36,32}... | collective-permute-start | bytes 3145736 | tf_op jit(solution)/shard_map/ppermute | solution.py:20
  92.6 1.9 %collective-permute-start.2 = (bf16[32,128,128]{2,1,0:T(8,128)(2,1)}, bf16[32,128,128]{2,1,0:T(8,128)(2,1)}, u32[]{:S(2)}, u32[]{:S(2)}) collective-permute-start(bf16[32,128,128]{2,1,0:T(8,128)(2,1)} %bitcast.5), channel_id=1, source_target_pairs={{0,4},{4,8},{8,12},{12,16},{16,20},{20,24},{24,28},{28,32},{32,36}... | collective-permute-start | bytes 3145736 | tf_op jit(solution)/shard_map/ppermute | solution.py:18
  94.6 0.0 copy-done.1
  94.6 0.1 iota_compare_fusion
  94.6 0.1 broadcast_in_dim.21
  94.8 0.0 copy-done.2
  94.8 0.1 compare_select_fusion
  94.9 0.1 reshape.93
  95.0 14.3 %collective-permute-done.3 = bf16[32,128,128]{2,1,0:T(8,128)(2,1)} collective-permute-done((bf16[32,128,128]{2,1,0:T(8,128)(2,1)}, bf16[32,128,128]{2,1,0:T(8,128)(2,1)}, u32[]{:S(2)}, u32[]{:S(2)}) %collective-permute-start.3) | collective-permute-done | bytes 1048608 | tf_op jit(solution)/shard_map/ppermute | solution.py:20
  109.4 5.5 %collective-permute-done.2 = bf16[32,128,128]{2,1,0:T(8,128)(2,1)} collective-permute-done((bf16[32,128,128]{2,1,0:T(8,128)(2,1)}, bf16[32,128,128]{2,1,0:T(8,128)(2,1)}, u32[]{:S(2)}, u32[]{:S(2)}) %collective-permute-start.2) | collective-permute-done | bytes 1048608 | tf_op jit(solution)/shard_map/ppermute | solution.py:18
  114.9 3.3 %pad_maximum_fusion = bf16[96,128,128]{2,1,0:T(8,128)(2,1)} fusion(bf16[32,128,128]{2,1,0:T(8,128)(2,1)} %collective-permute-done.3, bf16[32,128,128]{2,1,0:T(8,128)(2,1)} %bitcast.5, bf16[32,128,128]{2,1,0:T(8,128)(2,1)} %collective-permute-done.2), kind=kLoop, calls=%fused_computation.9 | loop fusion | flops 3145728 | bytes 6291456 | tf_op jit(solution)/shard_map/concatenate | solution.py:16
  118.2 10.5 %gather_fusion = bf16[256,128,128]{2,1,0:T(8,128)(2,1)} fusion(bf16[96,128,128]{2,1,0:T(8,128)(2,1)} %pad_maximum_fusion, s32[1024]{0:T(1024)S(1)} %pad_clamp_fusion), kind=kCustom, calls=%fused_computation | custom fusion | bytes 16778240 | tf_op jit(solution)/shard_map/gather | solution.py:56
  128.7 7.0 %bitcast_select_fusion = bf16[64,512,128]{2,1,0:T(8,128)(2,1)S(1)} fusion(pred[64,512]{1,0:T(8,128)(4,1)S(1)} %bitcast.28, bf16[64,512,128]{2,1,0:T(8,128)(2,1)} %bitcast.23), kind=kLoop, calls=%fused_computation.1 | loop fusion | flops 4194304 | bytes 16809984 | tf_op jit(solution)/shard_map/jit(_where)/select_n | solution.py:57
  135.7 7.0 %convolution_convert_fusion.1 = bf16[64,128,128]{1,2,0:T(8,128)(2,1)} fusion(bf16[64,128,512]{2,1,0:T(8,128)(2,1)} %param.8, bf16[64,512,128]{2,1,0:T(8,128)(2,1)S(1)} %bitcast_select_fusion), kind=kOutput, calls=%fused_computation.10 | convolution fusion | flops 1074790400 | bytes 18874368 | tf_op jit(solution)/shard_map/uij,ujc->uic/dot_general | solution.py:59
  (3 shorter events, 0.0 us)
Async XLA Ops:
  6.5 17.0 %copy-start = (bf16[32,128,384]{2,1,0:T(8,128)(2,1)S(1)}, bf16[32,128,384]{2,1,0:T(8,128)(2,1)}, u32[]{:S(2)}) copy-start(bf16[32,128,384]{2,1,0:T(8,128)(2,1)} %param.7) | copy-start | bytes 9437188
  6.5 73.1 %all-gather.2.cloned.1.call-start = ((), (), s32[]{:S(2)}) async-start(), calls=%async_computation | async-start | bytes 5242880 | tf_op jit(solution)/shard_map/all_gather | solution.py:45
  7.5 13.4 %collective-permute-start = (bf16[128,128]{1,0:T(8,128)(2,1)S(1)}, bf16[128,128]{1,0:T(8,128)(2,1)S(1)}, u32[]{:S(2)}, u32[]{:S(2)}) collective-permute-start(bf16[128,128]{1,0:T(8,128)(2,1)S(1)} %get-tuple-element.7), channel_id=1, source_target_pairs={{0,4},{4,8},{8,12},{12,16},{16,20},{20,24},{24,28},{28,32},{32,36}... | collective-permute-start | bytes 98312 | tf_op jit(solution)/shard_map/ppermute | solution.py:18
  12.0 9.9 %collective-permute-start.1 = (bf16[128,128]{1,0:T(8,128)(2,1)S(1)}, bf16[128,128]{1,0:T(8,128)(2,1)S(1)}, u32[]{:S(2)}, u32[]{:S(2)}) collective-permute-start(bf16[128,128]{1,0:T(8,128)(2,1)S(1)} %get-tuple-element.8), channel_id=1, source_target_pairs={{4,0},{8,4},{12,8},{16,12},{20,16},{24,20},{28,24},{32,28},{36,32}... | collective-permute-start | bytes 98312 | tf_op jit(solution)/shard_map/ppermute | solution.py:20
  26.8 67.8 %copy-start.1 = (s32[64]{0:T(128)S(1)}, s32[64]{0:T(128)}, u32[]{:S(2)}) copy-start(s32[64]{0:T(128)} %param.11) | copy-start | bytes 772
  26.8 68.0 %copy-start.2 = (s32[64]{0:T(128)S(1)}, s32[64]{0:T(128)}, u32[]{:S(2)}) copy-start(s32[64]{0:T(128)} %param.10) | copy-start | bytes 772
  84.1 25.3 %collective-permute-start.3 = (bf16[32,128,128]{2,1,0:T(8,128)(2,1)}, bf16[32,128,128]{2,1,0:T(8,128)(2,1)}, u32[]{:S(2)}, u32[]{:S(2)}) collective-permute-start(bf16[32,128,128]{2,1,0:T(8,128)(2,1)} %bitcast.5), channel_id=1, source_target_pairs={{4,0},{8,4},{12,8},{16,12},{20,16},{24,20},{28,24},{32,28},{36,32}... | collective-permute-start | bytes 3145736 | tf_op jit(solution)/shard_map/ppermute | solution.py:20
  92.6 22.3 %collective-permute-start.2 = (bf16[32,128,128]{2,1,0:T(8,128)(2,1)}, bf16[32,128,128]{2,1,0:T(8,128)(2,1)}, u32[]{:S(2)}, u32[]{:S(2)}) collective-permute-start(bf16[32,128,128]{2,1,0:T(8,128)(2,1)} %bitcast.5), channel_id=1, source_target_pairs={{0,4},{4,8},{8,12},{12,16},{16,20},{20,24},{24,28},{28,32},{32,36}... | collective-permute-start | bytes 3145736 | tf_op jit(solution)/shard_map/ppermute | solution.py:18
Sparse Core Ops, SparseCore 0:
  26.9 52.6 all-gather.1
where the time goes:
time: 152 us; the launch traced here: 150 us
  waiting for transfers between devices  73.7 us (48%)
  starting transfers between devices  23.8 us (16%)
  matrix products  14.7 us (10%)
  between operations  13.5 us (9%)
  other arithmetic  12.2 us (8%)
  local copies, waits for them, and re-layouts  11.7 us (8%)
    all_gather x1, waiting for transfers between devices, on_device(): lax.all_gather(whitened_rows, 'trait', axis=1, tiled=True)  52.8 us
    ppermute x2, starting transfers between devices, padded_2(): lax.ppermute(head, axis, [((i + 1) % count, i) for i in range(ends)])  17.4 us
    ppermute x2, waiting for transfers between devices, padded_2(): lax.ppermute(head, axis, [((i + 1) % count, i) for i in range(ends)])  15.3 us
    gather x1, local copies, waits for them, and re-layouts, on_device(): picked = extended[wanted]  10.5 us
    dot_general x1, matrix products, on_device(): jnp.einsum('uij,ujc->uic', ld_untyped, window_rows, preferred_element_typ...  7.04 us
    select_n x1, other arithmetic, on_device(): chosen = jnp.where(usable[:, :, None, None], picked, jnp.zeros_like(picked))  7.01 us
    ppermute x2, starting transfers between devices, padded_2(): lax.ppermute(tail, axis, [(i, (i + 1) % count) for i in range(ends)])  6.42 us
    ppermute x2, waiting for transfers between devices, padded_2(): lax.ppermute(tail, axis, [(i, (i + 1) % count) for i in range(ends)])  5.54 us
  transfers between devices with their start and end apart: 5, of which 4 were waited for; matrix products, arithmetic and copies ran while one was open for 0% of the time, Pallas kernels for 0%

commit v1 on v0

v1 whole, which is shorter than its diff:
```python
import functools

import jax
import jax.numpy as jnp
import numpy as np
from jax import lax
from jax.experimental import pallas as pl
from jax.experimental.pallas import tpu as pltpu
from jax.sharding import PartitionSpec as P

BLK = 128
WIN = 4
COLS = 128
TB = 32
UB = 64
BF = jnp.bfloat16
F32 = jnp.float32
ROWS = ("sec", "var")
ANY = pl.BlockSpec(memory_space=pl.ANY)
HBM = pl.BlockSpec(memory_space=pltpu.HBM)
SMEM = pl.BlockSpec(memory_space=pltpu.SMEM)
VM = pl.BlockSpec(memory_space=pltpu.VMEM)
PARAMS = pltpu.CompilerParams(vmem_limit_bytes=40 * 1024 * 1024)


def shaped(rows, dtype=BF):
    return jax.ShapeDtypeStruct((rows, COLS), dtype)


def dot(left, right):
    return jnp.dot(left, right, preferred_element_type=F32)


def whiten_mid(place, z, band, mix, w_a, w_b, first, last, mix_a, mix_b, zs, bs, sems):
    zcopy = pltpu.make_async_copy(z.at[pl.ds(7 * BLK, 18 * BLK)], zs, sems.at[0])
    zcopy.start()
    bands = []
    for k in range(4):
        bands.append(
            pltpu.make_async_copy(band.at[pl.ds(8 + 4 * k, 4)], bs.at[pl.ds(4 * k, 4)], sems.at[1 + k])
        )
        bands[-1].start()
    others = [
        pltpu.make_async_copy(z.at[pl.ds(0, BLK)], first, sems.at[5]),
        pltpu.make_async_copy(z.at[pl.ds((TB - 1) * BLK, BLK)], last, sems.at[6]),
    ]
    t, a, b = place[0], place[1], place[2]
    n = 7
    for target, near, far in ((mix_a, a, b), (mix_b, b, a)):
        for i, row in enumerate((t, near)):
            for j, col in enumerate((t, far)):
                source = mix.at[
                    pl.ds(pl.multiple_of(row * COLS, COLS), COLS), pl.ds(pl.multiple_of(col * COLS, COLS), COLS)
                ]
                others.append(
                    pltpu.make_async_copy(
                        source, target.at[pl.ds(i * COLS, COLS), pl.ds(j * COLS, COLS)], sems.at[n]
                    )
                )
                n += 1
    for copy in others:
        copy.start()
    zcopy.wait()
    for k in range(4):
        bands[k].wait()
        for i in range(4 * k, 4 * k + 4):
            rows = dot(bs[i], zs[pl.ds(i * BLK, 3 * BLK), :]).astype(BF)
            if i < 8:
                w_a[pl.ds(i * BLK, BLK), :] = rows
            else:
                w_b[pl.ds((i - 8) * BLK, BLK), :] = rows
    for copy in others:
        copy.wait()


def whiten_edge(place, z, band, from_left, from_right, w_a, w_b, zs, bs, sems):
    copies = [
        pltpu.make_async_copy(z.at[pl.ds(0, 9 * BLK)], zs.at[pl.ds(BLK, 9 * BLK)], sems.at[0]),
        pltpu.make_async_copy(z.at[pl.ds(23 * BLK, 9 * BLK)], zs.at[pl.ds(10 * BLK, 9 * BLK)], sems.at[1]),
    ]
    for k in range(2):
        copies.append(
            pltpu.make_async_copy(band.at[pl.ds(24 * k, 8)], bs.at[pl.ds(8 * k, 8)], sems.at[2 + k])
        )
    for copy in copies:
        copy.start()
    nothing = jnp.zeros((BLK, COLS), BF)
    zs[pl.ds(0, BLK), :] = jnp.where(place[3] == 0, nothing, from_left[...])
    zs[pl.ds(19 * BLK, BLK), :] = jnp.where(place[3] == place[4] - 1, nothing, from_right[...])
    for copy in copies:
        copy.wait()
    for i in range(8):
        w_a[pl.ds(i * BLK, BLK), :] = dot(bs[i], zs[pl.ds(i * BLK, 3 * BLK), :]).astype(BF)
        w_b[pl.ds(i * BLK, BLK), :] = dot(bs[8 + i], zs[pl.ds((10 + i) * BLK, 3 * BLK), :]).astype(BF)


def partial_sums(w_a, got_a, w_b, got_b, mix_a, mix_b, send_a, send_b, own):
    rows = w_a.shape[0]
    for k, (w, got, mix, send) in enumerate(((w_a, got_a, mix_a, send_a), (w_b, got_b, mix_b, send_b))):
        sums = dot(w[...], mix[pl.ds(0, COLS), :]) + dot(got[...], mix[pl.ds(COLS, COLS), :])
        own[pl.ds(k * rows, rows), :] = sums[:, :COLS]
        send[...] = sums[:, COLS:].astype(BF)


def combine(own, got_a, got_b, out):
    rows = got_a.shape[0]
    out[pl.ds(0, rows), :] = (own[pl.ds(0, rows), :] + got_a[...].astype(F32)).astype(BF)
    out[pl.ds(rows, rows), :] = (own[pl.ds(rows, rows), :] + got_b[...].astype(F32)).astype(BF)


GROUP = 8


def impute(place, starts, counts, own1, own2, l1, l2, r1, r2, ld, out, ext, sems):
    step = pl.program_id(0)

    @pl.when(step == 0)
    def _():
        copies = []
        for k, (mid, edge) in enumerate(((l1, l2), (own1, own2), (r1, r2))):
            at = 32 * k * BLK
            copies.append(pltpu.make_async_copy(edge.at[pl.ds(0, 8 * BLK)], ext.at[pl.ds(at, 8 * BLK)], sems.at[3 * k]))
            copies.append(pltpu.make_async_copy(mid, ext.at[pl.ds(at + 8 * BLK, 16 * BLK)], sems.at[3 * k + 1]))
            copies.append(
                pltpu.make_async_copy(
                    edge.at[pl.ds(8 * BLK, 8 * BLK)], ext.at[pl.ds(at + 24 * BLK, 8 * BLK)], sems.at[3 * k + 2]
                )
            )
        for copy in copies:
            copy.start()
        ext[pl.ds(96 * BLK, 3 * BLK), :] = jnp.zeros((3 * BLK, COLS), BF)
        for copy in copies:
            copy.wait()

    lowest = place[3] * TB - TB
    for i in range(GROUP):
        u = step * GROUP + i
        at = jnp.clip(starts[u] - lowest, 0, 95)
        count = counts[u]
        rows = ld[i]
        kept = [rows[:, :BLK]]
        for s in range(1, WIN):
            part = rows[:, s * BLK : (s + 1) * BLK]
            kept.append(jnp.where(s < count, part, jnp.zeros_like(part)))
        window = ext[pl.ds(pl.multiple_of(at * BLK, BLK), WIN * BLK), :]
        out[pl.ds(i * BLK, BLK), :] = dot(jnp.concatenate(kept, axis=1), window).astype(BF)


def on_device(z, band, ld, mix, starts, counts):
    t = lax.axis_index("trait")
    g = lax.axis_index(ROWS)
    owners = lax.axis_size(ROWS)
    lane = lax.iota(jnp.int32, 8)
    place = jnp.where(
        lane == 0, t, jnp.where(lane == 1, t ^ 1, jnp.where(lane == 2, 3 - t, jnp.where(lane == 3, g, owners)))
    ).astype(jnp.int32)
    pair_a = [(i, i ^ 1) for i in range(4)]
    pair_b = [(i, 3 - i) for i in range(4)]
    to_right = [(i, (i + 1) % owners) for i in range(owners)]
    to_left = [((i + 1) % owners, i) for i in range(owners)]

    w1a, w1b, first, last, mix_a, mix_b = pl.pallas_call(
        whiten_mid,
        name="whiten_mid",
        out_shape=(
            shaped(1024),
            shaped(1024),
            shaped(BLK),
            shaped(BLK),
            jax.ShapeDtypeStruct((256, 256), BF),
            jax.ShapeDtypeStruct((256, 256), BF),
        ),
        in_specs=[SMEM, HBM, HBM, HBM],
        out_specs=(VM,) * 6,
        scratch_shapes=[
            pltpu.VMEM((18 * BLK, COLS), BF),
            pltpu.VMEM((16, BLK, 3 * BLK), BF),
            pltpu.SemaphoreType.DMA((15,)),
        ],
        compiler_params=PARAMS,
    )(place, z, band, mix)

    def exchange(w_a, w_b, pairs):
        return lax.ppermute(w_a, "trait", pairs[0]), lax.ppermute(w_b, "trait", pairs[1])

    def mixing(w_a, w_b, got_a, got_b):
        rows = w_a.shape[0]
        return pl.pallas_call(
            partial_sums,
            name="partial_sums",
            out_shape=(shaped(rows), shaped(rows), shaped(2 * rows, F32)),
            in_specs=[VM] * 6,
            out_specs=(VM,) * 3,
            compiler_params=PARAMS,
        )(w_a, got_a, w_b, got_b, mix_a, mix_b)

    def combined(own, got_a, got_b):
        return pl.pallas_call(
            combine,
            name="combine",
            out_shape=shaped(own.shape[0]),
            in_specs=[VM] * 3,
            out_specs=VM,
            compiler_params=PARAMS,
        )(own, got_a, got_b)

    got1a, got1b = exchange(w1a, w1b, (pair_a, pair_b))
    from_left = lax.ppermute(last, ROWS, to_right)
    from_right = lax.ppermute(first, ROWS, to_left)
    send1a, send1b, own1 = mixing(w1a, w1b, got1a, got1b)
    far1a, far1b = exchange(send1a, send1b, (pair_b, pair_a))
    from_left, from_right, send1a = lax.optimization_barrier((from_left, from_right, send1a))
    w2a, w2b = pl.pallas_call(
        whiten_edge,
        name="whiten_edge",
        out_shape=(shaped(1024), shaped(1024)),
        in_specs=[SMEM, HBM, HBM, VM, VM],
        out_specs=(VM,) * 2,
        scratch_shapes=[
            pltpu.VMEM((20 * BLK, COLS), BF),
            pltpu.VMEM((16, BLK, 3 * BLK), BF),
            pltpu.SemaphoreType.DMA((4,)),
        ],
        compiler_params=PARAMS,
    )(place, z, band, from_left, from_right)
    got2a, got2b = exchange(w2a, w2b, (pair_a, pair_b))
    mixed1 = combined(own1, far1a, far1b)
    left1 = lax.ppermute(mixed1, ROWS, to_right)
    right1 = lax.ppermute(mixed1, ROWS, to_left)
    got2a, got2b, mixed1 = lax.optimization_barrier((got2a, got2b, mixed1))
    send2a, send2b, own2 = mixing(w2a, w2b, got2a, got2b)
    far2a, far2b = exchange(send2a, send2b, (pair_b, pair_a))
    mixed2 = combined(own2, far2a, far2b)
    left2 = lax.ppermute(mixed2, ROWS, to_right)
    right2 = lax.ppermute(mixed2, ROWS, to_left)
    return pl.pallas_call(
        impute,
        name="impute",
        grid=(UB // GROUP,),
        out_shape=shaped(UB * BLK),
        in_specs=[SMEM, SMEM, SMEM] + [ANY] * 6 + [pl.BlockSpec((GROUP, BLK, WIN * BLK), lambda i: (i, 0, 0))],
        out_specs=pl.BlockSpec((GROUP * BLK, COLS), lambda i: (i, 0)),
        scratch_shapes=[pltpu.VMEM((99 * BLK, COLS), BF), pltpu.SemaphoreType.DMA((9,))],
        compiler_params=PARAMS,
    )(place, starts, counts, mixed1, mixed2, left1, left2, right1, right2, ld)


def solution(mesh):
    in_specs = (
        P(ROWS, "trait"),
        P(ROWS, None, None),
        P(ROWS, None, None),
        P(),
        P(ROWS),
        P(ROWS),
    )
    return jax.shard_map(on_device, mesh=mesh, in_specs=in_specs, out_specs=P(ROWS, "trait"), check_vma=False)
```

time: 152 us -> 76.7 us (0.50); the launches traced: 150 us -> 76.5 us
  waiting for transfers between devices: 73.7 us -> 29.6 us
  matrix products: 14.7 us -> 0 us
  between operations: 13.5 us -> 0.09 us
  other arithmetic: 12.2 us -> 0.01 us
  Pallas kernels: 0 us -> 11.8 us
  local copies, waits for them, and re-layouts: 11.7 us -> 4.17 us
  starting transfers between devices: 23.8 us -> 30.8 us
    all_gather x1 -> x0, waiting for transfers between devices: 52.8 us -> none  [on_device(): lax.all_gather(whitened_rows, 'trait', axis=1, tiled=True)]
    dot_general x3 -> x0, matrix products: 14.7 us -> none  [the longest x1 7.04 us: on_device(): jnp.einsum('uij,ujc->uic', ld_untyped, window_rows, preferred_element_typ...]
    pallas_call x0 -> x7, Pallas kernels: none -> 11.8 us  [the longest x1 6 us: on_device(): pl.pallas_call(impute, name='impute', grid=(UB // GROUP,), out_shape=shap...]
    gather x1 -> x0, local copies, waits for them, and re-layouts: 10.5 us -> none  [on_device(): picked = extended[wanted]]
    ppermute x4 -> x14, waiting for transfers between devices: 20.9 us -> 29.6 us  [the longest x1 6.09 us: on_device(): left1 = lax.ppermute(mixed1, ROWS, to_right)]
    select_n x2 -> x1, other arithmetic: 7.09 us -> 0.01 us  [on_device(): jnp.where(lane == 0, t, jnp.where(lane == 1, t ^ 1, jnp.where(lane == 2,...]
    ppermute x4 -> x14, starting transfers between devices: 23.8 us -> 30.8 us  [the longest x1 7.51 us: on_device(): from_right = lax.ppermute(first, ROWS, to_left)]
    concatenate x2 -> x0, other arithmetic: 4.97 us -> none  [padded_2(): jnp.concatenate([lax.ppermute(tail, axis, [(i, (i + 1) % count) for i in...]
  transfers between devices with their start and end apart: 5 -> 14, of which waited for: 4 -> 10; matrix products, arithmetic and copies ran while one was open for 0% -> 0% of each run, Pallas kernels for 0% -> 3%
where the time goes in v1:
time: 76.7 us; the launch traced here: 76.5 us
  starting transfers between devices  30.8 us (40%)
  waiting for transfers between devices  29.6 us (39%)
  Pallas kernels  11.8 us (15%)
  local copies, waits for them, and re-layouts  4.17 us (5%)
    ppermute x1, starting transfers between devices, on_device(): from_right = lax.ppermute(first, ROWS, to_left)  7.51 us
    ppermute x4, starting transfers between devices, exchange(): lax.ppermute(w_a, 'trait', pairs[0])  6.47 us
    ppermute x1, waiting for transfers between devices, on_device(): left1 = lax.ppermute(mixed1, ROWS, to_right)  6.09 us
    ppermute x1, starting transfers between devices, on_device(): right1 = lax.ppermute(mixed1, ROWS, to_left)  6.02 us
    pallas_call x1, Pallas kernels, on_device(): pl.pallas_call(impute, name='impute', grid=(UB // GROUP,), out_shape=shap...  6 us
    ppermute x4, waiting for transfers between devices, exchange(): lax.ppermute(w_a, 'trait', pairs[0])  5.94 us
    ppermute x1, starting transfers between devices, on_device(): right2 = lax.ppermute(mixed2, ROWS, to_left)  5.32 us
    ppermute x1, waiting for transfers between devices, on_device(): right1 = lax.ppermute(mixed1, ROWS, to_left)  5.26 us
  transfers between devices with their start and end apart: 14, of which 10 were waited for; matrix products, arithmetic and copies ran while one was open for 0% of the time, Pallas kernels for 3%

profile of v1, /device:TPU:1, one launch (start us, length us, event | category | flops | bytes accessed | tf_op | source)
XLA Modules:
  0.0 76.5 jit_solution(10371217654292947982)
XLA Ops:
  0.0 0.0 copy-start
  0.0 1.9 %copy-done = bf16[32,128,384]{2,1,0:T(8,128)(2,1)S(1)} copy-done((bf16[32,128,384]{2,1,0:T(8,128)(2,1)S(1)}, bf16[32,128,384]{2,1,0:T(8,128)(2,1)}, u32[]{:S(2)}) %copy-start) | copy-done | bytes 3145752
  1.9 0.0 copy-start.3
  1.9 1.2 %copy-done.3 = bf16[4096,128]{1,0:T(8,128)(2,1)S(1)} copy-done((bf16[4096,128]{1,0:T(8,128)(2,1)S(1)}, bf16[4096,128]{1,0:T(8,128)(2,1)}, u32[]{:S(2)}) %copy-start.3) | copy-done | bytes 1048600
  3.1 0.0 copy-start.5
  3.1 1.0 %copy-done.5 = bf16[512,512]{1,0:T(8,128)(2,1)S(1)} copy-done((bf16[512,512]{1,0:T(8,128)(2,1)S(1)}, bf16[512,512]{1,0:T(8,128)(2,1)}, u32[]{:S(2)}) %copy-start.5) | copy-done | bytes 524312
  4.2 2.8 %whiten_mid.1 = (bf16[1024,128]{1,0:T(8,128)(2,1)S(1)}, bf16[1024,128]{1,0:T(8,128)(2,1)S(1)}, bf16[128,128]{1,0:T(8,128)(2,1)S(1)}, bf16[128,128]{1,0:T(8,128)(...) custom-call(s32[8]{0:T(128)S(1)} %compare_select_fusion.3.place, bf16[4096,128]{1,0:T(8,128)(2,1)S(1)} %copy-done.3, ...), custom_call_target="tpu_custom_call" | custom-call | tf_op jit(solution)/shard_map/whiten_mid/pallas_call | solution.py:162
  6.9 2.1 %collective-permute-start.2 = (bf16[1024,128]{1,0:T(8,128)(2,1)S(1)}, bf16[1024,128]{1,0:T(8,128)(2,1)S(1)}, u32[]{:S(2)}, u32[]{:S(2)}) collective-permute-start(bf16[1024,128]{1,0:T(8,128)(2,1)S(1)} %get-tuple-element.26.w_a), channel_id=1, source_target_pairs={{0,1},{1,0},{2,3},{3,2},{4,5},{5,4},{6,7},{7,6},{8,9},{9,8},{10,11... | collective-permute-start | bytes 786440 | tf_op jit(solution)/shard_map/ppermute | solution.py:184
  9.1 1.8 %collective-permute-start.3 = (bf16[1024,128]{1,0:T(8,128)(2,1)S(1)}, bf16[1024,128]{1,0:T(8,128)(2,1)S(1)}, u32[]{:S(2)}, u32[]{:S(2)}) collective-permute-start(bf16[1024,128]{1,0:T(8,128)(2,1)S(1)} %get-tuple-element.27.w_b), channel_id=1, source_target_pairs={{0,3},{1,2},{2,1},{3,0},{4,7},{5,6},{6,5},{7,4},{8,11},{9,10},{10,... | collective-permute-start | bytes 786440 | tf_op jit(solution)/shard_map/ppermute | solution.py:184
  10.9 1.6 %collective-permute-start = (bf16[128,128]{1,0:T(8,128)(2,1)S(1)}, bf16[128,128]{1,0:T(8,128)(2,1)S(1)}, u32[]{:S(2)}, u32[]{:S(2)}) collective-permute-start(bf16[128,128]{1,0:T(8,128)(2,1)S(1)} %get-tuple-element.24), channel_id=1, source_target_pairs={{0,4},{4,8},{8,12},{12,16},{16,20},{20,24},{24,28},{28,32},{32,36}... | collective-permute-start | bytes 98312 | tf_op jit(solution)/shard_map/ppermute | solution.py:208
  12.5 7.5 %collective-permute-start.1 = (bf16[128,128]{1,0:T(8,128)(2,1)S(1)}, bf16[128,128]{1,0:T(8,128)(2,1)S(1)}, u32[]{:S(2)}, u32[]{:S(2)}) collective-permute-start(bf16[128,128]{1,0:T(8,128)(2,1)S(1)} %get-tuple-element.25), channel_id=1, source_target_pairs={{4,0},{8,4},{12,8},{16,12},{20,16},{24,20},{28,24},{32,28},{36,32}... | collective-permute-start | bytes 98312 | tf_op jit(solution)/shard_map/ppermute | solution.py:209
  20.0 0.0 collective-permute-done.2.got_a
  20.0 0.0 collective-permute-done.3.got_b
  20.0 0.7 partial_sums.2
  20.7 0.9 %collective-permute-start.6 = (bf16[1024,128]{1,0:T(8,128)(2,1)S(1)}, bf16[1024,128]{1,0:T(8,128)(2,1)S(1)}, u32[]{:S(2)}, u32[]{:S(2)}) collective-permute-start(bf16[1024,128]{1,0:T(8,128)(2,1)S(1)} %get-tuple-element.30), channel_id=1, source_target_pairs={{0,3},{1,2},{2,1},{3,0},{4,7},{5,6},{6,5},{7,4},{8,11},{9,10},{10,... | collective-permute-start | bytes 786440 | tf_op jit(solution)/shard_map/ppermute | solution.py:184
  21.7 0.0 collective-permute-done.from_left
  21.7 0.0 collective-permute-done.1.from_right
  21.7 0.2 collective-permute-start.7
  21.9 0.0 copy-done.1
  21.9 0.0 copy-done.4
  21.9 1.4 %whiten_edge.1 = (bf16[1024,128]{1,0:T(8,128)(2,1)S(1)}, bf16[1024,128]{1,0:T(8,128)(2,1)S(1)}) custom-call(s32[8]{0:T(128)S(1)} %compare_select_fusion.3.place, bf16[4096,128]{1,0:T(8,128)(2,1)S(1)} %copy-done.4, bf16[32,128,384]{2,1,0:T(8,128)(2,1)S(1)} %copy-done.1, bf16[128,128]{1,0:T(8,128)(2,1)S(1)} %collective-permute-done.from_left, ...), custom_call_target="tpu_custom_call" | custom-call | tf_op jit(solution)/shard_map/whiten_edge/pallas_call | solution.py:213
  23.4 0.0 copy-start.6
  23.4 0.0 copy-start.7
  23.4 1.3 %collective-permute-start.4 = (bf16[1024,128]{1,0:T(8,128)(2,1)S(1)}, bf16[1024,128]{1,0:T(8,128)(2,1)S(1)}, u32[]{:S(2)}, u32[]{:S(2)}) collective-permute-start(bf16[1024,128]{1,0:T(8,128)(2,1)S(1)} %get-tuple-element.33.w_a), channel_id=1, source_target_pairs={{0,1},{1,0},{2,3},{3,2},{4,5},{5,4},{6,7},{7,6},{8,9},{9,8},{10,11... | collective-permute-start | bytes 786440 | tf_op jit(solution)/shard_map/ppermute | solution.py:184
  24.7 1.8 %collective-permute-start.5 = (bf16[1024,128]{1,0:T(8,128)(2,1)S(1)}, bf16[1024,128]{1,0:T(8,128)(2,1)S(1)}, u32[]{:S(2)}, u32[]{:S(2)}) collective-permute-start(bf16[1024,128]{1,0:T(8,128)(2,1)S(1)} %get-tuple-element.34.w_b), channel_id=1, source_target_pairs={{0,3},{1,2},{2,1},{3,0},{4,7},{5,6},{6,5},{7,4},{8,11},{9,10},{10,... | collective-permute-start | bytes 786440 | tf_op jit(solution)/shard_map/ppermute | solution.py:184
  26.5 2.9 %collective-permute-done.7.got_b = bf16[1024,128]{1,0:T(8,128)(2,1)S(1)} collective-permute-done((bf16[1024,128]{1,0:T(8,128)(2,1)S(1)}, bf16[1024,128]{1,0:T(8,128)(2,1)S(1)}, u32[]{:S(2)}, u32[]{:S(2)}) %collective-permute-start.7) | collective-permute-done | bytes 262176 | tf_op jit(solution)/shard_map/ppermute | solution.py:184
  29.4 0.9 %collective-permute-done.6.got_a = bf16[1024,128]{1,0:T(8,128)(2,1)S(1)} collective-permute-done((bf16[1024,128]{1,0:T(8,128)(2,1)S(1)}, bf16[1024,128]{1,0:T(8,128)(2,1)S(1)}, u32[]{:S(2)}, u32[]{:S(2)}) %collective-permute-start.6) | collective-permute-done | bytes 262176 | tf_op jit(solution)/shard_map/ppermute | solution.py:184
  30.4 0.1 combine.2.own1
  30.5 4.5 %collective-permute-done.4.got_a = bf16[1024,128]{1,0:T(8,128)(2,1)S(1)} collective-permute-done((bf16[1024,128]{1,0:T(8,128)(2,1)S(1)}, bf16[1024,128]{1,0:T(8,128)(2,1)S(1)}, u32[]{:S(2)}, u32[]{:S(2)}) %collective-permute-start.4) | collective-permute-done | bytes 262176 | tf_op jit(solution)/shard_map/ppermute | solution.py:184
  35.0 0.4 collective-permute-done.5.got_b
  35.4 0.7 partial_sums.3
  36.1 2.1 %collective-permute-start.8 = (bf16[1024,128]{1,0:T(8,128)(2,1)S(1)}, bf16[1024,128]{1,0:T(8,128)(2,1)S(1)}, u32[]{:S(2)}, u32[]{:S(2)}) collective-permute-start(bf16[1024,128]{1,0:T(8,128)(2,1)S(1)} %get-tuple-element.41), channel_id=1, source_target_pairs={{0,3},{1,2},{2,1},{3,0},{4,7},{5,6},{6,5},{7,4},{8,11},{9,10},{10,... | collective-permute-start | bytes 786440 | tf_op jit(solution)/shard_map/ppermute | solution.py:184
  38.2 0.0 collective-permute-start.9
  38.2 6.0 %collective-permute-start.12 = (bf16[2048,128]{1,0:T(8,128)(2,1)S(1)}, bf16[2048,128]{1,0:T(8,128)(2,1)S(1)}, u32[]{:S(2)}, u32[]{:S(2)}) collective-permute-start(bf16[2048,128]{1,0:T(8,128)(2,1)S(1)} %combine.2.own1), channel_id=1, source_target_pairs={{4,0},{8,4},{12,8},{16,12},{20,16},{24,20},{28,24},{32,28},{36,32}... | collective-permute-start | bytes 1572872 | tf_op jit(solution)/shard_map/ppermute | solution.py:229
  44.3 0.0 collective-permute-start.10
  44.3 0.4 collective-permute-done.8.got_a
  44.7 0.7 collective-permute-done.9.got_b
  45.4 0.1 combine.3.own2
  45.5 5.3 %collective-permute-start.13 = (bf16[2048,128]{1,0:T(8,128)(2,1)S(1)}, bf16[2048,128]{1,0:T(8,128)(2,1)S(1)}, u32[]{:S(2)}, u32[]{:S(2)}) collective-permute-start(bf16[2048,128]{1,0:T(8,128)(2,1)S(1)} %combine.3.own2), channel_id=1, source_target_pairs={{4,0},{8,4},{12,8},{16,12},{20,16},{24,20},{28,24},{32,28},{36,32}... | collective-permute-start | bytes 1572872 | tf_op jit(solution)/shard_map/ppermute | solution.py:235
  50.8 0.0 collective-permute-start.11
  50.8 5.3 %collective-permute-done.12.r1 = bf16[2048,128]{1,0:T(8,128)(2,1)S(1)} collective-permute-done((bf16[2048,128]{1,0:T(8,128)(2,1)S(1)}, bf16[2048,128]{1,0:T(8,128)(2,1)S(1)}, u32[]{:S(2)}, u32[]{:S(2)}) %collective-permute-start.12) | collective-permute-done | bytes 524320 | tf_op jit(solution)/shard_map/ppermute | solution.py:229
  56.1 6.1 %collective-permute-done.10.l1 = bf16[2048,128]{1,0:T(8,128)(2,1)S(1)} collective-permute-done((bf16[2048,128]{1,0:T(8,128)(2,1)S(1)}, bf16[2048,128]{1,0:T(8,128)(2,1)S(1)}, u32[]{:S(2)}, u32[]{:S(2)}) %collective-permute-start.10) | collective-permute-done | bytes 524320 | tf_op jit(solution)/shard_map/ppermute | solution.py:228
  62.2 3.4 %collective-permute-done.13.r2 = bf16[2048,128]{1,0:T(8,128)(2,1)S(1)} collective-permute-done((bf16[2048,128]{1,0:T(8,128)(2,1)S(1)}, bf16[2048,128]{1,0:T(8,128)(2,1)S(1)}, u32[]{:S(2)}, u32[]{:S(2)}) %collective-permute-start.13) | collective-permute-done | bytes 524320 | tf_op jit(solution)/shard_map/ppermute | solution.py:235
  65.6 4.9 %collective-permute-done.11.l2 = bf16[2048,128]{1,0:T(8,128)(2,1)S(1)} collective-permute-done((bf16[2048,128]{1,0:T(8,128)(2,1)S(1)}, bf16[2048,128]{1,0:T(8,128)(2,1)S(1)}, u32[]{:S(2)}, u32[]{:S(2)}) %collective-permute-start.11) | collective-permute-done | bytes 524320 | tf_op jit(solution)/shard_map/ppermute | solution.py:234
  70.5 0.0 copy-done.2
  70.5 0.0 copy-done.6
  70.5 0.0 copy-done.7
  70.5 6.0 %impute.1 = bf16[8192,128]{1,0:T(8,128)(2,1)} custom-call(s32[8]{0:T(128)S(1)} %compare_select_fusion.3.place, s32[64]{0:T(128)S(1)} %copy-done.6, s32[64]{0:T(128)S(1)} %copy-done.7, bf16[2048,128]{1,0:T(8,128)(2,1)S(1)} %combine.2.own1, bf16[2048,128]{1,0:T(8,128)(2,1)S(1)} %combine.3.own2, bf16[2048,128]{1,0:T(8,128)(2,1)S(1)} %collective-permute-done.10.l1, ...), custom_call_target="tpu_custom_call" | custom-call | tf_op jit(solution)/shard_map/impute/pallas_call | solution.py:236
  (4 shorter events, 0.0 us)
Async XLA Ops:
  0.0 1.9 %copy-start = (bf16[32,128,384]{2,1,0:T(8,128)(2,1)S(1)}, bf16[32,128,384]{2,1,0:T(8,128)(2,1)}, u32[]{:S(2)}) copy-start(bf16[32,128,384]{2,1,0:T(8,128)(2,1)} %band.3) | copy-start | bytes 9437188
  1.9 1.2 %copy-start.3 = (bf16[4096,128]{1,0:T(8,128)(2,1)S(1)}, bf16[4096,128]{1,0:T(8,128)(2,1)}, u32[]{:S(2)}) copy-start(bf16[4096,128]{1,0:T(8,128)(2,1)} %z.3) | copy-start | bytes 3145732
  3.1 1.0 %copy-start.5 = (bf16[512,512]{1,0:T(8,128)(2,1)S(1)}, bf16[512,512]{1,0:T(8,128)(2,1)}, u32[]{:S(2)}) copy-start(bf16[512,512]{1,0:T(8,128)(2,1)} %mix.1) | copy-start | bytes 1572868
  4.2 17.8 %copy-start.1 = (bf16[32,128,384]{2,1,0:T(8,128)(2,1)S(1)}, bf16[32,128,384]{2,1,0:T(8,128)(2,1)}, u32[]{:S(2)}) copy-start(bf16[32,128,384]{2,1,0:T(8,128)(2,1)} %band.3) | copy-start | bytes 9437188
  4.2 17.8 %copy-start.4 = (bf16[4096,128]{1,0:T(8,128)(2,1)S(1)}, bf16[4096,128]{1,0:T(8,128)(2,1)}, u32[]{:S(2)}) copy-start(bf16[4096,128]{1,0:T(8,128)(2,1)} %z.3) | copy-start | bytes 3145732
  6.9 13.1 %collective-permute-start.2 = (bf16[1024,128]{1,0:T(8,128)(2,1)S(1)}, bf16[1024,128]{1,0:T(8,128)(2,1)S(1)}, u32[]{:S(2)}, u32[]{:S(2)}) collective-permute-start(bf16[1024,128]{1,0:T(8,128)(2,1)S(1)} %get-tuple-element.26.w_a), channel_id=1, source_target_pairs={{0,1},{1,0},{2,3},{3,2},{4,5},{5,4},{6,7},{7,6},{8,9},{9,8},{10,11... | collective-permute-start | bytes 786440 | tf_op jit(solution)/shard_map/ppermute | solution.py:184
  9.1 11.0 %collective-permute-start.3 = (bf16[1024,128]{1,0:T(8,128)(2,1)S(1)}, bf16[1024,128]{1,0:T(8,128)(2,1)S(1)}, u32[]{:S(2)}, u32[]{:S(2)}) collective-permute-start(bf16[1024,128]{1,0:T(8,128)(2,1)S(1)} %get-tuple-element.27.w_b), channel_id=1, source_target_pairs={{0,3},{1,2},{2,1},{3,0},{4,7},{5,6},{6,5},{7,4},{8,11},{9,10},{10,... | collective-permute-start | bytes 786440 | tf_op jit(solution)/shard_map/ppermute | solution.py:184
  10.9 10.8 %collective-permute-start = (bf16[128,128]{1,0:T(8,128)(2,1)S(1)}, bf16[128,128]{1,0:T(8,128)(2,1)S(1)}, u32[]{:S(2)}, u32[]{:S(2)}) collective-permute-start(bf16[128,128]{1,0:T(8,128)(2,1)S(1)} %get-tuple-element.24), channel_id=1, source_target_pairs={{0,4},{4,8},{8,12},{12,16},{16,20},{20,24},{24,28},{28,32},{32,36}... | collective-permute-start | bytes 98312 | tf_op jit(solution)/shard_map/ppermute | solution.py:208
  12.5 9.2 %collective-permute-start.1 = (bf16[128,128]{1,0:T(8,128)(2,1)S(1)}, bf16[128,128]{1,0:T(8,128)(2,1)S(1)}, u32[]{:S(2)}, u32[]{:S(2)}) collective-permute-start(bf16[128,128]{1,0:T(8,128)(2,1)S(1)} %get-tuple-element.25), channel_id=1, source_target_pairs={{4,0},{8,4},{12,8},{16,12},{20,16},{24,20},{28,24},{32,28},{36,32}... | collective-permute-start | bytes 98312 | tf_op jit(solution)/shard_map/ppermute | solution.py:209
  20.7 9.6 %collective-permute-start.6 = (bf16[1024,128]{1,0:T(8,128)(2,1)S(1)}, bf16[1024,128]{1,0:T(8,128)(2,1)S(1)}, u32[]{:S(2)}, u32[]{:S(2)}) collective-permute-start(bf16[1024,128]{1,0:T(8,128)(2,1)S(1)} %get-tuple-element.30), channel_id=1, source_target_pairs={{0,3},{1,2},{2,1},{3,0},{4,7},{5,6},{6,5},{7,4},{8,11},{9,10},{10,... | collective-permute-start | bytes 786440 | tf_op jit(solution)/shard_map/ppermute | solution.py:184
  21.7 7.7 %collective-permute-start.7 = (bf16[1024,128]{1,0:T(8,128)(2,1)S(1)}, bf16[1024,128]{1,0:T(8,128)(2,1)S(1)}, u32[]{:S(2)}, u32[]{:S(2)}) collective-permute-start(bf16[1024,128]{1,0:T(8,128)(2,1)S(1)} %get-tuple-element.36), channel_id=1, source_target_pairs={{0,1},{1,0},{2,3},{3,2},{4,5},{5,4},{6,7},{7,6},{8,9},{9,8},{10,11... | collective-permute-start | bytes 786440 | tf_op jit(solution)/shard_map/ppermute | solution.py:184
  21.9 48.5 %copy-start.2 = (bf16[64,128,512]{2,1,0:T(8,128)(2,1)S(1)}, bf16[64,128,512]{2,1,0:T(8,128)(2,1)}, u32[]{:S(2)}) copy-start(bf16[64,128,512]{2,1,0:T(8,128)(2,1)} %ld.1) | copy-start | bytes 25165828
  23.4 47.1 %copy-start.6 = (s32[64]{0:T(128)S(1)}, s32[64]{0:T(128)}, u32[]{:S(2)}) copy-start(s32[64]{0:T(128)} %starts.1) | copy-start | bytes 772
  23.4 47.1 %copy-start.7 = (s32[64]{0:T(128)S(1)}, s32[64]{0:T(128)}, u32[]{:S(2)}) copy-start(s32[64]{0:T(128)} %counts.1) | copy-start | bytes 772
  23.4 11.6 %collective-permute-start.4 = (bf16[1024,128]{1,0:T(8,128)(2,1)S(1)}, bf16[1024,128]{1,0:T(8,128)(2,1)S(1)}, u32[]{:S(2)}, u32[]{:S(2)}) collective-permute-start(bf16[1024,128]{1,0:T(8,128)(2,1)S(1)} %get-tuple-element.33.w_a), channel_id=1, source_target_pairs={{0,1},{1,0},{2,3},{3,2},{4,5},{5,4},{6,7},{7,6},{8,9},{9,8},{10,11... | collective-permute-start | bytes 786440 | tf_op jit(solution)/shard_map/ppermute | solution.py:184
  24.7 10.8 %collective-permute-start.5 = (bf16[1024,128]{1,0:T(8,128)(2,1)S(1)}, bf16[1024,128]{1,0:T(8,128)(2,1)S(1)}, u32[]{:S(2)}, u32[]{:S(2)}) collective-permute-start(bf16[1024,128]{1,0:T(8,128)(2,1)S(1)} %get-tuple-element.34.w_b), channel_id=1, source_target_pairs={{0,3},{1,2},{2,1},{3,0},{4,7},{5,6},{6,5},{7,4},{8,11},{9,10},{10,... | collective-permute-start | bytes 786440 | tf_op jit(solution)/shard_map/ppermute | solution.py:184
  36.1 8.6 %collective-permute-start.8 = (bf16[1024,128]{1,0:T(8,128)(2,1)S(1)}, bf16[1024,128]{1,0:T(8,128)(2,1)S(1)}, u32[]{:S(2)}, u32[]{:S(2)}) collective-permute-start(bf16[1024,128]{1,0:T(8,128)(2,1)S(1)} %get-tuple-element.41), channel_id=1, source_target_pairs={{0,3},{1,2},{2,1},{3,0},{4,7},{5,6},{6,5},{7,4},{8,11},{9,10},{10,... | collective-permute-start | bytes 786440 | tf_op jit(solution)/shard_map/ppermute | solution.py:184
  38.2 7.2 %collective-permute-start.9 = (bf16[1024,128]{1,0:T(8,128)(2,1)S(1)}, bf16[1024,128]{1,0:T(8,128)(2,1)S(1)}, u32[]{:S(2)}, u32[]{:S(2)}) collective-permute-start(bf16[1024,128]{1,0:T(8,128)(2,1)S(1)} %get-tuple-element.42), channel_id=1, source_target_pairs={{0,1},{1,0},{2,3},{3,2},{4,5},{5,4},{6,7},{7,6},{8,9},{9,8},{10,11... | collective-permute-start | bytes 786440 | tf_op jit(solution)/shard_map/ppermute | solution.py:184
  38.2 17.8 %collective-permute-start.12 = (bf16[2048,128]{1,0:T(8,128)(2,1)S(1)}, bf16[2048,128]{1,0:T(8,128)(2,1)S(1)}, u32[]{:S(2)}, u32[]{:S(2)}) collective-permute-start(bf16[2048,128]{1,0:T(8,128)(2,1)S(1)} %combine.2.own1), channel_id=1, source_target_pairs={{4,0},{8,4},{12,8},{16,12},{20,16},{24,20},{28,24},{32,28},{36,32}... | collective-permute-start | bytes 1572872 | tf_op jit(solution)/shard_map/ppermute | solution.py:229
  44.3 17.9 %collective-permute-start.10 = (bf16[2048,128]{1,0:T(8,128)(2,1)S(1)}, bf16[2048,128]{1,0:T(8,128)(2,1)S(1)}, u32[]{:S(2)}, u32[]{:S(2)}) collective-permute-start(bf16[2048,128]{1,0:T(8,128)(2,1)S(1)} %combine.2.own1), channel_id=1, source_target_pairs={{0,4},{4,8},{8,12},{12,16},{16,20},{20,24},{24,28},{28,32},{32,36}... | collective-permute-start | bytes 1572872 | tf_op jit(solution)/shard_map/ppermute | solution.py:228
  45.5 20.1 %collective-permute-start.13 = (bf16[2048,128]{1,0:T(8,128)(2,1)S(1)}, bf16[2048,128]{1,0:T(8,128)(2,1)S(1)}, u32[]{:S(2)}, u32[]{:S(2)}) collective-permute-start(bf16[2048,128]{1,0:T(8,128)(2,1)S(1)} %combine.3.own2), channel_id=1, source_target_pairs={{4,0},{8,4},{12,8},{16,12},{20,16},{24,20},{28,24},{32,28},{36,32}... | collective-permute-start | bytes 1572872 | tf_op jit(solution)/shard_map/ppermute | solution.py:235
  50.8 19.7 %collective-permute-start.11 = (bf16[2048,128]{1,0:T(8,128)(2,1)S(1)}, bf16[2048,128]{1,0:T(8,128)(2,1)S(1)}, u32[]{:S(2)}, u32[]{:S(2)}) collective-permute-start(bf16[2048,128]{1,0:T(8,128)(2,1)S(1)} %combine.3.own2), channel_id=1, source_target_pairs={{0,4},{4,8},{8,12},{12,16},{16,20},{20,24},{24,28},{28,32},{32,36}... | collective-permute-start | bytes 1572872 | tf_op jit(solution)/shard_map/ppermute | solution.py:234

commit v2 on v0

v2 whole, which is shorter than its diff:
```python
import jax
import jax.numpy as jnp
from jax import lax
from jax.experimental import pallas as pl
from jax.experimental.pallas import tpu as pltpu
from jax.sharding import PartitionSpec as P

BLK = 128
WIN = 4
COLS = 128
TB = 32
UB = 64
EXT = 3 * TB + WIN - 1
UNROLL = 4
BF = jnp.bfloat16
F32 = jnp.float32
ROWS = ("sec", "var")
HBM = pl.BlockSpec(memory_space=pltpu.HBM)
SMEM = pl.BlockSpec(memory_space=pltpu.SMEM)
VM = pl.BlockSpec(memory_space=pltpu.VMEM)
PARAMS = pltpu.CompilerParams(vmem_limit_bytes=40 * 1024 * 1024)
MID = 8
MID_END = 24
HALF1 = (MID_END - MID) // 2
HALF2 = MID - 1


def shaped(blocks, dtype=BF):
    return jax.ShapeDtypeStruct((blocks * BLK, COLS), dtype)


def dot(left, right):
    return jnp.dot(left, right, preferred_element_type=F32)


def at(block, blocks=1):
    start = block * BLK
    return pl.ds(start if isinstance(start, int) else pl.multiple_of(start, BLK), blocks * BLK)


def copy_all(pairs, sems, first=0):
    copies = [pltpu.make_async_copy(a, b, sems.at[first + k]) for k, (a, b) in enumerate(pairs)]
    for copy in copies:
        copy.start()
    return copies


def pieces(blocks):
    return [(k, min(4, blocks - k)) for k in range(0, blocks, 4)]


def whiten_1(place, z, band, mix, w_a, w_b, halo_e, halo_o, mix_a, mix_b, zs, bs, sems):
    zcopy = copy_all([(z.at[at(MID - 1, 2 * HALF1 + 2)], zs)], sems)
    cuts = pieces(2 * HALF1)
    bands = copy_all([(band.at[pl.ds(MID + k, n)], bs.at[pl.ds(k, n)]) for k, n in cuts], sems, 1)
    t, a, b, odd = place[0], place[1], place[2], place[5]
    pairs = [(z.at[at((1 - odd) * (TB - 1))], halo_e), (z.at[at(odd * (TB - 1))], halo_o)]
    for target, near, far in ((mix_a, a, b), (mix_b, b, a)):
        for i, row in enumerate((t, near)):
            for j, col in enumerate((t, far)):
                pairs.append((mix.at[at(row), at(col)], target.at[at(i), at(j)]))
    others = copy_all(pairs, sems, 1 + len(cuts))
    zcopy[0].wait()
    for (k, n), copy in zip(cuts, bands):
        copy.wait()
        for i in range(k, k + n):
            w = w_a if i < HALF1 else w_b
            w[at(i % HALF1), :] = dot(bs[i], zs[at(i, 3), :]).astype(BF)
    for copy in others:
        copy.wait()


def whiten_2(z, band, w_a, w_b, zs, bs, sems):
    zcopies = copy_all(
        [
            (z.at[at(0, HALF2 + 2)], zs.at[at(0, HALF2 + 2)]),
            (z.at[at(MID_END - 1, HALF2 + 2)], zs.at[at(HALF2 + 2, HALF2 + 2)]),
        ],
        sems,
    )
    cuts = [(side, k, n) for side in range(2) for k, n in pieces(HALF2)]
    bands = copy_all(
        [(band.at[pl.ds((1, MID_END)[side] + k, n)], bs.at[pl.ds(side * HALF2 + k, n)]) for side, k, n in cuts], sems, 2
    )
    for (side, k, n), copy in zip(cuts, bands):
        if k == 0:
            zcopies[side].wait()
        copy.wait()
        for i in range(k, k + n):
            rows = dot(bs[side * HALF2 + i], zs[at(side * (HALF2 + 2) + i, 3), :])
            (w_a, w_b)[side][at(i), :] = rows.astype(BF)


def sums(own_rows, got_rows, mix):
    return dot(own_rows, mix[pl.ds(0, COLS), :]) + dot(got_rows, mix[pl.ds(COLS, COLS), :])


def partial_1(w_a, got_a, w_b, got_b, mix_a, mix_b, send_a, send_b, own):
    for k, (w, got, mix, send) in enumerate(((w_a, got_a, mix_a, send_a), (w_b, got_b, mix_b, send_b))):
        both = sums(w[...], got[...], mix)
        own[at(k * HALF1, HALF1), :] = both[:, :COLS]
        send[...] = both[:, COLS:].astype(BF)


def partial_2(
    place, z, band, halo_e, halo_o, w_a, got_a, w_b, got_b, mix_a, mix_b, send_a, send_b, own, zs, bs, sems
):
    copies = copy_all(
        [
            (z.at[at(0, 2)], zs.at[at(1, 2)]),
            (z.at[at(TB - 2, 2)], zs.at[at(3, 2)]),
            (band.at[0], bs.at[0]),
            (band.at[TB - 1], bs.at[1]),
        ],
        sems,
    )
    for k, (w, got, mix, send) in enumerate(((w_a, got_a, mix_a, send_a), (w_b, got_b, mix_b, send_b))):
        both = sums(w[...], got[...], mix)
        own[at(k * HALF2, HALF2), :] = both[:, :COLS]
        send[at(0, HALF2), :] = both[:, COLS:].astype(BF)
    odd = place[5] == 1
    nothing = jnp.zeros((BLK, COLS), BF)
    from_left = jnp.where(odd, halo_e[...], halo_o[...])
    from_right = jnp.where(odd, halo_o[...], halo_e[...])
    zs[at(0), :] = jnp.where(place[3] == 0, nothing, from_left)
    zs[at(5), :] = jnp.where(place[3] == place[4] - 1, nothing, from_right)
    for copy in copies:
        copy.wait()
    send_a[at(HALF2), :] = dot(bs[0], zs[at(0, 3), :]).astype(BF)
    send_b[at(HALF2), :] = dot(bs[1], zs[at(3, 3), :]).astype(BF)


def combine_1(own, far_a, far_b, out):
    for k, far in enumerate((far_a, far_b)):
        out[at(k * HALF1, HALF1), :] = (own[at(k * HALF1, HALF1), :] + far[...].astype(F32)).astype(BF)


def combine_2(own, far_a, far_b, sent_a, sent_b, mix_a, mix_b, out, send_first, send_last, own_edge):
    for k, (far, sent, mix, send) in enumerate(((far_a, sent_a, mix_b, send_first), (far_b, sent_b, mix_a, send_last))):
        both = sums(sent[at(HALF2), :], far[at(HALF2), :], mix)
        own_edge[at(k), :] = both[:, :COLS]
        send[...] = both[:, COLS:].astype(BF)
        out[at(k * HALF2, HALF2), :] = (own[at(k * HALF2, HALF2), :] + far[at(0, HALF2), :].astype(F32)).astype(BF)


def combine_edge(own, far_first, far_last, out):
    for k, far in enumerate((far_first, far_last)):
        out[at(k), :] = (own[at(k), :] + far[...].astype(F32)).astype(BF)


def to_out(u, n, out, staged, sems):
    return pltpu.make_async_copy(staged.at[n], out.at[at(u)], sems.at[n])


def on_list(index, count, starts, counts, lowest, ld, ext, out, staged, sems):
    def several(k, carry):
        for i in range(UNROLL):
            u = index[jnp.minimum(UNROLL * k + i, count - 1)]
            first = jnp.clip(starts[u] - lowest, 0, 3 * TB - 1)
            have = counts[u]
            rows = ld[u]
            kept = [rows[:, :BLK]]
            for s in range(1, WIN):
                part = rows[:, s * BLK : (s + 1) * BLK]
                kept.append(jnp.where(s < have, part, jnp.zeros_like(part)))
            staged[UNROLL * k + i] = dot(jnp.concatenate(kept, axis=1), ext[at(first, WIN), :]).astype(BF)
        for i in range(UNROLL):
            n = UNROLL * k + i

            @pl.when(n < count)
            def _():
                to_out(index[n], n, out, staged, sems).start()

        return carry

    def finish(n, carry):
        to_out(index[n], n, out, staged, sems).wait()
        return carry

    lax.fori_loop(0, (count + UNROLL - 1) // UNROLL, several, 0)
    lax.fori_loop(0, count, finish, 0)


def set_1(ext, base, mid):
    return [(mid, ext.at[at(base + MID, 2 * HALF1)])]


def set_2(ext, base, rest, edge):
    return [
        (edge.at[at(0)], ext.at[at(base)]),
        (rest.at[at(0, HALF2)], ext.at[at(base + 1, HALF2)]),
        (rest.at[at(HALF2, HALF2)], ext.at[at(base + MID_END, HALF2)]),
        (edge.at[at(1)], ext.at[at(base + TB - 1)]),
    ]


def impute_ready(
    place, starts, counts, mid, rest, edge, mid_e, mid_o, ld, ext, late, out, ready, staged, sems, out_sems
):
    base_e = 2 * TB * (1 - place[5])
    base_o = 2 * TB * place[5]
    copies = copy_all(
        set_1(ext, TB, mid) + set_2(ext, TB, rest, edge) + set_1(ext, base_e, mid_e) + set_1(ext, base_o, mid_o), sems
    )
    ext[at(3 * TB, WIN - 1), :] = jnp.zeros(((WIN - 1) * BLK, COLS), BF)
    for k in (0, MID_END, 2 * TB, 2 * TB + MID_END):
        ext[at(k, MID), :] = jnp.zeros((MID * BLK, COLS), BF)
    lowest = place[3] * TB - TB

    def sort(u, sizes):
        now, later = sizes
        first = jnp.clip(starts[u] - lowest, 0, 3 * TB - 1)
        last = first + counts[u] - 1
        waits = first < MID
        for low, high in ((MID_END, TB), (2 * TB, 2 * TB + MID), (2 * TB + MID_END, 3 * TB)):
            waits = waits | ((last >= low) & (first < high))
        waits = waits.astype(jnp.int32)
        ready[now] = u
        late[later] = u
        return now + 1 - waits, later + waits

    now, later = lax.fori_loop(0, UB, sort, (0, 0))
    late[UB + 1] = later
    for copy in copies:
        copy.wait()

    @pl.when(now > 0)
    def _():
        on_list(ready, now, starts, counts, lowest, ld, ext, out, staged, out_sems)


def impute_late(
    place, starts, counts, late, rest_e, rest_o, edge_e, edge_o, ld, before, done, ext, out, staged, sems, out_sems
):
    base_e = 2 * TB * (1 - place[5])
    base_o = 2 * TB * place[5]
    copies = copy_all(set_2(ext, base_e, rest_e, edge_e) + set_2(ext, base_o, rest_o, edge_o), sems)
    count = late[UB + 1]
    for copy in copies:
        copy.wait()

    @pl.when(count > 0)
    def _():
        on_list(late, count, starts, counts, place[3] * TB - TB, ld, ext, out, staged, out_sems)


def call(kernel, outs, ins, args, scratch=(), aliases=None):
    return pl.pallas_call(
        kernel,
        name=kernel.__name__,
        out_shape=tuple(shape for shape, _ in outs),
        in_specs=ins,
        out_specs=tuple(spec for _, spec in outs),
        scratch_shapes=list(scratch),
        input_output_aliases=aliases or {},
        compiler_params=PARAMS,
    )(*args)


def in_vmem(*shapes):
    return [(shape, VM) for shape in shapes]


def on_device(z, band, ld, mix, starts, counts):
    t = lax.axis_index("trait")
    g = lax.axis_index(ROWS)
    owners = lax.axis_size(ROWS)
    lane = lax.iota(jnp.int32, 8)
    place = jnp.zeros((8,), jnp.int32)
    for k, value in enumerate((t, t ^ 1, 3 - t, g, owners, g % 2)):
        place = jnp.where(lane == k, value, place)
    pairs_a = [(i, i ^ 1) for i in range(4)]
    pairs_b = [(i, 3 - i) for i in range(4)]
    pairs_e = [(i, i ^ 1) for i in range(owners)]
    pairs_o = [(i, (i + 1) % owners if i % 2 else (i - 1) % owners) for i in range(owners)]

    def along_trait(x, y, pairs_x, pairs_y):
        return lax.ppermute(x, "trait", pairs_x), lax.ppermute(y, "trait", pairs_y)

    def along_rows(x, y):
        return lax.ppermute(x, ROWS, pairs_e), lax.ppermute(y, ROWS, pairs_o)

    z, band, mix = (pltpu.with_memory_space_constraint(x, pltpu.HBM) for x in (z, band, mix))
    mix_part = jax.ShapeDtypeStruct((2 * COLS, 2 * COLS), BF)
    w1a, w1b, halo_e, halo_o, mix_a, mix_b = call(
        whiten_1,
        in_vmem(shaped(HALF1), shaped(HALF1), shaped(1), shaped(1), mix_part, mix_part),
        [SMEM, HBM, HBM, HBM],
        (place, z, band, mix),
        [
            pltpu.VMEM(((2 * HALF1 + 2) * BLK, COLS), BF),
            pltpu.VMEM((2 * HALF1, BLK, 3 * BLK), BF),
            pltpu.SemaphoreType.DMA((11 + len(pieces(2 * HALF1)),)),
        ],
    )
    got1a, got1b = along_trait(w1a, w1b, pairs_a, pairs_b)
    z, _ = lax.optimization_barrier((z, w1a))
    w2a, w2b = call(
        whiten_2,
        in_vmem(shaped(HALF2), shaped(HALF2)),
        [HBM, HBM],
        (z, band),
        [
            pltpu.VMEM(((2 * HALF2 + 4) * BLK, COLS), BF),
            pltpu.VMEM((2 * HALF2, BLK, 3 * BLK), BF),
            pltpu.SemaphoreType.DMA((2 + 2 * len(pieces(HALF2)),)),
        ],
    )
    got2a, got2b = along_trait(w2a, w2b, pairs_a, pairs_b)
    halo_e, halo_o, _ = lax.optimization_barrier((halo_e, halo_o, w2a))
    halo_e, halo_o = along_rows(halo_e, halo_o)
    send1a, send1b, own1 = call(
        partial_1,
        in_vmem(shaped(HALF1), shaped(HALF1), shaped(2 * HALF1, F32)),
        [VM] * 6,
        (w1a, got1a, w1b, got1b, mix_a, mix_b),
    )
    far1a, far1b = along_trait(send1a, send1b, pairs_b, pairs_a)
    got2a, got2b, halo_e, halo_o, _ = lax.optimization_barrier((got2a, got2b, halo_e, halo_o, send1a))
    send2a, send2b, own2 = call(
        partial_2,
        in_vmem(shaped(HALF2 + 1), shaped(HALF2 + 1), shaped(2 * HALF2, F32)),
        [SMEM, HBM, HBM] + [VM] * 8,
        (place, z, band, halo_e, halo_o, w2a, got2a, w2b, got2b, mix_a, mix_b),
        [
            pltpu.VMEM((6 * BLK, COLS), BF),
            pltpu.VMEM((2, BLK, 3 * BLK), BF),
            pltpu.SemaphoreType.DMA((4,)),
        ],
    )
    far2a, far2b = along_trait(send2a, send2b, pairs_b, pairs_a)
    far1a, far1b, _ = lax.optimization_barrier((far1a, far1b, send2a))
    (mixed1,) = call(combine_1, in_vmem(shaped(2 * HALF1)), [VM] * 3, (own1, far1a, far1b))
    mid_e, mid_o = along_rows(mixed1, mixed1)
    far2a, far2b, _ = lax.optimization_barrier((far2a, far2b, mixed1))
    mixed2, send_first, send_last, own_edge = call(
        combine_2,
        in_vmem(shaped(2 * HALF2), shaped(1), shaped(1), shaped(2, F32)),
        [VM] * 7,
        (own2, far2a, far2b, send2a, send2b, mix_a, mix_b),
    )
    far_first, far_last = along_trait(send_first, send_last, pairs_a, pairs_b)
    rest_e, rest_o = along_rows(mixed2, mixed2)
    (mixed3,) = call(combine_edge, in_vmem(shaped(2)), [VM] * 3, (own_edge, far_first, far_last))
    edge_e, edge_o = along_rows(mixed3, mixed3)
    window_scratch = [
        pltpu.VMEM((UB, BLK, COLS), BF),
        pltpu.SemaphoreType.DMA((8,)),
        pltpu.SemaphoreType.DMA((UB,)),
    ]
    ext, late, done = call(
        impute_ready,
        [(shaped(EXT), VM), (jax.ShapeDtypeStruct((UB + 2,), jnp.int32), SMEM), (shaped(UB), HBM)],
        [SMEM] * 3 + [VM] * 6,
        (place, starts, counts, mixed1, mixed2, mixed3, mid_e, mid_o, ld),
        [pltpu.SMEM((UB + 1,), jnp.int32)] + window_scratch,
    )
    _, out = call(
        impute_late,
        [(shaped(EXT), VM), (shaped(UB), HBM)],
        [SMEM] * 4 + [VM] * 6 + [HBM],
        (place, starts, counts, late, rest_e, rest_o, edge_e, edge_o, ld, ext, done),
        window_scratch,
        {9: 0, 10: 1},
    )
    return out


def solution(mesh):
    in_specs = (
        P(ROWS, "trait"),
        P(ROWS, None, None),
        P(ROWS, None, None),
        P(),
        P(ROWS),
        P(ROWS),
    )
    return jax.shard_map(on_device, mesh=mesh, in_specs=in_specs, out_specs=P(ROWS, "trait"), check_vma=False)
```

time: 152 us -> 71 us (0.47); the launches traced: 150 us -> 70.9 us
  waiting for transfers between devices: 73.7 us -> 11.6 us
  Pallas kernels: 0 us -> 21.3 us
  matrix products: 14.7 us -> 0 us
  starting transfers between devices: 23.8 us -> 37.8 us
  between operations: 13.5 us -> 0.17 us
  other arithmetic: 12.2 us -> 0.01 us
  local copies, waits for them, and re-layouts: 11.7 us -> 0.02 us
    all_gather x1 -> x0, waiting for transfers between devices: 52.8 us -> none  [on_device(): lax.all_gather(whitened_rows, 'trait', axis=1, tiled=True)]
    pallas_call x0 -> x9, Pallas kernels: none -> 21.3 us  [call(): pl.pallas_call(kernel, name=kernel.__name__, out_shape=tuple((shape for s...]
    dot_general x3 -> x0, matrix products: 14.7 us -> none  [the longest x1 7.04 us: on_device(): jnp.einsum('uij,ujc->uic', ld_untyped, window_rows, preferred_element_typ...]
    ppermute x4 -> x18, starting transfers between devices: 23.8 us -> 37.8 us  [the longest x8 26.3 us: along_rows(): return (lax.ppermute(x, ROWS, pairs_e), lax.ppermute(y, ROWS, pairs_o))]
    gather x1 -> x0, local copies, waits for them, and re-layouts: 10.5 us -> none  [on_device(): picked = extended[wanted]]
    ppermute x4 -> x18, waiting for transfers between devices: 20.9 us -> 11.6 us  [the longest x5 4.95 us: along_trait(): lax.ppermute(x, 'trait', pairs_x)]
    select_n x2 -> x1, other arithmetic: 7.09 us -> 0.01 us  [on_device(): place = jnp.where(lane == k, value, place)]
    concatenate x2 -> x0, other arithmetic: 4.97 us -> none  [padded_2(): jnp.concatenate([lax.ppermute(tail, axis, [(i, (i + 1) % count) for i in...]
  transfers between devices with their start and end apart: 5 -> 18, of which waited for: 4 -> 6; matrix products, arithmetic and copies ran while one was open for 0% -> 0% of each run, Pallas kernels for 0% -> 19%
where the time goes in v2:
time: 71 us; the launch traced here: 70.9 us
  starting transfers between devices  37.8 us (53%)
  Pallas kernels  21.3 us (30%)
  waiting for transfers between devices  11.6 us (16%)
    ppermute x8, starting transfers between devices, along_rows(): return (lax.ppermute(x, ROWS, pairs_e), lax.ppermute(y, ROWS, pairs_o))  26.3 us
    pallas_call x9, Pallas kernels, call(): pl.pallas_call(kernel, name=kernel.__name__, out_shape=tuple((shape for s...  21.3 us
    ppermute x5, starting transfers between devices, along_trait(): lax.ppermute(y, 'trait', pairs_y)  7.35 us
    ppermute x5, waiting for transfers between devices, along_trait(): lax.ppermute(x, 'trait', pairs_x)  4.95 us
    ppermute x5, starting transfers between devices, along_trait(): lax.ppermute(x, 'trait', pairs_x)  4.11 us
    ppermute x5, waiting for transfers between devices, along_trait(): lax.ppermute(y, 'trait', pairs_y)  3.43 us
    ppermute x8, waiting for transfers between devices, along_rows(): return (lax.ppermute(x, ROWS, pairs_e), lax.ppermute(y, ROWS, pairs_o))  3.21 us
  transfers between devices with their start and end apart: 18, of which 6 were waited for; matrix products, arithmetic and copies ran while one was open for 0% of the time, Pallas kernels for 19%

profile of v2, /device:TPU:1, one launch (start us, length us, event | category | flops | bytes accessed | tf_op | source)
XLA Modules:
  0.0 70.9 jit_solution(6544990475917892876)
XLA Ops:
  0.0 2.9 %whiten_1.1 = (bf16[1024,128]{1,0:T(8,128)(2,1)S(1)}, bf16[1024,128]{1,0:T(8,128)(2,1)S(1)}, bf16[128,128]{1,0:T(8,128)(2,1)S(1)}, bf16[128,128]{1,0:T(8,128)(2,...) custom-call(s32[8]{0:T(128)S(1)} %compare_select_fusion.5.place, bf16[4096,128]{1,0:T(8,128)(2,1)} %z.3, ...), custom_call_target="tpu_custom_call" | custom-call | tf_op jit(solution)/shard_map/whiten_1/pallas_call | solution.py:248
  2.9 3.4 %collective-permute-start.1 = (bf16[1024,128]{1,0:T(8,128)(2,1)S(1)}, bf16[1024,128]{1,0:T(8,128)(2,1)S(1)}, u32[]{:S(2)}, u32[]{:S(2)}) collective-permute-start(bf16[1024,128]{1,0:T(8,128)(2,1)S(1)} %get-tuple-element.39.w_b), channel_id=1, source_target_pairs={{0,3},{1,2},{2,1},{3,0},{4,7},{5,6},{6,5},{7,4},{8,11},{9,10},{10,... | collective-permute-start | bytes 786440 | tf_op jit(solution)/shard_map/ppermute | solution.py:278
  6.3 0.0 collective-permute-start
  6.3 2.4 %whiten_2.1 = (bf16[896,128]{1,0:T(8,128)(2,1)S(1)}, bf16[896,128]{1,0:T(8,128)(2,1)S(1)}) custom-call(bf16[4096,128]{1,0:T(8,128)(2,1)} %z.3, bf16[32,128,384]{2,1,0:T(8,128)(2,1)} %band.5), custom_call_target="tpu_custom_call" | custom-call | tf_op jit(solution)/shard_map/whiten_2/pallas_call | solution.py:248
  8.7 0.9 %collective-permute-start.5 = (bf16[896,128]{1,0:T(8,128)(2,1)S(1)}, bf16[896,128]{1,0:T(8,128)(2,1)S(1)}, u32[]{:S(2)}, u32[]{:S(2)}) collective-permute-start(bf16[896,128]{1,0:T(8,128)(2,1)S(1)} %get-tuple-element.47.w_b), channel_id=1, source_target_pairs={{0,3},{1,2},{2,1},{3,0},{4,7},{5,6},{6,5},{7,4},{8,11},{9,10},{10,... | collective-permute-start | bytes 688136 | tf_op jit(solution)/shard_map/ppermute | solution.py:278
  9.6 0.8 %collective-permute-start.4 = (bf16[896,128]{1,0:T(8,128)(2,1)S(1)}, bf16[896,128]{1,0:T(8,128)(2,1)S(1)}, u32[]{:S(2)}, u32[]{:S(2)}) collective-permute-start(bf16[896,128]{1,0:T(8,128)(2,1)S(1)} %get-tuple-element.46.w_a), channel_id=1, source_target_pairs={{0,1},{1,0},{2,3},{3,2},{4,5},{5,4},{6,7},{7,6},{8,9},{9,8},{10,11... | collective-permute-start | bytes 688136 | tf_op jit(solution)/shard_map/ppermute | solution.py:278
  10.4 0.9 %collective-permute-done.1.got_b = bf16[1024,128]{1,0:T(8,128)(2,1)S(1)} collective-permute-done((bf16[1024,128]{1,0:T(8,128)(2,1)S(1)}, bf16[1024,128]{1,0:T(8,128)(2,1)S(1)}, u32[]{:S(2)}, u32[]{:S(2)}) %collective-permute-start.1) | collective-permute-done | bytes 262176 | tf_op jit(solution)/shard_map/ppermute | solution.py:278
  11.3 1.9 %collective-permute-done.got_a = bf16[1024,128]{1,0:T(8,128)(2,1)S(1)} collective-permute-done((bf16[1024,128]{1,0:T(8,128)(2,1)S(1)}, bf16[1024,128]{1,0:T(8,128)(2,1)S(1)}, u32[]{:S(2)}, u32[]{:S(2)}) %collective-permute-start) | collective-permute-done | bytes 262176 | tf_op jit(solution)/shard_map/ppermute | solution.py:278
  13.2 0.7 partial_1.1
  13.9 0.2 collective-permute-start.3
  14.0 1.6 %collective-permute-start.2 = (bf16[1024,128]{1,0:T(8,128)(2,1)S(1)}, bf16[1024,128]{1,0:T(8,128)(2,1)S(1)}, u32[]{:S(2)}, u32[]{:S(2)}) collective-permute-start(bf16[1024,128]{1,0:T(8,128)(2,1)S(1)} %get-tuple-element.43), channel_id=1, source_target_pairs={{0,3},{1,2},{2,1},{3,0},{4,7},{5,6},{6,5},{7,4},{8,11},{9,10},{10,... | collective-permute-start | bytes 786440 | tf_op jit(solution)/shard_map/ppermute | solution.py:278
  15.6 1.6 %collective-permute-start.6 = (bf16[128,128]{1,0:T(8,128)(2,1)S(1)}, bf16[128,128]{1,0:T(8,128)(2,1)S(1)}, u32[]{:S(2)}, u32[]{:S(2)}) collective-permute-start(bf16[128,128]{1,0:T(8,128)(2,1)S(1)} %get-tuple-element.50), channel_id=1, source_target_pairs={{0,4},{4,0},{8,12},{12,8},{16,20},{20,16},{24,28},{28,24},{32,36},... | collective-permute-start | bytes 98312 | tf_op jit(solution)/shard_map/ppermute | solution.py:281
  17.2 1.6 %collective-permute-done.6.halo_e = bf16[128,128]{1,0:T(8,128)(2,1)S(1)} collective-permute-done((bf16[128,128]{1,0:T(8,128)(2,1)S(1)}, bf16[128,128]{1,0:T(8,128)(2,1)S(1)}, u32[]{:S(2)}, u32[]{:S(2)}) %collective-permute-start.6) | collective-permute-done | bytes 32800 | tf_op jit(solution)/shard_map/ppermute | solution.py:281
  18.8 11.6 %collective-permute-start.7 = (bf16[128,128]{1,0:T(8,128)(2,1)S(1)}, bf16[128,128]{1,0:T(8,128)(2,1)S(1)}, u32[]{:S(2)}, u32[]{:S(2)}) collective-permute-start(bf16[128,128]{1,0:T(8,128)(2,1)S(1)} %get-tuple-element.51), channel_id=1, source_target_pairs={{0,252},{4,8},{8,4},{12,16},{16,12},{20,24},{24,20},{28,32},{32,28... | collective-permute-start | bytes 98312 | tf_op jit(solution)/shard_map/ppermute | solution.py:281
  30.4 1.6 %collective-permute-done.7.halo_o = bf16[128,128]{1,0:T(8,128)(2,1)S(1)} collective-permute-done((bf16[128,128]{1,0:T(8,128)(2,1)S(1)}, bf16[128,128]{1,0:T(8,128)(2,1)S(1)}, u32[]{:S(2)}, u32[]{:S(2)}) %collective-permute-start.7) | collective-permute-done | bytes 32800 | tf_op jit(solution)/shard_map/ppermute | solution.py:281
  32.0 0.0 collective-permute-done.5.got_b
  32.0 0.0 collective-permute-done.4.got_a
  32.0 2.2 %partial_2.1 = (bf16[1024,128]{1,0:T(8,128)(2,1)S(1)}, bf16[1024,128]{1,0:T(8,128)(2,1)S(1)}, f32[1792,128]{1,0:T(8,128)S(1)}) custom-call(s32[8]{0:T(128)S(1)} %compare_select_fusion.5.place, bf16[4096,128]{1,0:T(8,128)(2,1)} %z.3, bf16[32,128,384]{2,1,0:T(8,128)(2,1)} %band.5, bf16[128,128]{1,0:T(8,128)(2,1)S(1)} %collective-permute-done.6.halo_e, ...), custom_call_target="tpu_custom_call" | custom-call | tf_op jit(solution)/shard_map/partial_2/pallas_call | solution.py:248
  34.3 0.0 copy-start
  34.3 0.0 copy-start.1
  34.3 1.1 %collective-permute-start.9 = (bf16[1024,128]{1,0:T(8,128)(2,1)S(1)}, bf16[1024,128]{1,0:T(8,128)(2,1)S(1)}, u32[]{:S(2)}, u32[]{:S(2)}) collective-permute-start(bf16[1024,128]{1,0:T(8,128)(2,1)S(1)} %get-tuple-element.60.sent_b), channel_id=1, source_target_pairs={{0,1},{1,0},{2,3},{3,2},{4,5},{5,4},{6,7},{7,6},{8,9},{9,8},{10,11... | collective-permute-start | bytes 786440 | tf_op jit(solution)/shard_map/ppermute | solution.py:278
  35.4 1.8 %collective-permute-start.8 = (bf16[1024,128]{1,0:T(8,128)(2,1)S(1)}, bf16[1024,128]{1,0:T(8,128)(2,1)S(1)}, u32[]{:S(2)}, u32[]{:S(2)}) collective-permute-start(bf16[1024,128]{1,0:T(8,128)(2,1)S(1)} %get-tuple-element.56.sent_a), channel_id=1, source_target_pairs={{0,3},{1,2},{2,1},{3,0},{4,7},{5,6},{6,5},{7,4},{8,11},{9,10},{10,... | collective-permute-start | bytes 786440 | tf_op jit(solution)/shard_map/ppermute | solution.py:278
  37.2 0.0 collective-permute-done.3.far_b
  37.2 0.0 collective-permute-done.2.far_a
  37.2 0.1 combine_1.1.mid
  37.3 5.7 %collective-permute-start.13 = (bf16[2048,128]{1,0:T(8,128)(2,1)S(1)}, bf16[2048,128]{1,0:T(8,128)(2,1)S(1)}, u32[]{:S(2)}, u32[]{:S(2)}) collective-permute-start(bf16[2048,128]{1,0:T(8,128)(2,1)S(1)} %combine_1.1.mid), channel_id=1, source_target_pairs={{0,252},{4,8},{8,4},{12,16},{16,12},{20,24},{24,20},{28,32},{32,28... | collective-permute-start | bytes 1572872 | tf_op jit(solution)/shard_map/ppermute | solution.py:281
  43.0 0.0 collective-permute-start.12
  43.0 0.0 collective-permute-done.9.far_b
  43.0 0.0 collective-permute-done.8.far_a
  43.0 0.3 combine_2.1
  43.3 5.4 %collective-permute-start.15 = (bf16[1792,128]{1,0:T(8,128)(2,1)S(1)}, bf16[1792,128]{1,0:T(8,128)(2,1)S(1)}, u32[]{:S(2)}, u32[]{:S(2)}) collective-permute-start(bf16[1792,128]{1,0:T(8,128)(2,1)S(1)} %get-tuple-element.63.rest), channel_id=1, source_target_pairs={{0,252},{4,8},{8,4},{12,16},{16,12},{20,24},{24,20},{28,32},{32,28... | collective-permute-start | bytes 1376264 | tf_op jit(solution)/shard_map/ppermute | solution.py:281
  48.7 0.0 collective-permute-start.14
  48.7 0.0 collective-permute-start.10
  48.7 3.1 %collective-permute-done.10.far_first = bf16[128,128]{1,0:T(8,128)(2,1)S(1)} collective-permute-done((bf16[128,128]{1,0:T(8,128)(2,1)S(1)}, bf16[128,128]{1,0:T(8,128)(2,1)S(1)}, u32[]{:S(2)}, u32[]{:S(2)}) %collective-permute-start.10) | collective-permute-done | bytes 32800 | tf_op jit(solution)/shard_map/ppermute | solution.py:278
  51.8 1.8 %collective-permute-start.11 = (bf16[128,128]{1,0:T(8,128)(2,1)S(1)}, bf16[128,128]{1,0:T(8,128)(2,1)S(1)}, u32[]{:S(2)}, u32[]{:S(2)}) collective-permute-start(bf16[128,128]{1,0:T(8,128)(2,1)S(1)} %get-tuple-element.66), channel_id=1, source_target_pairs={{0,3},{1,2},{2,1},{3,0},{4,7},{5,6},{6,5},{7,4},{8,11},{9,10},{10,... | collective-permute-start | bytes 98312 | tf_op jit(solution)/shard_map/ppermute | solution.py:278
  53.6 2.5 %collective-permute-done.11.far_last = bf16[128,128]{1,0:T(8,128)(2,1)S(1)} collective-permute-done((bf16[128,128]{1,0:T(8,128)(2,1)S(1)}, bf16[128,128]{1,0:T(8,128)(2,1)S(1)}, u32[]{:S(2)}, u32[]{:S(2)}) %collective-permute-start.11) | collective-permute-done | bytes 32800 | tf_op jit(solution)/shard_map/ppermute | solution.py:278
  56.1 2.0 %collective-permute-start.17 = (bf16[256,128]{1,0:T(8,128)(2,1)S(1)}, bf16[256,128]{1,0:T(8,128)(2,1)S(1)}, u32[]{:S(2)}, u32[]{:S(2)}) collective-permute-start(bf16[256,128]{1,0:T(8,128)(2,1)S(1)} %combine_edge.1.edge), channel_id=1, source_target_pairs={{0,252},{4,8},{8,4},{12,16},{16,12},{20,24},{24,20},{28,32},{32,28... | collective-permute-start | bytes 196616 | tf_op jit(solution)/shard_map/ppermute | solution.py:281
  58.1 0.0 collective-permute-done.13.mid_o
  58.1 0.0 collective-permute-start.16
  58.1 0.0 collective-permute-done.12.mid_e
  58.1 0.0 slice-done
  58.1 0.0 slice-done.1
  58.1 7.9 %impute_ready.1 = (bf16[12672,128]{1,0:T(8,128)(2,1)S(1)}, s32[66]{0:T(128)S(1)}, bf16[8192,128]{1,0:T(8,128)(2,1)}) custom-call(s32[8]{0:T(128)S(1)} %compare_select_fusion.5.place, s32[64]{0:T(128)S(1)} %copy-done, s32[64]{0:T(128)S(1)} %copy-done.1, bf16[2048,128]{1,0:T(8,128)(2,1)S(1)} %combine_1.1.mid, bf16[1792,128]{1,0:T(8,128)(2,1)S(1)} %get-tuple-element.63.rest, ...), custom_call_target="tpu_custom_call" | custom-call | tf_op jit(solution)/shard_map/impute_ready/pallas_call | solution.py:248
  66.1 0.0 collective-permute-done.17.edge_o
  66.1 0.0 collective-permute-done.16.edge_e
  66.1 0.0 collective-permute-done.15.rest_o
  66.1 0.0 collective-permute-done.14.rest_e
  66.1 4.7 %impute_late.1 = (bf16[12672,128]{1,0:T(8,128)(2,1)S(1)}, bf16[8192,128]{1,0:T(8,128)(2,1)}) custom-call(s32[8]{0:T(128)S(1)} %compare_select_fusion.5.place, s32[64]{0:T(128)S(1)} %copy-done, s32[64]{0:T(128)S(1)} %copy-done.1, s32[66]{0:T(128)S(1)} %get-tuple-element.67.late, ...), custom_call_target="tpu_custom_call", output_to_operand_aliasing={{0}: (9, {}), {1}: (10, {})} | custom-call | tf_op jit(solution)/shard_map/impute_late/pallas_call | solution.py:248
  (7 shorter events, 0.0 us)
Async XLA Ops:
  2.9 8.4 %collective-permute-start.1 = (bf16[1024,128]{1,0:T(8,128)(2,1)S(1)}, bf16[1024,128]{1,0:T(8,128)(2,1)S(1)}, u32[]{:S(2)}, u32[]{:S(2)}) collective-permute-start(bf16[1024,128]{1,0:T(8,128)(2,1)S(1)} %get-tuple-element.39.w_b), channel_id=1, source_target_pairs={{0,3},{1,2},{2,1},{3,0},{4,7},{5,6},{6,5},{7,4},{8,11},{9,10},{10,... | collective-permute-start | bytes 786440 | tf_op jit(solution)/shard_map/ppermute | solution.py:278
  6.3 6.9 %collective-permute-start = (bf16[1024,128]{1,0:T(8,128)(2,1)S(1)}, bf16[1024,128]{1,0:T(8,128)(2,1)S(1)}, u32[]{:S(2)}, u32[]{:S(2)}) collective-permute-start(bf16[1024,128]{1,0:T(8,128)(2,1)S(1)} %get-tuple-element.38.w_a), channel_id=1, source_target_pairs={{0,1},{1,0},{2,3},{3,2},{4,5},{5,4},{6,7},{7,6},{8,9},{9,8},{10,11... | collective-permute-start | bytes 786440 | tf_op jit(solution)/shard_map/ppermute | solution.py:278
  6.3 51.8 %slice-start = ((s8[8388608]{0:T(1024)(128)(4,1)}), s8[4194304]{0:T(1024)(128)(4,1)S(1)}, s32[]{:S(2)}) async-start(s8[8388608]{0:T(1024)(128)(4,1)} %bitcast), calls=%async_computation | async-start | bytes 8388608
  8.7 23.3 %collective-permute-start.5 = (bf16[896,128]{1,0:T(8,128)(2,1)S(1)}, bf16[896,128]{1,0:T(8,128)(2,1)S(1)}, u32[]{:S(2)}, u32[]{:S(2)}) collective-permute-start(bf16[896,128]{1,0:T(8,128)(2,1)S(1)} %get-tuple-element.47.w_b), channel_id=1, source_target_pairs={{0,3},{1,2},{2,1},{3,0},{4,7},{5,6},{6,5},{7,4},{8,11},{9,10},{10,... | collective-permute-start | bytes 688136 | tf_op jit(solution)/shard_map/ppermute | solution.py:278
  9.6 22.4 %collective-permute-start.4 = (bf16[896,128]{1,0:T(8,128)(2,1)S(1)}, bf16[896,128]{1,0:T(8,128)(2,1)S(1)}, u32[]{:S(2)}, u32[]{:S(2)}) collective-permute-start(bf16[896,128]{1,0:T(8,128)(2,1)S(1)} %get-tuple-element.46.w_a), channel_id=1, source_target_pairs={{0,1},{1,0},{2,3},{3,2},{4,5},{5,4},{6,7},{7,6},{8,9},{9,8},{10,11... | collective-permute-start | bytes 688136 | tf_op jit(solution)/shard_map/ppermute | solution.py:278
  13.9 23.3 %collective-permute-start.3 = (bf16[1024,128]{1,0:T(8,128)(2,1)S(1)}, bf16[1024,128]{1,0:T(8,128)(2,1)S(1)}, u32[]{:S(2)}, u32[]{:S(2)}) collective-permute-start(bf16[1024,128]{1,0:T(8,128)(2,1)S(1)} %get-tuple-element.44), channel_id=1, source_target_pairs={{0,1},{1,0},{2,3},{3,2},{4,5},{5,4},{6,7},{7,6},{8,9},{9,8},{10,11... | collective-permute-start | bytes 786440 | tf_op jit(solution)/shard_map/ppermute | solution.py:278
  14.0 23.2 %collective-permute-start.2 = (bf16[1024,128]{1,0:T(8,128)(2,1)S(1)}, bf16[1024,128]{1,0:T(8,128)(2,1)S(1)}, u32[]{:S(2)}, u32[]{:S(2)}) collective-permute-start(bf16[1024,128]{1,0:T(8,128)(2,1)S(1)} %get-tuple-element.43), channel_id=1, source_target_pairs={{0,3},{1,2},{2,1},{3,0},{4,7},{5,6},{6,5},{7,4},{8,11},{9,10},{10,... | collective-permute-start | bytes 786440 | tf_op jit(solution)/shard_map/ppermute | solution.py:278
  15.6 42.5 %slice-start.1 = ((s8[8388608]{0:T(1024)(128)(4,1)}), s8[4194304]{0:T(1024)(128)(4,1)S(1)}, s32[]{:S(2)}) async-start(s8[8388608]{0:T(1024)(128)(4,1)} %bitcast), calls=%async_computation.1 | async-start | bytes 8388608
  15.6 3.2 %collective-permute-start.6 = (bf16[128,128]{1,0:T(8,128)(2,1)S(1)}, bf16[128,128]{1,0:T(8,128)(2,1)S(1)}, u32[]{:S(2)}, u32[]{:S(2)}) collective-permute-start(bf16[128,128]{1,0:T(8,128)(2,1)S(1)} %get-tuple-element.50), channel_id=1, source_target_pairs={{0,4},{4,0},{8,12},{12,8},{16,20},{20,16},{24,28},{28,24},{32,36},... | collective-permute-start | bytes 98312 | tf_op jit(solution)/shard_map/ppermute | solution.py:281
  18.8 13.2 %collective-permute-start.7 = (bf16[128,128]{1,0:T(8,128)(2,1)S(1)}, bf16[128,128]{1,0:T(8,128)(2,1)S(1)}, u32[]{:S(2)}, u32[]{:S(2)}) collective-permute-start(bf16[128,128]{1,0:T(8,128)(2,1)S(1)} %get-tuple-element.51), channel_id=1, source_target_pairs={{0,252},{4,8},{8,4},{12,16},{16,12},{20,24},{24,20},{28,32},{32,28... | collective-permute-start | bytes 98312 | tf_op jit(solution)/shard_map/ppermute | solution.py:281
  34.3 23.9 %copy-start = (s32[64]{0:T(128)S(1)}, s32[64]{0:T(128)}, u32[]{:S(2)}) copy-start(s32[64]{0:T(128)} %starts.3) | copy-start | bytes 772
  34.3 23.9 %copy-start.1 = (s32[64]{0:T(128)S(1)}, s32[64]{0:T(128)}, u32[]{:S(2)}) copy-start(s32[64]{0:T(128)} %counts.3) | copy-start | bytes 772
  34.3 8.7 %collective-permute-start.9 = (bf16[1024,128]{1,0:T(8,128)(2,1)S(1)}, bf16[1024,128]{1,0:T(8,128)(2,1)S(1)}, u32[]{:S(2)}, u32[]{:S(2)}) collective-permute-start(bf16[1024,128]{1,0:T(8,128)(2,1)S(1)} %get-tuple-element.60.sent_b), channel_id=1, source_target_pairs={{0,1},{1,0},{2,3},{3,2},{4,5},{5,4},{6,7},{7,6},{8,9},{9,8},{10,11... | collective-permute-start | bytes 786440 | tf_op jit(solution)/shard_map/ppermute | solution.py:278
  35.4 7.6 %collective-permute-start.8 = (bf16[1024,128]{1,0:T(8,128)(2,1)S(1)}, bf16[1024,128]{1,0:T(8,128)(2,1)S(1)}, u32[]{:S(2)}, u32[]{:S(2)}) collective-permute-start(bf16[1024,128]{1,0:T(8,128)(2,1)S(1)} %get-tuple-element.56.sent_a), channel_id=1, source_target_pairs={{0,3},{1,2},{2,1},{3,0},{4,7},{5,6},{6,5},{7,4},{8,11},{9,10},{10,... | collective-permute-start | bytes 786440 | tf_op jit(solution)/shard_map/ppermute | solution.py:278
  37.3 20.8 %collective-permute-start.13 = (bf16[2048,128]{1,0:T(8,128)(2,1)S(1)}, bf16[2048,128]{1,0:T(8,128)(2,1)S(1)}, u32[]{:S(2)}, u32[]{:S(2)}) collective-permute-start(bf16[2048,128]{1,0:T(8,128)(2,1)S(1)} %combine_1.1.mid), channel_id=1, source_target_pairs={{0,252},{4,8},{8,4},{12,16},{16,12},{20,24},{24,20},{28,32},{32,28... | collective-permute-start | bytes 1572872 | tf_op jit(solution)/shard_map/ppermute | solution.py:281
  43.0 15.1 %collective-permute-start.12 = (bf16[2048,128]{1,0:T(8,128)(2,1)S(1)}, bf16[2048,128]{1,0:T(8,128)(2,1)S(1)}, u32[]{:S(2)}, u32[]{:S(2)}) collective-permute-start(bf16[2048,128]{1,0:T(8,128)(2,1)S(1)} %combine_1.1.mid), channel_id=1, source_target_pairs={{0,4},{4,0},{8,12},{12,8},{16,20},{20,16},{24,28},{28,24},{32,36},... | collective-permute-start | bytes 1572872 | tf_op jit(solution)/shard_map/ppermute | solution.py:281
  43.3 22.8 %collective-permute-start.15 = (bf16[1792,128]{1,0:T(8,128)(2,1)S(1)}, bf16[1792,128]{1,0:T(8,128)(2,1)S(1)}, u32[]{:S(2)}, u32[]{:S(2)}) collective-permute-start(bf16[1792,128]{1,0:T(8,128)(2,1)S(1)} %get-tuple-element.63.rest), channel_id=1, source_target_pairs={{0,252},{4,8},{8,4},{12,16},{16,12},{20,24},{24,20},{28,32},{32,28... | collective-permute-start | bytes 1376264 | tf_op jit(solution)/shard_map/ppermute | solution.py:281
  48.7 17.4 %collective-permute-start.14 = (bf16[1792,128]{1,0:T(8,128)(2,1)S(1)}, bf16[1792,128]{1,0:T(8,128)(2,1)S(1)}, u32[]{:S(2)}, u32[]{:S(2)}) collective-permute-start(bf16[1792,128]{1,0:T(8,128)(2,1)S(1)} %get-tuple-element.63.rest), channel_id=1, source_target_pairs={{0,4},{4,0},{8,12},{12,8},{16,20},{20,16},{24,28},{28,24},{32,36},... | collective-permute-start | bytes 1376264 | tf_op jit(solution)/shard_map/ppermute | solution.py:281
  48.7 3.1 %collective-permute-start.10 = (bf16[128,128]{1,0:T(8,128)(2,1)S(1)}, bf16[128,128]{1,0:T(8,128)(2,1)S(1)}, u32[]{:S(2)}, u32[]{:S(2)}) collective-permute-start(bf16[128,128]{1,0:T(8,128)(2,1)S(1)} %get-tuple-element.65), channel_id=1, source_target_pairs={{0,1},{1,0},{2,3},{3,2},{4,5},{5,4},{6,7},{7,6},{8,9},{9,8},{10,11... | collective-permute-start | bytes 98312 | tf_op jit(solution)/shard_map/ppermute | solution.py:278
  51.8 4.3 %collective-permute-start.11 = (bf16[128,128]{1,0:T(8,128)(2,1)S(1)}, bf16[128,128]{1,0:T(8,128)(2,1)S(1)}, u32[]{:S(2)}, u32[]{:S(2)}) collective-permute-start(bf16[128,128]{1,0:T(8,128)(2,1)S(1)} %get-tuple-element.66), channel_id=1, source_target_pairs={{0,3},{1,2},{2,1},{3,0},{4,7},{5,6},{6,5},{7,4},{8,11},{9,10},{10,... | collective-permute-start | bytes 98312 | tf_op jit(solution)/shard_map/ppermute | solution.py:278
  56.1 10.0 %collective-permute-start.17 = (bf16[256,128]{1,0:T(8,128)(2,1)S(1)}, bf16[256,128]{1,0:T(8,128)(2,1)S(1)}, u32[]{:S(2)}, u32[]{:S(2)}) collective-permute-start(bf16[256,128]{1,0:T(8,128)(2,1)S(1)} %combine_edge.1.edge), channel_id=1, source_target_pairs={{0,252},{4,8},{8,4},{12,16},{16,12},{20,24},{24,20},{28,32},{32,28... | collective-permute-start | bytes 196616 | tf_op jit(solution)/shard_map/ppermute | solution.py:281
  58.1 8.0 %collective-permute-start.16 = (bf16[256,128]{1,0:T(8,128)(2,1)S(1)}, bf16[256,128]{1,0:T(8,128)(2,1)S(1)}, u32[]{:S(2)}, u32[]{:S(2)}) collective-permute-start(bf16[256,128]{1,0:T(8,128)(2,1)S(1)} %combine_edge.1.edge), channel_id=1, source_target_pairs={{0,4},{4,0},{8,12},{12,8},{16,20},{20,16},{24,28},{28,24},{32,36},... | collective-permute-start | bytes 196616 | tf_op jit(solution)/shard_map/ppermute | solution.py:281

commit v3 on v2

v3 whole, which is shorter than its diff:
```python
import jax
import jax.numpy as jnp
from jax import lax
from jax.experimental import pallas as pl
from jax.experimental.pallas import tpu as pltpu
from jax.sharding import PartitionSpec as P

BLK = 128
WIN = 4
COLS = 128
TB = 32
UB = 64
ZERO = 3 * TB
EXT = ZERO + 1
UNROLL = 8
BF = jnp.bfloat16
F32 = jnp.float32
ROWS = ("sec", "var")
HBM = pl.BlockSpec(memory_space=pltpu.HBM)
SMEM = pl.BlockSpec(memory_space=pltpu.SMEM)
VM = pl.BlockSpec(memory_space=pltpu.VMEM)
PARAMS = pltpu.CompilerParams(vmem_limit_bytes=40 * 1024 * 1024)
MID = 8
MID_END = TB - MID
HALF1 = (MID_END - MID) // 2
HALF2 = MID


def shaped(blocks, dtype=BF):
    return jax.ShapeDtypeStruct((blocks * BLK, COLS), dtype)


def dot(left, right):
    return jnp.dot(left, right, preferred_element_type=F32)


def at(block, blocks=1):
    start = block * BLK
    return pl.ds(start if isinstance(start, int) else pl.multiple_of(start, BLK), blocks * BLK)


def copy_all(pairs, sems, first=0):
    copies = [pltpu.make_async_copy(a, b, sems.at[first + k]) for k, (a, b) in enumerate(pairs)]
    for copy in copies:
        copy.start()
    return copies


def pieces(blocks):
    return [(k, min(4, blocks - k)) for k in range(0, blocks, 4)]


def whiten_1(place, z, band, mix, w_a, w_b, mix_a, mix_b, zs, bs, sems):
    zcopy = copy_all([(z.at[at(MID - 1, 2 * HALF1 + 2)], zs)], sems)
    cuts = pieces(2 * HALF1)
    bands = copy_all([(band.at[pl.ds(MID + k, n)], bs.at[pl.ds(k, n)]) for k, n in cuts], sems, 1)
    t, a, b = place[0], place[1], place[2]
    pairs = [(z.at[at(0)], w_a.at[at(HALF1)]), (z.at[at(TB - 1)], w_b.at[at(HALF1)])]
    for target, near, far in ((mix_a, a, b), (mix_b, b, a)):
        for i, row in enumerate((t, near)):
            for j, col in enumerate((t, far)):
                pairs.append((mix.at[at(row), at(col)], target.at[at(i), at(j)]))
    others = copy_all(pairs, sems, 1 + len(cuts))
    zcopy[0].wait()
    for (k, n), copy in zip(cuts, bands):
        copy.wait()
        for i in range(k, k + n):
            w = w_a if i < HALF1 else w_b
            w[at(i % HALF1), :] = dot(bs[i], zs[at(i, 3), :]).astype(BF)
    for copy in others:
        copy.wait()


def whiten_2(z, band, w_a, w_b, edge_band, zs, bs, sems):
    zcopies = copy_all(
        [
            (z.at[at(0, HALF2 + 1)], zs.at[at(1, HALF2 + 1)]),
            (z.at[at(MID_END - 1, HALF2 + 1)], zs.at[at(HALF2 + 2, HALF2 + 1)]),
        ],
        sems,
    )
    cuts = [(side, k, n) for side in range(2) for k, n in pieces(HALF2)]
    bands = copy_all(
        [(band.at[pl.ds(side * MID_END + k, n)], bs.at[pl.ds(side * HALF2 + k, n)]) for side, k, n in cuts], sems, 2
    )
    zs[at(0), :] = jnp.zeros((BLK, COLS), BF)
    zs[at(2 * HALF2 + 3), :] = jnp.zeros((BLK, COLS), BF)
    for (side, k, n), copy in zip(cuts, bands):
        if k == 0:
            zcopies[side].wait()
        copy.wait()
        for i in range(k, k + n):
            rows = dot(bs[side * HALF2 + i], zs[at(side * (HALF2 + 2) + i, 3), :])
            (w_a, w_b)[side][at(i), :] = rows.astype(BF)
    edge_band[at(0), :] = bs[0, :, pl.ds(0, BLK)]
    edge_band[at(1), :] = bs[2 * HALF2 - 1, :, pl.ds(2 * BLK, BLK)]


def sums(own_rows, got_rows, mix):
    return dot(own_rows, mix[pl.ds(0, COLS), :]) + dot(got_rows, mix[pl.ds(COLS, COLS), :])


def partial(w_a, got_a, w_b, got_b, mix_a, mix_b, send_a, send_b, own):
    rows = w_a.shape[0]
    for k, (w, got, mix, send) in enumerate(((w_a, got_a, mix_a, send_a), (w_b, got_b, mix_b, send_b))):
        both = sums(w[...], got[...], mix)
        own[pl.ds(k * rows, rows), :] = both[:, :COLS]
        send[...] = both[:, COLS:].astype(BF)


def combine_1(place, own, far_a, far_b, out_e, out_o):
    for k, far in enumerate((far_a, far_b)):
        rows = (own[at(k * (HALF1 + 1), HALF1), :] + far[at(0, HALF1), :].astype(F32)).astype(BF)
        out_e[at(k * HALF1, HALF1), :] = rows
        out_o[at(k * HALF1, HALF1), :] = rows
    first = (own[at(HALF1), :] + far_a[at(HALF1), :].astype(F32)).astype(BF)
    last = (own[at(2 * HALF1 + 1), :] + far_b[at(HALF1), :].astype(F32)).astype(BF)
    odd = place[5] == 1
    out_e[at(2 * HALF1), :] = jnp.where(odd, first, last)
    out_o[at(2 * HALF1), :] = jnp.where(odd, last, first)


def combine_2(own, far_a, far_b, out, edge):
    inner = HALF2 - 1
    edge[at(0), :] = own[at(0), :] + far_a[at(0), :].astype(F32)
    out[at(0, inner), :] = (own[at(1, inner), :] + far_a[at(1, inner), :].astype(F32)).astype(BF)
    out[at(inner, inner), :] = (own[at(HALF2, inner), :] + far_b[at(0, inner), :].astype(F32)).astype(BF)
    edge[at(1), :] = own[at(2 * HALF2 - 1), :] + far_b[at(inner), :].astype(F32)


def finish_edge(place, edge, edge_band, got_e, got_o, out):
    odd = place[5] == 1
    nothing = jnp.zeros((BLK, COLS), BF)
    end_e = got_e[at(2 * HALF1), :]
    end_o = got_o[at(2 * HALF1), :]
    from_left = jnp.where(place[3] == 0, nothing, jnp.where(odd, end_e, end_o))
    from_right = jnp.where(place[3] == place[4] - 1, nothing, jnp.where(odd, end_o, end_e))
    for k, rows in enumerate((from_left, from_right)):
        out[at(k), :] = (edge[at(k), :] + dot(edge_band[at(k), :], rows)).astype(BF)


def to_out(u, n, out, staged, sems):
    return pltpu.make_async_copy(staged.at[n], out.at[at(u)], sems.at[n])


def on_list(index, count, starts, counts, lowest, ld, ext, out, staged, sems):
    def several(k, carry):
        for i in range(UNROLL):
            u = index[jnp.minimum(UNROLL * k + i, count - 1)]
            first = jnp.clip(starts[u] - lowest, 0, 3 * TB - 1)
            have = counts[u]
            window = [ext[at(jnp.where(s < have, jnp.minimum(first + s, ZERO), ZERO)), :] for s in range(WIN)]
            staged[UNROLL * k + i] = dot(ld[u], jnp.concatenate(window, axis=0)).astype(BF)
        for i in range(UNROLL):
            n = UNROLL * k + i

            @pl.when(n < count)
            def _():
                to_out(index[n], n, out, staged, sems).start()

        return carry

    def finish(n, carry):
        to_out(index[n], n, out, staged, sems).wait()
        return carry

    lax.fori_loop(0, (count + UNROLL - 1) // UNROLL, several, 0)
    lax.fori_loop(0, count, finish, 0)


def set_1(ext, base, mid):
    return [(mid.at[at(0, 2 * HALF1)], ext.at[at(base + MID, 2 * HALF1)])]


def set_2(ext, base, rest, edge):
    inner = HALF2 - 1
    return [
        (edge.at[at(0)], ext.at[at(base)]),
        (rest.at[at(0, inner)], ext.at[at(base + 1, inner)]),
        (rest.at[at(inner, inner)], ext.at[at(base + MID_END, inner)]),
        (edge.at[at(1)], ext.at[at(base + TB - 1)]),
    ]


def impute_ready(
    place, starts, counts, mid, rest, edge, mid_e, mid_o, ld, ext, late, out, ready, staged, sems, out_sems
):
    base_e = 2 * TB * (1 - place[5])
    base_o = 2 * TB * place[5]
    copies = copy_all(
        set_1(ext, TB, mid) + set_2(ext, TB, rest, edge) + set_1(ext, base_e, mid_e) + set_1(ext, base_o, mid_o), sems
    )
    ext[at(ZERO), :] = jnp.zeros((BLK, COLS), BF)
    lowest = place[3] * TB - TB

    def sort(u, sizes):
        now, later = sizes
        first = jnp.clip(starts[u] - lowest, 0, 3 * TB - 1)
        last = first + counts[u] - 1
        waits = first < MID
        for low, high in ((MID_END, TB), (2 * TB, 2 * TB + MID), (2 * TB + MID_END, 3 * TB)):
            waits = waits | ((last >= low) & (first < high))
        waits = waits.astype(jnp.int32)
        ready[now] = u
        late[later] = u
        return now + 1 - waits, later + waits

    now, later = lax.fori_loop(0, UB, sort, (0, 0))
    late[UB + 1] = later
    for copy in copies:
        copy.wait()

    @pl.when(now > 0)
    def _():
        on_list(ready, now, starts, counts, lowest, ld, ext, out, staged, out_sems)


def impute_late(
    place, starts, counts, late, rest_e, rest_o, edge_e, edge_o, ld, before, done, ext, out, staged, sems, out_sems
):
    base_e = 2 * TB * (1 - place[5])
    base_o = 2 * TB * place[5]
    copies = copy_all(set_2(ext, base_e, rest_e, edge_e) + set_2(ext, base_o, rest_o, edge_o), sems)
    count = late[UB + 1]
    for copy in copies:
        copy.wait()

    @pl.when(count > 0)
    def _():
        on_list(late, count, starts, counts, place[3] * TB - TB, ld, ext, out, staged, out_sems)


def call(kernel, outs, ins, args, scratch=(), aliases=None):
    return pl.pallas_call(
        kernel,
        name=kernel.__name__,
        out_shape=tuple(shape for shape, _ in outs),
        in_specs=ins,
        out_specs=tuple(spec for _, spec in outs),
        scratch_shapes=list(scratch),
        input_output_aliases=aliases or {},
        compiler_params=PARAMS,
    )(*args)


def in_vmem(*shapes):
    return [(shape, VM) for shape in shapes]


def on_device(z, band, ld, mix, starts, counts):
    t = lax.axis_index("trait")
    g = lax.axis_index(ROWS)
    owners = lax.axis_size(ROWS)
    lane = lax.iota(jnp.int32, 8)
    place = jnp.zeros((8,), jnp.int32)
    for k, value in enumerate((t, t ^ 1, 3 - t, g, owners, g % 2)):
        place = jnp.where(lane == k, value, place)
    pairs_a = [(i, i ^ 1) for i in range(4)]
    pairs_b = [(i, 3 - i) for i in range(4)]
    pairs_e = [(i, i ^ 1) for i in range(owners)]
    pairs_o = [(i, (i + 1) % owners if i % 2 else (i - 1) % owners) for i in range(owners)]

    def along_trait(x, y, pairs_x, pairs_y):
        return lax.ppermute(x, "trait", pairs_x), lax.ppermute(y, "trait", pairs_y)

    def along_rows(x, y):
        return lax.ppermute(x, ROWS, pairs_e), lax.ppermute(y, ROWS, pairs_o)

    z, band, mix = (pltpu.with_memory_space_constraint(x, pltpu.HBM) for x in (z, band, mix))
    mix_part = jax.ShapeDtypeStruct((2 * COLS, 2 * COLS), BF)
    w1a, w1b, mix_a, mix_b = call(
        whiten_1,
        in_vmem(shaped(HALF1 + 1), shaped(HALF1 + 1), mix_part, mix_part),
        [SMEM, HBM, HBM, HBM],
        (place, z, band, mix),
        [
            pltpu.VMEM(((2 * HALF1 + 2) * BLK, COLS), BF),
            pltpu.VMEM((2 * HALF1, BLK, 3 * BLK), BF),
            pltpu.SemaphoreType.DMA((11 + len(pieces(2 * HALF1)),)),
        ],
    )
    got1a, got1b = along_trait(w1a, w1b, pairs_a, pairs_b)
    z, _ = lax.optimization_barrier((z, w1a))
    w2a, w2b, edge_band = call(
        whiten_2,
        in_vmem(shaped(HALF2), shaped(HALF2), shaped(2)),
        [HBM, HBM],
        (z, band),
        [
            pltpu.VMEM(((2 * HALF2 + 4) * BLK, COLS), BF),
            pltpu.VMEM((2 * HALF2, BLK, 3 * BLK), BF),
            pltpu.SemaphoreType.DMA((2 + 2 * len(pieces(HALF2)),)),
        ],
    )
    got2a, got2b = along_trait(w2a, w2b, pairs_a, pairs_b)

    def mixing(w_a, got_a, w_b, got_b):
        blocks = w_a.shape[0] // BLK
        outs = in_vmem(shaped(blocks), shaped(blocks), shaped(2 * blocks, F32))
        send_a, send_b, own = call(partial, outs, [VM] * 6, (w_a, got_a, w_b, got_b, mix_a, mix_b))
        return (own, *along_trait(send_a, send_b, pairs_b, pairs_a)), send_a

    (own1, far1a, far1b), after = mixing(w1a, got1a, w1b, got1b)
    got2a, got2b, _ = lax.optimization_barrier((got2a, got2b, after))
    (own2, far2a, far2b), after = mixing(w2a, got2a, w2b, got2b)
    far1a, far1b, _ = lax.optimization_barrier((far1a, far1b, after))
    to_e, to_o = call(
        combine_1,
        in_vmem(shaped(2 * HALF1 + 1), shaped(2 * HALF1 + 1)),
        [SMEM] + [VM] * 3,
        (place, own1, far1a, far1b),
    )
    mid_e, mid_o = along_rows(to_e, to_o)
    far2a, far2b, _ = lax.optimization_barrier((far2a, far2b, to_e))
    mixed2, edge_sums = call(
        combine_2, in_vmem(shaped(2 * HALF2 - 2), shaped(2, F32)), [VM] * 3, (own2, far2a, far2b)
    )
    rest_e, rest_o = along_rows(mixed2, mixed2)
    (mixed3,) = call(
        finish_edge, in_vmem(shaped(2)), [SMEM] + [VM] * 4, (place, edge_sums, edge_band, mid_e, mid_o)
    )
    edge_e, edge_o = along_rows(mixed3, mixed3)
    window_scratch = [
        pltpu.VMEM((UB, BLK, COLS), BF),
        pltpu.SemaphoreType.DMA((8,)),
        pltpu.SemaphoreType.DMA((UB,)),
    ]
    ext, late, done = call(
        impute_ready,
        [(shaped(EXT), VM), (jax.ShapeDtypeStruct((UB + 2,), jnp.int32), SMEM), (shaped(UB), HBM)],
        [SMEM] * 3 + [VM] * 6,
        (place, starts, counts, to_e, mixed2, mixed3, mid_e, mid_o, ld),
        [pltpu.SMEM((UB + 1,), jnp.int32)] + window_scratch,
    )
    _, out = call(
        impute_late,
        [(shaped(EXT), VM), (shaped(UB), HBM)],
        [SMEM] * 4 + [VM] * 6 + [HBM],
        (place, starts, counts, late, rest_e, rest_o, edge_e, edge_o, ld, ext, done),
        window_scratch,
        {9: 0, 10: 1},
    )
    return out


def solution(mesh):
    in_specs = (
        P(ROWS, "trait"),
        P(ROWS, None, None),
        P(ROWS, None, None),
        P(),
        P(ROWS),
        P(ROWS),
    )
    return jax.shard_map(on_device, mesh=mesh, in_specs=in_specs, out_specs=P(ROWS, "trait"), check_vma=False)
```

time: 71 us -> 69 us (0.972)
  starting transfers between devices: 37.8 us -> 26.9 us
  waiting for transfers between devices: 11.6 us -> 21.7 us
  Pallas kernels: 21.3 us -> 20.1 us
    ppermute x8 -> x6, waiting for transfers between devices: 3.21 us -> 11.1 us  [along_rows(): return (lax.ppermute(x, ROWS, pairs_e), lax.ppermute(y, ROWS, pairs_o))]
    ppermute x8 -> x6, starting transfers between devices: 26.3 us -> 18.5 us  [along_rows(): return (lax.ppermute(x, ROWS, pairs_e), lax.ppermute(y, ROWS, pairs_o))]
    ppermute x5 -> x4, starting transfers between devices: 7.35 us -> 4.18 us  [along_trait(): lax.ppermute(y, 'trait', pairs_y)]
    ppermute x5 -> x4, waiting for transfers between devices: 3.43 us -> 5.58 us  [along_trait(): lax.ppermute(y, 'trait', pairs_y)]
    pallas_call x9, Pallas kernels: 21.3 us -> 20.1 us  [call(): pl.pallas_call(kernel, name=kernel.__name__, out_shape=tuple((shape for s...]
    ppermute x5 -> x4, starting transfers between devices: 4.11 us -> 4.2 us  [along_trait(): lax.ppermute(x, 'trait', pairs_x)]
    ppermute x5 -> x4, waiting for transfers between devices: 4.95 us -> 4.99 us  [along_trait(): lax.ppermute(x, 'trait', pairs_x)]
  transfers between devices with their start and end apart: 18 -> 14, of which waited for: 6 -> 6; matrix products, arithmetic and copies ran while one was open for 0% -> 0% of each run, Pallas kernels for 19% -> 18%
where the time goes in v3:
time: 69 us; the launch traced here: 68.9 us
  starting transfers between devices  26.9 us (39%)
  waiting for transfers between devices  21.7 us (31%)
  Pallas kernels  20.1 us (29%)
    pallas_call x9, Pallas kernels, call(): pl.pallas_call(kernel, name=kernel.__name__, out_shape=tuple((shape for s...  20.1 us
    ppermute x6, starting transfers between devices, along_rows(): return (lax.ppermute(x, ROWS, pairs_e), lax.ppermute(y, ROWS, pairs_o))  18.5 us
    ppermute x6, waiting for transfers between devices, along_rows(): return (lax.ppermute(x, ROWS, pairs_e), lax.ppermute(y, ROWS, pairs_o))  11.1 us
    ppermute x4, waiting for transfers between devices, along_trait(): lax.ppermute(y, 'trait', pairs_y)  5.58 us
    ppermute x4, waiting for transfers between devices, along_trait(): lax.ppermute(x, 'trait', pairs_x)  4.99 us
    ppermute x4, starting transfers between devices, along_trait(): lax.ppermute(x, 'trait', pairs_x)  4.2 us
    ppermute x4, starting transfers between devices, along_trait(): lax.ppermute(y, 'trait', pairs_y)  4.18 us
  transfers between devices with their start and end apart: 14, of which 6 were waited for; matrix products, arithmetic and copies ran while one was open for 0% of the time, Pallas kernels for 18%

profile of v3, /device:TPU:1, one launch (start us, length us, event | category | flops | bytes accessed | tf_op | source)
XLA Modules:
  0.0 68.9 jit_solution(12064901108416660644)
XLA Ops:
  0.0 0.0 slice-start
  0.0 3.2 %whiten_1.1 = (bf16[1152,128]{1,0:T(8,128)(2,1)S(1)}, bf16[1152,128]{1,0:T(8,128)(2,1)S(1)}, bf16[256,256]{1,0:T(8,128)(2,1)S(1)}, bf16[256,256]{1,0:T(8,128)(2,1)S(1)}) custom-call(s32[8]{0:T(128)S(1)} %compare_select_fusion.5.place, bf16[4096,128]{1,0:T(8,128)(2,1)} %z.2, bf16[32,128,384]{2,1,0:T(8,128)(2,1)} %band.3, bf16[512,512]{1,0:T(8,128)(2,1)} %mix.1), custom_call_target="tpu_custom_call" | custom-call | tf_op jit(solution)/shard_map/whiten_1/pallas_call | solution.py:234
  3.2 3.4 %collective-permute-start.1 = (bf16[1152,128]{1,0:T(8,128)(2,1)S(1)}, bf16[1152,128]{1,0:T(8,128)(2,1)S(1)}, u32[]{:S(2)}, u32[]{:S(2)}) collective-permute-start(bf16[1152,128]{1,0:T(8,128)(2,1)S(1)} %get-tuple-element.34.w_b), channel_id=1, source_target_pairs={{0,3},{1,2},{2,1},{3,0},{4,7},{5,6},{6,5},{7,4},{8,11},{9,10},{10,... | collective-permute-start | bytes 884744 | tf_op jit(solution)/shard_map/ppermute | solution.py:264
  6.6 0.0 slice-start.1
  6.6 0.0 collective-permute-start
  6.6 2.4 %whiten_2.1 = (bf16[1024,128]{1,0:T(8,128)(2,1)S(1)}, bf16[1024,128]{1,0:T(8,128)(2,1)S(1)}, bf16[256,128]{1,0:T(8,128)(2,1)S(1)}) custom-call(bf16[4096,128]{1,0:T(8,128)(2,1)} %z.2, bf16[32,128,384]{2,1,0:T(8,128)(2,1)} %band.3), custom_call_target="tpu_custom_call" | custom-call | tf_op jit(solution)/shard_map/whiten_2/pallas_call | solution.py:234
  9.1 1.4 %collective-permute-start.4 = (bf16[1024,128]{1,0:T(8,128)(2,1)S(1)}, bf16[1024,128]{1,0:T(8,128)(2,1)S(1)}, u32[]{:S(2)}, u32[]{:S(2)}) collective-permute-start(bf16[1024,128]{1,0:T(8,128)(2,1)S(1)} %get-tuple-element.41.w_a), channel_id=1, source_target_pairs={{0,1},{1,0},{2,3},{3,2},{4,5},{5,4},{6,7},{7,6},{8,9},{9,8},{10,11... | collective-permute-start | bytes 786440 | tf_op jit(solution)/shard_map/ppermute | solution.py:264
  10.5 0.5 collective-permute-start.5
  11.0 1.3 %collective-permute-done.1.got_b = bf16[1152,128]{1,0:T(8,128)(2,1)S(1)} collective-permute-done((bf16[1152,128]{1,0:T(8,128)(2,1)S(1)}, bf16[1152,128]{1,0:T(8,128)(2,1)S(1)}, u32[]{:S(2)}, u32[]{:S(2)}) %collective-permute-start.1) | collective-permute-done | bytes 294944 | tf_op jit(solution)/shard_map/ppermute | solution.py:264
  12.3 1.9 %collective-permute-done.got_a = bf16[1152,128]{1,0:T(8,128)(2,1)S(1)} collective-permute-done((bf16[1152,128]{1,0:T(8,128)(2,1)S(1)}, bf16[1152,128]{1,0:T(8,128)(2,1)S(1)}, u32[]{:S(2)}, u32[]{:S(2)}) %collective-permute-start) | collective-permute-done | bytes 294944 | tf_op jit(solution)/shard_map/ppermute | solution.py:264
  14.2 0.8 %partial.2 = (bf16[1152,128]{1,0:T(8,128)(2,1)S(1)}, bf16[1152,128]{1,0:T(8,128)(2,1)S(1)}, f32[2304,128]{1,0:T(8,128)S(1)}) custom-call(bf16[1152,128]{1,0:T(8,128)(2,1)S(1)} %get-tuple-element.33.w_a, bf16[1152,128]{1,0:T(8,128)(2,1)S(1)} %collective-permute-done.got_a, bf16[1152,128]{1,0:T(8,128)(2,1)S(1)} %get-tuple-element.34.w_b, ...), custom_call_target="tpu_custom_call" | custom-call | tf_op jit(solution)/shard_map/partial/pallas_call | solution.py:234
  14.9 0.0 copy-start
  15.0 0.0 copy-start.1
  15.0 0.1 collective-permute-start.3
  15.1 1.6 %collective-permute-start.2 = (bf16[1152,128]{1,0:T(8,128)(2,1)S(1)}, bf16[1152,128]{1,0:T(8,128)(2,1)S(1)}, u32[]{:S(2)}, u32[]{:S(2)}) collective-permute-start(bf16[1152,128]{1,0:T(8,128)(2,1)S(1)} %get-tuple-element.38), channel_id=1, source_target_pairs={{0,3},{1,2},{2,1},{3,0},{4,7},{5,6},{6,5},{7,4},{8,11},{9,10},{10,... | collective-permute-start | bytes 884744 | tf_op jit(solution)/shard_map/ppermute | solution.py:264
  16.7 3.1 %collective-permute-done.4.got_a = bf16[1024,128]{1,0:T(8,128)(2,1)S(1)} collective-permute-done((bf16[1024,128]{1,0:T(8,128)(2,1)S(1)}, bf16[1024,128]{1,0:T(8,128)(2,1)S(1)}, u32[]{:S(2)}, u32[]{:S(2)}) %collective-permute-start.4) | collective-permute-done | bytes 262176 | tf_op jit(solution)/shard_map/ppermute | solution.py:264
  19.8 0.0 collective-permute-done.5.got_b
  19.8 0.7 %partial.3 = (bf16[1024,128]{1,0:T(8,128)(2,1)S(1)}, bf16[1024,128]{1,0:T(8,128)(2,1)S(1)}, f32[2048,128]{1,0:T(8,128)S(1)}) custom-call(bf16[1024,128]{1,0:T(8,128)(2,1)S(1)} %get-tuple-element.41.w_a, bf16[1024,128]{1,0:T(8,128)(2,1)S(1)} %collective-permute-done.4.got_a, bf16[1024,128]{1,0:T(8,128)(2,1)S(1)} %get-tuple-element.42.w_b, ...), custom_call_target="tpu_custom_call" | custom-call | tf_op jit(solution)/shard_map/partial/pallas_call | solution.py:234
  20.5 0.1 collective-permute-start.7
  20.6 1.2 %collective-permute-start.6 = (bf16[1024,128]{1,0:T(8,128)(2,1)S(1)}, bf16[1024,128]{1,0:T(8,128)(2,1)S(1)}, u32[]{:S(2)}, u32[]{:S(2)}) collective-permute-start(bf16[1024,128]{1,0:T(8,128)(2,1)S(1)} %get-tuple-element.45), channel_id=1, source_target_pairs={{0,3},{1,2},{2,1},{3,0},{4,7},{5,6},{6,5},{7,4},{8,11},{9,10},{10,... | collective-permute-start | bytes 786440 | tf_op jit(solution)/shard_map/ppermute | solution.py:264
  21.9 4.2 %collective-permute-done.3.far_b = bf16[1152,128]{1,0:T(8,128)(2,1)S(1)} collective-permute-done((bf16[1152,128]{1,0:T(8,128)(2,1)S(1)}, bf16[1152,128]{1,0:T(8,128)(2,1)S(1)}, u32[]{:S(2)}, u32[]{:S(2)}) %collective-permute-start.3) | collective-permute-done | bytes 294944 | tf_op jit(solution)/shard_map/ppermute | solution.py:264
  26.1 0.0 collective-permute-done.2.far_a
  26.1 0.6 combine_1.1
  26.8 11.3 %collective-permute-start.9 = (bf16[2176,128]{1,0:T(8,128)(2,1)S(1)}, bf16[2176,128]{1,0:T(8,128)(2,1)S(1)}, u32[]{:S(2)}, u32[]{:S(2)}) collective-permute-start(bf16[2176,128]{1,0:T(8,128)(2,1)S(1)} %get-tuple-element.56), channel_id=1, source_target_pairs={{0,252},{4,8},{8,4},{12,16},{16,12},{20,24},{24,20},{28,32},{32,28... | collective-permute-start | bytes 1671176 | tf_op jit(solution)/shard_map/ppermute | solution.py:267
  38.1 0.0 collective-permute-start.8
  38.1 0.0 collective-permute-done.7.far_b
  38.1 0.0 collective-permute-done.6.far_a
  38.1 0.1 combine_2.1
  38.2 3.5 %collective-permute-start.11 = (bf16[1792,128]{1,0:T(8,128)(2,1)S(1)}, bf16[1792,128]{1,0:T(8,128)(2,1)S(1)}, u32[]{:S(2)}, u32[]{:S(2)}) collective-permute-start(bf16[1792,128]{1,0:T(8,128)(2,1)S(1)} %get-tuple-element.53.rest), channel_id=1, source_target_pairs={{0,252},{4,8},{8,4},{12,16},{16,12},{20,24},{24,20},{28,32},{32,28... | collective-permute-start | bytes 1376264 | tf_op jit(solution)/shard_map/ppermute | solution.py:267
  41.7 0.0 collective-permute-start.10
  41.7 9.9 %collective-permute-done.9.got_o.mid_o = bf16[2176,128]{1,0:T(8,128)(2,1)S(1)} collective-permute-done((bf16[2176,128]{1,0:T(8,128)(2,1)S(1)}, bf16[2176,128]{1,0:T(8,128)(2,1)S(1)}, u32[]{:S(2)}, u32[]{:S(2)}) %collective-permute-start.9) | collective-permute-done | bytes 557088 | tf_op jit(solution)/shard_map/ppermute | solution.py:267
  51.6 1.2 %collective-permute-done.8.got_e.mid_e = bf16[2176,128]{1,0:T(8,128)(2,1)S(1)} collective-permute-done((bf16[2176,128]{1,0:T(8,128)(2,1)S(1)}, bf16[2176,128]{1,0:T(8,128)(2,1)S(1)}, u32[]{:S(2)}, u32[]{:S(2)}) %collective-permute-start.8) | collective-permute-done | bytes 557088 | tf_op jit(solution)/shard_map/ppermute | solution.py:267
  52.8 0.7 %finish_edge.1.edge = bf16[256,128]{1,0:T(8,128)(2,1)S(1)} custom-call(s32[8]{0:T(128)S(1)} %compare_select_fusion.5.place, f32[256,128]{1,0:T(8,128)S(1)} %get-tuple-element.54.edge, bf16[256,128]{1,0:T(8,128)(2,1)S(1)} %get-tuple-element.55.edge_band, bf16[2176,128]{1,0:T(8,128)(2,1)S(1)} %collective-permute-done.8.got_e.mid_e, ...), custom_call_target="tpu_custom_call" | custom-call | tf_op jit(solution)/shard_map/finish_edge/pallas_call | solution.py:234
  53.5 3.7 %collective-permute-start.13 = (bf16[256,128]{1,0:T(8,128)(2,1)S(1)}, bf16[256,128]{1,0:T(8,128)(2,1)S(1)}, u32[]{:S(2)}, u32[]{:S(2)}) collective-permute-start(bf16[256,128]{1,0:T(8,128)(2,1)S(1)} %finish_edge.1.edge), channel_id=1, source_target_pairs={{0,252},{4,8},{8,4},{12,16},{16,12},{20,24},{24,20},{28,32},{32,28... | collective-permute-start | bytes 196616 | tf_op jit(solution)/shard_map/ppermute | solution.py:267
  57.2 0.0 collective-permute-start.12
  57.2 0.0 slice-done
  57.2 0.0 slice-done.1
  57.2 0.0 copy-done
  57.2 0.0 copy-done.1
  57.2 6.9 %impute_ready.1 = (bf16[12416,128]{1,0:T(8,128)(2,1)S(1)}, s32[66]{0:T(128)S(1)}, bf16[8192,128]{1,0:T(8,128)(2,1)}) custom-call(s32[8]{0:T(128)S(1)} %compare_select_fusion.5.place, s32[64]{0:T(128)S(1)} %copy-done, s32[64]{0:T(128)S(1)} %copy-done.1, bf16[2176,128]{1,0:T(8,128)(2,1)S(1)} %get-tuple-element.48.mid, ...), custom_call_target="tpu_custom_call" | custom-call | tf_op jit(solution)/shard_map/impute_ready/pallas_call | solution.py:234
  64.2 0.0 collective-permute-done.11.rest_o
  64.2 0.0 collective-permute-done.10.rest_e
  64.2 0.0 collective-permute-done.13.edge_o
  64.2 0.0 collective-permute-done.12.edge_e
  64.2 4.6 %impute_late.1 = (bf16[12416,128]{1,0:T(8,128)(2,1)S(1)}, bf16[8192,128]{1,0:T(8,128)(2,1)}) custom-call(s32[8]{0:T(128)S(1)} %compare_select_fusion.5.place, s32[64]{0:T(128)S(1)} %copy-done, s32[64]{0:T(128)S(1)} %copy-done.1, s32[66]{0:T(128)S(1)} %get-tuple-element.57.late, ...), custom_call_target="tpu_custom_call", output_to_operand_aliasing={{0}: (9, {}), {1}: (10, {})} | custom-call | tf_op jit(solution)/shard_map/impute_late/pallas_call | solution.py:234
  (2 shorter events, 0.0 us)
Async XLA Ops:
  0.0 57.2 %slice-start = ((s8[8388608]{0:T(1024)(128)(4,1)}), s8[4194304]{0:T(1024)(128)(4,1)S(1)}, s32[]{:S(2)}) async-start(s8[8388608]{0:T(1024)(128)(4,1)} %bitcast), calls=%async_computation | async-start | bytes 8388608
  3.2 9.1 %collective-permute-start.1 = (bf16[1152,128]{1,0:T(8,128)(2,1)S(1)}, bf16[1152,128]{1,0:T(8,128)(2,1)S(1)}, u32[]{:S(2)}, u32[]{:S(2)}) collective-permute-start(bf16[1152,128]{1,0:T(8,128)(2,1)S(1)} %get-tuple-element.34.w_b), channel_id=1, source_target_pairs={{0,3},{1,2},{2,1},{3,0},{4,7},{5,6},{6,5},{7,4},{8,11},{9,10},{10,... | collective-permute-start | bytes 884744 | tf_op jit(solution)/shard_map/ppermute | solution.py:264
  6.6 50.6 %slice-start.1 = ((s8[8388608]{0:T(1024)(128)(4,1)}), s8[4194304]{0:T(1024)(128)(4,1)S(1)}, s32[]{:S(2)}) async-start(s8[8388608]{0:T(1024)(128)(4,1)} %bitcast), calls=%async_computation.1 | async-start | bytes 8388608
  6.6 7.6 %collective-permute-start = (bf16[1152,128]{1,0:T(8,128)(2,1)S(1)}, bf16[1152,128]{1,0:T(8,128)(2,1)S(1)}, u32[]{:S(2)}, u32[]{:S(2)}) collective-permute-start(bf16[1152,128]{1,0:T(8,128)(2,1)S(1)} %get-tuple-element.33.w_a), channel_id=1, source_target_pairs={{0,1},{1,0},{2,3},{3,2},{4,5},{5,4},{6,7},{7,6},{8,9},{9,8},{10,11... | collective-permute-start | bytes 884744 | tf_op jit(solution)/shard_map/ppermute | solution.py:264
  9.1 10.7 %collective-permute-start.4 = (bf16[1024,128]{1,0:T(8,128)(2,1)S(1)}, bf16[1024,128]{1,0:T(8,128)(2,1)S(1)}, u32[]{:S(2)}, u32[]{:S(2)}) collective-permute-start(bf16[1024,128]{1,0:T(8,128)(2,1)S(1)} %get-tuple-element.41.w_a), channel_id=1, source_target_pairs={{0,1},{1,0},{2,3},{3,2},{4,5},{5,4},{6,7},{7,6},{8,9},{9,8},{10,11... | collective-permute-start | bytes 786440 | tf_op jit(solution)/shard_map/ppermute | solution.py:264
  10.5 9.3 %collective-permute-start.5 = (bf16[1024,128]{1,0:T(8,128)(2,1)S(1)}, bf16[1024,128]{1,0:T(8,128)(2,1)S(1)}, u32[]{:S(2)}, u32[]{:S(2)}) collective-permute-start(bf16[1024,128]{1,0:T(8,128)(2,1)S(1)} %get-tuple-element.42.w_b), channel_id=1, source_target_pairs={{0,3},{1,2},{2,1},{3,0},{4,7},{5,6},{6,5},{7,4},{8,11},{9,10},{10,... | collective-permute-start | bytes 786440 | tf_op jit(solution)/shard_map/ppermute | solution.py:264
  14.9 42.3 %copy-start = (s32[64]{0:T(128)S(1)}, s32[64]{0:T(128)}, u32[]{:S(2)}) copy-start(s32[64]{0:T(128)} %starts.3) | copy-start | bytes 772
  15.0 42.3 %copy-start.1 = (s32[64]{0:T(128)S(1)}, s32[64]{0:T(128)}, u32[]{:S(2)}) copy-start(s32[64]{0:T(128)} %counts.3) | copy-start | bytes 772
  15.0 11.1 %collective-permute-start.3 = (bf16[1152,128]{1,0:T(8,128)(2,1)S(1)}, bf16[1152,128]{1,0:T(8,128)(2,1)S(1)}, u32[]{:S(2)}, u32[]{:S(2)}) collective-permute-start(bf16[1152,128]{1,0:T(8,128)(2,1)S(1)} %get-tuple-element.39), channel_id=1, source_target_pairs={{0,1},{1,0},{2,3},{3,2},{4,5},{5,4},{6,7},{7,6},{8,9},{9,8},{10,11... | collective-permute-start | bytes 884744 | tf_op jit(solution)/shard_map/ppermute | solution.py:264
  15.1 11.0 %collective-permute-start.2 = (bf16[1152,128]{1,0:T(8,128)(2,1)S(1)}, bf16[1152,128]{1,0:T(8,128)(2,1)S(1)}, u32[]{:S(2)}, u32[]{:S(2)}) collective-permute-start(bf16[1152,128]{1,0:T(8,128)(2,1)S(1)} %get-tuple-element.38), channel_id=1, source_target_pairs={{0,3},{1,2},{2,1},{3,0},{4,7},{5,6},{6,5},{7,4},{8,11},{9,10},{10,... | collective-permute-start | bytes 884744 | tf_op jit(solution)/shard_map/ppermute | solution.py:264
  20.5 17.6 %collective-permute-start.7 = (bf16[1024,128]{1,0:T(8,128)(2,1)S(1)}, bf16[1024,128]{1,0:T(8,128)(2,1)S(1)}, u32[]{:S(2)}, u32[]{:S(2)}) collective-permute-start(bf16[1024,128]{1,0:T(8,128)(2,1)S(1)} %get-tuple-element.50), channel_id=1, source_target_pairs={{0,1},{1,0},{2,3},{3,2},{4,5},{5,4},{6,7},{7,6},{8,9},{9,8},{10,11... | collective-permute-start | bytes 786440 | tf_op jit(solution)/shard_map/ppermute | solution.py:264
  20.6 17.5 %collective-permute-start.6 = (bf16[1024,128]{1,0:T(8,128)(2,1)S(1)}, bf16[1024,128]{1,0:T(8,128)(2,1)S(1)}, u32[]{:S(2)}, u32[]{:S(2)}) collective-permute-start(bf16[1024,128]{1,0:T(8,128)(2,1)S(1)} %get-tuple-element.45), channel_id=1, source_target_pairs={{0,3},{1,2},{2,1},{3,0},{4,7},{5,6},{6,5},{7,4},{8,11},{9,10},{10,... | collective-permute-start | bytes 786440 | tf_op jit(solution)/shard_map/ppermute | solution.py:264
  26.8 24.9 %collective-permute-start.9 = (bf16[2176,128]{1,0:T(8,128)(2,1)S(1)}, bf16[2176,128]{1,0:T(8,128)(2,1)S(1)}, u32[]{:S(2)}, u32[]{:S(2)}) collective-permute-start(bf16[2176,128]{1,0:T(8,128)(2,1)S(1)} %get-tuple-element.56), channel_id=1, source_target_pairs={{0,252},{4,8},{8,4},{12,16},{16,12},{20,24},{24,20},{28,32},{32,28... | collective-permute-start | bytes 1671176 | tf_op jit(solution)/shard_map/ppermute | solution.py:267
  38.1 14.7 %collective-permute-start.8 = (bf16[2176,128]{1,0:T(8,128)(2,1)S(1)}, bf16[2176,128]{1,0:T(8,128)(2,1)S(1)}, u32[]{:S(2)}, u32[]{:S(2)}) collective-permute-start(bf16[2176,128]{1,0:T(8,128)(2,1)S(1)} %get-tuple-element.48.mid), channel_id=1, source_target_pairs={{0,4},{4,0},{8,12},{12,8},{16,20},{20,16},{24,28},{28,24},{32,36},... | collective-permute-start | bytes 1671176 | tf_op jit(solution)/shard_map/ppermute | solution.py:267
  38.2 26.0 %collective-permute-start.11 = (bf16[1792,128]{1,0:T(8,128)(2,1)S(1)}, bf16[1792,128]{1,0:T(8,128)(2,1)S(1)}, u32[]{:S(2)}, u32[]{:S(2)}) collective-permute-start(bf16[1792,128]{1,0:T(8,128)(2,1)S(1)} %get-tuple-element.53.rest), channel_id=1, source_target_pairs={{0,252},{4,8},{8,4},{12,16},{16,12},{20,24},{24,20},{28,32},{32,28... | collective-permute-start | bytes 1376264 | tf_op jit(solution)/shard_map/ppermute | solution.py:267
  41.7 22.5 %collective-permute-start.10 = (bf16[1792,128]{1,0:T(8,128)(2,1)S(1)}, bf16[1792,128]{1,0:T(8,128)(2,1)S(1)}, u32[]{:S(2)}, u32[]{:S(2)}) collective-permute-start(bf16[1792,128]{1,0:T(8,128)(2,1)S(1)} %get-tuple-element.53.rest), channel_id=1, source_target_pairs={{0,4},{4,0},{8,12},{12,8},{16,20},{20,16},{24,28},{28,24},{32,36},... | collective-permute-start | bytes 1376264 | tf_op jit(solution)/shard_map/ppermute | solution.py:267
  53.5 10.7 %collective-permute-start.13 = (bf16[256,128]{1,0:T(8,128)(2,1)S(1)}, bf16[256,128]{1,0:T(8,128)(2,1)S(1)}, u32[]{:S(2)}, u32[]{:S(2)}) collective-permute-start(bf16[256,128]{1,0:T(8,128)(2,1)S(1)} %finish_edge.1.edge), channel_id=1, source_target_pairs={{0,252},{4,8},{8,4},{12,16},{16,12},{20,24},{24,20},{28,32},{32,28... | collective-permute-start | bytes 196616 | tf_op jit(solution)/shard_map/ppermute | solution.py:267
  57.2 7.0 %collective-permute-start.12 = (bf16[256,128]{1,0:T(8,128)(2,1)S(1)}, bf16[256,128]{1,0:T(8,128)(2,1)S(1)}, u32[]{:S(2)}, u32[]{:S(2)}) collective-permute-start(bf16[256,128]{1,0:T(8,128)(2,1)S(1)} %finish_edge.1.edge), channel_id=1, source_target_pairs={{0,4},{4,0},{8,12},{12,8},{16,20},{20,16},{24,28},{28,24},{32,36},... | collective-permute-start | bytes 196616 | tf_op jit(solution)/shard_map/ppermute | solution.py:267

commit v4 on v3

--- a/solution.py
+++ b/solution.py
@@ -19,7 +19,7 @@
 HBM = pl.BlockSpec(memory_space=pltpu.HBM)
 SMEM = pl.BlockSpec(memory_space=pltpu.SMEM)
 VM = pl.BlockSpec(memory_space=pltpu.VMEM)
-PARAMS = pltpu.CompilerParams(vmem_limit_bytes=40 * 1024 * 1024)
+PARAMS = pltpu.CompilerParams(vmem_limit_bytes=8 * 1024 * 1024)
 MID = 8
 MID_END = TB - MID
 HALF1 = (MID_END - MID) // 2
@@ -143,10 +143,22 @@
     return pltpu.make_async_copy(staged.at[n], out.at[at(u)], sems.at[n])
 
 
-def on_list(index, count, starts, counts, lowest, ld, ext, out, staged, sems):
+def on_ranges(ranges, starts, counts, lowest, ld, ext, out, staged, sems):
+    total = 0
+    parts = []
+    for low, high in ranges:
+        parts.append((total, low))
+        total = total + high - low
+
+    def window_of(n):
+        u = n + parts[0][1]
+        for before, low in parts[1:]:
+            u = jnp.where(n >= before, n - before + low, u)
+        return u
+
     def several(k, carry):
         for i in range(UNROLL):
-            u = index[jnp.minimum(UNROLL * k + i, count - 1)]
+            u = window_of(jnp.minimum(UNROLL * k + i, total - 1))
             first = jnp.clip(starts[u] - lowest, 0, 3 * TB - 1)
             have = counts[u]
             window = [ext[at(jnp.where(s < have, jnp.minimum(first + s, ZERO), ZERO)), :] for s in range(WIN)]
@@ -154,18 +166,18 @@
         for i in range(UNROLL):
             n = UNROLL * k + i
 
-            @pl.when(n < count)
+            @pl.when(n < total)
             def _():
-                to_out(index[n], n, out, staged, sems).start()
+                to_out(window_of(n), n, out, staged, sems).start()
 
         return carry
 
     def finish(n, carry):
-        to_out(index[n], n, out, staged, sems).wait()
+        to_out(window_of(n), n, out, staged, sems).wait()
         return carry
 
-    lax.fori_loop(0, (count + UNROLL - 1) // UNROLL, several, 0)
-    lax.fori_loop(0, count, finish, 0)
+    lax.fori_loop(0, (total + UNROLL - 1) // UNROLL, several, 0)
+    lax.fori_loop(0, total, finish, 0)
 
 
 def set_1(ext, base, mid):
@@ -182,52 +194,61 @@
     ]
 
 
-def impute_ready(
-    place, starts, counts, mid, rest, edge, mid_e, mid_o, ld, ext, late, out, ready, staged, sems, out_sems
+LIMITS = (
+    MID,
+    MID_END - WIN + 1,
+    TB,
+    TB + 1,
+    2 * TB - WIN,
+    2 * TB - WIN + 1,
+    2 * TB + MID,
+    2 * TB + MID_END - WIN + 1,
+)
+
+
+def impute_own(place, starts, counts, below, mid, rest, ld, ext, ld_here, out, staged, sems, out_sems):
+    inner = HALF2 - 1
+    quarter = UB // 4
+    whole = [(ld.at[pl.ds(k, quarter)], ld_here.at[pl.ds(k, quarter)]) for k in range(0, UB, quarter)]
+    loads = copy_all(whole, sems, 4)
+    copies = copy_all(
+        set_1(ext, TB, mid)
+        + [
+            (rest.at[at(0, inner)], ext.at[at(TB + 1, inner)]),
+            (rest.at[at(inner, inner)], ext.at[at(TB + MID_END, inner)]),
+        ],
+        sems,
+    )
+    ext[at(ZERO), :] = jnp.zeros((BLK, COLS), BF)
+    for copy in copies + loads:
+        copy.wait()
+    ranges = [(below[3], below[4])]
+    on_ranges(ranges, starts, counts, place[3] * TB - TB, ld_here, ext, out, staged, out_sems)
+
+
+def impute_near(
+    place, starts, counts, below, edge, mid_e, mid_o, ld, before, done, ext, out, staged, sems, out_sems
 ):
     base_e = 2 * TB * (1 - place[5])
     base_o = 2 * TB * place[5]
-    copies = copy_all(
-        set_1(ext, TB, mid) + set_2(ext, TB, rest, edge) + set_1(ext, base_e, mid_e) + set_1(ext, base_o, mid_o), sems
-    )
-    ext[at(ZERO), :] = jnp.zeros((BLK, COLS), BF)
-    lowest = place[3] * TB - TB
-
-    def sort(u, sizes):
-        now, later = sizes
-        first = jnp.clip(starts[u] - lowest, 0, 3 * TB - 1)
-        last = first + counts[u] - 1
-        waits = first < MID
-        for low, high in ((MID_END, TB), (2 * TB, 2 * TB + MID), (2 * TB + MID_END, 3 * TB)):
-            waits = waits | ((last >= low) & (first < high))
-        waits = waits.astype(jnp.int32)
-        ready[now] = u
-        late[later] = u
-        return now + 1 - waits, later + waits
-
-    now, later = lax.fori_loop(0, UB, sort, (0, 0))
-    late[UB + 1] = later
+    own_edge = [(edge.at[at(0)], ext.at[at(TB)]), (edge.at[at(1)], ext.at[at(2 * TB - 1)])]
+    copies = copy_all(own_edge + set_1(ext, base_e, mid_e) + set_1(ext, base_o, mid_o), sems)
     for copy in copies:
         copy.wait()
-
-    @pl.when(now > 0)
-    def _():
-        on_list(ready, now, starts, counts, lowest, ld, ext, out, staged, out_sems)
-
-
-def impute_late(
-    place, starts, counts, late, rest_e, rest_o, edge_e, edge_o, ld, before, done, ext, out, staged, sems, out_sems
+    ranges = [(below[k], below[k + 1]) for k in (0, 2, 4, 6)]
+    on_ranges(ranges, starts, counts, place[3] * TB - TB, ld, ext, out, staged, out_sems)
+
+
+def impute_far(
+    place, starts, counts, below, rest_e, rest_o, edge_e, edge_o, ld, before, done, ext, out, staged, sems, out_sems
 ):
     base_e = 2 * TB * (1 - place[5])
     base_o = 2 * TB * place[5]
     copies = copy_all(set_2(ext, base_e, rest_e, edge_e) + set_2(ext, base_o, rest_o, edge_o), sems)
-    count = late[UB + 1]
     for copy in copies:
         copy.wait()
-
-    @pl.when(count > 0)
-    def _():
-        on_list(late, count, starts, counts, place[3] * TB - TB, ld, ext, out, staged, out_sems)
+    ranges = [(0, below[0]), (below[1], below[2]), (below[5], below[6]), (below[7], UB)]
+    on_ranges(ranges, starts, counts, place[3] * TB - TB, ld, ext, out, staged, out_sems)
 
 
 def call(kernel, outs, ins, args, scratch=(), aliases=None):
@@ -258,7 +279,7 @@
     pairs_a = [(i, i ^ 1) for i in range(4)]
     pairs_b = [(i, 3 - i) for i in range(4)]
     pairs_e = [(i, i ^ 1) for i in range(owners)]
-    pairs_o = [(i, (i + 1) % owners if i % 2 else (i - 1) % owners) for i in range(owners)]
+    pairs_o = [(i, min(i + 1, owners - 1) if i % 2 else max(i - 1, 0)) for i in range(owners)]
 
     def along_trait(x, y, pairs_x, pairs_y):
         return lax.ppermute(x, "trait", pairs_x), lax.ppermute(y, "trait", pairs_y)
@@ -266,7 +287,7 @@
     def along_rows(x, y):
         return lax.ppermute(x, ROWS, pairs_e), lax.ppermute(y, ROWS, pairs_o)
 
-    z, band, mix = (pltpu.with_memory_space_constraint(x, pltpu.HBM) for x in (z, band, mix))
+    z, band, mix, ld = (pltpu.with_memory_space_constraint(x, pltpu.HBM) for x in (z, band, mix, ld))
     mix_part = jax.ShapeDtypeStruct((2 * COLS, 2 * COLS), BF)
     w1a, w1b, mix_a, mix_b = call(
         whiten_1,
@@ -316,27 +337,40 @@
         combine_2, in_vmem(shaped(2 * HALF2 - 2), shaped(2, F32)), [VM] * 3, (own2, far2a, far2b)
     )
     rest_e, rest_o = along_rows(mixed2, mixed2)
-    (mixed3,) = call(
-        finish_edge, in_vmem(shaped(2)), [SMEM] + [VM] * 4, (place, edge_sums, edge_band, mid_e, mid_o)
-    )
-    edge_e, edge_o = along_rows(mixed3, mixed3)
+    starts_here = starts - (g * TB - TB)
+    below = jnp.sum(starts_here[None, :] < jnp.array(LIMITS, jnp.int32)[:, None], axis=1, dtype=jnp.int32)
     window_scratch = [
         pltpu.VMEM((UB, BLK, COLS), BF),
         pltpu.SemaphoreType.DMA((8,)),
         pltpu.SemaphoreType.DMA((UB,)),
     ]
-    ext, late, done = call(
-        impute_ready,
-        [(shaped(EXT), VM), (jax.ShapeDtypeStruct((UB + 2,), jnp.int32), SMEM), (shaped(UB), HBM)],
-        [SMEM] * 3 + [VM] * 6,
-        (place, starts, counts, to_e, mixed2, mixed3, mid_e, mid_o, ld),
-        [pltpu.SMEM((UB + 1,), jnp.int32)] + window_scratch,
+    outs = [(shaped(EXT), VM), (shaped(UB), HBM)]
+    plan = (place, starts, counts, below)
+    ext, ld, done = call(
+        impute_own,
+        [outs[0], (jax.ShapeDtypeStruct(ld.shape, BF), VM), outs[1]],
+        [SMEM] * 4 + [VM] * 2 + [HBM],
+        (*plan, to_e, mixed2, ld),
+        window_scratch,
+    )
+    mid_e, mid_o, ext = lax.optimization_barrier((mid_e, mid_o, ext))
+    (mixed3,) = call(
+        finish_edge, in_vmem(shaped(2)), [SMEM] + [VM] * 4, (place, edge_sums, edge_band, mid_e, mid_o)
+    )
+    edge_e, edge_o = along_rows(mixed3, mixed3)
+    ext, done = call(
+        impute_near,
+        outs,
+        [SMEM] * 4 + [VM] * 5 + [HBM],
+        (*plan, mixed3, mid_e, mid_o, ld, ext, done),
+        window_scratch,
+        {8: 0, 9: 1},
     )
     _, out = call(
-        impute_late,
-        [(shaped(EXT), VM), (shaped(UB), HBM)],
+        impute_far,
+        outs,
         [SMEM] * 4 + [VM] * 6 + [HBM],
-        (place, starts, counts, late, rest_e, rest_o, edge_e, edge_o, ld, ext, done),
+        (*plan, rest_e, rest_o, edge_e, edge_o, ld, ext, done),
         window_scratch,
         {9: 0, 10: 1},
     )

time: 69 us -> 69.2 us (level)
  waiting for transfers between devices: 21.7 us -> 9.36 us
  starting transfers between devices: 26.9 us -> 35.6 us
  Pallas kernels: 20.1 us -> 23.6 us
    ppermute x6, waiting for transfers between devices: 11.1 us -> 0.02 us  [along_rows(): return (lax.ppermute(x, ROWS, pairs_e), lax.ppermute(y, ROWS, pairs_o))]
    ppermute x6, starting transfers between devices: 18.5 us -> 26.2 us  [along_rows(): return (lax.ppermute(x, ROWS, pairs_e), lax.ppermute(y, ROWS, pairs_o))]
    pallas_call x9 -> x10, Pallas kernels: 20.1 us -> 23.6 us  [call(): pl.pallas_call(kernel, name=kernel.__name__, out_shape=tuple((shape for s...]
    ppermute x4, starting transfers between devices: 4.2 us -> 6.91 us  [along_trait(): lax.ppermute(x, 'trait', pairs_x)]
    ppermute x4, starting transfers between devices: 4.18 us -> 2.47 us  [along_trait(): lax.ppermute(y, 'trait', pairs_y)]
    ppermute x4, waiting for transfers between devices: 4.99 us -> 4.22 us  [along_trait(): lax.ppermute(x, 'trait', pairs_x)]
  transfers between devices with their start and end apart: 14 -> 14, of which waited for: 6 -> 5; matrix products, arithmetic and copies ran while one was open for 0% -> 0% of each run, Pallas kernels for 18% -> 23%
where the time goes in v4:
time: 69.2 us; the launch traced here: 69 us
  starting transfers between devices  35.6 us (51%)
  Pallas kernels  23.6 us (34%)
  waiting for transfers between devices  9.36 us (14%)
    ppermute x6, starting transfers between devices, along_rows(): return (lax.ppermute(x, ROWS, pairs_e), lax.ppermute(y, ROWS, pairs_o))  26.2 us
    pallas_call x10, Pallas kernels, call(): pl.pallas_call(kernel, name=kernel.__name__, out_shape=tuple((shape for s...  23.6 us
    ppermute x4, starting transfers between devices, along_trait(): lax.ppermute(x, 'trait', pairs_x)  6.91 us
    ppermute x4, waiting for transfers between devices, along_trait(): lax.ppermute(y, 'trait', pairs_y)  5.13 us
    ppermute x4, waiting for transfers between devices, along_trait(): lax.ppermute(x, 'trait', pairs_x)  4.22 us
    ppermute x4, starting transfers between devices, along_trait(): lax.ppermute(y, 'trait', pairs_y)  2.47 us
  transfers between devices with their start and end apart: 14, of which 5 were waited for; matrix products, arithmetic and copies ran while one was open for 0% of the time, Pallas kernels for 23%

profile of v4, /device:TPU:1, one launch (start us, length us, event | category | flops | bytes accessed | tf_op | source)
XLA Modules:
  0.0 69.0 jit_solution(3115668200844492714)
XLA Ops:
  0.0 2.9 %whiten_1.1 = (bf16[1152,128]{1,0:T(8,128)(2,1)S(1)}, bf16[1152,128]{1,0:T(8,128)(2,1)S(1)}, bf16[256,256]{1,0:T(8,128)(2,1)S(1)}, bf16[256,256]{1,0:T(8,128)(2,1)S(1)}) custom-call(s32[8]{0:T(128)S(1)} %compare_select_fusion.5.place, bf16[4096,128]{1,0:T(8,128)(2,1)} %z.2, bf16[32,128,384]{2,1,0:T(8,128)(2,1)} %band.3, bf16[512,512]{1,0:T(8,128)(2,1)} %mix.1), custom_call_target="tpu_custom_call" | custom-call | tf_op jit(solution)/shard_map/whiten_1/pallas_call | solution.py:255
  2.9 2.1 %collective-permute-start.2 = (bf16[1152,128]{1,0:T(8,128)(2,1)S(1)}, bf16[1152,128]{1,0:T(8,128)(2,1)S(1)}, u32[]{:S(2)}, u32[]{:S(2)}) collective-permute-start(bf16[1152,128]{1,0:T(8,128)(2,1)S(1)} %get-tuple-element.38.w_a), channel_id=1, source_target_pairs={{0,1},{1,0},{2,3},{3,2},{4,5},{5,4},{6,7},{7,6},{8,9},{9,8},{10,11... | collective-permute-start | bytes 884744 | tf_op jit(solution)/shard_map/ppermute | solution.py:285
  5.1 1.8 %collective-permute-start.3 = (bf16[1152,128]{1,0:T(8,128)(2,1)S(1)}, bf16[1152,128]{1,0:T(8,128)(2,1)S(1)}, u32[]{:S(2)}, u32[]{:S(2)}) collective-permute-start(bf16[1152,128]{1,0:T(8,128)(2,1)S(1)} %get-tuple-element.42.w_b), channel_id=1, source_target_pairs={{0,3},{1,2},{2,1},{3,0},{4,7},{5,6},{6,5},{7,4},{8,11},{9,10},{10,... | collective-permute-start | bytes 884744 | tf_op jit(solution)/shard_map/ppermute | solution.py:285
  6.9 2.3 %whiten_2.1 = (bf16[1024,128]{1,0:T(8,128)(2,1)S(1)}, bf16[1024,128]{1,0:T(8,128)(2,1)S(1)}, bf16[256,128]{1,0:T(8,128)(2,1)S(1)}) custom-call(bf16[4096,128]{1,0:T(8,128)(2,1)} %z.2, bf16[32,128,384]{2,1,0:T(8,128)(2,1)} %band.3), custom_call_target="tpu_custom_call" | custom-call | tf_op jit(solution)/shard_map/whiten_2/pallas_call | solution.py:255
  9.2 0.0 copy-start
  9.2 0.0 copy-start.2
  9.2 0.0 copy-start.1
  9.2 0.4 collective-permute-start
  9.6 0.7 collective-permute-start.1
  10.3 0.2 collective-permute-done.2.got_a
  10.5 3.0 %collective-permute-done.3.got_b = bf16[1152,128]{1,0:T(8,128)(2,1)S(1)} collective-permute-done((bf16[1152,128]{1,0:T(8,128)(2,1)S(1)}, bf16[1152,128]{1,0:T(8,128)(2,1)S(1)}, u32[]{:S(2)}, u32[]{:S(2)}) %collective-permute-start.3) | collective-permute-done | bytes 294944 | tf_op jit(solution)/shard_map/ppermute | solution.py:285
  13.5 0.8 %partial.2 = (bf16[1152,128]{1,0:T(8,128)(2,1)S(1)}, bf16[1152,128]{1,0:T(8,128)(2,1)S(1)}, f32[2304,128]{1,0:T(8,128)S(1)}) custom-call(bf16[1152,128]{1,0:T(8,128)(2,1)S(1)} %get-tuple-element.38.w_a, bf16[1152,128]{1,0:T(8,128)(2,1)S(1)} %collective-permute-done.2.got_a, bf16[1152,128]{1,0:T(8,128)(2,1)S(1)} %get-tuple-element.42.w_b, ...), custom_call_target="tpu_custom_call" | custom-call | tf_op jit(solution)/shard_map/partial/pallas_call | solution.py:255
  14.2 2.2 %collective-permute-start.6 = (bf16[1152,128]{1,0:T(8,128)(2,1)S(1)}, bf16[1152,128]{1,0:T(8,128)(2,1)S(1)}, u32[]{:S(2)}, u32[]{:S(2)}) collective-permute-start(bf16[1152,128]{1,0:T(8,128)(2,1)S(1)} %get-tuple-element.45), channel_id=1, source_target_pairs={{0,3},{1,2},{2,1},{3,0},{4,7},{5,6},{6,5},{7,4},{8,11},{9,10},{10,... | collective-permute-start | bytes 884744 | tf_op jit(solution)/shard_map/ppermute | solution.py:285
  16.5 0.0 collective-permute-start.7
  16.5 0.6 collective-permute-done.got_a
  17.1 2.1 %collective-permute-done.1.got_b = bf16[1024,128]{1,0:T(8,128)(2,1)S(1)} collective-permute-done((bf16[1024,128]{1,0:T(8,128)(2,1)S(1)}, bf16[1024,128]{1,0:T(8,128)(2,1)S(1)}, u32[]{:S(2)}, u32[]{:S(2)}) %collective-permute-start.1) | collective-permute-done | bytes 262176 | tf_op jit(solution)/shard_map/ppermute | solution.py:285
  19.2 0.7 %partial.3 = (bf16[1024,128]{1,0:T(8,128)(2,1)S(1)}, bf16[1024,128]{1,0:T(8,128)(2,1)S(1)}, f32[2048,128]{1,0:T(8,128)S(1)}) custom-call(bf16[1024,128]{1,0:T(8,128)(2,1)S(1)} %get-tuple-element.40.w_a, bf16[1024,128]{1,0:T(8,128)(2,1)S(1)} %collective-permute-done.got_a, bf16[1024,128]{1,0:T(8,128)(2,1)S(1)} %get-tuple-element.41.w_b, ...), custom_call_target="tpu_custom_call" | custom-call | tf_op jit(solution)/shard_map/partial/pallas_call | solution.py:255
  19.9 2.1 %collective-permute-start.4 = (bf16[1024,128]{1,0:T(8,128)(2,1)S(1)}, bf16[1024,128]{1,0:T(8,128)(2,1)S(1)}, u32[]{:S(2)}, u32[]{:S(2)}) collective-permute-start(bf16[1024,128]{1,0:T(8,128)(2,1)S(1)} %get-tuple-element.49), channel_id=1, source_target_pairs={{0,3},{1,2},{2,1},{3,0},{4,7},{5,6},{6,5},{7,4},{8,11},{9,10},{10,... | collective-permute-start | bytes 786440 | tf_op jit(solution)/shard_map/ppermute | solution.py:285
  22.0 0.0 collective-permute-start.5
  22.1 3.4 %collective-permute-done.6.far_a = bf16[1152,128]{1,0:T(8,128)(2,1)S(1)} collective-permute-done((bf16[1152,128]{1,0:T(8,128)(2,1)S(1)}, bf16[1152,128]{1,0:T(8,128)(2,1)S(1)}, u32[]{:S(2)}, u32[]{:S(2)}) %collective-permute-start.6) | collective-permute-done | bytes 294944 | tf_op jit(solution)/shard_map/ppermute | solution.py:285
  25.5 0.0 collective-permute-done.7.far_b
  25.5 1.5 %combine_1.1 = (bf16[2176,128]{1,0:T(8,128)(2,1)S(1)}, bf16[2176,128]{1,0:T(8,128)(2,1)}) custom-call(s32[8]{0:T(128)S(1)} %compare_select_fusion.5.place, f32[2304,128]{1,0:T(8,128)S(1)} %get-tuple-element.51.own, bf16[1152,128]{1,0:T(8,128)(2,1)S(1)} %collective-permute-done.6.far_a, bf16[1152,128]{1,0:T(8,128)(2,1)S(1)} %collective-permute-done.7.far_b), custom_call_target="tpu_custom_call" | custom-call | tf_op jit(solution)/shard_map/combine_1/pallas_call | solution.py:255
  26.9 1.9 %collective-permute-start.10 = (bf16[2176,128]{1,0:T(8,128)(2,1)S(1)}, bf16[2176,128]{1,0:T(8,128)(2,1)S(1)}, u32[]{:S(2)}, u32[]{:S(2)}) collective-permute-start(bf16[2176,128]{1,0:T(8,128)(2,1)S(1)} %get-tuple-element.55.mid), channel_id=1, source_target_pairs={{0,4},{4,0},{8,12},{12,8},{16,20},{20,16},{24,28},{28,24},{32,36},... | collective-permute-start | bytes 1671176 | tf_op jit(solution)/shard_map/ppermute | solution.py:288
  28.8 12.7 %collective-permute-start.11 = (bf16[2176,128]{1,0:T(8,128)(2,1)}, bf16[2176,128]{1,0:T(8,128)(2,1)S(1)}, u32[]{:S(2)}, u32[]{:S(2)}) collective-permute-start(bf16[2176,128]{1,0:T(8,128)(2,1)} %get-tuple-element.61), channel_id=1, source_target_pairs={{0,0},{4,8},{8,4},{12,16},{16,12},{20,24},{24,20},{28,32},{32,28},... | collective-permute-start | bytes 1671176 | tf_op jit(solution)/shard_map/ppermute | solution.py:288
  41.5 0.0 collective-permute-done.4.far_a
  41.5 0.0 collective-permute-done.5.far_b
  41.5 0.1 combine_2.1
  41.6 0.1 collective-permute-start.8
  41.7 3.9 %collective-permute-start.9 = (bf16[1792,128]{1,0:T(8,128)(2,1)S(1)}, bf16[1792,128]{1,0:T(8,128)(2,1)S(1)}, u32[]{:S(2)}, u32[]{:S(2)}) collective-permute-start(bf16[1792,128]{1,0:T(8,128)(2,1)S(1)} %get-tuple-element.58.rest), channel_id=1, source_target_pairs={{0,0},{4,8},{8,4},{12,16},{16,12},{20,24},{24,20},{28,32},{32,28},... | collective-permute-start | bytes 1376264 | tf_op jit(solution)/shard_map/ppermute | solution.py:288
  45.6 0.0 copy-done
  45.6 0.0 copy-done.2
  45.6 0.2 convert_reduce_fusion.below
  45.8 0.0 copy-done.1
  45.8 6.7 %impute_own.1 = (bf16[12416,128]{1,0:T(8,128)(2,1)S(1)}, bf16[64,128,512]{2,1,0:T(8,128)(2,1)S(1)}, bf16[8192,128]{1,0:T(8,128)(2,1)}) custom-call(s32[8]{0:T(128)S(1)} %compare_select_fusion.5.place, s32[64]{0:T(128)S(1)} %copy-done, s32[64]{0:T(128)S(1)} %copy-done.1, s32[8]{0:T(128)S(1)} %convert_reduce_fusion.below, ...), custom_call_target="tpu_custom_call" | custom-call | tf_op jit(solution)/shard_map/impute_own/pallas_call | solution.py:255
  52.5 0.0 collective-permute-done.10.got_e.mid_e
  52.5 0.0 collective-permute-done.11.got_o.mid_o
  52.5 0.7 %finish_edge.1.edge = bf16[256,128]{1,0:T(8,128)(2,1)S(1)} custom-call(s32[8]{0:T(128)S(1)} %compare_select_fusion.5.place, f32[256,128]{1,0:T(8,128)S(1)} %get-tuple-element.59.edge, bf16[256,128]{1,0:T(8,128)(2,1)S(1)} %get-tuple-element.60.edge_band, bf16[2176,128]{1,0:T(8,128)(2,1)S(1)} %collective-permute-done.10.got_e.mid_e, ...), custom_call_target="tpu_custom_call" | custom-call | tf_op jit(solution)/shard_map/finish_edge/pallas_call | solution.py:255
  53.2 0.1 collective-permute-start.12
  53.3 7.6 %collective-permute-start.13 = (bf16[256,128]{1,0:T(8,128)(2,1)S(1)}, bf16[256,128]{1,0:T(8,128)(2,1)S(1)}, u32[]{:S(2)}, u32[]{:S(2)}) collective-permute-start(bf16[256,128]{1,0:T(8,128)(2,1)S(1)} %finish_edge.1.edge), channel_id=1, source_target_pairs={{0,0},{4,8},{8,4},{12,16},{16,12},{20,24},{24,20},{28,32},{32,28},... | collective-permute-start | bytes 196616 | tf_op jit(solution)/shard_map/ppermute | solution.py:288
  60.9 3.0 %impute_near.1 = (bf16[12416,128]{1,0:T(8,128)(2,1)S(1)}, bf16[8192,128]{1,0:T(8,128)(2,1)}) custom-call(s32[8]{0:T(128)S(1)} %compare_select_fusion.5.place, s32[64]{0:T(128)S(1)} %copy-done, s32[64]{0:T(128)S(1)} %copy-done.1, s32[8]{0:T(128)S(1)} %convert_reduce_fusion.below, ...), custom_call_target="tpu_custom_call", output_to_operand_aliasing={{0}: (8, {}), {1}: (9, {})} | custom-call | tf_op jit(solution)/shard_map/impute_near/pallas_call | solution.py:255
  63.9 0.0 collective-permute-done.8.rest_e
  63.9 0.0 collective-permute-done.9.rest_o
  63.9 0.0 collective-permute-done.12.edge_e
  63.9 0.0 collective-permute-done.13.edge_o
  63.9 5.1 %impute_far.1 = (bf16[12416,128]{1,0:T(8,128)(2,1)S(1)}, bf16[8192,128]{1,0:T(8,128)(2,1)}) custom-call(s32[8]{0:T(128)S(1)} %compare_select_fusion.5.place, s32[64]{0:T(128)S(1)} %copy-done, s32[64]{0:T(128)S(1)} %copy-done.1, s32[8]{0:T(128)S(1)} %convert_reduce_fusion.below, ...), custom_call_target="tpu_custom_call", output_to_operand_aliasing={{0}: (9, {}), {1}: (10, {})} | custom-call | tf_op jit(solution)/shard_map/impute_far/pallas_call | solution.py:255
  (2 shorter events, 0.0 us)
Async XLA Ops:
  2.9 7.5 %collective-permute-start.2 = (bf16[1152,128]{1,0:T(8,128)(2,1)S(1)}, bf16[1152,128]{1,0:T(8,128)(2,1)S(1)}, u32[]{:S(2)}, u32[]{:S(2)}) collective-permute-start(bf16[1152,128]{1,0:T(8,128)(2,1)S(1)} %get-tuple-element.38.w_a), channel_id=1, source_target_pairs={{0,1},{1,0},{2,3},{3,2},{4,5},{5,4},{6,7},{7,6},{8,9},{9,8},{10,11... | collective-permute-start | bytes 884744 | tf_op jit(solution)/shard_map/ppermute | solution.py:285
  5.1 8.4 %collective-permute-start.3 = (bf16[1152,128]{1,0:T(8,128)(2,1)S(1)}, bf16[1152,128]{1,0:T(8,128)(2,1)S(1)}, u32[]{:S(2)}, u32[]{:S(2)}) collective-permute-start(bf16[1152,128]{1,0:T(8,128)(2,1)S(1)} %get-tuple-element.42.w_b), channel_id=1, source_target_pairs={{0,3},{1,2},{2,1},{3,0},{4,7},{5,6},{6,5},{7,4},{8,11},{9,10},{10,... | collective-permute-start | bytes 884744 | tf_op jit(solution)/shard_map/ppermute | solution.py:285
  9.2 36.4 %copy-start = (s32[64]{0:T(128)S(1)}, s32[64]{0:T(128)}, u32[]{:S(2)}) copy-start(s32[64]{0:T(128)} %starts.5) | copy-start | bytes 772
  9.2 36.4 %copy-start.2 = (s32[8]{0:T(128)S(1)}, s32[8]{0:T(128)}, u32[]{:S(2)}) copy-start(s32[8]{0:T(128)} %constant.48.clone) | copy-start | bytes 100
  9.2 36.6 %copy-start.1 = (s32[64]{0:T(128)S(1)}, s32[64]{0:T(128)}, u32[]{:S(2)}) copy-start(s32[64]{0:T(128)} %counts.5) | copy-start | bytes 772
  9.2 7.9 %collective-permute-start = (bf16[1024,128]{1,0:T(8,128)(2,1)S(1)}, bf16[1024,128]{1,0:T(8,128)(2,1)S(1)}, u32[]{:S(2)}, u32[]{:S(2)}) collective-permute-start(bf16[1024,128]{1,0:T(8,128)(2,1)S(1)} %get-tuple-element.40.w_a), channel_id=1, source_target_pairs={{0,1},{1,0},{2,3},{3,2},{4,5},{5,4},{6,7},{7,6},{8,9},{9,8},{10,11... | collective-permute-start | bytes 786440 | tf_op jit(solution)/shard_map/ppermute | solution.py:285
  9.6 9.6 %collective-permute-start.1 = (bf16[1024,128]{1,0:T(8,128)(2,1)S(1)}, bf16[1024,128]{1,0:T(8,128)(2,1)S(1)}, u32[]{:S(2)}, u32[]{:S(2)}) collective-permute-start(bf16[1024,128]{1,0:T(8,128)(2,1)S(1)} %get-tuple-element.41.w_b), channel_id=1, source_target_pairs={{0,3},{1,2},{2,1},{3,0},{4,7},{5,6},{6,5},{7,4},{8,11},{9,10},{10,... | collective-permute-start | bytes 786440 | tf_op jit(solution)/shard_map/ppermute | solution.py:285
  14.2 11.2 %collective-permute-start.6 = (bf16[1152,128]{1,0:T(8,128)(2,1)S(1)}, bf16[1152,128]{1,0:T(8,128)(2,1)S(1)}, u32[]{:S(2)}, u32[]{:S(2)}) collective-permute-start(bf16[1152,128]{1,0:T(8,128)(2,1)S(1)} %get-tuple-element.45), channel_id=1, source_target_pairs={{0,3},{1,2},{2,1},{3,0},{4,7},{5,6},{6,5},{7,4},{8,11},{9,10},{10,... | collective-permute-start | bytes 884744 | tf_op jit(solution)/shard_map/ppermute | solution.py:285
  16.5 9.0 %collective-permute-start.7 = (bf16[1152,128]{1,0:T(8,128)(2,1)S(1)}, bf16[1152,128]{1,0:T(8,128)(2,1)S(1)}, u32[]{:S(2)}, u32[]{:S(2)}) collective-permute-start(bf16[1152,128]{1,0:T(8,128)(2,1)S(1)} %get-tuple-element.52), channel_id=1, source_target_pairs={{0,1},{1,0},{2,3},{3,2},{4,5},{5,4},{6,7},{7,6},{8,9},{9,8},{10,11... | collective-permute-start | bytes 884744 | tf_op jit(solution)/shard_map/ppermute | solution.py:285
  19.9 21.6 %collective-permute-start.4 = (bf16[1024,128]{1,0:T(8,128)(2,1)S(1)}, bf16[1024,128]{1,0:T(8,128)(2,1)S(1)}, u32[]{:S(2)}, u32[]{:S(2)}) collective-permute-start(bf16[1024,128]{1,0:T(8,128)(2,1)S(1)} %get-tuple-element.49), channel_id=1, source_target_pairs={{0,3},{1,2},{2,1},{3,0},{4,7},{5,6},{6,5},{7,4},{8,11},{9,10},{10,... | collective-permute-start | bytes 786440 | tf_op jit(solution)/shard_map/ppermute | solution.py:285
  22.0 19.4 %collective-permute-start.5 = (bf16[1024,128]{1,0:T(8,128)(2,1)S(1)}, bf16[1024,128]{1,0:T(8,128)(2,1)S(1)}, u32[]{:S(2)}, u32[]{:S(2)}) collective-permute-start(bf16[1024,128]{1,0:T(8,128)(2,1)S(1)} %get-tuple-element.50), channel_id=1, source_target_pairs={{0,1},{1,0},{2,3},{3,2},{4,5},{5,4},{6,7},{7,6},{8,9},{9,8},{10,11... | collective-permute-start | bytes 786440 | tf_op jit(solution)/shard_map/ppermute | solution.py:285
  26.9 25.6 %collective-permute-start.10 = (bf16[2176,128]{1,0:T(8,128)(2,1)S(1)}, bf16[2176,128]{1,0:T(8,128)(2,1)S(1)}, u32[]{:S(2)}, u32[]{:S(2)}) collective-permute-start(bf16[2176,128]{1,0:T(8,128)(2,1)S(1)} %get-tuple-element.55.mid), channel_id=1, source_target_pairs={{0,4},{4,0},{8,12},{12,8},{16,20},{20,16},{24,28},{28,24},{32,36},... | collective-permute-start | bytes 1671176 | tf_op jit(solution)/shard_map/ppermute | solution.py:288
  28.8 23.7 %collective-permute-start.11 = (bf16[2176,128]{1,0:T(8,128)(2,1)}, bf16[2176,128]{1,0:T(8,128)(2,1)S(1)}, u32[]{:S(2)}, u32[]{:S(2)}) collective-permute-start(bf16[2176,128]{1,0:T(8,128)(2,1)} %get-tuple-element.61), channel_id=1, source_target_pairs={{0,0},{4,8},{8,4},{12,16},{16,12},{20,24},{24,20},{28,32},{32,28},... | collective-permute-start | bytes 1671176 | tf_op jit(solution)/shard_map/ppermute | solution.py:288
  41.6 22.3 %collective-permute-start.8 = (bf16[1792,128]{1,0:T(8,128)(2,1)S(1)}, bf16[1792,128]{1,0:T(8,128)(2,1)S(1)}, u32[]{:S(2)}, u32[]{:S(2)}) collective-permute-start(bf16[1792,128]{1,0:T(8,128)(2,1)S(1)} %get-tuple-element.58.rest), channel_id=1, source_target_pairs={{0,4},{4,0},{8,12},{12,8},{16,20},{20,16},{24,28},{28,24},{32,36},... | collective-permute-start | bytes 1376264 | tf_op jit(solution)/shard_map/ppermute | solution.py:288
  41.7 22.2 %collective-permute-start.9 = (bf16[1792,128]{1,0:T(8,128)(2,1)S(1)}, bf16[1792,128]{1,0:T(8,128)(2,1)S(1)}, u32[]{:S(2)}, u32[]{:S(2)}) collective-permute-start(bf16[1792,128]{1,0:T(8,128)(2,1)S(1)} %get-tuple-element.58.rest), channel_id=1, source_target_pairs={{0,0},{4,8},{8,4},{12,16},{16,12},{20,24},{24,20},{28,32},{32,28},... | collective-permute-start | bytes 1376264 | tf_op jit(solution)/shard_map/ppermute | solution.py:288
  53.2 10.7 %collective-permute-start.12 = (bf16[256,128]{1,0:T(8,128)(2,1)S(1)}, bf16[256,128]{1,0:T(8,128)(2,1)S(1)}, u32[]{:S(2)}, u32[]{:S(2)}) collective-permute-start(bf16[256,128]{1,0:T(8,128)(2,1)S(1)} %finish_edge.1.edge), channel_id=1, source_target_pairs={{0,4},{4,0},{8,12},{12,8},{16,20},{20,16},{24,28},{28,24},{32,36},... | collective-permute-start | bytes 196616 | tf_op jit(solution)/shard_map/ppermute | solution.py:288
  53.3 10.6 %collective-permute-start.13 = (bf16[256,128]{1,0:T(8,128)(2,1)S(1)}, bf16[256,128]{1,0:T(8,128)(2,1)S(1)}, u32[]{:S(2)}, u32[]{:S(2)}) collective-permute-start(bf16[256,128]{1,0:T(8,128)(2,1)S(1)} %finish_edge.1.edge), channel_id=1, source_target_pairs={{0,0},{4,8},{8,4},{12,16},{16,12},{20,24},{24,20},{28,32},{32,28},... | collective-permute-start | bytes 196616 | tf_op jit(solution)/shard_map/ppermute | solution.py:288

commit v5 on v4

--- a/solution.py
+++ b/solution.py
@@ -19,7 +19,7 @@
 HBM = pl.BlockSpec(memory_space=pltpu.HBM)
 SMEM = pl.BlockSpec(memory_space=pltpu.SMEM)
 VM = pl.BlockSpec(memory_space=pltpu.VMEM)
-PARAMS = pltpu.CompilerParams(vmem_limit_bytes=8 * 1024 * 1024)
+PARAMS = pltpu.CompilerParams(vmem_limit_bytes=16 * 1024 * 1024)
 MID = 8
 MID_END = TB - MID
 HALF1 = (MID_END - MID) // 2
@@ -143,7 +143,7 @@
     return pltpu.make_async_copy(staged.at[n], out.at[at(u)], sems.at[n])
 
 
-def on_ranges(ranges, starts, counts, lowest, ld, ext, out, staged, sems):
+def on_ranges(ranges, starts, counts, lowest, ld, fill, ext, out, ld_here, staged, ld_sems, out_sems):
     total = 0
     parts = []
     for low, high in ranges:
@@ -156,42 +156,49 @@
             u = jnp.where(n >= before, n - before + low, u)
         return u
 
+    def load(n):
+        return pltpu.make_async_copy(ld.at[window_of(n)], ld_here.at[n], ld_sems.at[n])
+
+    def begin(n, carry):
+        load(n).start()
+        return carry
+
     def several(k, carry):
         for i in range(UNROLL):
-            u = window_of(jnp.minimum(UNROLL * k + i, total - 1))
+            n = UNROLL * k + i
+
+            @pl.when(n < total)
+            def _():
+                load(n).wait()
+
+        for i in range(UNROLL):
+            n = jnp.minimum(UNROLL * k + i, total - 1)
+            u = window_of(n)
             first = jnp.clip(starts[u] - lowest, 0, 3 * TB - 1)
             have = counts[u]
             window = [ext[at(jnp.where(s < have, jnp.minimum(first + s, ZERO), ZERO)), :] for s in range(WIN)]
-            staged[UNROLL * k + i] = dot(ld[u], jnp.concatenate(window, axis=0)).astype(BF)
+            staged[UNROLL * k + i] = dot(ld_here[n], jnp.concatenate(window, axis=0)).astype(BF)
         for i in range(UNROLL):
             n = UNROLL * k + i
 
             @pl.when(n < total)
             def _():
-                to_out(window_of(n), n, out, staged, sems).start()
+                to_out(window_of(n), n, out, staged, out_sems).start()
 
         return carry
 
     def finish(n, carry):
-        to_out(window_of(n), n, out, staged, sems).wait()
+        to_out(window_of(n), n, out, staged, out_sems).wait()
         return carry
 
+    lax.fori_loop(0, total, begin, 0)
+    fill()
     lax.fori_loop(0, (total + UNROLL - 1) // UNROLL, several, 0)
     lax.fori_loop(0, total, finish, 0)
 
 
-def set_1(ext, base, mid):
-    return [(mid.at[at(0, 2 * HALF1)], ext.at[at(base + MID, 2 * HALF1)])]
-
-
-def set_2(ext, base, rest, edge):
-    inner = HALF2 - 1
-    return [
-        (edge.at[at(0)], ext.at[at(base)]),
-        (rest.at[at(0, inner)], ext.at[at(base + 1, inner)]),
-        (rest.at[at(inner, inner)], ext.at[at(base + MID_END, inner)]),
-        (edge.at[at(1)], ext.at[at(base + TB - 1)]),
-    ]
+def move(ext, block, source, first, blocks):
+    ext[at(block, blocks), :] = source[at(first, blocks), :]
 
 
 LIMITS = (
@@ -206,49 +213,41 @@
 )
 
 
-def impute_own(place, starts, counts, below, mid, rest, ld, ext, ld_here, out, staged, sems, out_sems):
+def impute_own(place, starts, counts, below, mid, rest, ld, ext, out, *scratch):
     inner = HALF2 - 1
-    quarter = UB // 4
-    whole = [(ld.at[pl.ds(k, quarter)], ld_here.at[pl.ds(k, quarter)]) for k in range(0, UB, quarter)]
-    loads = copy_all(whole, sems, 4)
-    copies = copy_all(
-        set_1(ext, TB, mid)
-        + [
-            (rest.at[at(0, inner)], ext.at[at(TB + 1, inner)]),
-            (rest.at[at(inner, inner)], ext.at[at(TB + MID_END, inner)]),
-        ],
-        sems,
-    )
-    ext[at(ZERO), :] = jnp.zeros((BLK, COLS), BF)
-    for copy in copies + loads:
-        copy.wait()
-    ranges = [(below[3], below[4])]
-    on_ranges(ranges, starts, counts, place[3] * TB - TB, ld_here, ext, out, staged, out_sems)
-
-
-def impute_near(
-    place, starts, counts, below, edge, mid_e, mid_o, ld, before, done, ext, out, staged, sems, out_sems
-):
-    base_e = 2 * TB * (1 - place[5])
-    base_o = 2 * TB * place[5]
-    own_edge = [(edge.at[at(0)], ext.at[at(TB)]), (edge.at[at(1)], ext.at[at(2 * TB - 1)])]
-    copies = copy_all(own_edge + set_1(ext, base_e, mid_e) + set_1(ext, base_o, mid_o), sems)
-    for copy in copies:
-        copy.wait()
+
+    def fill():
+        move(ext, TB + 1, rest, 0, inner)
+        move(ext, TB + MID, mid, 0, 2 * HALF1)
+        move(ext, TB + MID_END, rest, inner, inner)
+        ext[at(ZERO), :] = jnp.zeros((BLK, COLS), BF)
+
+    on_ranges([(below[3], below[4])], starts, counts, place[3] * TB - TB, ld, fill, ext, out, *scratch)
+
+
+def impute_near(place, starts, counts, below, edge, mid_e, mid_o, ld, before, done, ext, out, *scratch):
+    def fill():
+        move(ext, TB, edge, 0, 1)
+        move(ext, 2 * TB - 1, edge, 1, 1)
+        move(ext, 2 * TB * (1 - place[5]) + MID, mid_e, 0, 2 * HALF1)
+        move(ext, 2 * TB * place[5] + MID, mid_o, 0, 2 * HALF1)
+
     ranges = [(below[k], below[k + 1]) for k in (0, 2, 4, 6)]
-    on_ranges(ranges, starts, counts, place[3] * TB - TB, ld, ext, out, staged, out_sems)
-
-
-def impute_far(
-    place, starts, counts, below, rest_e, rest_o, edge_e, edge_o, ld, before, done, ext, out, staged, sems, out_sems
-):
-    base_e = 2 * TB * (1 - place[5])
-    base_o = 2 * TB * place[5]
-    copies = copy_all(set_2(ext, base_e, rest_e, edge_e) + set_2(ext, base_o, rest_o, edge_o), sems)
-    for copy in copies:
-        copy.wait()
+    on_ranges(ranges, starts, counts, place[3] * TB - TB, ld, fill, ext, out, *scratch)
+
+
+def impute_far(place, starts, counts, below, rest_e, rest_o, edge_e, edge_o, ld, before, done, ext, out, *scratch):
+    inner = HALF2 - 1
+
+    def fill():
+        for base, rest, edge in ((2 * TB * (1 - place[5]), rest_e, edge_e), (2 * TB * place[5], rest_o, edge_o)):
+            move(ext, base, edge, 0, 1)
+            move(ext, base + 1, rest, 0, inner)
+            move(ext, base + MID_END, rest, inner, inner)
+            move(ext, base + TB - 1, edge, 1, 1)
+
     ranges = [(0, below[0]), (below[1], below[2]), (below[5], below[6]), (below[7], UB)]
-    on_ranges(ranges, starts, counts, place[3] * TB - TB, ld, ext, out, staged, out_sems)
+    on_ranges(ranges, starts, counts, place[3] * TB - TB, ld, fill, ext, out, *scratch)
 
 
 def call(kernel, outs, ins, args, scratch=(), aliases=None):
@@ -279,7 +278,7 @@
     pairs_a = [(i, i ^ 1) for i in range(4)]
     pairs_b = [(i, 3 - i) for i in range(4)]
     pairs_e = [(i, i ^ 1) for i in range(owners)]
-    pairs_o = [(i, min(i + 1, owners - 1) if i % 2 else max(i - 1, 0)) for i in range(owners)]
+    pairs_o = [(i, (i + 1) % owners if i % 2 else (i - 1) % owners) for i in range(owners)]
 
     def along_trait(x, y, pairs_x, pairs_y):
         return lax.ppermute(x, "trait", pairs_x), lax.ppermute(y, "trait", pairs_y)
@@ -340,19 +339,14 @@
     starts_here = starts - (g * TB - TB)
     below = jnp.sum(starts_here[None, :] < jnp.array(LIMITS, jnp.int32)[:, None], axis=1, dtype=jnp.int32)
     window_scratch = [
+        pltpu.VMEM((UB, BLK, WIN * BLK), BF),
         pltpu.VMEM((UB, BLK, COLS), BF),
-        pltpu.SemaphoreType.DMA((8,)),
+        pltpu.SemaphoreType.DMA((UB,)),
         pltpu.SemaphoreType.DMA((UB,)),
     ]
     outs = [(shaped(EXT), VM), (shaped(UB), HBM)]
     plan = (place, starts, counts, below)
-    ext, ld, done = call(
-        impute_own,
-        [outs[0], (jax.ShapeDtypeStruct(ld.shape, BF), VM), outs[1]],
-        [SMEM] * 4 + [VM] * 2 + [HBM],
-        (*plan, to_e, mixed2, ld),
-        window_scratch,
-    )
+    ext, done = call(impute_own, outs, [SMEM] * 4 + [VM] * 2 + [HBM], (*plan, to_e, mixed2, ld), window_scratch)
     mid_e, mid_o, ext = lax.optimization_barrier((mid_e, mid_o, ext))
     (mixed3,) = call(
         finish_edge, in_vmem(shaped(2)), [SMEM] + [VM] * 4, (place, edge_sums, edge_band, mid_e, mid_o)
@@ -361,7 +355,7 @@
     ext, done = call(
         impute_near,
         outs,
-        [SMEM] * 4 + [VM] * 5 + [HBM],
+        [SMEM] * 4 + [VM] * 3 + [HBM, VM, HBM],
         (*plan, mixed3, mid_e, mid_o, ld, ext, done),
         window_scratch,
         {8: 0, 9: 1},
@@ -369,7 +363,7 @@
     _, out = call(
         impute_far,
         outs,
-        [SMEM] * 4 + [VM] * 6 + [HBM],
+        [SMEM] * 4 + [VM] * 4 + [HBM, VM, HBM],
         (*plan, rest_e, rest_o, edge_e, edge_o, ld, ext, done),
         window_scratch,
         {9: 0, 10: 1},

time: 69.2 us -> 68.8 us (level)
  starting transfers between devices: 35.6 us -> 29.6 us
  waiting for transfers between devices: 9.36 us -> 14.6 us
    ppermute x6, starting transfers between devices: 26.2 us -> 20.3 us  [along_rows(): return (lax.ppermute(x, ROWS, pairs_e), lax.ppermute(y, ROWS, pairs_o))]
    ppermute x6, waiting for transfers between devices: 0.02 us -> 5.28 us  [along_rows(): return (lax.ppermute(x, ROWS, pairs_e), lax.ppermute(y, ROWS, pairs_o))]
  transfers between devices with their start and end apart: 14 -> 14, of which waited for: 5 -> 6; matrix products, arithmetic and copies ran while one was open for 0% -> 0% of each run, Pallas kernels for 23% -> 23%
where the time goes in v5:
time: 68.8 us; the launch traced here: 68.7 us
  starting transfers between devices  29.6 us (43%)
  Pallas kernels  24 us (35%)
  waiting for transfers between devices  14.6 us (21%)
    pallas_call x10, Pallas kernels, call(): pl.pallas_call(kernel, name=kernel.__name__, out_shape=tuple((shape for s...  24 us
    ppermute x6, starting transfers between devices, along_rows(): return (lax.ppermute(x, ROWS, pairs_e), lax.ppermute(y, ROWS, pairs_o))  20.3 us
    ppermute x4, starting transfers between devices, along_trait(): lax.ppermute(x, 'trait', pairs_x)  6.91 us
    ppermute x6, waiting for transfers between devices, along_rows(): return (lax.ppermute(x, ROWS, pairs_e), lax.ppermute(y, ROWS, pairs_o))  5.28 us
    ppermute x4, waiting for transfers between devices, along_trait(): lax.ppermute(y, 'trait', pairs_y)  5.13 us
    ppermute x4, waiting for transfers between devices, along_trait(): lax.ppermute(x, 'trait', pairs_x)  4.22 us
    ppermute x4, starting transfers between devices, along_trait(): lax.ppermute(y, 'trait', pairs_y)  2.47 us
  transfers between devices with their start and end apart: 14, of which 6 were waited for; matrix products, arithmetic and copies ran while one was open for 0% of the time, Pallas kernels for 23%

profile of v5, /device:TPU:1, one launch (start us, length us, event | category | flops | bytes accessed | tf_op | source)
XLA Modules:
  0.0 68.7 jit_solution(1544038309919241509)
XLA Ops:
  0.0 2.9 %whiten_1.1 = (bf16[1152,128]{1,0:T(8,128)(2,1)S(1)}, bf16[1152,128]{1,0:T(8,128)(2,1)S(1)}, bf16[256,256]{1,0:T(8,128)(2,1)S(1)}, bf16[256,256]{1,0:T(8,128)(2,1)S(1)}) custom-call(s32[8]{0:T(128)S(1)} %compare_select_fusion.5.place, bf16[4096,128]{1,0:T(8,128)(2,1)} %z.2, bf16[32,128,384]{2,1,0:T(8,128)(2,1)} %band.3, bf16[512,512]{1,0:T(8,128)(2,1)} %mix.1), custom_call_target="tpu_custom_call" | custom-call | tf_op jit(solution)/shard_map/whiten_1/pallas_call | solution.py:254
  2.9 2.1 %collective-permute-start.2 = (bf16[1152,128]{1,0:T(8,128)(2,1)S(1)}, bf16[1152,128]{1,0:T(8,128)(2,1)S(1)}, u32[]{:S(2)}, u32[]{:S(2)}) collective-permute-start(bf16[1152,128]{1,0:T(8,128)(2,1)S(1)} %get-tuple-element.37.w_a), channel_id=1, source_target_pairs={{0,1},{1,0},{2,3},{3,2},{4,5},{5,4},{6,7},{7,6},{8,9},{9,8},{10,11... | collective-permute-start | bytes 884744 | tf_op jit(solution)/shard_map/ppermute | solution.py:284
  5.1 1.8 %collective-permute-start.3 = (bf16[1152,128]{1,0:T(8,128)(2,1)S(1)}, bf16[1152,128]{1,0:T(8,128)(2,1)S(1)}, u32[]{:S(2)}, u32[]{:S(2)}) collective-permute-start(bf16[1152,128]{1,0:T(8,128)(2,1)S(1)} %get-tuple-element.41.w_b), channel_id=1, source_target_pairs={{0,3},{1,2},{2,1},{3,0},{4,7},{5,6},{6,5},{7,4},{8,11},{9,10},{10,... | collective-permute-start | bytes 884744 | tf_op jit(solution)/shard_map/ppermute | solution.py:284
  6.9 2.3 %whiten_2.1 = (bf16[1024,128]{1,0:T(8,128)(2,1)S(1)}, bf16[1024,128]{1,0:T(8,128)(2,1)S(1)}, bf16[256,128]{1,0:T(8,128)(2,1)S(1)}) custom-call(bf16[4096,128]{1,0:T(8,128)(2,1)} %z.2, bf16[32,128,384]{2,1,0:T(8,128)(2,1)} %band.3), custom_call_target="tpu_custom_call" | custom-call | tf_op jit(solution)/shard_map/whiten_2/pallas_call | solution.py:254
  9.2 0.0 copy-start
  9.2 0.0 copy-start.2
  9.2 0.0 copy-start.1
  9.2 0.4 collective-permute-start
  9.6 0.7 collective-permute-start.1
  10.3 0.2 collective-permute-done.2.got_a
  10.5 3.0 %collective-permute-done.3.got_b = bf16[1152,128]{1,0:T(8,128)(2,1)S(1)} collective-permute-done((bf16[1152,128]{1,0:T(8,128)(2,1)S(1)}, bf16[1152,128]{1,0:T(8,128)(2,1)S(1)}, u32[]{:S(2)}, u32[]{:S(2)}) %collective-permute-start.3) | collective-permute-done | bytes 294944 | tf_op jit(solution)/shard_map/ppermute | solution.py:284
  13.5 0.8 %partial.2 = (bf16[1152,128]{1,0:T(8,128)(2,1)S(1)}, bf16[1152,128]{1,0:T(8,128)(2,1)S(1)}, f32[2304,128]{1,0:T(8,128)S(1)}) custom-call(bf16[1152,128]{1,0:T(8,128)(2,1)S(1)} %get-tuple-element.37.w_a, bf16[1152,128]{1,0:T(8,128)(2,1)S(1)} %collective-permute-done.2.got_a, bf16[1152,128]{1,0:T(8,128)(2,1)S(1)} %get-tuple-element.41.w_b, ...), custom_call_target="tpu_custom_call" | custom-call | tf_op jit(solution)/shard_map/partial/pallas_call | solution.py:254
  14.2 2.2 %collective-permute-start.6 = (bf16[1152,128]{1,0:T(8,128)(2,1)S(1)}, bf16[1152,128]{1,0:T(8,128)(2,1)S(1)}, u32[]{:S(2)}, u32[]{:S(2)}) collective-permute-start(bf16[1152,128]{1,0:T(8,128)(2,1)S(1)} %get-tuple-element.44), channel_id=1, source_target_pairs={{0,3},{1,2},{2,1},{3,0},{4,7},{5,6},{6,5},{7,4},{8,11},{9,10},{10,... | collective-permute-start | bytes 884744 | tf_op jit(solution)/shard_map/ppermute | solution.py:284
  16.5 0.0 collective-permute-start.7
  16.5 0.6 collective-permute-done.got_a
  17.1 2.1 %collective-permute-done.1.got_b = bf16[1024,128]{1,0:T(8,128)(2,1)S(1)} collective-permute-done((bf16[1024,128]{1,0:T(8,128)(2,1)S(1)}, bf16[1024,128]{1,0:T(8,128)(2,1)S(1)}, u32[]{:S(2)}, u32[]{:S(2)}) %collective-permute-start.1) | collective-permute-done | bytes 262176 | tf_op jit(solution)/shard_map/ppermute | solution.py:284
  19.2 0.7 %partial.3 = (bf16[1024,128]{1,0:T(8,128)(2,1)S(1)}, bf16[1024,128]{1,0:T(8,128)(2,1)S(1)}, f32[2048,128]{1,0:T(8,128)S(1)}) custom-call(bf16[1024,128]{1,0:T(8,128)(2,1)S(1)} %get-tuple-element.39.w_a, bf16[1024,128]{1,0:T(8,128)(2,1)S(1)} %collective-permute-done.got_a, bf16[1024,128]{1,0:T(8,128)(2,1)S(1)} %get-tuple-element.40.w_b, ...), custom_call_target="tpu_custom_call" | custom-call | tf_op jit(solution)/shard_map/partial/pallas_call | solution.py:254
  19.9 2.1 %collective-permute-start.4 = (bf16[1024,128]{1,0:T(8,128)(2,1)S(1)}, bf16[1024,128]{1,0:T(8,128)(2,1)S(1)}, u32[]{:S(2)}, u32[]{:S(2)}) collective-permute-start(bf16[1024,128]{1,0:T(8,128)(2,1)S(1)} %get-tuple-element.48), channel_id=1, source_target_pairs={{0,3},{1,2},{2,1},{3,0},{4,7},{5,6},{6,5},{7,4},{8,11},{9,10},{10,... | collective-permute-start | bytes 786440 | tf_op jit(solution)/shard_map/ppermute | solution.py:284
  22.0 0.0 collective-permute-start.5
  22.1 3.4 %collective-permute-done.6.far_a = bf16[1152,128]{1,0:T(8,128)(2,1)S(1)} collective-permute-done((bf16[1152,128]{1,0:T(8,128)(2,1)S(1)}, bf16[1152,128]{1,0:T(8,128)(2,1)S(1)}, u32[]{:S(2)}, u32[]{:S(2)}) %collective-permute-start.6) | collective-permute-done | bytes 294944 | tf_op jit(solution)/shard_map/ppermute | solution.py:284
  25.5 0.0 collective-permute-done.7.far_b
  25.5 1.5 %combine_1.1 = (bf16[2176,128]{1,0:T(8,128)(2,1)S(1)}, bf16[2176,128]{1,0:T(8,128)(2,1)}) custom-call(s32[8]{0:T(128)S(1)} %compare_select_fusion.5.place, f32[2304,128]{1,0:T(8,128)S(1)} %get-tuple-element.50.own, bf16[1152,128]{1,0:T(8,128)(2,1)S(1)} %collective-permute-done.6.far_a, bf16[1152,128]{1,0:T(8,128)(2,1)S(1)} %collective-permute-done.7.far_b), custom_call_target="tpu_custom_call" | custom-call | tf_op jit(solution)/shard_map/combine_1/pallas_call | solution.py:254
  26.9 1.9 %collective-permute-start.10 = (bf16[2176,128]{1,0:T(8,128)(2,1)S(1)}, bf16[2176,128]{1,0:T(8,128)(2,1)S(1)}, u32[]{:S(2)}, u32[]{:S(2)}) collective-permute-start(bf16[2176,128]{1,0:T(8,128)(2,1)S(1)} %get-tuple-element.54.mid), channel_id=1, source_target_pairs={{0,4},{4,0},{8,12},{12,8},{16,20},{20,16},{24,28},{28,24},{32,36},... | collective-permute-start | bytes 1671176 | tf_op jit(solution)/shard_map/ppermute | solution.py:287
  28.8 10.8 %collective-permute-start.11 = (bf16[2176,128]{1,0:T(8,128)(2,1)}, bf16[2176,128]{1,0:T(8,128)(2,1)S(1)}, u32[]{:S(2)}, u32[]{:S(2)}) collective-permute-start(bf16[2176,128]{1,0:T(8,128)(2,1)} %get-tuple-element.60), channel_id=1, source_target_pairs={{0,252},{4,8},{8,4},{12,16},{16,12},{20,24},{24,20},{28,32},{32,28... | collective-permute-start | bytes 1671176 | tf_op jit(solution)/shard_map/ppermute | solution.py:287
  39.6 0.0 collective-permute-done.4.far_a
  39.6 0.0 collective-permute-done.5.far_b
  39.6 0.1 combine_2.1
  39.7 0.1 collective-permute-start.8
  39.8 2.6 %collective-permute-start.9 = (bf16[1792,128]{1,0:T(8,128)(2,1)S(1)}, bf16[1792,128]{1,0:T(8,128)(2,1)S(1)}, u32[]{:S(2)}, u32[]{:S(2)}) collective-permute-start(bf16[1792,128]{1,0:T(8,128)(2,1)S(1)} %get-tuple-element.57.rest), channel_id=1, source_target_pairs={{0,252},{4,8},{8,4},{12,16},{16,12},{20,24},{24,20},{28,32},{32,28... | collective-permute-start | bytes 1376264 | tf_op jit(solution)/shard_map/ppermute | solution.py:287
  42.4 0.0 copy-done
  42.4 0.0 copy-done.2
  42.4 0.2 convert_reduce_fusion.below
  42.6 0.0 copy-done.1
  42.6 5.5 %impute_own.1 = (bf16[12416,128]{1,0:T(8,128)(2,1)S(1)}, bf16[8192,128]{1,0:T(8,128)(2,1)}) custom-call(s32[8]{0:T(128)S(1)} %compare_select_fusion.5.place, s32[64]{0:T(128)S(1)} %copy-done, s32[64]{0:T(128)S(1)} %copy-done.1, s32[8]{0:T(128)S(1)} %convert_reduce_fusion.below, bf16[2176,128]{1,0:T(8,128)(2,1)S(1)} %get-tuple-element.54.mid, ...), custom_call_target="tpu_custom_call" | custom-call | tf_op jit(solution)/shard_map/impute_own/pallas_call | solution.py:254
  48.0 0.0 collective-permute-done.10.got_e.mid_e
  48.0 5.3 %collective-permute-done.11.got_o.mid_o = bf16[2176,128]{1,0:T(8,128)(2,1)S(1)} collective-permute-done((bf16[2176,128]{1,0:T(8,128)(2,1)}, bf16[2176,128]{1,0:T(8,128)(2,1)S(1)}, u32[]{:S(2)}, u32[]{:S(2)}) %collective-permute-start.11) | collective-permute-done | bytes 557088 | tf_op jit(solution)/shard_map/ppermute | solution.py:287
  53.3 0.7 %finish_edge.1.edge = bf16[256,128]{1,0:T(8,128)(2,1)S(1)} custom-call(s32[8]{0:T(128)S(1)} %compare_select_fusion.5.place, f32[256,128]{1,0:T(8,128)S(1)} %get-tuple-element.58.edge, bf16[256,128]{1,0:T(8,128)(2,1)S(1)} %get-tuple-element.59.edge_band, bf16[2176,128]{1,0:T(8,128)(2,1)S(1)} %collective-permute-done.10.got_e.mid_e, ...), custom_call_target="tpu_custom_call" | custom-call | tf_op jit(solution)/shard_map/finish_edge/pallas_call | solution.py:254
  54.0 0.1 collective-permute-start.12
  54.1 4.9 %collective-permute-start.13 = (bf16[256,128]{1,0:T(8,128)(2,1)S(1)}, bf16[256,128]{1,0:T(8,128)(2,1)S(1)}, u32[]{:S(2)}, u32[]{:S(2)}) collective-permute-start(bf16[256,128]{1,0:T(8,128)(2,1)S(1)} %finish_edge.1.edge), channel_id=1, source_target_pairs={{0,252},{4,8},{8,4},{12,16},{16,12},{20,24},{24,20},{28,32},{32,28... | collective-permute-start | bytes 196616 | tf_op jit(solution)/shard_map/ppermute | solution.py:287
  59.0 4.6 %impute_near.1 = (bf16[12416,128]{1,0:T(8,128)(2,1)S(1)}, bf16[8192,128]{1,0:T(8,128)(2,1)}) custom-call(s32[8]{0:T(128)S(1)} %compare_select_fusion.5.place, s32[64]{0:T(128)S(1)} %copy-done, s32[64]{0:T(128)S(1)} %copy-done.1, s32[8]{0:T(128)S(1)} %convert_reduce_fusion.below, ...), custom_call_target="tpu_custom_call", output_to_operand_aliasing={{0}: (8, {}), {1}: (9, {})} | custom-call | tf_op jit(solution)/shard_map/impute_near/pallas_call | solution.py:254
  63.6 0.0 collective-permute-done.8.rest_e
  63.6 0.0 collective-permute-done.9.rest_o
  63.6 0.0 collective-permute-done.12.edge_e
  63.6 0.0 collective-permute-done.13.edge_o
  63.6 5.1 %impute_far.1 = (bf16[12416,128]{1,0:T(8,128)(2,1)S(1)}, bf16[8192,128]{1,0:T(8,128)(2,1)}) custom-call(s32[8]{0:T(128)S(1)} %compare_select_fusion.5.place, s32[64]{0:T(128)S(1)} %copy-done, s32[64]{0:T(128)S(1)} %copy-done.1, s32[8]{0:T(128)S(1)} %convert_reduce_fusion.below, ...), custom_call_target="tpu_custom_call", output_to_operand_aliasing={{0}: (9, {}), {1}: (10, {})} | custom-call | tf_op jit(solution)/shard_map/impute_far/pallas_call | solution.py:254
  (2 shorter events, 0.0 us)
Async XLA Ops:
  2.9 7.5 %collective-permute-start.2 = (bf16[1152,128]{1,0:T(8,128)(2,1)S(1)}, bf16[1152,128]{1,0:T(8,128)(2,1)S(1)}, u32[]{:S(2)}, u32[]{:S(2)}) collective-permute-start(bf16[1152,128]{1,0:T(8,128)(2,1)S(1)} %get-tuple-element.37.w_a), channel_id=1, source_target_pairs={{0,1},{1,0},{2,3},{3,2},{4,5},{5,4},{6,7},{7,6},{8,9},{9,8},{10,11... | collective-permute-start | bytes 884744 | tf_op jit(solution)/shard_map/ppermute | solution.py:284
  5.1 8.4 %collective-permute-start.3 = (bf16[1152,128]{1,0:T(8,128)(2,1)S(1)}, bf16[1152,128]{1,0:T(8,128)(2,1)S(1)}, u32[]{:S(2)}, u32[]{:S(2)}) collective-permute-start(bf16[1152,128]{1,0:T(8,128)(2,1)S(1)} %get-tuple-element.41.w_b), channel_id=1, source_target_pairs={{0,3},{1,2},{2,1},{3,0},{4,7},{5,6},{6,5},{7,4},{8,11},{9,10},{10,... | collective-permute-start | bytes 884744 | tf_op jit(solution)/shard_map/ppermute | solution.py:284
  9.2 33.2 %copy-start = (s32[64]{0:T(128)S(1)}, s32[64]{0:T(128)}, u32[]{:S(2)}) copy-start(s32[64]{0:T(128)} %starts.5) | copy-start | bytes 772
  9.2 33.2 %copy-start.2 = (s32[8]{0:T(128)S(1)}, s32[8]{0:T(128)}, u32[]{:S(2)}) copy-start(s32[8]{0:T(128)} %constant.48.clone) | copy-start | bytes 100
  9.2 33.4 %copy-start.1 = (s32[64]{0:T(128)S(1)}, s32[64]{0:T(128)}, u32[]{:S(2)}) copy-start(s32[64]{0:T(128)} %counts.5) | copy-start | bytes 772
  9.2 7.9 %collective-permute-start = (bf16[1024,128]{1,0:T(8,128)(2,1)S(1)}, bf16[1024,128]{1,0:T(8,128)(2,1)S(1)}, u32[]{:S(2)}, u32[]{:S(2)}) collective-permute-start(bf16[1024,128]{1,0:T(8,128)(2,1)S(1)} %get-tuple-element.39.w_a), channel_id=1, source_target_pairs={{0,1},{1,0},{2,3},{3,2},{4,5},{5,4},{6,7},{7,6},{8,9},{9,8},{10,11... | collective-permute-start | bytes 786440 | tf_op jit(solution)/shard_map/ppermute | solution.py:284
  9.6 9.6 %collective-permute-start.1 = (bf16[1024,128]{1,0:T(8,128)(2,1)S(1)}, bf16[1024,128]{1,0:T(8,128)(2,1)S(1)}, u32[]{:S(2)}, u32[]{:S(2)}) collective-permute-start(bf16[1024,128]{1,0:T(8,128)(2,1)S(1)} %get-tuple-element.40.w_b), channel_id=1, source_target_pairs={{0,3},{1,2},{2,1},{3,0},{4,7},{5,6},{6,5},{7,4},{8,11},{9,10},{10,... | collective-permute-start | bytes 786440 | tf_op jit(solution)/shard_map/ppermute | solution.py:284
  14.2 11.2 %collective-permute-start.6 = (bf16[1152,128]{1,0:T(8,128)(2,1)S(1)}, bf16[1152,128]{1,0:T(8,128)(2,1)S(1)}, u32[]{:S(2)}, u32[]{:S(2)}) collective-permute-start(bf16[1152,128]{1,0:T(8,128)(2,1)S(1)} %get-tuple-element.44), channel_id=1, source_target_pairs={{0,3},{1,2},{2,1},{3,0},{4,7},{5,6},{6,5},{7,4},{8,11},{9,10},{10,... | collective-permute-start | bytes 884744 | tf_op jit(solution)/shard_map/ppermute | solution.py:284
  16.5 9.0 %collective-permute-start.7 = (bf16[1152,128]{1,0:T(8,128)(2,1)S(1)}, bf16[1152,128]{1,0:T(8,128)(2,1)S(1)}, u32[]{:S(2)}, u32[]{:S(2)}) collective-permute-start(bf16[1152,128]{1,0:T(8,128)(2,1)S(1)} %get-tuple-element.51), channel_id=1, source_target_pairs={{0,1},{1,0},{2,3},{3,2},{4,5},{5,4},{6,7},{7,6},{8,9},{9,8},{10,11... | collective-permute-start | bytes 884744 | tf_op jit(solution)/shard_map/ppermute | solution.py:284
  19.9 19.6 %collective-permute-start.4 = (bf16[1024,128]{1,0:T(8,128)(2,1)S(1)}, bf16[1024,128]{1,0:T(8,128)(2,1)S(1)}, u32[]{:S(2)}, u32[]{:S(2)}) collective-permute-start(bf16[1024,128]{1,0:T(8,128)(2,1)S(1)} %get-tuple-element.48), channel_id=1, source_target_pairs={{0,3},{1,2},{2,1},{3,0},{4,7},{5,6},{6,5},{7,4},{8,11},{9,10},{10,... | collective-permute-start | bytes 786440 | tf_op jit(solution)/shard_map/ppermute | solution.py:284
  22.0 17.5 %collective-permute-start.5 = (bf16[1024,128]{1,0:T(8,128)(2,1)S(1)}, bf16[1024,128]{1,0:T(8,128)(2,1)S(1)}, u32[]{:S(2)}, u32[]{:S(2)}) collective-permute-start(bf16[1024,128]{1,0:T(8,128)(2,1)S(1)} %get-tuple-element.49), channel_id=1, source_target_pairs={{0,1},{1,0},{2,3},{3,2},{4,5},{5,4},{6,7},{7,6},{8,9},{9,8},{10,11... | collective-permute-start | bytes 786440 | tf_op jit(solution)/shard_map/ppermute | solution.py:284
  26.9 21.1 %collective-permute-start.10 = (bf16[2176,128]{1,0:T(8,128)(2,1)S(1)}, bf16[2176,128]{1,0:T(8,128)(2,1)S(1)}, u32[]{:S(2)}, u32[]{:S(2)}) collective-permute-start(bf16[2176,128]{1,0:T(8,128)(2,1)S(1)} %get-tuple-element.54.mid), channel_id=1, source_target_pairs={{0,4},{4,0},{8,12},{12,8},{16,20},{20,16},{24,28},{28,24},{32,36},... | collective-permute-start | bytes 1671176 | tf_op jit(solution)/shard_map/ppermute | solution.py:287
  28.8 24.5 %collective-permute-start.11 = (bf16[2176,128]{1,0:T(8,128)(2,1)}, bf16[2176,128]{1,0:T(8,128)(2,1)S(1)}, u32[]{:S(2)}, u32[]{:S(2)}) collective-permute-start(bf16[2176,128]{1,0:T(8,128)(2,1)} %get-tuple-element.60), channel_id=1, source_target_pairs={{0,252},{4,8},{8,4},{12,16},{16,12},{20,24},{24,20},{28,32},{32,28... | collective-permute-start | bytes 1671176 | tf_op jit(solution)/shard_map/ppermute | solution.py:287
  39.7 23.9 %collective-permute-start.8 = (bf16[1792,128]{1,0:T(8,128)(2,1)S(1)}, bf16[1792,128]{1,0:T(8,128)(2,1)S(1)}, u32[]{:S(2)}, u32[]{:S(2)}) collective-permute-start(bf16[1792,128]{1,0:T(8,128)(2,1)S(1)} %get-tuple-element.57.rest), channel_id=1, source_target_pairs={{0,4},{4,0},{8,12},{12,8},{16,20},{20,16},{24,28},{28,24},{32,36},... | collective-permute-start | bytes 1376264 | tf_op jit(solution)/shard_map/ppermute | solution.py:287
  39.8 23.8 %collective-permute-start.9 = (bf16[1792,128]{1,0:T(8,128)(2,1)S(1)}, bf16[1792,128]{1,0:T(8,128)(2,1)S(1)}, u32[]{:S(2)}, u32[]{:S(2)}) collective-permute-start(bf16[1792,128]{1,0:T(8,128)(2,1)S(1)} %get-tuple-element.57.rest), channel_id=1, source_target_pairs={{0,252},{4,8},{8,4},{12,16},{16,12},{20,24},{24,20},{28,32},{32,28... | collective-permute-start | bytes 1376264 | tf_op jit(solution)/shard_map/ppermute | solution.py:287
  54.0 9.6 %collective-permute-start.12 = (bf16[256,128]{1,0:T(8,128)(2,1)S(1)}, bf16[256,128]{1,0:T(8,128)(2,1)S(1)}, u32[]{:S(2)}, u32[]{:S(2)}) collective-permute-start(bf16[256,128]{1,0:T(8,128)(2,1)S(1)} %finish_edge.1.edge), channel_id=1, source_target_pairs={{0,4},{4,0},{8,12},{12,8},{16,20},{20,16},{24,28},{28,24},{32,36},... | collective-permute-start | bytes 196616 | tf_op jit(solution)/shard_map/ppermute | solution.py:287
  54.1 9.5 %collective-permute-start.13 = (bf16[256,128]{1,0:T(8,128)(2,1)S(1)}, bf16[256,128]{1,0:T(8,128)(2,1)S(1)}, u32[]{:S(2)}, u32[]{:S(2)}) collective-permute-start(bf16[256,128]{1,0:T(8,128)(2,1)S(1)} %finish_edge.1.edge), channel_id=1, source_target_pairs={{0,252},{4,8},{8,4},{12,16},{16,12},{20,24},{24,20},{28,32},{32,28... | collective-permute-start | bytes 196616 | tf_op jit(solution)/shard_map/ppermute | solution.py:287

commit v6 on v5

--- a/solution.py
+++ b/solution.py
@@ -108,16 +108,11 @@
         send[...] = both[:, COLS:].astype(BF)
 
 
-def combine_1(place, own, far_a, far_b, out_e, out_o):
+def combine_1(own, far_a, far_b, out):
     for k, far in enumerate((far_a, far_b)):
-        rows = (own[at(k * (HALF1 + 1), HALF1), :] + far[at(0, HALF1), :].astype(F32)).astype(BF)
-        out_e[at(k * HALF1, HALF1), :] = rows
-        out_o[at(k * HALF1, HALF1), :] = rows
-    first = (own[at(HALF1), :] + far_a[at(HALF1), :].astype(F32)).astype(BF)
-    last = (own[at(2 * HALF1 + 1), :] + far_b[at(HALF1), :].astype(F32)).astype(BF)
-    odd = place[5] == 1
-    out_e[at(2 * HALF1), :] = jnp.where(odd, first, last)
-    out_o[at(2 * HALF1), :] = jnp.where(odd, last, first)
+        rows = (own[at(k * (HALF1 + 1), HALF1 + 1), :] + far[...].astype(F32)).astype(BF)
+        out[at(k * HALF1, HALF1), :] = rows[: HALF1 * BLK]
+        out[at(2 * HALF1 + k), :] = rows[HALF1 * BLK :]
 
 
 def combine_2(own, far_a, far_b, out, edge):
@@ -131,19 +126,15 @@
 def finish_edge(place, edge, edge_band, got_e, got_o, out):
     odd = place[5] == 1
     nothing = jnp.zeros((BLK, COLS), BF)
-    end_e = got_e[at(2 * HALF1), :]
-    end_o = got_o[at(2 * HALF1), :]
-    from_left = jnp.where(place[3] == 0, nothing, jnp.where(odd, end_e, end_o))
-    from_right = jnp.where(place[3] == place[4] - 1, nothing, jnp.where(odd, end_o, end_e))
+    from_left = jnp.where(odd, got_e[at(2 * HALF1 + 1), :], got_o[at(2 * HALF1 + 1), :])
+    from_right = jnp.where(odd, got_o[at(2 * HALF1), :], got_e[at(2 * HALF1), :])
+    from_left = jnp.where(place[3] == 0, nothing, from_left)
+    from_right = jnp.where(place[3] == place[4] - 1, nothing, from_right)
     for k, rows in enumerate((from_left, from_right)):
         out[at(k), :] = (edge[at(k), :] + dot(edge_band[at(k), :], rows)).astype(BF)
 
 
-def to_out(u, n, out, staged, sems):
-    return pltpu.make_async_copy(staged.at[n], out.at[at(u)], sems.at[n])
-
-
-def on_ranges(ranges, starts, counts, lowest, ld, fill, ext, out, ld_here, staged, ld_sems, out_sems):
+def on_ranges(ranges, starts, counts, lowest, ld, ext, out, ready=None):
     total = 0
     parts = []
     for low, high in ranges:
@@ -156,45 +147,18 @@
             u = jnp.where(n >= before, n - before + low, u)
         return u
 
-    def load(n):
-        return pltpu.make_async_copy(ld.at[window_of(n)], ld_here.at[n], ld_sems.at[n])
-
-    def begin(n, carry):
-        load(n).start()
-        return carry
-
     def several(k, carry):
+        if ready is not None:
+            ready(k)
         for i in range(UNROLL):
-            n = UNROLL * k + i
-
-            @pl.when(n < total)
-            def _():
-                load(n).wait()
-
-        for i in range(UNROLL):
-            n = jnp.minimum(UNROLL * k + i, total - 1)
-            u = window_of(n)
+            u = window_of(jnp.minimum(UNROLL * k + i, total - 1))
             first = jnp.clip(starts[u] - lowest, 0, 3 * TB - 1)
             have = counts[u]
             window = [ext[at(jnp.where(s < have, jnp.minimum(first + s, ZERO), ZERO)), :] for s in range(WIN)]
-            staged[UNROLL * k + i] = dot(ld_here[n], jnp.concatenate(window, axis=0)).astype(BF)
-        for i in range(UNROLL):
-            n = UNROLL * k + i
-
-            @pl.when(n < total)
-            def _():
-                to_out(window_of(n), n, out, staged, out_sems).start()
-
+            out[at(u), :] = dot(ld[u], jnp.concatenate(window, axis=0)).astype(BF)
         return carry
 
-    def finish(n, carry):
-        to_out(window_of(n), n, out, staged, out_sems).wait()
-        return carry
-
-    lax.fori_loop(0, total, begin, 0)
-    fill()
     lax.fori_loop(0, (total + UNROLL - 1) // UNROLL, several, 0)
-    lax.fori_loop(0, total, finish, 0)
 
 
 def move(ext, block, source, first, blocks):
@@ -213,41 +177,57 @@
 )
 
 
-def impute_own(place, starts, counts, below, mid, rest, ld, ext, out, *scratch):
+def impute_own(place, starts, counts, below, mid, rest, ld, ext, out, ld_here, sems):
     inner = HALF2 - 1
-
-    def fill():
-        move(ext, TB + 1, rest, 0, inner)
-        move(ext, TB + MID, mid, 0, 2 * HALF1)
-        move(ext, TB + MID_END, rest, inner, inner)
-        ext[at(ZERO), :] = jnp.zeros((BLK, COLS), BF)
-
-    on_ranges([(below[3], below[4])], starts, counts, place[3] * TB - TB, ld, fill, ext, out, *scratch)
-
-
-def impute_near(place, starts, counts, below, edge, mid_e, mid_o, ld, before, done, ext, out, *scratch):
-    def fill():
-        move(ext, TB, edge, 0, 1)
-        move(ext, 2 * TB - 1, edge, 1, 1)
-        move(ext, 2 * TB * (1 - place[5]) + MID, mid_e, 0, 2 * HALF1)
-        move(ext, 2 * TB * place[5] + MID, mid_o, 0, 2 * HALF1)
-
+    low, high = below[3], below[4]
+    groups = (high - low + UNROLL - 1) // UNROLL
+
+    def load(k):
+        part = pl.ds(pl.multiple_of((low // UNROLL + k) % (UB // UNROLL) * UNROLL, UNROLL), UNROLL)
+        return pltpu.make_async_copy(ld.at[part], ld_here.at[part], sems.at[k])
+
+    def ready(k):
+        @pl.when(k + 1 < UB // UNROLL)
+        def _():
+            load(k + 1).wait()
+
+    def rest_ready(k, carry):
+        load(k).wait()
+        return carry
+
+    for k in range(UB // UNROLL):
+        load(k).start()
+    move(ext, TB + 1, rest, 0, inner)
+    move(ext, TB + MID, mid, 0, 2 * HALF1)
+    move(ext, TB + MID_END, rest, inner, inner)
+    ext[at(ZERO), :] = jnp.zeros((BLK, COLS), BF)
+    load(0).wait()
+    on_ranges([(low, high)], starts, counts, place[3] * TB - TB, ld_here, ext, out, ready)
+    lax.fori_loop(groups + 1, UB // UNROLL, rest_ready, 0)
+
+
+def impute_near(place, starts, counts, below, edge, mid_e, mid_o, ld, before, done, ext, out):
+    move(ext, TB, edge, 0, 1)
+    move(ext, 2 * TB - 1, edge, 1, 1)
+    move(ext, 2 * TB * (1 - place[5]) + MID, mid_e, 0, 2 * HALF1)
+    move(ext, 2 * TB * place[5] + MID, mid_o, 0, 2 * HALF1)
     ranges = [(below[k], below[k + 1]) for k in (0, 2, 4, 6)]
-    on_ranges(ranges, starts, counts, place[3] * TB - TB, ld, fill, ext, out, *scratch)
-
-
-def impute_far(place, starts, counts, below, rest_e, rest_o, edge_e, edge_o, ld, before, done, ext, out, *scratch):
+    on_ranges(ranges, starts, counts, place[3] * TB - TB, ld, ext, out)
+
+
+def impute_far(place, starts, counts, below, rest_e, rest_o, edge_e, edge_o, ld, before, done, ext, rows, out, sems):
     inner = HALF2 - 1
-
-    def fill():
-        for base, rest, edge in ((2 * TB * (1 - place[5]), rest_e, edge_e), (2 * TB * place[5], rest_o, edge_o)):
-            move(ext, base, edge, 0, 1)
-            move(ext, base + 1, rest, 0, inner)
-            move(ext, base + MID_END, rest, inner, inner)
-            move(ext, base + TB - 1, edge, 1, 1)
-
+    for base, rest, edge in ((2 * TB * (1 - place[5]), rest_e, edge_e), (2 * TB * place[5], rest_o, edge_o)):
+        move(ext, base, edge, 0, 1)
+        move(ext, base + 1, rest, 0, inner)
+        move(ext, base + MID_END, rest, inner, inner)
+        move(ext, base + TB - 1, edge, 1, 1)
     ranges = [(0, below[0]), (below[1], below[2]), (below[5], below[6]), (below[7], UB)]
-    on_ranges(ranges, starts, counts, place[3] * TB - TB, ld, fill, ext, out, *scratch)
+    on_ranges(ranges, starts, counts, place[3] * TB - TB, ld, ext, rows)
+    quarter = UB // 4
+    parts = [(rows.at[at(k, quarter)], out.at[at(k, quarter)]) for k in range(0, UB, quarter)]
+    for copy in copy_all(parts, sems):
+        copy.wait()
 
 
 def call(kernel, outs, ins, args, scratch=(), aliases=None):
@@ -324,29 +304,23 @@
     got2a, got2b, _ = lax.optimization_barrier((got2a, got2b, after))
     (own2, far2a, far2b), after = mixing(w2a, got2a, w2b, got2b)
     far1a, far1b, _ = lax.optimization_barrier((far1a, far1b, after))
-    to_e, to_o = call(
-        combine_1,
-        in_vmem(shaped(2 * HALF1 + 1), shaped(2 * HALF1 + 1)),
-        [SMEM] + [VM] * 3,
-        (place, own1, far1a, far1b),
-    )
-    mid_e, mid_o = along_rows(to_e, to_o)
-    far2a, far2b, _ = lax.optimization_barrier((far2a, far2b, to_e))
+    (mixed1,) = call(combine_1, in_vmem(shaped(2 * HALF1 + 2)), [VM] * 3, (own1, far1a, far1b))
+    mid_e, mid_o = along_rows(mixed1, mixed1)
+    far2a, far2b, _ = lax.optimization_barrier((far2a, far2b, mixed1))
     mixed2, edge_sums = call(
         combine_2, in_vmem(shaped(2 * HALF2 - 2), shaped(2, F32)), [VM] * 3, (own2, far2a, far2b)
     )
     rest_e, rest_o = along_rows(mixed2, mixed2)
     starts_here = starts - (g * TB - TB)
     below = jnp.sum(starts_here[None, :] < jnp.array(LIMITS, jnp.int32)[:, None], axis=1, dtype=jnp.int32)
-    window_scratch = [
-        pltpu.VMEM((UB, BLK, WIN * BLK), BF),
-        pltpu.VMEM((UB, BLK, COLS), BF),
-        pltpu.SemaphoreType.DMA((UB,)),
-        pltpu.SemaphoreType.DMA((UB,)),
-    ]
-    outs = [(shaped(EXT), VM), (shaped(UB), HBM)]
     plan = (place, starts, counts, below)
-    ext, done = call(impute_own, outs, [SMEM] * 4 + [VM] * 2 + [HBM], (*plan, to_e, mixed2, ld), window_scratch)
+    ext, done, ld = call(
+        impute_own,
+        in_vmem(shaped(EXT), shaped(UB), jax.ShapeDtypeStruct(ld.shape, BF)),
+        [SMEM] * 4 + [VM] * 2 + [HBM],
+        (*plan, mixed1, mixed2, ld),
+        [pltpu.SemaphoreType.DMA((UB // UNROLL,))],
+    )
     mid_e, mid_o, ext = lax.optimization_barrier((mid_e, mid_o, ext))
     (mixed3,) = call(
         finish_edge, in_vmem(shaped(2)), [SMEM] + [VM] * 4, (place, edge_sums, edge_band, mid_e, mid_o)
@@ -354,18 +328,18 @@
     edge_e, edge_o = along_rows(mixed3, mixed3)
     ext, done = call(
         impute_near,
-        outs,
-        [SMEM] * 4 + [VM] * 3 + [HBM, VM, HBM],
+        in_vmem(shaped(EXT), shaped(UB)),
+        [SMEM] * 4 + [VM] * 6,
         (*plan, mixed3, mid_e, mid_o, ld, ext, done),
-        window_scratch,
+        (),
         {8: 0, 9: 1},
     )
-    _, out = call(
+    _, _, out = call(
         impute_far,
-        outs,
-        [SMEM] * 4 + [VM] * 4 + [HBM, VM, HBM],
+        in_vmem(shaped(EXT), shaped(UB)) + [(shaped(UB), HBM)],
+        [SMEM] * 4 + [VM] * 7,
         (*plan, rest_e, rest_o, edge_e, edge_o, ld, ext, done),
-        window_scratch,
+        [pltpu.SemaphoreType.DMA((4,))],
         {9: 0, 10: 1},
     )
     return out

time: 68.8 us -> 64.8 us (0.942)
  Pallas kernels: 24 us -> 17.3 us
  waiting for transfers between devices: 14.6 us -> 20.1 us
  starting transfers between devices: 29.6 us -> 27.2 us
    pallas_call x10, Pallas kernels: 24 us -> 17.3 us  [call(): pl.pallas_call(kernel, name=kernel.__name__, out_shape=tuple((shape for s...]
    ppermute x6, waiting for transfers between devices: 5.28 us -> 9.12 us  [along_rows(): return (lax.ppermute(x, ROWS, pairs_e), lax.ppermute(y, ROWS, pairs_o))]
    ppermute x4, starting transfers between devices: 6.91 us -> 4.33 us  [along_trait(): lax.ppermute(x, 'trait', pairs_x)]
    ppermute x4, starting transfers between devices: 2.47 us -> 3.81 us  [along_trait(): lax.ppermute(y, 'trait', pairs_y)]
    ppermute x6, starting transfers between devices: 20.3 us -> 19.1 us  [along_rows(): return (lax.ppermute(x, ROWS, pairs_e), lax.ppermute(y, ROWS, pairs_o))]
    ppermute x4, waiting for transfers between devices: 5.13 us -> 5.98 us  [along_trait(): lax.ppermute(y, 'trait', pairs_y)]
    ppermute x4, waiting for transfers between devices: 4.22 us -> 5 us  [along_trait(): lax.ppermute(x, 'trait', pairs_x)]
  transfers between devices with their start and end apart: 14 -> 14, of which waited for: 6 -> 8; matrix products, arithmetic and copies ran while one was open for 0% -> 0% of each run, Pallas kernels for 23% -> 16%
where the time goes in v6:
time: 64.8 us; the launch traced here: 64.9 us
  starting transfers between devices  27.2 us (42%)
  waiting for transfers between devices  20.1 us (31%)
  Pallas kernels  17.3 us (27%)
    ppermute x6, starting transfers between devices, along_rows(): return (lax.ppermute(x, ROWS, pairs_e), lax.ppermute(y, ROWS, pairs_o))  19.1 us
    pallas_call x10, Pallas kernels, call(): pl.pallas_call(kernel, name=kernel.__name__, out_shape=tuple((shape for s...  17.3 us
    ppermute x6, waiting for transfers between devices, along_rows(): return (lax.ppermute(x, ROWS, pairs_e), lax.ppermute(y, ROWS, pairs_o))  9.12 us
    ppermute x4, waiting for transfers between devices, along_trait(): lax.ppermute(y, 'trait', pairs_y)  5.98 us
    ppermute x4, waiting for transfers between devices, along_trait(): lax.ppermute(x, 'trait', pairs_x)  5 us
    ppermute x4, starting transfers between devices, along_trait(): lax.ppermute(x, 'trait', pairs_x)  4.33 us
    ppermute x4, starting transfers between devices, along_trait(): lax.ppermute(y, 'trait', pairs_y)  3.81 us
  transfers between devices with their start and end apart: 14, of which 8 were waited for; matrix products, arithmetic and copies ran while one was open for 0% of the time, Pallas kernels for 16%

profile of v6, /device:TPU:1, one launch (start us, length us, event | category | flops | bytes accessed | tf_op | source)
XLA Modules:
  0.0 64.9 jit_solution(13901694460001257482)
XLA Ops:
  0.0 2.9 %whiten_1.1 = (bf16[1152,128]{1,0:T(8,128)(2,1)S(1)}, bf16[1152,128]{1,0:T(8,128)(2,1)S(1)}, bf16[256,256]{1,0:T(8,128)(2,1)S(1)}, bf16[256,256]{1,0:T(8,128)(2,1)S(1)}) custom-call(s32[8]{0:T(128)S(1)} %compare_select_fusion.5.place, bf16[4096,128]{1,0:T(8,128)(2,1)} %z.2, bf16[32,128,384]{2,1,0:T(8,128)(2,1)} %band.3, bf16[512,512]{1,0:T(8,128)(2,1)} %mix.1), custom_call_target="tpu_custom_call" | custom-call | tf_op jit(solution)/shard_map/whiten_1/pallas_call | solution.py:234
  2.9 3.4 %collective-permute-start.3 = (bf16[1152,128]{1,0:T(8,128)(2,1)S(1)}, bf16[1152,128]{1,0:T(8,128)(2,1)S(1)}, u32[]{:S(2)}, u32[]{:S(2)}) collective-permute-start(bf16[1152,128]{1,0:T(8,128)(2,1)S(1)} %get-tuple-element.40.w_b), channel_id=1, source_target_pairs={{0,3},{1,2},{2,1},{3,0},{4,7},{5,6},{6,5},{7,4},{8,11},{9,10},{10,... | collective-permute-start | bytes 884744 | tf_op jit(solution)/shard_map/ppermute | solution.py:264
  6.3 0.0 collective-permute-start.2
  6.3 2.3 %whiten_2.1 = (bf16[1024,128]{1,0:T(8,128)(2,1)S(1)}, bf16[1024,128]{1,0:T(8,128)(2,1)S(1)}, bf16[256,128]{1,0:T(8,128)(2,1)S(1)}) custom-call(bf16[4096,128]{1,0:T(8,128)(2,1)} %z.2, bf16[32,128,384]{2,1,0:T(8,128)(2,1)} %band.3), custom_call_target="tpu_custom_call" | custom-call | tf_op jit(solution)/shard_map/whiten_2/pallas_call | solution.py:234
  8.6 1.5 %collective-permute-start = (bf16[1024,128]{1,0:T(8,128)(2,1)S(1)}, bf16[1024,128]{1,0:T(8,128)(2,1)S(1)}, u32[]{:S(2)}, u32[]{:S(2)}) collective-permute-start(bf16[1024,128]{1,0:T(8,128)(2,1)S(1)} %get-tuple-element.38.w_a), channel_id=1, source_target_pairs={{0,1},{1,0},{2,3},{3,2},{4,5},{5,4},{6,7},{7,6},{8,9},{9,8},{10,11... | collective-permute-start | bytes 786440 | tf_op jit(solution)/shard_map/ppermute | solution.py:264
  10.2 0.1 collective-permute-start.1
  10.3 1.7 %collective-permute-done.3.got_b = bf16[1152,128]{1,0:T(8,128)(2,1)S(1)} collective-permute-done((bf16[1152,128]{1,0:T(8,128)(2,1)S(1)}, bf16[1152,128]{1,0:T(8,128)(2,1)S(1)}, u32[]{:S(2)}, u32[]{:S(2)}) %collective-permute-start.3) | collective-permute-done | bytes 294944 | tf_op jit(solution)/shard_map/ppermute | solution.py:264
  12.0 1.9 %collective-permute-done.2.got_a = bf16[1152,128]{1,0:T(8,128)(2,1)S(1)} collective-permute-done((bf16[1152,128]{1,0:T(8,128)(2,1)S(1)}, bf16[1152,128]{1,0:T(8,128)(2,1)S(1)}, u32[]{:S(2)}, u32[]{:S(2)}) %collective-permute-start.2) | collective-permute-done | bytes 294944 | tf_op jit(solution)/shard_map/ppermute | solution.py:264
  13.9 0.0 copy-start
  13.9 0.0 copy-start.2
  13.9 0.0 copy-start.1
  13.9 0.8 %partial.2 = (bf16[1152,128]{1,0:T(8,128)(2,1)S(1)}, bf16[1152,128]{1,0:T(8,128)(2,1)S(1)}, f32[2304,128]{1,0:T(8,128)S(1)}) custom-call(bf16[1152,128]{1,0:T(8,128)(2,1)S(1)} %get-tuple-element.36.w_a, bf16[1152,128]{1,0:T(8,128)(2,1)S(1)} %collective-permute-done.2.got_a, bf16[1152,128]{1,0:T(8,128)(2,1)S(1)} %get-tuple-element.40.w_b, ...), custom_call_target="tpu_custom_call" | custom-call | tf_op jit(solution)/shard_map/partial/pallas_call | solution.py:234
  14.6 0.2 collective-permute-start.7
  14.8 1.6 %collective-permute-start.6 = (bf16[1152,128]{1,0:T(8,128)(2,1)S(1)}, bf16[1152,128]{1,0:T(8,128)(2,1)S(1)}, u32[]{:S(2)}, u32[]{:S(2)}) collective-permute-start(bf16[1152,128]{1,0:T(8,128)(2,1)S(1)} %get-tuple-element.43), channel_id=1, source_target_pairs={{0,3},{1,2},{2,1},{3,0},{4,7},{5,6},{6,5},{7,4},{8,11},{9,10},{10,... | collective-permute-start | bytes 884744 | tf_op jit(solution)/shard_map/ppermute | solution.py:264
  16.4 3.1 %collective-permute-done.got_a = bf16[1024,128]{1,0:T(8,128)(2,1)S(1)} collective-permute-done((bf16[1024,128]{1,0:T(8,128)(2,1)S(1)}, bf16[1024,128]{1,0:T(8,128)(2,1)S(1)}, u32[]{:S(2)}, u32[]{:S(2)}) %collective-permute-start) | collective-permute-done | bytes 262176 | tf_op jit(solution)/shard_map/ppermute | solution.py:264
  19.5 0.0 collective-permute-done.1.got_b
  19.5 0.7 %partial.3 = (bf16[1024,128]{1,0:T(8,128)(2,1)S(1)}, bf16[1024,128]{1,0:T(8,128)(2,1)S(1)}, f32[2048,128]{1,0:T(8,128)S(1)}) custom-call(bf16[1024,128]{1,0:T(8,128)(2,1)S(1)} %get-tuple-element.38.w_a, bf16[1024,128]{1,0:T(8,128)(2,1)S(1)} %collective-permute-done.got_a, bf16[1024,128]{1,0:T(8,128)(2,1)S(1)} %get-tuple-element.39.w_b, ...), custom_call_target="tpu_custom_call" | custom-call | tf_op jit(solution)/shard_map/partial/pallas_call | solution.py:234
  20.2 0.2 collective-permute-start.5
  20.4 1.2 %collective-permute-start.4 = (bf16[1024,128]{1,0:T(8,128)(2,1)S(1)}, bf16[1024,128]{1,0:T(8,128)(2,1)S(1)}, u32[]{:S(2)}, u32[]{:S(2)}) collective-permute-start(bf16[1024,128]{1,0:T(8,128)(2,1)S(1)} %get-tuple-element.47), channel_id=1, source_target_pairs={{0,3},{1,2},{2,1},{3,0},{4,7},{5,6},{6,5},{7,4},{8,11},{9,10},{10,... | collective-permute-start | bytes 786440 | tf_op jit(solution)/shard_map/ppermute | solution.py:264
  21.6 4.3 %collective-permute-done.7.far_b = bf16[1152,128]{1,0:T(8,128)(2,1)S(1)} collective-permute-done((bf16[1152,128]{1,0:T(8,128)(2,1)S(1)}, bf16[1152,128]{1,0:T(8,128)(2,1)S(1)}, u32[]{:S(2)}, u32[]{:S(2)}) %collective-permute-start.7) | collective-permute-done | bytes 294944 | tf_op jit(solution)/shard_map/ppermute | solution.py:264
  25.8 0.0 collective-permute-done.6.far_a
  25.8 0.1 combine_1.1.mid
  25.9 11.3 %collective-permute-start.11 = (bf16[2304,128]{1,0:T(8,128)(2,1)S(1)}, bf16[2304,128]{1,0:T(8,128)(2,1)S(1)}, u32[]{:S(2)}, u32[]{:S(2)}) collective-permute-start(bf16[2304,128]{1,0:T(8,128)(2,1)S(1)} %combine_1.1.mid), channel_id=1, source_target_pairs={{0,252},{4,8},{8,4},{12,16},{16,12},{20,24},{24,20},{28,32},{32,28... | collective-permute-start | bytes 1769480 | tf_op jit(solution)/shard_map/ppermute | solution.py:267
  37.3 0.0 collective-permute-start.10
  37.3 0.0 collective-permute-done.5.far_b
  37.3 0.0 collective-permute-done.4.far_a
  37.3 0.1 combine_2.1
  37.4 4.0 %collective-permute-start.9 = (bf16[1792,128]{1,0:T(8,128)(2,1)S(1)}, bf16[1792,128]{1,0:T(8,128)(2,1)S(1)}, u32[]{:S(2)}, u32[]{:S(2)}) collective-permute-start(bf16[1792,128]{1,0:T(8,128)(2,1)S(1)} %get-tuple-element.55.rest), channel_id=1, source_target_pairs={{0,252},{4,8},{8,4},{12,16},{16,12},{20,24},{24,20},{28,32},{32,28... | collective-permute-start | bytes 1376264 | tf_op jit(solution)/shard_map/ppermute | solution.py:267
  41.4 0.0 collective-permute-start.8
  41.4 0.0 copy-done
  41.4 0.0 copy-done.2
  41.4 0.2 convert_reduce_fusion.below
  41.6 0.0 copy-done.1
  41.6 4.1 %impute_own.1 = (bf16[12416,128]{1,0:T(8,128)(2,1)S(1)}, bf16[8192,128]{1,0:T(8,128)(2,1)S(1)}, bf16[64,128,512]{2,1,0:T(8,128)(2,1)S(1)}) custom-call(s32[8]{0:T(128)S(1)} %compare_select_fusion.5.place, s32[64]{0:T(128)S(1)} %copy-done, s32[64]{0:T(128)S(1)} %copy-done.1, s32[8]{0:T(128)S(1)} %convert_reduce_fusion.below, ...), custom_call_target="tpu_custom_call" | custom-call | tf_op jit(solution)/shard_map/impute_own/pallas_call | solution.py:234
  45.7 5.8 %collective-permute-done.11.got_o.mid_o = bf16[2304,128]{1,0:T(8,128)(2,1)S(1)} collective-permute-done((bf16[2304,128]{1,0:T(8,128)(2,1)S(1)}, bf16[2304,128]{1,0:T(8,128)(2,1)S(1)}, u32[]{:S(2)}, u32[]{:S(2)}) %collective-permute-start.11) | collective-permute-done | bytes 589856 | tf_op jit(solution)/shard_map/ppermute | solution.py:267
  51.5 1.2 %collective-permute-done.10.got_e.mid_e = bf16[2304,128]{1,0:T(8,128)(2,1)S(1)} collective-permute-done((bf16[2304,128]{1,0:T(8,128)(2,1)S(1)}, bf16[2304,128]{1,0:T(8,128)(2,1)S(1)}, u32[]{:S(2)}, u32[]{:S(2)}) %collective-permute-start.10) | collective-permute-done | bytes 589856 | tf_op jit(solution)/shard_map/ppermute | solution.py:267
  52.7 0.7 %finish_edge.1.edge = bf16[256,128]{1,0:T(8,128)(2,1)S(1)} custom-call(s32[8]{0:T(128)S(1)} %compare_select_fusion.5.place, f32[256,128]{1,0:T(8,128)S(1)} %get-tuple-element.56.edge, bf16[256,128]{1,0:T(8,128)(2,1)S(1)} %get-tuple-element.57.edge_band, bf16[2304,128]{1,0:T(8,128)(2,1)S(1)} %collective-permute-done.10.got_e.mid_e, ...), custom_call_target="tpu_custom_call" | custom-call | tf_op jit(solution)/shard_map/finish_edge/pallas_call | solution.py:234
  53.4 3.7 %collective-permute-start.13 = (bf16[256,128]{1,0:T(8,128)(2,1)S(1)}, bf16[256,128]{1,0:T(8,128)(2,1)S(1)}, u32[]{:S(2)}, u32[]{:S(2)}) collective-permute-start(bf16[256,128]{1,0:T(8,128)(2,1)S(1)} %finish_edge.1.edge), channel_id=1, source_target_pairs={{0,252},{4,8},{8,4},{12,16},{16,12},{20,24},{24,20},{28,32},{32,28... | collective-permute-start | bytes 196616 | tf_op jit(solution)/shard_map/ppermute | solution.py:267
  57.1 0.0 collective-permute-start.12
  57.1 2.0 %impute_near.1 = (bf16[12416,128]{1,0:T(8,128)(2,1)S(1)}, bf16[8192,128]{1,0:T(8,128)(2,1)S(1)}) custom-call(s32[8]{0:T(128)S(1)} %compare_select_fusion.5.place, s32[64]{0:T(128)S(1)} %copy-done, s32[64]{0:T(128)S(1)} %copy-done.1, s32[8]{0:T(128)S(1)} %convert_reduce_fusion.below, ...), custom_call_target="tpu_custom_call", output_to_operand_aliasing={{0}: (8, {}), {1}: (9, {})} | custom-call | tf_op jit(solution)/shard_map/impute_near/pallas_call | solution.py:234
  59.0 0.0 collective-permute-done.9.rest_o
  59.1 1.4 %collective-permute-done.8.rest_e = bf16[1792,128]{1,0:T(8,128)(2,1)S(1)} collective-permute-done((bf16[1792,128]{1,0:T(8,128)(2,1)S(1)}, bf16[1792,128]{1,0:T(8,128)(2,1)S(1)}, u32[]{:S(2)}, u32[]{:S(2)}) %collective-permute-start.8) | collective-permute-done | bytes 458784 | tf_op jit(solution)/shard_map/ppermute | solution.py:267
  60.5 0.0 collective-permute-done.13.edge_o
  60.5 0.7 %collective-permute-done.12.edge_e = bf16[256,128]{1,0:T(8,128)(2,1)S(1)} collective-permute-done((bf16[256,128]{1,0:T(8,128)(2,1)S(1)}, bf16[256,128]{1,0:T(8,128)(2,1)S(1)}, u32[]{:S(2)}, u32[]{:S(2)}) %collective-permute-start.12) | collective-permute-done | bytes 65568 | tf_op jit(solution)/shard_map/ppermute | solution.py:267
  61.2 3.8 %impute_far.1 = (bf16[12416,128]{1,0:T(8,128)(2,1)S(1)}, bf16[8192,128]{1,0:T(8,128)(2,1)S(1)}, bf16[8192,128]{1,0:T(8,128)(2,1)}) custom-call(s32[8]{0:T(128)S(1)} %compare_select_fusion.5.place, s32[64]{0:T(128)S(1)} %copy-done, s32[64]{0:T(128)S(1)} %copy-done.1, s32[8]{0:T(128)S(1)} %convert_reduce_fusion.below, ...), custom_call_target="tpu_custom_call", output_to_operand_aliasing={{0}: (9, {}), {1}: (10, {})} | custom-call | tf_op jit(solution)/shard_map/impute_far/pallas_call | solution.py:234
  (2 shorter events, 0.0 us)
Async XLA Ops:
  2.9 9.1 %collective-permute-start.3 = (bf16[1152,128]{1,0:T(8,128)(2,1)S(1)}, bf16[1152,128]{1,0:T(8,128)(2,1)S(1)}, u32[]{:S(2)}, u32[]{:S(2)}) collective-permute-start(bf16[1152,128]{1,0:T(8,128)(2,1)S(1)} %get-tuple-element.40.w_b), channel_id=1, source_target_pairs={{0,3},{1,2},{2,1},{3,0},{4,7},{5,6},{6,5},{7,4},{8,11},{9,10},{10,... | collective-permute-start | bytes 884744 | tf_op jit(solution)/shard_map/ppermute | solution.py:264
  6.3 7.6 %collective-permute-start.2 = (bf16[1152,128]{1,0:T(8,128)(2,1)S(1)}, bf16[1152,128]{1,0:T(8,128)(2,1)S(1)}, u32[]{:S(2)}, u32[]{:S(2)}) collective-permute-start(bf16[1152,128]{1,0:T(8,128)(2,1)S(1)} %get-tuple-element.36.w_a), channel_id=1, source_target_pairs={{0,1},{1,0},{2,3},{3,2},{4,5},{5,4},{6,7},{7,6},{8,9},{9,8},{10,11... | collective-permute-start | bytes 884744 | tf_op jit(solution)/shard_map/ppermute | solution.py:264
  8.6 10.9 %collective-permute-start = (bf16[1024,128]{1,0:T(8,128)(2,1)S(1)}, bf16[1024,128]{1,0:T(8,128)(2,1)S(1)}, u32[]{:S(2)}, u32[]{:S(2)}) collective-permute-start(bf16[1024,128]{1,0:T(8,128)(2,1)S(1)} %get-tuple-element.38.w_a), channel_id=1, source_target_pairs={{0,1},{1,0},{2,3},{3,2},{4,5},{5,4},{6,7},{7,6},{8,9},{9,8},{10,11... | collective-permute-start | bytes 786440 | tf_op jit(solution)/shard_map/ppermute | solution.py:264
  10.2 9.3 %collective-permute-start.1 = (bf16[1024,128]{1,0:T(8,128)(2,1)S(1)}, bf16[1024,128]{1,0:T(8,128)(2,1)S(1)}, u32[]{:S(2)}, u32[]{:S(2)}) collective-permute-start(bf16[1024,128]{1,0:T(8,128)(2,1)S(1)} %get-tuple-element.39.w_b), channel_id=1, source_target_pairs={{0,3},{1,2},{2,1},{3,0},{4,7},{5,6},{6,5},{7,4},{8,11},{9,10},{10,... | collective-permute-start | bytes 786440 | tf_op jit(solution)/shard_map/ppermute | solution.py:264
  13.9 27.5 %copy-start = (s32[64]{0:T(128)S(1)}, s32[64]{0:T(128)}, u32[]{:S(2)}) copy-start(s32[64]{0:T(128)} %starts.5) | copy-start | bytes 772
  13.9 27.5 %copy-start.2 = (s32[8]{0:T(128)S(1)}, s32[8]{0:T(128)}, u32[]{:S(2)}) copy-start(s32[8]{0:T(128)} %constant.48.clone) | copy-start | bytes 100
  13.9 27.7 %copy-start.1 = (s32[64]{0:T(128)S(1)}, s32[64]{0:T(128)}, u32[]{:S(2)}) copy-start(s32[64]{0:T(128)} %counts.5) | copy-start | bytes 772
  14.6 11.2 %collective-permute-start.7 = (bf16[1152,128]{1,0:T(8,128)(2,1)S(1)}, bf16[1152,128]{1,0:T(8,128)(2,1)S(1)}, u32[]{:S(2)}, u32[]{:S(2)}) collective-permute-start(bf16[1152,128]{1,0:T(8,128)(2,1)S(1)} %get-tuple-element.50), channel_id=1, source_target_pairs={{0,1},{1,0},{2,3},{3,2},{4,5},{5,4},{6,7},{7,6},{8,9},{9,8},{10,11... | collective-permute-start | bytes 884744 | tf_op jit(solution)/shard_map/ppermute | solution.py:264
  14.8 11.0 %collective-permute-start.6 = (bf16[1152,128]{1,0:T(8,128)(2,1)S(1)}, bf16[1152,128]{1,0:T(8,128)(2,1)S(1)}, u32[]{:S(2)}, u32[]{:S(2)}) collective-permute-start(bf16[1152,128]{1,0:T(8,128)(2,1)S(1)} %get-tuple-element.43), channel_id=1, source_target_pairs={{0,3},{1,2},{2,1},{3,0},{4,7},{5,6},{6,5},{7,4},{8,11},{9,10},{10,... | collective-permute-start | bytes 884744 | tf_op jit(solution)/shard_map/ppermute | solution.py:264
  20.2 17.1 %collective-permute-start.5 = (bf16[1024,128]{1,0:T(8,128)(2,1)S(1)}, bf16[1024,128]{1,0:T(8,128)(2,1)S(1)}, u32[]{:S(2)}, u32[]{:S(2)}) collective-permute-start(bf16[1024,128]{1,0:T(8,128)(2,1)S(1)} %get-tuple-element.48), channel_id=1, source_target_pairs={{0,1},{1,0},{2,3},{3,2},{4,5},{5,4},{6,7},{7,6},{8,9},{9,8},{10,11... | collective-permute-start | bytes 786440 | tf_op jit(solution)/shard_map/ppermute | solution.py:264
  20.4 16.9 %collective-permute-start.4 = (bf16[1024,128]{1,0:T(8,128)(2,1)S(1)}, bf16[1024,128]{1,0:T(8,128)(2,1)S(1)}, u32[]{:S(2)}, u32[]{:S(2)}) collective-permute-start(bf16[1024,128]{1,0:T(8,128)(2,1)S(1)} %get-tuple-element.47), channel_id=1, source_target_pairs={{0,3},{1,2},{2,1},{3,0},{4,7},{5,6},{6,5},{7,4},{8,11},{9,10},{10,... | collective-permute-start | bytes 786440 | tf_op jit(solution)/shard_map/ppermute | solution.py:264
  25.9 25.6 %collective-permute-start.11 = (bf16[2304,128]{1,0:T(8,128)(2,1)S(1)}, bf16[2304,128]{1,0:T(8,128)(2,1)S(1)}, u32[]{:S(2)}, u32[]{:S(2)}) collective-permute-start(bf16[2304,128]{1,0:T(8,128)(2,1)S(1)} %combine_1.1.mid), channel_id=1, source_target_pairs={{0,252},{4,8},{8,4},{12,16},{16,12},{20,24},{24,20},{28,32},{32,28... | collective-permute-start | bytes 1769480 | tf_op jit(solution)/shard_map/ppermute | solution.py:267
  37.3 15.4 %collective-permute-start.10 = (bf16[2304,128]{1,0:T(8,128)(2,1)S(1)}, bf16[2304,128]{1,0:T(8,128)(2,1)S(1)}, u32[]{:S(2)}, u32[]{:S(2)}) collective-permute-start(bf16[2304,128]{1,0:T(8,128)(2,1)S(1)} %combine_1.1.mid), channel_id=1, source_target_pairs={{0,4},{4,0},{8,12},{12,8},{16,20},{20,16},{24,28},{28,24},{32,36},... | collective-permute-start | bytes 1769480 | tf_op jit(solution)/shard_map/ppermute | solution.py:267
  37.4 21.7 %collective-permute-start.9 = (bf16[1792,128]{1,0:T(8,128)(2,1)S(1)}, bf16[1792,128]{1,0:T(8,128)(2,1)S(1)}, u32[]{:S(2)}, u32[]{:S(2)}) collective-permute-start(bf16[1792,128]{1,0:T(8,128)(2,1)S(1)} %get-tuple-element.55.rest), channel_id=1, source_target_pairs={{0,252},{4,8},{8,4},{12,16},{16,12},{20,24},{24,20},{28,32},{32,28... | collective-permute-start | bytes 1376264 | tf_op jit(solution)/shard_map/ppermute | solution.py:267
  41.4 19.1 %collective-permute-start.8 = (bf16[1792,128]{1,0:T(8,128)(2,1)S(1)}, bf16[1792,128]{1,0:T(8,128)(2,1)S(1)}, u32[]{:S(2)}, u32[]{:S(2)}) collective-permute-start(bf16[1792,128]{1,0:T(8,128)(2,1)S(1)} %get-tuple-element.55.rest), channel_id=1, source_target_pairs={{0,4},{4,0},{8,12},{12,8},{16,20},{20,16},{24,28},{28,24},{32,36},... | collective-permute-start | bytes 1376264 | tf_op jit(solution)/shard_map/ppermute | solution.py:267
  53.4 7.1 %collective-permute-start.13 = (bf16[256,128]{1,0:T(8,128)(2,1)S(1)}, bf16[256,128]{1,0:T(8,128)(2,1)S(1)}, u32[]{:S(2)}, u32[]{:S(2)}) collective-permute-start(bf16[256,128]{1,0:T(8,128)(2,1)S(1)} %finish_edge.1.edge), channel_id=1, source_target_pairs={{0,252},{4,8},{8,4},{12,16},{16,12},{20,24},{24,20},{28,32},{32,28... | collective-permute-start | bytes 196616 | tf_op jit(solution)/shard_map/ppermute | solution.py:267
  57.1 4.1 %collective-permute-start.12 = (bf16[256,128]{1,0:T(8,128)(2,1)S(1)}, bf16[256,128]{1,0:T(8,128)(2,1)S(1)}, u32[]{:S(2)}, u32[]{:S(2)}) collective-permute-start(bf16[256,128]{1,0:T(8,128)(2,1)S(1)} %finish_edge.1.edge), channel_id=1, source_target_pairs={{0,4},{4,0},{8,12},{12,8},{16,20},{20,16},{24,28},{28,24},{32,36},... | collective-permute-start | bytes 196616 | tf_op jit(solution)/shard_map/ppermute | solution.py:267

commit v7 on v6

--- a/solution.py
+++ b/solution.py
@@ -20,7 +20,7 @@
 SMEM = pl.BlockSpec(memory_space=pltpu.SMEM)
 VM = pl.BlockSpec(memory_space=pltpu.VMEM)
 PARAMS = pltpu.CompilerParams(vmem_limit_bytes=16 * 1024 * 1024)
-MID = 8
+MID = 9
 MID_END = TB - MID
 HALF1 = (MID_END - MID) // 2
 HALF2 = MID
@@ -134,7 +134,7 @@
         out[at(k), :] = (edge[at(k), :] + dot(edge_band[at(k), :], rows)).astype(BF)
 
 
-def on_ranges(ranges, starts, counts, lowest, ld, ext, out, ready=None):
+def on_ranges(ranges, starts, counts, lowest, ld, ext, out, ready=None, send=None):
     total = 0
     parts = []
     for low, high in ranges:
@@ -156,9 +156,14 @@
             have = counts[u]
             window = [ext[at(jnp.where(s < have, jnp.minimum(first + s, ZERO), ZERO)), :] for s in range(WIN)]
             out[at(u), :] = dot(ld[u], jnp.concatenate(window, axis=0)).astype(BF)
-        return carry
-
-    lax.fori_loop(0, (total + UNROLL - 1) // UNROLL, several, 0)
+        if send is None:
+            return carry
+        after = UNROLL * (k + 1)
+        complete = jnp.where(after < total, window_of(after), UB) // UNROLL
+        lax.fori_loop(carry, complete, send, 0)
+        return jnp.maximum(carry, complete)
+
+    return lax.fori_loop(0, (total + UNROLL - 1) // UNROLL, several, 0)
 
 
 def move(ext, block, source, first, blocks):
@@ -223,11 +228,19 @@
         move(ext, base + MID_END, rest, inner, inner)
         move(ext, base + TB - 1, edge, 1, 1)
     ranges = [(0, below[0]), (below[1], below[2]), (below[5], below[6]), (below[7], UB)]
-    on_ranges(ranges, starts, counts, place[3] * TB - TB, ld, ext, rows)
-    quarter = UB // 4
-    parts = [(rows.at[at(k, quarter)], out.at[at(k, quarter)]) for k in range(0, UB, quarter)]
-    for copy in copy_all(parts, sems):
-        copy.wait()
+
+    def leave(k):
+        part = at(k * UNROLL, UNROLL)
+        return pltpu.make_async_copy(rows.at[part], out.at[part], sems.at[k])
+
+    def send(k, carry):
+        leave(k).start()
+        return carry
+
+    sent = on_ranges(ranges, starts, counts, place[3] * TB - TB, ld, ext, rows, send=send)
+    lax.fori_loop(sent, UB // UNROLL, send, 0)
+    for k in range(UB // UNROLL):
+        leave(k).wait()
 
 
 def call(kernel, outs, ins, args, scratch=(), aliases=None):
@@ -339,7 +352,7 @@
         in_vmem(shaped(EXT), shaped(UB)) + [(shaped(UB), HBM)],
         [SMEM] * 4 + [VM] * 7,
         (*plan, rest_e, rest_o, edge_e, edge_o, ld, ext, done),
-        [pltpu.SemaphoreType.DMA((4,))],
+        [pltpu.SemaphoreType.DMA((UB // UNROLL,))],
         {9: 0, 10: 1},
     )
     return out

time: 64.8 us -> 63.9 us (0.986)
    ppermute x4, starting transfers between devices: 4.33 us -> 3.21 us  [along_trait(): lax.ppermute(x, 'trait', pairs_x)]
    ppermute x4, waiting for transfers between devices: 5.98 us -> 5.17 us  [along_trait(): lax.ppermute(y, 'trait', pairs_y)]
    ppermute x4, waiting for transfers between devices: 5 us -> 5.78 us  [along_trait(): lax.ppermute(x, 'trait', pairs_x)]
    ppermute x6, starting transfers between devices: 19.1 us -> 19.8 us  [along_rows(): return (lax.ppermute(x, ROWS, pairs_e), lax.ppermute(y, ROWS, pairs_o))]
  transfers between devices with their start and end apart: 14 -> 14, of which waited for: 8 -> 9; matrix products, arithmetic and copies ran while one was open for 0% -> 0% of each run, Pallas kernels for 16% -> 17%
where the time goes in v7:
time: 63.9 us; the launch traced here: 63.8 us
  starting transfers between devices  26.9 us (42%)
  waiting for transfers between devices  19.8 us (31%)
  Pallas kernels  16.8 us (26%)
    ppermute x6, starting transfers between devices, along_rows(): return (lax.ppermute(x, ROWS, pairs_e), lax.ppermute(y, ROWS, pairs_o))  19.8 us
    pallas_call x10, Pallas kernels, call(): pl.pallas_call(kernel, name=kernel.__name__, out_shape=tuple((shape for s...  16.8 us
    ppermute x6, waiting for transfers between devices, along_rows(): return (lax.ppermute(x, ROWS, pairs_e), lax.ppermute(y, ROWS, pairs_o))  8.86 us
    ppermute x4, waiting for transfers between devices, along_trait(): lax.ppermute(x, 'trait', pairs_x)  5.78 us
    ppermute x4, waiting for transfers between devices, along_trait(): lax.ppermute(y, 'trait', pairs_y)  5.17 us
    ppermute x4, starting transfers between devices, along_trait(): lax.ppermute(y, 'trait', pairs_y)  3.89 us
    ppermute x4, starting transfers between devices, along_trait(): lax.ppermute(x, 'trait', pairs_x)  3.21 us
  transfers between devices with their start and end apart: 14, of which 9 were waited for; matrix products, arithmetic and copies ran while one was open for 0% of the time, Pallas kernels for 17%

profile of v7, /device:TPU:1, one launch (start us, length us, event | category | flops | bytes accessed | tf_op | source)
XLA Modules:
  0.0 63.8 jit_solution(15773035671142565296)
XLA Ops:
  0.0 2.8 %whiten_1.1 = (bf16[1024,128]{1,0:T(8,128)(2,1)S(1)}, bf16[1024,128]{1,0:T(8,128)(2,1)S(1)}, bf16[256,256]{1,0:T(8,128)(2,1)S(1)}, bf16[256,256]{1,0:T(8,128)(2,1)S(1)}) custom-call(s32[8]{0:T(128)S(1)} %compare_select_fusion.5.place, bf16[4096,128]{1,0:T(8,128)(2,1)} %z.2, bf16[32,128,384]{2,1,0:T(8,128)(2,1)} %band.3, bf16[512,512]{1,0:T(8,128)(2,1)} %mix.1), custom_call_target="tpu_custom_call" | custom-call | tf_op jit(solution)/shard_map/whiten_1/pallas_call | solution.py:247
  2.8 3.4 %collective-permute-start.3 = (bf16[1024,128]{1,0:T(8,128)(2,1)S(1)}, bf16[1024,128]{1,0:T(8,128)(2,1)S(1)}, u32[]{:S(2)}, u32[]{:S(2)}) collective-permute-start(bf16[1024,128]{1,0:T(8,128)(2,1)S(1)} %get-tuple-element.40.w_b), channel_id=1, source_target_pairs={{0,3},{1,2},{2,1},{3,0},{4,7},{5,6},{6,5},{7,4},{8,11},{9,10},{10,... | collective-permute-start | bytes 786440 | tf_op jit(solution)/shard_map/ppermute | solution.py:277
  6.2 0.0 collective-permute-start.2
  6.3 2.7 %whiten_2.1 = (bf16[1152,128]{1,0:T(8,128)(2,1)S(1)}, bf16[1152,128]{1,0:T(8,128)(2,1)S(1)}, bf16[256,128]{1,0:T(8,128)(2,1)S(1)}) custom-call(bf16[4096,128]{1,0:T(8,128)(2,1)} %z.2, bf16[32,128,384]{2,1,0:T(8,128)(2,1)} %band.3), custom_call_target="tpu_custom_call" | custom-call | tf_op jit(solution)/shard_map/whiten_2/pallas_call | solution.py:247
  8.9 1.5 %collective-permute-start = (bf16[1152,128]{1,0:T(8,128)(2,1)S(1)}, bf16[1152,128]{1,0:T(8,128)(2,1)S(1)}, u32[]{:S(2)}, u32[]{:S(2)}) collective-permute-start(bf16[1152,128]{1,0:T(8,128)(2,1)S(1)} %get-tuple-element.38.w_a), channel_id=1, source_target_pairs={{0,1},{1,0},{2,3},{3,2},{4,5},{5,4},{6,7},{7,6},{8,9},{9,8},{10,11... | collective-permute-start | bytes 884744 | tf_op jit(solution)/shard_map/ppermute | solution.py:277
  10.5 0.1 collective-permute-start.1
  10.6 0.6 collective-permute-done.3.got_b
  11.2 1.9 %collective-permute-done.2.got_a = bf16[1024,128]{1,0:T(8,128)(2,1)S(1)} collective-permute-done((bf16[1024,128]{1,0:T(8,128)(2,1)S(1)}, bf16[1024,128]{1,0:T(8,128)(2,1)S(1)}, u32[]{:S(2)}, u32[]{:S(2)}) %collective-permute-start.2) | collective-permute-done | bytes 262176 | tf_op jit(solution)/shard_map/ppermute | solution.py:277
  13.1 0.0 copy-start
  13.1 0.0 copy-start.2
  13.1 0.0 copy-start.1
  13.1 0.7 %partial.2 = (bf16[1024,128]{1,0:T(8,128)(2,1)S(1)}, bf16[1024,128]{1,0:T(8,128)(2,1)S(1)}, f32[2048,128]{1,0:T(8,128)S(1)}) custom-call(bf16[1024,128]{1,0:T(8,128)(2,1)S(1)} %get-tuple-element.36.w_a, bf16[1024,128]{1,0:T(8,128)(2,1)S(1)} %collective-permute-done.2.got_a, bf16[1024,128]{1,0:T(8,128)(2,1)S(1)} %get-tuple-element.40.w_b, ...), custom_call_target="tpu_custom_call" | custom-call | tf_op jit(solution)/shard_map/partial/pallas_call | solution.py:247
  13.8 0.1 collective-permute-start.7
  14.0 1.6 %collective-permute-start.6 = (bf16[1024,128]{1,0:T(8,128)(2,1)S(1)}, bf16[1024,128]{1,0:T(8,128)(2,1)S(1)}, u32[]{:S(2)}, u32[]{:S(2)}) collective-permute-start(bf16[1024,128]{1,0:T(8,128)(2,1)S(1)} %get-tuple-element.43), channel_id=1, source_target_pairs={{0,3},{1,2},{2,1},{3,0},{4,7},{5,6},{6,5},{7,4},{8,11},{9,10},{10,... | collective-permute-start | bytes 786440 | tf_op jit(solution)/shard_map/ppermute | solution.py:277
  15.5 3.9 %collective-permute-done.got_a = bf16[1152,128]{1,0:T(8,128)(2,1)S(1)} collective-permute-done((bf16[1152,128]{1,0:T(8,128)(2,1)S(1)}, bf16[1152,128]{1,0:T(8,128)(2,1)S(1)}, u32[]{:S(2)}, u32[]{:S(2)}) %collective-permute-start) | collective-permute-done | bytes 294944 | tf_op jit(solution)/shard_map/ppermute | solution.py:277
  19.4 0.0 collective-permute-done.1.got_b
  19.4 0.8 %partial.3 = (bf16[1152,128]{1,0:T(8,128)(2,1)S(1)}, bf16[1152,128]{1,0:T(8,128)(2,1)S(1)}, f32[2304,128]{1,0:T(8,128)S(1)}) custom-call(bf16[1152,128]{1,0:T(8,128)(2,1)S(1)} %get-tuple-element.38.w_a, bf16[1152,128]{1,0:T(8,128)(2,1)S(1)} %collective-permute-done.got_a, bf16[1152,128]{1,0:T(8,128)(2,1)S(1)} %get-tuple-element.39.w_b, ...), custom_call_target="tpu_custom_call" | custom-call | tf_op jit(solution)/shard_map/partial/pallas_call | solution.py:247
  20.2 0.2 collective-permute-start.5
  20.4 0.1 collective-permute-start.4
  20.5 4.5 %collective-permute-done.7.far_b = bf16[1024,128]{1,0:T(8,128)(2,1)S(1)} collective-permute-done((bf16[1024,128]{1,0:T(8,128)(2,1)S(1)}, bf16[1024,128]{1,0:T(8,128)(2,1)S(1)}, u32[]{:S(2)}, u32[]{:S(2)}) %collective-permute-start.7) | collective-permute-done | bytes 262176 | tf_op jit(solution)/shard_map/ppermute | solution.py:277
  25.0 0.0 collective-permute-done.6.far_a
  25.0 0.1 combine_1.1.mid
  25.1 11.6 %collective-permute-start.11 = (bf16[2048,128]{1,0:T(8,128)(2,1)S(1)}, bf16[2048,128]{1,0:T(8,128)(2,1)S(1)}, u32[]{:S(2)}, u32[]{:S(2)}) collective-permute-start(bf16[2048,128]{1,0:T(8,128)(2,1)S(1)} %combine_1.1.mid), channel_id=1, source_target_pairs={{0,252},{4,8},{8,4},{12,16},{16,12},{20,24},{24,20},{28,32},{32,28... | collective-permute-start | bytes 1572872 | tf_op jit(solution)/shard_map/ppermute | solution.py:280
  36.8 0.0 collective-permute-start.10
  36.8 0.0 collective-permute-done.5.far_b
  36.8 0.0 collective-permute-done.4.far_a
  36.8 0.1 combine_2.1
  36.9 4.5 %collective-permute-start.9 = (bf16[2048,128]{1,0:T(8,128)(2,1)S(1)}, bf16[2048,128]{1,0:T(8,128)(2,1)S(1)}, u32[]{:S(2)}, u32[]{:S(2)}) collective-permute-start(bf16[2048,128]{1,0:T(8,128)(2,1)S(1)} %get-tuple-element.55.rest), channel_id=1, source_target_pairs={{0,252},{4,8},{8,4},{12,16},{16,12},{20,24},{24,20},{28,32},{32,28... | collective-permute-start | bytes 1572872 | tf_op jit(solution)/shard_map/ppermute | solution.py:280
  41.3 0.0 collective-permute-start.8
  41.3 0.0 copy-done
  41.3 0.0 copy-done.2
  41.4 0.2 convert_reduce_fusion.below
  41.5 0.0 copy-done.1
  41.5 4.1 %impute_own.1 = (bf16[12416,128]{1,0:T(8,128)(2,1)S(1)}, bf16[8192,128]{1,0:T(8,128)(2,1)S(1)}, bf16[64,128,512]{2,1,0:T(8,128)(2,1)S(1)}) custom-call(s32[8]{0:T(128)S(1)} %compare_select_fusion.5.place, s32[64]{0:T(128)S(1)} %copy-done, s32[64]{0:T(128)S(1)} %copy-done.1, s32[8]{0:T(128)S(1)} %convert_reduce_fusion.below, ...), custom_call_target="tpu_custom_call" | custom-call | tf_op jit(solution)/shard_map/impute_own/pallas_call | solution.py:247
  45.6 4.0 %collective-permute-done.11.got_o.mid_o = bf16[2048,128]{1,0:T(8,128)(2,1)S(1)} collective-permute-done((bf16[2048,128]{1,0:T(8,128)(2,1)S(1)}, bf16[2048,128]{1,0:T(8,128)(2,1)S(1)}, u32[]{:S(2)}, u32[]{:S(2)}) %collective-permute-start.11) | collective-permute-done | bytes 524320 | tf_op jit(solution)/shard_map/ppermute | solution.py:280
  49.6 1.2 %collective-permute-done.10.got_e.mid_e = bf16[2048,128]{1,0:T(8,128)(2,1)S(1)} collective-permute-done((bf16[2048,128]{1,0:T(8,128)(2,1)S(1)}, bf16[2048,128]{1,0:T(8,128)(2,1)S(1)}, u32[]{:S(2)}, u32[]{:S(2)}) %collective-permute-start.10) | collective-permute-done | bytes 524320 | tf_op jit(solution)/shard_map/ppermute | solution.py:280
  50.8 0.7 %finish_edge.1.edge = bf16[256,128]{1,0:T(8,128)(2,1)S(1)} custom-call(s32[8]{0:T(128)S(1)} %compare_select_fusion.5.place, f32[256,128]{1,0:T(8,128)S(1)} %get-tuple-element.56.edge, bf16[256,128]{1,0:T(8,128)(2,1)S(1)} %get-tuple-element.57.edge_band, bf16[2048,128]{1,0:T(8,128)(2,1)S(1)} %collective-permute-done.10.got_e.mid_e, ...), custom_call_target="tpu_custom_call" | custom-call | tf_op jit(solution)/shard_map/finish_edge/pallas_call | solution.py:247
  51.5 3.7 %collective-permute-start.13 = (bf16[256,128]{1,0:T(8,128)(2,1)S(1)}, bf16[256,128]{1,0:T(8,128)(2,1)S(1)}, u32[]{:S(2)}, u32[]{:S(2)}) collective-permute-start(bf16[256,128]{1,0:T(8,128)(2,1)S(1)} %finish_edge.1.edge), channel_id=1, source_target_pairs={{0,252},{4,8},{8,4},{12,16},{16,12},{20,24},{24,20},{28,32},{32,28... | collective-permute-start | bytes 196616 | tf_op jit(solution)/shard_map/ppermute | solution.py:280
  55.2 0.0 collective-permute-start.12
  55.2 1.5 %impute_near.1 = (bf16[12416,128]{1,0:T(8,128)(2,1)S(1)}, bf16[8192,128]{1,0:T(8,128)(2,1)S(1)}) custom-call(s32[8]{0:T(128)S(1)} %compare_select_fusion.5.place, s32[64]{0:T(128)S(1)} %copy-done, s32[64]{0:T(128)S(1)} %copy-done.1, s32[8]{0:T(128)S(1)} %convert_reduce_fusion.below, ...), custom_call_target="tpu_custom_call", output_to_operand_aliasing={{0}: (8, {}), {1}: (9, {})} | custom-call | tf_op jit(solution)/shard_map/impute_near/pallas_call | solution.py:247
  56.7 1.0 %collective-permute-done.9.rest_o = bf16[2048,128]{1,0:T(8,128)(2,1)S(1)} collective-permute-done((bf16[2048,128]{1,0:T(8,128)(2,1)S(1)}, bf16[2048,128]{1,0:T(8,128)(2,1)S(1)}, u32[]{:S(2)}, u32[]{:S(2)}) %collective-permute-start.9) | collective-permute-done | bytes 524320 | tf_op jit(solution)/shard_map/ppermute | solution.py:280
  57.6 2.1 %collective-permute-done.8.rest_e = bf16[2048,128]{1,0:T(8,128)(2,1)S(1)} collective-permute-done((bf16[2048,128]{1,0:T(8,128)(2,1)S(1)}, bf16[2048,128]{1,0:T(8,128)(2,1)S(1)}, u32[]{:S(2)}, u32[]{:S(2)}) %collective-permute-start.8) | collective-permute-done | bytes 524320 | tf_op jit(solution)/shard_map/ppermute | solution.py:280
  59.7 0.0 collective-permute-done.13.edge_o
  59.7 0.7 %collective-permute-done.12.edge_e = bf16[256,128]{1,0:T(8,128)(2,1)S(1)} collective-permute-done((bf16[256,128]{1,0:T(8,128)(2,1)S(1)}, bf16[256,128]{1,0:T(8,128)(2,1)S(1)}, u32[]{:S(2)}, u32[]{:S(2)}) %collective-permute-start.12) | collective-permute-done | bytes 65568 | tf_op jit(solution)/shard_map/ppermute | solution.py:280
  60.4 3.4 %impute_far.1 = (bf16[12416,128]{1,0:T(8,128)(2,1)S(1)}, bf16[8192,128]{1,0:T(8,128)(2,1)S(1)}, bf16[8192,128]{1,0:T(8,128)(2,1)}) custom-call(s32[8]{0:T(128)S(1)} %compare_select_fusion.5.place, s32[64]{0:T(128)S(1)} %copy-done, s32[64]{0:T(128)S(1)} %copy-done.1, s32[8]{0:T(128)S(1)} %convert_reduce_fusion.below, ...), custom_call_target="tpu_custom_call", output_to_operand_aliasing={{0}: (9, {}), {1}: (10, {})} | custom-call | tf_op jit(solution)/shard_map/impute_far/pallas_call | solution.py:247
  (2 shorter events, 0.0 us)
Async XLA Ops:
  2.8 8.4 %collective-permute-start.3 = (bf16[1024,128]{1,0:T(8,128)(2,1)S(1)}, bf16[1024,128]{1,0:T(8,128)(2,1)S(1)}, u32[]{:S(2)}, u32[]{:S(2)}) collective-permute-start(bf16[1024,128]{1,0:T(8,128)(2,1)S(1)} %get-tuple-element.40.w_b), channel_id=1, source_target_pairs={{0,3},{1,2},{2,1},{3,0},{4,7},{5,6},{6,5},{7,4},{8,11},{9,10},{10,... | collective-permute-start | bytes 786440 | tf_op jit(solution)/shard_map/ppermute | solution.py:277
  6.2 6.9 %collective-permute-start.2 = (bf16[1024,128]{1,0:T(8,128)(2,1)S(1)}, bf16[1024,128]{1,0:T(8,128)(2,1)S(1)}, u32[]{:S(2)}, u32[]{:S(2)}) collective-permute-start(bf16[1024,128]{1,0:T(8,128)(2,1)S(1)} %get-tuple-element.36.w_a), channel_id=1, source_target_pairs={{0,1},{1,0},{2,3},{3,2},{4,5},{5,4},{6,7},{7,6},{8,9},{9,8},{10,11... | collective-permute-start | bytes 786440 | tf_op jit(solution)/shard_map/ppermute | solution.py:277
  8.9 10.5 %collective-permute-start = (bf16[1152,128]{1,0:T(8,128)(2,1)S(1)}, bf16[1152,128]{1,0:T(8,128)(2,1)S(1)}, u32[]{:S(2)}, u32[]{:S(2)}) collective-permute-start(bf16[1152,128]{1,0:T(8,128)(2,1)S(1)} %get-tuple-element.38.w_a), channel_id=1, source_target_pairs={{0,1},{1,0},{2,3},{3,2},{4,5},{5,4},{6,7},{7,6},{8,9},{9,8},{10,11... | collective-permute-start | bytes 884744 | tf_op jit(solution)/shard_map/ppermute | solution.py:277
  10.5 8.9 %collective-permute-start.1 = (bf16[1152,128]{1,0:T(8,128)(2,1)S(1)}, bf16[1152,128]{1,0:T(8,128)(2,1)S(1)}, u32[]{:S(2)}, u32[]{:S(2)}) collective-permute-start(bf16[1152,128]{1,0:T(8,128)(2,1)S(1)} %get-tuple-element.39.w_b), channel_id=1, source_target_pairs={{0,3},{1,2},{2,1},{3,0},{4,7},{5,6},{6,5},{7,4},{8,11},{9,10},{10,... | collective-permute-start | bytes 884744 | tf_op jit(solution)/shard_map/ppermute | solution.py:277
  13.1 28.2 %copy-start = (s32[64]{0:T(128)S(1)}, s32[64]{0:T(128)}, u32[]{:S(2)}) copy-start(s32[64]{0:T(128)} %starts.5) | copy-start | bytes 772
  13.1 28.2 %copy-start.2 = (s32[8]{0:T(128)S(1)}, s32[8]{0:T(128)}, u32[]{:S(2)}) copy-start(s32[8]{0:T(128)} %constant.48.clone) | copy-start | bytes 100
  13.1 28.4 %copy-start.1 = (s32[64]{0:T(128)S(1)}, s32[64]{0:T(128)}, u32[]{:S(2)}) copy-start(s32[64]{0:T(128)} %counts.5) | copy-start | bytes 772
  13.8 11.2 %collective-permute-start.7 = (bf16[1024,128]{1,0:T(8,128)(2,1)S(1)}, bf16[1024,128]{1,0:T(8,128)(2,1)S(1)}, u32[]{:S(2)}, u32[]{:S(2)}) collective-permute-start(bf16[1024,128]{1,0:T(8,128)(2,1)S(1)} %get-tuple-element.50), channel_id=1, source_target_pairs={{0,1},{1,0},{2,3},{3,2},{4,5},{5,4},{6,7},{7,6},{8,9},{9,8},{10,11... | collective-permute-start | bytes 786440 | tf_op jit(solution)/shard_map/ppermute | solution.py:277
  14.0 11.1 %collective-permute-start.6 = (bf16[1024,128]{1,0:T(8,128)(2,1)S(1)}, bf16[1024,128]{1,0:T(8,128)(2,1)S(1)}, u32[]{:S(2)}, u32[]{:S(2)}) collective-permute-start(bf16[1024,128]{1,0:T(8,128)(2,1)S(1)} %get-tuple-element.43), channel_id=1, source_target_pairs={{0,3},{1,2},{2,1},{3,0},{4,7},{5,6},{6,5},{7,4},{8,11},{9,10},{10,... | collective-permute-start | bytes 786440 | tf_op jit(solution)/shard_map/ppermute | solution.py:277
  20.2 16.6 %collective-permute-start.5 = (bf16[1152,128]{1,0:T(8,128)(2,1)S(1)}, bf16[1152,128]{1,0:T(8,128)(2,1)S(1)}, u32[]{:S(2)}, u32[]{:S(2)}) collective-permute-start(bf16[1152,128]{1,0:T(8,128)(2,1)S(1)} %get-tuple-element.48), channel_id=1, source_target_pairs={{0,1},{1,0},{2,3},{3,2},{4,5},{5,4},{6,7},{7,6},{8,9},{9,8},{10,11... | collective-permute-start | bytes 884744 | tf_op jit(solution)/shard_map/ppermute | solution.py:277
  20.4 16.3 %collective-permute-start.4 = (bf16[1152,128]{1,0:T(8,128)(2,1)S(1)}, bf16[1152,128]{1,0:T(8,128)(2,1)S(1)}, u32[]{:S(2)}, u32[]{:S(2)}) collective-permute-start(bf16[1152,128]{1,0:T(8,128)(2,1)S(1)} %get-tuple-element.47), channel_id=1, source_target_pairs={{0,3},{1,2},{2,1},{3,0},{4,7},{5,6},{6,5},{7,4},{8,11},{9,10},{10,... | collective-permute-start | bytes 884744 | tf_op jit(solution)/shard_map/ppermute | solution.py:277
  25.1 24.5 %collective-permute-start.11 = (bf16[2048,128]{1,0:T(8,128)(2,1)S(1)}, bf16[2048,128]{1,0:T(8,128)(2,1)S(1)}, u32[]{:S(2)}, u32[]{:S(2)}) collective-permute-start(bf16[2048,128]{1,0:T(8,128)(2,1)S(1)} %combine_1.1.mid), channel_id=1, source_target_pairs={{0,252},{4,8},{8,4},{12,16},{16,12},{20,24},{24,20},{28,32},{32,28... | collective-permute-start | bytes 1572872 | tf_op jit(solution)/shard_map/ppermute | solution.py:280
  36.8 14.0 %collective-permute-start.10 = (bf16[2048,128]{1,0:T(8,128)(2,1)S(1)}, bf16[2048,128]{1,0:T(8,128)(2,1)S(1)}, u32[]{:S(2)}, u32[]{:S(2)}) collective-permute-start(bf16[2048,128]{1,0:T(8,128)(2,1)S(1)} %combine_1.1.mid), channel_id=1, source_target_pairs={{0,4},{4,0},{8,12},{12,8},{16,20},{20,16},{24,28},{28,24},{32,36},... | collective-permute-start | bytes 1572872 | tf_op jit(solution)/shard_map/ppermute | solution.py:280
  36.9 20.8 %collective-permute-start.9 = (bf16[2048,128]{1,0:T(8,128)(2,1)S(1)}, bf16[2048,128]{1,0:T(8,128)(2,1)S(1)}, u32[]{:S(2)}, u32[]{:S(2)}) collective-permute-start(bf16[2048,128]{1,0:T(8,128)(2,1)S(1)} %get-tuple-element.55.rest), channel_id=1, source_target_pairs={{0,252},{4,8},{8,4},{12,16},{16,12},{20,24},{24,20},{28,32},{32,28... | collective-permute-start | bytes 1572872 | tf_op jit(solution)/shard_map/ppermute | solution.py:280
  41.3 18.4 %collective-permute-start.8 = (bf16[2048,128]{1,0:T(8,128)(2,1)S(1)}, bf16[2048,128]{1,0:T(8,128)(2,1)S(1)}, u32[]{:S(2)}, u32[]{:S(2)}) collective-permute-start(bf16[2048,128]{1,0:T(8,128)(2,1)S(1)} %get-tuple-element.55.rest), channel_id=1, source_target_pairs={{0,4},{4,0},{8,12},{12,8},{16,20},{20,16},{24,28},{28,24},{32,36},... | collective-permute-start | bytes 1572872 | tf_op jit(solution)/shard_map/ppermute | solution.py:280
  51.5 8.2 %collective-permute-start.13 = (bf16[256,128]{1,0:T(8,128)(2,1)S(1)}, bf16[256,128]{1,0:T(8,128)(2,1)S(1)}, u32[]{:S(2)}, u32[]{:S(2)}) collective-permute-start(bf16[256,128]{1,0:T(8,128)(2,1)S(1)} %finish_edge.1.edge), channel_id=1, source_target_pairs={{0,252},{4,8},{8,4},{12,16},{16,12},{20,24},{24,20},{28,32},{32,28... | collective-permute-start | bytes 196616 | tf_op jit(solution)/shard_map/ppermute | solution.py:280
  55.2 5.2 %collective-permute-start.12 = (bf16[256,128]{1,0:T(8,128)(2,1)S(1)}, bf16[256,128]{1,0:T(8,128)(2,1)S(1)}, u32[]{:S(2)}, u32[]{:S(2)}) collective-permute-start(bf16[256,128]{1,0:T(8,128)(2,1)S(1)} %finish_edge.1.edge), channel_id=1, source_target_pairs={{0,4},{4,0},{8,12},{12,8},{16,20},{20,16},{24,28},{28,24},{32,36},... | collective-permute-start | bytes 196616 | tf_op jit(solution)/shard_map/ppermute | solution.py:280

commit v8 on v7

--- a/solution.py
+++ b/solution.py
@@ -123,7 +123,7 @@
     edge[at(1), :] = own[at(2 * HALF2 - 1), :] + far_b[at(inner), :].astype(F32)
 
 
-def finish_edge(place, edge, edge_band, got_e, got_o, out):
+def finish_edge(place, edge, edge_band, got_o, got_e, out):
     odd = place[5] == 1
     nothing = jnp.zeros((BLK, COLS), BF)
     from_left = jnp.where(odd, got_e[at(2 * HALF1 + 1), :], got_o[at(2 * HALF1 + 1), :])
@@ -211,7 +211,7 @@
     lax.fori_loop(groups + 1, UB // UNROLL, rest_ready, 0)
 
 
-def impute_near(place, starts, counts, below, edge, mid_e, mid_o, ld, before, done, ext, out):
+def impute_near(place, starts, counts, below, edge, mid_o, mid_e, ld, before, done, ext, out):
     move(ext, TB, edge, 0, 1)
     move(ext, 2 * TB - 1, edge, 1, 1)
     move(ext, 2 * TB * (1 - place[5]) + MID, mid_e, 0, 2 * HALF1)
@@ -220,7 +220,7 @@
     on_ranges(ranges, starts, counts, place[3] * TB - TB, ld, ext, out)
 
 
-def impute_far(place, starts, counts, below, rest_e, rest_o, edge_e, edge_o, ld, before, done, ext, rows, out, sems):
+def impute_far(place, starts, counts, below, rest_o, rest_e, edge_o, edge_e, ld, before, done, ext, rows, out, sems):
     inner = HALF2 - 1
     for base, rest, edge in ((2 * TB * (1 - place[5]), rest_e, edge_e), (2 * TB * place[5], rest_o, edge_o)):
         move(ext, base, edge, 0, 1)
@@ -273,11 +273,14 @@
     pairs_e = [(i, i ^ 1) for i in range(owners)]
     pairs_o = [(i, (i + 1) % owners if i % 2 else (i - 1) % owners) for i in range(owners)]
 
+    pairs_open = [(i, min(i + 1, owners - 1) if i % 2 else max(i - 1, 0)) for i in range(owners)]
+
     def along_trait(x, y, pairs_x, pairs_y):
         return lax.ppermute(x, "trait", pairs_x), lax.ppermute(y, "trait", pairs_y)
 
-    def along_rows(x, y):
-        return lax.ppermute(x, ROWS, pairs_e), lax.ppermute(y, ROWS, pairs_o)
+    def along_rows(x, pairs):
+        other = lax.ppermute(x, ROWS, pairs)
+        return lax.ppermute(x, ROWS, pairs_e), other
 
     z, band, mix, ld = (pltpu.with_memory_space_constraint(x, pltpu.HBM) for x in (z, band, mix, ld))
     mix_part = jax.ShapeDtypeStruct((2 * COLS, 2 * COLS), BF)
@@ -318,12 +321,12 @@
     (own2, far2a, far2b), after = mixing(w2a, got2a, w2b, got2b)
     far1a, far1b, _ = lax.optimization_barrier((far1a, far1b, after))
     (mixed1,) = call(combine_1, in_vmem(shaped(2 * HALF1 + 2)), [VM] * 3, (own1, far1a, far1b))
-    mid_e, mid_o = along_rows(mixed1, mixed1)
+    mid_e, mid_o = along_rows(mixed1, pairs_o)
     far2a, far2b, _ = lax.optimization_barrier((far2a, far2b, mixed1))
     mixed2, edge_sums = call(
         combine_2, in_vmem(shaped(2 * HALF2 - 2), shaped(2, F32)), [VM] * 3, (own2, far2a, far2b)
     )
-    rest_e, rest_o = along_rows(mixed2, mixed2)
+    rest_e, rest_o = along_rows(mixed2, pairs_open)
     starts_here = starts - (g * TB - TB)
     below = jnp.sum(starts_here[None, :] < jnp.array(LIMITS, jnp.int32)[:, None], axis=1, dtype=jnp.int32)
     plan = (place, starts, counts, below)
@@ -334,16 +337,16 @@
         (*plan, mixed1, mixed2, ld),
         [pltpu.SemaphoreType.DMA((UB // UNROLL,))],
     )
-    mid_e, mid_o, ext = lax.optimization_barrier((mid_e, mid_o, ext))
+    mid_o, mid_e, ext = lax.optimization_barrier((mid_o, mid_e, ext))
     (mixed3,) = call(
-        finish_edge, in_vmem(shaped(2)), [SMEM] + [VM] * 4, (place, edge_sums, edge_band, mid_e, mid_o)
-    )
-    edge_e, edge_o = along_rows(mixed3, mixed3)
+        finish_edge, in_vmem(shaped(2)), [SMEM] + [VM] * 4, (place, edge_sums, edge_band, mid_o, mid_e)
+    )
+    edge_e, edge_o = along_rows(mixed3, pairs_o)
     ext, done = call(
         impute_near,
         in_vmem(shaped(EXT), shaped(UB)),
         [SMEM] * 4 + [VM] * 6,
-        (*plan, mixed3, mid_e, mid_o, ld, ext, done),
+        (*plan, mixed3, mid_o, mid_e, ld, ext, done),
         (),
         {8: 0, 9: 1},
     )
@@ -351,7 +354,7 @@
         impute_far,
         in_vmem(shaped(EXT), shaped(UB)) + [(shaped(UB), HBM)],
         [SMEM] * 4 + [VM] * 7,
-        (*plan, rest_e, rest_o, edge_e, edge_o, ld, ext, done),
+        (*plan, rest_o, rest_e, edge_o, edge_e, ld, ext, done),
         [pltpu.SemaphoreType.DMA((UB // UNROLL,))],
         {9: 0, 10: 1},
     )

time: 63.9 us -> 60.1 us (0.941)
  waiting for transfers between devices: 19.8 us -> 12 us
  starting transfers between devices: 26.9 us -> 30.2 us
    ppermute x6, waiting for transfers between devices: 8.86 us -> 1.06 us  [the longest x3 1.05 us: along_rows(): other = lax.ppermute(x, ROWS, pairs)]
    ppermute x6, starting transfers between devices: 19.8 us -> 23.1 us  [the longest x3 21.2 us: along_rows(): other = lax.ppermute(x, ROWS, pairs)]
  transfers between devices with their start and end apart: 14 -> 14, of which waited for: 9 -> 5; matrix products, arithmetic and copies ran while one was open for 0% -> 0% of each run, Pallas kernels for 17% -> 18%
where the time goes in v8:
time: 60.1 us; the launch traced here: 59.8 us
  starting transfers between devices  30.2 us (50%)
  Pallas kernels  17.2 us (29%)
  waiting for transfers between devices  12 us (20%)
    ppermute x3, starting transfers between devices, along_rows(): other = lax.ppermute(x, ROWS, pairs)  21.2 us
    pallas_call x10, Pallas kernels, call(): pl.pallas_call(kernel, name=kernel.__name__, out_shape=tuple((shape for s...  17.2 us
    ppermute x4, waiting for transfers between devices, along_trait(): lax.ppermute(x, 'trait', pairs_x)  5.78 us
    ppermute x4, waiting for transfers between devices, along_trait(): lax.ppermute(y, 'trait', pairs_y)  5.17 us
    ppermute x4, starting transfers between devices, along_trait(): lax.ppermute(y, 'trait', pairs_y)  3.89 us
    ppermute x4, starting transfers between devices, along_trait(): lax.ppermute(x, 'trait', pairs_x)  3.21 us
    ppermute x3, starting transfers between devices, along_rows(): return (lax.ppermute(x, ROWS, pairs_e), other)  1.91 us
  transfers between devices with their start and end apart: 14, of which 5 were waited for; matrix products, arithmetic and copies ran while one was open for 0% of the time, Pallas kernels for 18%

profile of v8, /device:TPU:1, one launch (start us, length us, event | category | flops | bytes accessed | tf_op | source)
XLA Modules:
  0.0 59.8 jit_solution(3030481237709232716)
XLA Ops:
  0.0 2.8 %whiten_1.1 = (bf16[1024,128]{1,0:T(8,128)(2,1)S(1)}, bf16[1024,128]{1,0:T(8,128)(2,1)S(1)}, bf16[256,256]{1,0:T(8,128)(2,1)S(1)}, bf16[256,256]{1,0:T(8,128)(2,1)S(1)}) custom-call(s32[8]{0:T(128)S(1)} %compare_select_fusion.5.place, bf16[4096,128]{1,0:T(8,128)(2,1)} %z.2, bf16[32,128,384]{2,1,0:T(8,128)(2,1)} %band.3, bf16[512,512]{1,0:T(8,128)(2,1)} %mix.1), custom_call_target="tpu_custom_call" | custom-call | tf_op jit(solution)/shard_map/whiten_1/pallas_call | solution.py:247
  2.8 3.4 %collective-permute-start.3 = (bf16[1024,128]{1,0:T(8,128)(2,1)S(1)}, bf16[1024,128]{1,0:T(8,128)(2,1)S(1)}, u32[]{:S(2)}, u32[]{:S(2)}) collective-permute-start(bf16[1024,128]{1,0:T(8,128)(2,1)S(1)} %get-tuple-element.40.w_b), channel_id=1, source_target_pairs={{0,3},{1,2},{2,1},{3,0},{4,7},{5,6},{6,5},{7,4},{8,11},{9,10},{10,... | collective-permute-start | bytes 786440 | tf_op jit(solution)/shard_map/ppermute | solution.py:279
  6.2 0.0 collective-permute-start.2
  6.3 2.7 %whiten_2.1 = (bf16[1152,128]{1,0:T(8,128)(2,1)S(1)}, bf16[1152,128]{1,0:T(8,128)(2,1)S(1)}, bf16[256,128]{1,0:T(8,128)(2,1)S(1)}) custom-call(bf16[4096,128]{1,0:T(8,128)(2,1)} %z.2, bf16[32,128,384]{2,1,0:T(8,128)(2,1)} %band.3), custom_call_target="tpu_custom_call" | custom-call | tf_op jit(solution)/shard_map/whiten_2/pallas_call | solution.py:247
  8.9 1.5 %collective-permute-start = (bf16[1152,128]{1,0:T(8,128)(2,1)S(1)}, bf16[1152,128]{1,0:T(8,128)(2,1)S(1)}, u32[]{:S(2)}, u32[]{:S(2)}) collective-permute-start(bf16[1152,128]{1,0:T(8,128)(2,1)S(1)} %get-tuple-element.38.w_a), channel_id=1, source_target_pairs={{0,1},{1,0},{2,3},{3,2},{4,5},{5,4},{6,7},{7,6},{8,9},{9,8},{10,11... | collective-permute-start | bytes 884744 | tf_op jit(solution)/shard_map/ppermute | solution.py:279
  10.5 0.1 collective-permute-start.1
  10.6 0.6 %collective-permute-done.3.got_b = bf16[1024,128]{1,0:T(8,128)(2,1)S(1)} collective-permute-done((bf16[1024,128]{1,0:T(8,128)(2,1)S(1)}, bf16[1024,128]{1,0:T(8,128)(2,1)S(1)}, u32[]{:S(2)}, u32[]{:S(2)}) %collective-permute-start.3) | collective-permute-done | bytes 262176 | tf_op jit(solution)/shard_map/ppermute | solution.py:279
  11.2 1.9 %collective-permute-done.2.got_a = bf16[1024,128]{1,0:T(8,128)(2,1)S(1)} collective-permute-done((bf16[1024,128]{1,0:T(8,128)(2,1)S(1)}, bf16[1024,128]{1,0:T(8,128)(2,1)S(1)}, u32[]{:S(2)}, u32[]{:S(2)}) %collective-permute-start.2) | collective-permute-done | bytes 262176 | tf_op jit(solution)/shard_map/ppermute | solution.py:279
  13.1 0.0 copy-start
  13.1 0.0 copy-start.2
  13.1 0.0 copy-start.1
  13.1 0.7 %partial.2 = (bf16[1024,128]{1,0:T(8,128)(2,1)S(1)}, bf16[1024,128]{1,0:T(8,128)(2,1)S(1)}, f32[2048,128]{1,0:T(8,128)S(1)}) custom-call(bf16[1024,128]{1,0:T(8,128)(2,1)S(1)} %get-tuple-element.36.w_a, bf16[1024,128]{1,0:T(8,128)(2,1)S(1)} %collective-permute-done.2.got_a, bf16[1024,128]{1,0:T(8,128)(2,1)S(1)} %get-tuple-element.40.w_b, ...), custom_call_target="tpu_custom_call" | custom-call | tf_op jit(solution)/shard_map/partial/pallas_call | solution.py:247
  13.8 0.1 collective-permute-start.7
  14.0 1.6 %collective-permute-start.6 = (bf16[1024,128]{1,0:T(8,128)(2,1)S(1)}, bf16[1024,128]{1,0:T(8,128)(2,1)S(1)}, u32[]{:S(2)}, u32[]{:S(2)}) collective-permute-start(bf16[1024,128]{1,0:T(8,128)(2,1)S(1)} %get-tuple-element.43), channel_id=1, source_target_pairs={{0,3},{1,2},{2,1},{3,0},{4,7},{5,6},{6,5},{7,4},{8,11},{9,10},{10,... | collective-permute-start | bytes 786440 | tf_op jit(solution)/shard_map/ppermute | solution.py:279
  15.5 3.9 %collective-permute-done.got_a = bf16[1152,128]{1,0:T(8,128)(2,1)S(1)} collective-permute-done((bf16[1152,128]{1,0:T(8,128)(2,1)S(1)}, bf16[1152,128]{1,0:T(8,128)(2,1)S(1)}, u32[]{:S(2)}, u32[]{:S(2)}) %collective-permute-start) | collective-permute-done | bytes 294944 | tf_op jit(solution)/shard_map/ppermute | solution.py:279
  19.4 0.0 collective-permute-done.1.got_b
  19.4 0.8 %partial.3 = (bf16[1152,128]{1,0:T(8,128)(2,1)S(1)}, bf16[1152,128]{1,0:T(8,128)(2,1)S(1)}, f32[2304,128]{1,0:T(8,128)S(1)}) custom-call(bf16[1152,128]{1,0:T(8,128)(2,1)S(1)} %get-tuple-element.38.w_a, bf16[1152,128]{1,0:T(8,128)(2,1)S(1)} %collective-permute-done.got_a, bf16[1152,128]{1,0:T(8,128)(2,1)S(1)} %get-tuple-element.39.w_b, ...), custom_call_target="tpu_custom_call" | custom-call | tf_op jit(solution)/shard_map/partial/pallas_call | solution.py:247
  20.2 0.2 collective-permute-start.5
  20.4 0.1 collective-permute-start.4
  20.5 4.5 %collective-permute-done.7.far_b = bf16[1024,128]{1,0:T(8,128)(2,1)S(1)} collective-permute-done((bf16[1024,128]{1,0:T(8,128)(2,1)S(1)}, bf16[1024,128]{1,0:T(8,128)(2,1)S(1)}, u32[]{:S(2)}, u32[]{:S(2)}) %collective-permute-start.7) | collective-permute-done | bytes 262176 | tf_op jit(solution)/shard_map/ppermute | solution.py:279
  25.0 0.0 collective-permute-done.6.far_a
  25.0 0.1 combine_1.1.mid
  25.1 1.7 %collective-permute-start.11 = (bf16[2048,128]{1,0:T(8,128)(2,1)S(1)}, bf16[2048,128]{1,0:T(8,128)(2,1)S(1)}, u32[]{:S(2)}, u32[]{:S(2)}) collective-permute-start(bf16[2048,128]{1,0:T(8,128)(2,1)S(1)} %combine_1.1.mid), channel_id=1, source_target_pairs={{0,4},{4,0},{8,12},{12,8},{16,20},{20,16},{24,28},{28,24},{32,36},... | collective-permute-start | bytes 1572872 | tf_op jit(solution)/shard_map/ppermute | solution.py:283
  26.9 10.9 %collective-permute-start.10 = (bf16[2048,128]{1,0:T(8,128)(2,1)S(1)}, bf16[2048,128]{1,0:T(8,128)(2,1)S(1)}, u32[]{:S(2)}, u32[]{:S(2)}) collective-permute-start(bf16[2048,128]{1,0:T(8,128)(2,1)S(1)} %combine_1.1.mid), channel_id=1, source_target_pairs={{0,252},{4,8},{8,4},{12,16},{16,12},{20,24},{24,20},{28,32},{32,28... | collective-permute-start | bytes 1572872 | tf_op jit(solution)/shard_map/ppermute | solution.py:282
  37.8 0.0 collective-permute-done.5.far_b
  37.8 0.0 collective-permute-done.4.far_a
  37.8 0.1 combine_2.1
  37.9 0.1 collective-permute-start.9
  38.0 6.3 %collective-permute-start.8 = (bf16[2048,128]{1,0:T(8,128)(2,1)S(1)}, bf16[2048,128]{1,0:T(8,128)(2,1)S(1)}, u32[]{:S(2)}, u32[]{:S(2)}) collective-permute-start(bf16[2048,128]{1,0:T(8,128)(2,1)S(1)} %get-tuple-element.55.rest), channel_id=1, source_target_pairs={{0,0},{4,8},{8,4},{12,16},{16,12},{20,24},{24,20},{28,32},{32,28},... | collective-permute-start | bytes 1572872 | tf_op jit(solution)/shard_map/ppermute | solution.py:282
  44.2 0.0 copy-done
  44.3 0.0 copy-done.2
  44.3 0.2 convert_reduce_fusion.below
  44.5 0.0 copy-done.1
  44.5 4.1 %impute_own.1 = (bf16[12416,128]{1,0:T(8,128)(2,1)S(1)}, bf16[8192,128]{1,0:T(8,128)(2,1)S(1)}, bf16[64,128,512]{2,1,0:T(8,128)(2,1)S(1)}) custom-call(s32[8]{0:T(128)S(1)} %compare_select_fusion.5.place, s32[64]{0:T(128)S(1)} %copy-done, s32[64]{0:T(128)S(1)} %copy-done.1, s32[8]{0:T(128)S(1)} %convert_reduce_fusion.below, ...), custom_call_target="tpu_custom_call" | custom-call | tf_op jit(solution)/shard_map/impute_own/pallas_call | solution.py:247
  48.5 0.0 collective-permute-done.11.got_e.mid_e
  48.5 0.0 collective-permute-done.10.got_o.mid_o
  48.6 0.7 %finish_edge.1.edge = bf16[256,128]{1,0:T(8,128)(2,1)S(1)} custom-call(s32[8]{0:T(128)S(1)} %compare_select_fusion.5.place, f32[256,128]{1,0:T(8,128)S(1)} %get-tuple-element.56.edge, bf16[256,128]{1,0:T(8,128)(2,1)S(1)} %get-tuple-element.57.edge_band, bf16[2048,128]{1,0:T(8,128)(2,1)S(1)} %collective-permute-done.10.got_o.mid_o, ...), custom_call_target="tpu_custom_call" | custom-call | tf_op jit(solution)/shard_map/finish_edge/pallas_call | solution.py:247
  49.3 0.1 collective-permute-start.13
  49.4 4.1 %collective-permute-start.12 = (bf16[256,128]{1,0:T(8,128)(2,1)S(1)}, bf16[256,128]{1,0:T(8,128)(2,1)S(1)}, u32[]{:S(2)}, u32[]{:S(2)}) collective-permute-start(bf16[256,128]{1,0:T(8,128)(2,1)S(1)} %finish_edge.1.edge), channel_id=1, source_target_pairs={{0,252},{4,8},{8,4},{12,16},{16,12},{20,24},{24,20},{28,32},{32,28... | collective-permute-start | bytes 196616 | tf_op jit(solution)/shard_map/ppermute | solution.py:282
  53.4 2.0 %impute_near.1 = (bf16[12416,128]{1,0:T(8,128)(2,1)S(1)}, bf16[8192,128]{1,0:T(8,128)(2,1)S(1)}) custom-call(s32[8]{0:T(128)S(1)} %compare_select_fusion.5.place, s32[64]{0:T(128)S(1)} %copy-done, s32[64]{0:T(128)S(1)} %copy-done.1, s32[8]{0:T(128)S(1)} %convert_reduce_fusion.below, ...), custom_call_target="tpu_custom_call", output_to_operand_aliasing={{0}: (8, {}), {1}: (9, {})} | custom-call | tf_op jit(solution)/shard_map/impute_near/pallas_call | solution.py:247
  55.4 0.0 collective-permute-done.9.rest_e
  55.4 0.0 collective-permute-done.8.rest_o
  55.4 0.0 collective-permute-done.13.edge_e
  55.4 1.0 %collective-permute-done.12.edge_o = bf16[256,128]{1,0:T(8,128)(2,1)S(1)} collective-permute-done((bf16[256,128]{1,0:T(8,128)(2,1)S(1)}, bf16[256,128]{1,0:T(8,128)(2,1)S(1)}, u32[]{:S(2)}, u32[]{:S(2)}) %collective-permute-start.12) | collective-permute-done | bytes 65568 | tf_op jit(solution)/shard_map/ppermute | solution.py:282
  56.5 3.3 %impute_far.1 = (bf16[12416,128]{1,0:T(8,128)(2,1)S(1)}, bf16[8192,128]{1,0:T(8,128)(2,1)S(1)}, bf16[8192,128]{1,0:T(8,128)(2,1)}) custom-call(s32[8]{0:T(128)S(1)} %compare_select_fusion.5.place, s32[64]{0:T(128)S(1)} %copy-done, s32[64]{0:T(128)S(1)} %copy-done.1, s32[8]{0:T(128)S(1)} %convert_reduce_fusion.below, ...), custom_call_target="tpu_custom_call", output_to_operand_aliasing={{0}: (9, {}), {1}: (10, {})} | custom-call | tf_op jit(solution)/shard_map/impute_far/pallas_call | solution.py:247
  (2 shorter events, 0.0 us)
Async XLA Ops:
  2.8 8.4 %collective-permute-start.3 = (bf16[1024,128]{1,0:T(8,128)(2,1)S(1)}, bf16[1024,128]{1,0:T(8,128)(2,1)S(1)}, u32[]{:S(2)}, u32[]{:S(2)}) collective-permute-start(bf16[1024,128]{1,0:T(8,128)(2,1)S(1)} %get-tuple-element.40.w_b), channel_id=1, source_target_pairs={{0,3},{1,2},{2,1},{3,0},{4,7},{5,6},{6,5},{7,4},{8,11},{9,10},{10,... | collective-permute-start | bytes 786440 | tf_op jit(solution)/shard_map/ppermute | solution.py:279
  6.2 6.9 %collective-permute-start.2 = (bf16[1024,128]{1,0:T(8,128)(2,1)S(1)}, bf16[1024,128]{1,0:T(8,128)(2,1)S(1)}, u32[]{:S(2)}, u32[]{:S(2)}) collective-permute-start(bf16[1024,128]{1,0:T(8,128)(2,1)S(1)} %get-tuple-element.36.w_a), channel_id=1, source_target_pairs={{0,1},{1,0},{2,3},{3,2},{4,5},{5,4},{6,7},{7,6},{8,9},{9,8},{10,11... | collective-permute-start | bytes 786440 | tf_op jit(solution)/shard_map/ppermute | solution.py:279
  8.9 10.5 %collective-permute-start = (bf16[1152,128]{1,0:T(8,128)(2,1)S(1)}, bf16[1152,128]{1,0:T(8,128)(2,1)S(1)}, u32[]{:S(2)}, u32[]{:S(2)}) collective-permute-start(bf16[1152,128]{1,0:T(8,128)(2,1)S(1)} %get-tuple-element.38.w_a), channel_id=1, source_target_pairs={{0,1},{1,0},{2,3},{3,2},{4,5},{5,4},{6,7},{7,6},{8,9},{9,8},{10,11... | collective-permute-start | bytes 884744 | tf_op jit(solution)/shard_map/ppermute | solution.py:279
  10.5 8.9 %collective-permute-start.1 = (bf16[1152,128]{1,0:T(8,128)(2,1)S(1)}, bf16[1152,128]{1,0:T(8,128)(2,1)S(1)}, u32[]{:S(2)}, u32[]{:S(2)}) collective-permute-start(bf16[1152,128]{1,0:T(8,128)(2,1)S(1)} %get-tuple-element.39.w_b), channel_id=1, source_target_pairs={{0,3},{1,2},{2,1},{3,0},{4,7},{5,6},{6,5},{7,4},{8,11},{9,10},{10,... | collective-permute-start | bytes 884744 | tf_op jit(solution)/shard_map/ppermute | solution.py:279
  13.1 31.1 %copy-start = (s32[64]{0:T(128)S(1)}, s32[64]{0:T(128)}, u32[]{:S(2)}) copy-start(s32[64]{0:T(128)} %starts.5) | copy-start | bytes 772
  13.1 31.2 %copy-start.2 = (s32[8]{0:T(128)S(1)}, s32[8]{0:T(128)}, u32[]{:S(2)}) copy-start(s32[8]{0:T(128)} %constant.48.clone) | copy-start | bytes 100
  13.1 31.4 %copy-start.1 = (s32[64]{0:T(128)S(1)}, s32[64]{0:T(128)}, u32[]{:S(2)}) copy-start(s32[64]{0:T(128)} %counts.5) | copy-start | bytes 772
  13.8 11.2 %collective-permute-start.7 = (bf16[1024,128]{1,0:T(8,128)(2,1)S(1)}, bf16[1024,128]{1,0:T(8,128)(2,1)S(1)}, u32[]{:S(2)}, u32[]{:S(2)}) collective-permute-start(bf16[1024,128]{1,0:T(8,128)(2,1)S(1)} %get-tuple-element.50), channel_id=1, source_target_pairs={{0,1},{1,0},{2,3},{3,2},{4,5},{5,4},{6,7},{7,6},{8,9},{9,8},{10,11... | collective-permute-start | bytes 786440 | tf_op jit(solution)/shard_map/ppermute | solution.py:279
  14.0 11.1 %collective-permute-start.6 = (bf16[1024,128]{1,0:T(8,128)(2,1)S(1)}, bf16[1024,128]{1,0:T(8,128)(2,1)S(1)}, u32[]{:S(2)}, u32[]{:S(2)}) collective-permute-start(bf16[1024,128]{1,0:T(8,128)(2,1)S(1)} %get-tuple-element.43), channel_id=1, source_target_pairs={{0,3},{1,2},{2,1},{3,0},{4,7},{5,6},{6,5},{7,4},{8,11},{9,10},{10,... | collective-permute-start | bytes 786440 | tf_op jit(solution)/shard_map/ppermute | solution.py:279
  20.2 17.6 %collective-permute-start.5 = (bf16[1152,128]{1,0:T(8,128)(2,1)S(1)}, bf16[1152,128]{1,0:T(8,128)(2,1)S(1)}, u32[]{:S(2)}, u32[]{:S(2)}) collective-permute-start(bf16[1152,128]{1,0:T(8,128)(2,1)S(1)} %get-tuple-element.48), channel_id=1, source_target_pairs={{0,1},{1,0},{2,3},{3,2},{4,5},{5,4},{6,7},{7,6},{8,9},{9,8},{10,11... | collective-permute-start | bytes 884744 | tf_op jit(solution)/shard_map/ppermute | solution.py:279
  20.4 17.3 %collective-permute-start.4 = (bf16[1152,128]{1,0:T(8,128)(2,1)S(1)}, bf16[1152,128]{1,0:T(8,128)(2,1)S(1)}, u32[]{:S(2)}, u32[]{:S(2)}) collective-permute-start(bf16[1152,128]{1,0:T(8,128)(2,1)S(1)} %get-tuple-element.47), channel_id=1, source_target_pairs={{0,3},{1,2},{2,1},{3,0},{4,7},{5,6},{6,5},{7,4},{8,11},{9,10},{10,... | collective-permute-start | bytes 884744 | tf_op jit(solution)/shard_map/ppermute | solution.py:279
  25.1 23.4 %collective-permute-start.11 = (bf16[2048,128]{1,0:T(8,128)(2,1)S(1)}, bf16[2048,128]{1,0:T(8,128)(2,1)S(1)}, u32[]{:S(2)}, u32[]{:S(2)}) collective-permute-start(bf16[2048,128]{1,0:T(8,128)(2,1)S(1)} %combine_1.1.mid), channel_id=1, source_target_pairs={{0,4},{4,0},{8,12},{12,8},{16,20},{20,16},{24,28},{28,24},{32,36},... | collective-permute-start | bytes 1572872 | tf_op jit(solution)/shard_map/ppermute | solution.py:283
  26.9 21.7 %collective-permute-start.10 = (bf16[2048,128]{1,0:T(8,128)(2,1)S(1)}, bf16[2048,128]{1,0:T(8,128)(2,1)S(1)}, u32[]{:S(2)}, u32[]{:S(2)}) collective-permute-start(bf16[2048,128]{1,0:T(8,128)(2,1)S(1)} %combine_1.1.mid), channel_id=1, source_target_pairs={{0,252},{4,8},{8,4},{12,16},{16,12},{20,24},{24,20},{28,32},{32,28... | collective-permute-start | bytes 1572872 | tf_op jit(solution)/shard_map/ppermute | solution.py:282
  37.9 17.5 %collective-permute-start.9 = (bf16[2048,128]{1,0:T(8,128)(2,1)S(1)}, bf16[2048,128]{1,0:T(8,128)(2,1)S(1)}, u32[]{:S(2)}, u32[]{:S(2)}) collective-permute-start(bf16[2048,128]{1,0:T(8,128)(2,1)S(1)} %get-tuple-element.55.rest), channel_id=1, source_target_pairs={{0,4},{4,0},{8,12},{12,8},{16,20},{20,16},{24,28},{28,24},{32,36},... | collective-permute-start | bytes 1572872 | tf_op jit(solution)/shard_map/ppermute | solution.py:283
  38.0 17.4 %collective-permute-start.8 = (bf16[2048,128]{1,0:T(8,128)(2,1)S(1)}, bf16[2048,128]{1,0:T(8,128)(2,1)S(1)}, u32[]{:S(2)}, u32[]{:S(2)}) collective-permute-start(bf16[2048,128]{1,0:T(8,128)(2,1)S(1)} %get-tuple-element.55.rest), channel_id=1, source_target_pairs={{0,0},{4,8},{8,4},{12,16},{16,12},{20,24},{24,20},{28,32},{32,28},... | collective-permute-start | bytes 1572872 | tf_op jit(solution)/shard_map/ppermute | solution.py:282
  49.3 6.1 %collective-permute-start.13 = (bf16[256,128]{1,0:T(8,128)(2,1)S(1)}, bf16[256,128]{1,0:T(8,128)(2,1)S(1)}, u32[]{:S(2)}, u32[]{:S(2)}) collective-permute-start(bf16[256,128]{1,0:T(8,128)(2,1)S(1)} %finish_edge.1.edge), channel_id=1, source_target_pairs={{0,4},{4,0},{8,12},{12,8},{16,20},{20,16},{24,28},{28,24},{32,36},... | collective-permute-start | bytes 196616 | tf_op jit(solution)/shard_map/ppermute | solution.py:283
  49.4 7.1 %collective-permute-start.12 = (bf16[256,128]{1,0:T(8,128)(2,1)S(1)}, bf16[256,128]{1,0:T(8,128)(2,1)S(1)}, u32[]{:S(2)}, u32[]{:S(2)}) collective-permute-start(bf16[256,128]{1,0:T(8,128)(2,1)S(1)} %finish_edge.1.edge), channel_id=1, source_target_pairs={{0,252},{4,8},{8,4},{12,16},{16,12},{20,24},{24,20},{28,32},{32,28... | collective-permute-start | bytes 196616 | tf_op jit(solution)/shard_map/ppermute | solution.py:282

commit v9 on v7

--- a/solution.py
+++ b/solution.py
@@ -123,13 +123,10 @@
     edge[at(1), :] = own[at(2 * HALF2 - 1), :] + far_b[at(inner), :].astype(F32)
 
 
-def finish_edge(place, edge, edge_band, got_e, got_o, out):
-    odd = place[5] == 1
+def finish_edge(place, edge, edge_band, got_r, got_l, out):
     nothing = jnp.zeros((BLK, COLS), BF)
-    from_left = jnp.where(odd, got_e[at(2 * HALF1 + 1), :], got_o[at(2 * HALF1 + 1), :])
-    from_right = jnp.where(odd, got_o[at(2 * HALF1), :], got_e[at(2 * HALF1), :])
-    from_left = jnp.where(place[3] == 0, nothing, from_left)
-    from_right = jnp.where(place[3] == place[4] - 1, nothing, from_right)
+    from_left = jnp.where(place[3] == 0, nothing, got_l[at(2 * HALF1 + 1), :])
+    from_right = jnp.where(place[3] == place[4] - 1, nothing, got_r[at(2 * HALF1), :])
     for k, rows in enumerate((from_left, from_right)):
         out[at(k), :] = (edge[at(k), :] + dot(edge_band[at(k), :], rows)).astype(BF)
 
@@ -211,18 +208,18 @@
     lax.fori_loop(groups + 1, UB // UNROLL, rest_ready, 0)
 
 
-def impute_near(place, starts, counts, below, edge, mid_e, mid_o, ld, before, done, ext, out):
+def impute_near(place, starts, counts, below, edge, mid_r, mid_l, ld, before, done, ext, out):
     move(ext, TB, edge, 0, 1)
     move(ext, 2 * TB - 1, edge, 1, 1)
-    move(ext, 2 * TB * (1 - place[5]) + MID, mid_e, 0, 2 * HALF1)
-    move(ext, 2 * TB * place[5] + MID, mid_o, 0, 2 * HALF1)
+    move(ext, MID, mid_l, 0, 2 * HALF1)
+    move(ext, 2 * TB + MID, mid_r, 0, 2 * HALF1)
     ranges = [(below[k], below[k + 1]) for k in (0, 2, 4, 6)]
     on_ranges(ranges, starts, counts, place[3] * TB - TB, ld, ext, out)
 
 
-def impute_far(place, starts, counts, below, rest_e, rest_o, edge_e, edge_o, ld, before, done, ext, rows, out, sems):
+def impute_far(place, starts, counts, below, rest_r, rest_l, edge_r, edge_l, ld, before, done, ext, rows, out, sems):
     inner = HALF2 - 1
-    for base, rest, edge in ((2 * TB * (1 - place[5]), rest_e, edge_e), (2 * TB * place[5], rest_o, edge_o)):
+    for base, rest, edge in ((0, rest_l, edge_l), (2 * TB, rest_r, edge_r)):
         move(ext, base, edge, 0, 1)
         move(ext, base + 1, rest, 0, inner)
         move(ext, base + MID_END, rest, inner, inner)
@@ -266,18 +263,21 @@
     owners = lax.axis_size(ROWS)
     lane = lax.iota(jnp.int32, 8)
     place = jnp.zeros((8,), jnp.int32)
-    for k, value in enumerate((t, t ^ 1, 3 - t, g, owners, g % 2)):
+    for k, value in enumerate((t, t ^ 1, 3 - t, g, owners)):
         place = jnp.where(lane == k, value, place)
     pairs_a = [(i, i ^ 1) for i in range(4)]
     pairs_b = [(i, 3 - i) for i in range(4)]
-    pairs_e = [(i, i ^ 1) for i in range(owners)]
-    pairs_o = [(i, (i + 1) % owners if i % 2 else (i - 1) % owners) for i in range(owners)]
+    open_right = [(i, i + 1) for i in range(owners - 1)]
+    open_left = [(i + 1, i) for i in range(owners - 1)]
+    right = open_right + [(owners - 1, 0)]
+    left = open_left + [(0, owners - 1)]
 
     def along_trait(x, y, pairs_x, pairs_y):
         return lax.ppermute(x, "trait", pairs_x), lax.ppermute(y, "trait", pairs_y)
 
-    def along_rows(x, y):
-        return lax.ppermute(x, ROWS, pairs_e), lax.ppermute(y, ROWS, pairs_o)
+    def along_rows(x, to_right, to_left):
+        from_right = lax.ppermute(x, ROWS, to_left)
+        return from_right, lax.ppermute(x, ROWS, to_right)
 
     z, band, mix, ld = (pltpu.with_memory_space_constraint(x, pltpu.HBM) for x in (z, band, mix, ld))
     mix_part = jax.ShapeDtypeStruct((2 * COLS, 2 * COLS), BF)
@@ -318,12 +318,12 @@
     (own2, far2a, far2b), after = mixing(w2a, got2a, w2b, got2b)
     far1a, far1b, _ = lax.optimization_barrier((far1a, far1b, after))
     (mixed1,) = call(combine_1, in_vmem(shaped(2 * HALF1 + 2)), [VM] * 3, (own1, far1a, far1b))
-    mid_e, mid_o = along_rows(mixed1, mixed1)
+    mid_r, mid_l = along_rows(mixed1, right, left)
     far2a, far2b, _ = lax.optimization_barrier((far2a, far2b, mixed1))
     mixed2, edge_sums = call(
         combine_2, in_vmem(shaped(2 * HALF2 - 2), shaped(2, F32)), [VM] * 3, (own2, far2a, far2b)
     )
-    rest_e, rest_o = along_rows(mixed2, mixed2)
+    rest_r, rest_l = along_rows(mixed2, open_right, open_left)
     starts_here = starts - (g * TB - TB)
     below = jnp.sum(starts_here[None, :] < jnp.array(LIMITS, jnp.int32)[:, None], axis=1, dtype=jnp.int32)
     plan = (place, starts, counts, below)
@@ -334,16 +334,16 @@
         (*plan, mixed1, mixed2, ld),
         [pltpu.SemaphoreType.DMA((UB // UNROLL,))],
     )
-    mid_e, mid_o, ext = lax.optimization_barrier((mid_e, mid_o, ext))
+    mid_r, mid_l, ext = lax.optimization_barrier((mid_r, mid_l, ext))
     (mixed3,) = call(
-        finish_edge, in_vmem(shaped(2)), [SMEM] + [VM] * 4, (place, edge_sums, edge_band, mid_e, mid_o)
-    )
-    edge_e, edge_o = along_rows(mixed3, mixed3)
+        finish_edge, in_vmem(shaped(2)), [SMEM] + [VM] * 4, (place, edge_sums, edge_band, mid_r, mid_l)
+    )
+    edge_r, edge_l = along_rows(mixed3, right, left)
     ext, done = call(
         impute_near,
         in_vmem(shaped(EXT), shaped(UB)),
         [SMEM] * 4 + [VM] * 6,
-        (*plan, mixed3, mid_e, mid_o, ld, ext, done),
+        (*plan, mixed3, mid_r, mid_l, ld, ext, done),
         (),
         {8: 0, 9: 1},
     )
@@ -351,7 +351,7 @@
         impute_far,
         in_vmem(shaped(EXT), shaped(UB)) + [(shaped(UB), HBM)],
         [SMEM] * 4 + [VM] * 7,
-        (*plan, rest_e, rest_o, edge_e, edge_o, ld, ext, done),
+        (*plan, rest_r, rest_l, edge_r, edge_l, ld, ext, done),
         [pltpu.SemaphoreType.DMA((UB // UNROLL,))],
         {9: 0, 10: 1},
     )

time: 63.9 us -> 61.7 us (0.966)
  waiting for transfers between devices: 19.8 us -> 11.4 us
  starting transfers between devices: 26.9 us -> 32.8 us
    ppermute x6, waiting for transfers between devices: 8.86 us -> 0.42 us  [the longest x3 0.41 us: along_rows(): return (from_right, lax.ppermute(x, ROWS, to_right))]
    ppermute x6, starting transfers between devices: 19.8 us -> 25.7 us  [the longest x3 22 us: along_rows(): from_right = lax.ppermute(x, ROWS, to_left)]
  transfers between devices with their start and end apart: 14 -> 14, of which waited for: 9 -> 5; matrix products, arithmetic and copies ran while one was open for 0% -> 0% of each run, Pallas kernels for 17% -> 17%
where the time goes in v9:
time: 61.7 us
  starting transfers between devices  32.8 us (53%)
  Pallas kernels  17.2 us (28%)
  waiting for transfers between devices  11.4 us (18%)
    ppermute x3, starting transfers between devices, along_rows(): from_right = lax.ppermute(x, ROWS, to_left)  22 us
    pallas_call x10, Pallas kernels, call(): pl.pallas_call(kernel, name=kernel.__name__, out_shape=tuple((shape for s...  17.2 us
    ppermute x4, waiting for transfers between devices, along_trait(): lax.ppermute(x, 'trait', pairs_x)  5.78 us
    ppermute x4, waiting for transfers between devices, along_trait(): lax.ppermute(y, 'trait', pairs_y)  5.17 us
    ppermute x4, starting transfers between devices, along_trait(): lax.ppermute(y, 'trait', pairs_y)  3.9 us
    ppermute x3, starting transfers between devices, along_rows(): return (from_right, lax.ppermute(x, ROWS, to_right))  3.72 us
    ppermute x4, starting transfers between devices, along_trait(): lax.ppermute(x, 'trait', pairs_x)  3.2 us
  transfers between devices with their start and end apart: 14, of which 5 were waited for; matrix products, arithmetic and copies ran while one was open for 0% of the time, Pallas kernels for 17%

profile of v9, /device:TPU:1, one launch (start us, length us, event | category | flops | bytes accessed | tf_op | source)
XLA Modules:
  0.0 61.7 jit_solution(13257985874123369603)
XLA Ops:
  0.0 2.8 %whiten_1.1 = (bf16[1024,128]{1,0:T(8,128)(2,1)S(1)}, bf16[1024,128]{1,0:T(8,128)(2,1)S(1)}, bf16[256,256]{1,0:T(8,128)(2,1)S(1)}, bf16[256,256]{1,0:T(8,128)(2,1)S(1)}) custom-call(s32[8]{0:T(128)S(1)} %compare_select_fusion.4.place, bf16[4096,128]{1,0:T(8,128)(2,1)} %z.2, bf16[32,128,384]{2,1,0:T(8,128)(2,1)} %band.3, bf16[512,512]{1,0:T(8,128)(2,1)} %mix.1), custom_call_target="tpu_custom_call" | custom-call | tf_op jit(solution)/shard_map/whiten_1/pallas_call | solution.py:244
  2.8 3.4 %collective-permute-start.3 = (bf16[1024,128]{1,0:T(8,128)(2,1)S(1)}, bf16[1024,128]{1,0:T(8,128)(2,1)S(1)}, u32[]{:S(2)}, u32[]{:S(2)}) collective-permute-start(bf16[1024,128]{1,0:T(8,128)(2,1)S(1)} %get-tuple-element.40.w_b), channel_id=1, source_target_pairs={{0,3},{1,2},{2,1},{3,0},{4,7},{5,6},{6,5},{7,4},{8,11},{9,10},{10,... | collective-permute-start | bytes 786440 | tf_op jit(solution)/shard_map/ppermute | solution.py:276
  6.2 0.0 collective-permute-start.2
  6.3 2.7 %whiten_2.1 = (bf16[1152,128]{1,0:T(8,128)(2,1)S(1)}, bf16[1152,128]{1,0:T(8,128)(2,1)S(1)}, bf16[256,128]{1,0:T(8,128)(2,1)S(1)}) custom-call(bf16[4096,128]{1,0:T(8,128)(2,1)} %z.2, bf16[32,128,384]{2,1,0:T(8,128)(2,1)} %band.3), custom_call_target="tpu_custom_call" | custom-call | tf_op jit(solution)/shard_map/whiten_2/pallas_call | solution.py:244
  8.9 1.5 %collective-permute-start = (bf16[1152,128]{1,0:T(8,128)(2,1)S(1)}, bf16[1152,128]{1,0:T(8,128)(2,1)S(1)}, u32[]{:S(2)}, u32[]{:S(2)}) collective-permute-start(bf16[1152,128]{1,0:T(8,128)(2,1)S(1)} %get-tuple-element.38.w_a), channel_id=1, source_target_pairs={{0,1},{1,0},{2,3},{3,2},{4,5},{5,4},{6,7},{7,6},{8,9},{9,8},{10,11... | collective-permute-start | bytes 884744 | tf_op jit(solution)/shard_map/ppermute | solution.py:276
  10.5 0.1 collective-permute-start.1
  10.6 0.6 %collective-permute-done.3.got_b = bf16[1024,128]{1,0:T(8,128)(2,1)S(1)} collective-permute-done((bf16[1024,128]{1,0:T(8,128)(2,1)S(1)}, bf16[1024,128]{1,0:T(8,128)(2,1)S(1)}, u32[]{:S(2)}, u32[]{:S(2)}) %collective-permute-start.3) | collective-permute-done | bytes 262176 | tf_op jit(solution)/shard_map/ppermute | solution.py:276
  11.2 1.9 %collective-permute-done.2.got_a = bf16[1024,128]{1,0:T(8,128)(2,1)S(1)} collective-permute-done((bf16[1024,128]{1,0:T(8,128)(2,1)S(1)}, bf16[1024,128]{1,0:T(8,128)(2,1)S(1)}, u32[]{:S(2)}, u32[]{:S(2)}) %collective-permute-start.2) | collective-permute-done | bytes 262176 | tf_op jit(solution)/shard_map/ppermute | solution.py:276
  13.1 0.0 copy-start
  13.1 0.0 copy-start.2
  13.1 0.0 copy-start.1
  13.1 0.7 %partial.2 = (bf16[1024,128]{1,0:T(8,128)(2,1)S(1)}, bf16[1024,128]{1,0:T(8,128)(2,1)S(1)}, f32[2048,128]{1,0:T(8,128)S(1)}) custom-call(bf16[1024,128]{1,0:T(8,128)(2,1)S(1)} %get-tuple-element.36.w_a, bf16[1024,128]{1,0:T(8,128)(2,1)S(1)} %collective-permute-done.2.got_a, bf16[1024,128]{1,0:T(8,128)(2,1)S(1)} %get-tuple-element.40.w_b, ...), custom_call_target="tpu_custom_call" | custom-call | tf_op jit(solution)/shard_map/partial/pallas_call | solution.py:244
  13.8 0.2 collective-permute-start.7
  14.0 1.6 %collective-permute-start.6 = (bf16[1024,128]{1,0:T(8,128)(2,1)S(1)}, bf16[1024,128]{1,0:T(8,128)(2,1)S(1)}, u32[]{:S(2)}, u32[]{:S(2)}) collective-permute-start(bf16[1024,128]{1,0:T(8,128)(2,1)S(1)} %get-tuple-element.43), channel_id=1, source_target_pairs={{0,3},{1,2},{2,1},{3,0},{4,7},{5,6},{6,5},{7,4},{8,11},{9,10},{10,... | collective-permute-start | bytes 786440 | tf_op jit(solution)/shard_map/ppermute | solution.py:276
  15.5 3.9 %collective-permute-done.got_a = bf16[1152,128]{1,0:T(8,128)(2,1)S(1)} collective-permute-done((bf16[1152,128]{1,0:T(8,128)(2,1)S(1)}, bf16[1152,128]{1,0:T(8,128)(2,1)S(1)}, u32[]{:S(2)}, u32[]{:S(2)}) %collective-permute-start) | collective-permute-done | bytes 294944 | tf_op jit(solution)/shard_map/ppermute | solution.py:276
  19.4 0.0 collective-permute-done.1.got_b
  19.4 0.8 %partial.3 = (bf16[1152,128]{1,0:T(8,128)(2,1)S(1)}, bf16[1152,128]{1,0:T(8,128)(2,1)S(1)}, f32[2304,128]{1,0:T(8,128)S(1)}) custom-call(bf16[1152,128]{1,0:T(8,128)(2,1)S(1)} %get-tuple-element.38.w_a, bf16[1152,128]{1,0:T(8,128)(2,1)S(1)} %collective-permute-done.got_a, bf16[1152,128]{1,0:T(8,128)(2,1)S(1)} %get-tuple-element.39.w_b, ...), custom_call_target="tpu_custom_call" | custom-call | tf_op jit(solution)/shard_map/partial/pallas_call | solution.py:244
  20.2 0.2 collective-permute-start.5
  20.4 0.1 collective-permute-start.4
  20.5 4.5 %collective-permute-done.7.far_b = bf16[1024,128]{1,0:T(8,128)(2,1)S(1)} collective-permute-done((bf16[1024,128]{1,0:T(8,128)(2,1)S(1)}, bf16[1024,128]{1,0:T(8,128)(2,1)S(1)}, u32[]{:S(2)}, u32[]{:S(2)}) %collective-permute-start.7) | collective-permute-done | bytes 262176 | tf_op jit(solution)/shard_map/ppermute | solution.py:276
  25.0 0.0 collective-permute-done.6.far_a
  25.0 0.1 combine_1.1.mid
  25.1 1.7 %collective-permute-start.11 = (bf16[2048,128]{1,0:T(8,128)(2,1)S(1)}, bf16[2048,128]{1,0:T(8,128)(2,1)S(1)}, u32[]{:S(2)}, u32[]{:S(2)}) collective-permute-start(bf16[2048,128]{1,0:T(8,128)(2,1)S(1)} %combine_1.1.mid), channel_id=1, source_target_pairs={{0,4},{4,8},{8,12},{12,16},{16,20},{20,24},{24,28},{28,32},{32,36}... | collective-permute-start | bytes 1572872 | tf_op jit(solution)/shard_map/ppermute | solution.py:280
  26.9 10.0 %collective-permute-start.10 = (bf16[2048,128]{1,0:T(8,128)(2,1)S(1)}, bf16[2048,128]{1,0:T(8,128)(2,1)S(1)}, u32[]{:S(2)}, u32[]{:S(2)}) collective-permute-start(bf16[2048,128]{1,0:T(8,128)(2,1)S(1)} %combine_1.1.mid), channel_id=1, source_target_pairs={{4,0},{8,4},{12,8},{16,12},{20,16},{24,20},{28,24},{32,28},{36,32}... | collective-permute-start | bytes 1572872 | tf_op jit(solution)/shard_map/ppermute | solution.py:279
  36.8 0.0 collective-permute-done.5.far_b
  36.9 0.0 collective-permute-done.4.far_a
  36.9 0.1 combine_2.1
  37.0 1.9 %collective-permute-start.9 = (bf16[2048,128]{1,0:T(8,128)(2,1)S(1)}, bf16[2048,128]{1,0:T(8,128)(2,1)S(1)}, u32[]{:S(2)}, u32[]{:S(2)}) collective-permute-start(bf16[2048,128]{1,0:T(8,128)(2,1)S(1)} %get-tuple-element.55.rest), channel_id=1, source_target_pairs={{0,4},{4,8},{8,12},{12,16},{16,20},{20,24},{24,28},{28,32},{32,36}... | collective-permute-start | bytes 1572872 | tf_op jit(solution)/shard_map/ppermute | solution.py:280
  38.9 7.0 %collective-permute-start.8 = (bf16[2048,128]{1,0:T(8,128)(2,1)S(1)}, bf16[2048,128]{1,0:T(8,128)(2,1)S(1)}, u32[]{:S(2)}, u32[]{:S(2)}) collective-permute-start(bf16[2048,128]{1,0:T(8,128)(2,1)S(1)} %get-tuple-element.55.rest), channel_id=1, source_target_pairs={{4,0},{8,4},{12,8},{16,12},{20,16},{24,20},{28,24},{32,28},{36,32}... | collective-permute-start | bytes 1572872 | tf_op jit(solution)/shard_map/ppermute | solution.py:279
  45.9 0.0 copy-done
  45.9 0.0 copy-done.2
  45.9 0.2 convert_reduce_fusion.below
  46.1 0.0 copy-done.1
  46.1 4.1 %impute_own.1 = (bf16[12416,128]{1,0:T(8,128)(2,1)S(1)}, bf16[8192,128]{1,0:T(8,128)(2,1)S(1)}, bf16[64,128,512]{2,1,0:T(8,128)(2,1)S(1)}) custom-call(s32[8]{0:T(128)S(1)} %compare_select_fusion.4.place, s32[64]{0:T(128)S(1)} %copy-done, s32[64]{0:T(128)S(1)} %copy-done.1, s32[8]{0:T(128)S(1)} %convert_reduce_fusion.below, ...), custom_call_target="tpu_custom_call" | custom-call | tf_op jit(solution)/shard_map/impute_own/pallas_call | solution.py:244
  50.2 0.0 collective-permute-done.11.got_l.mid_l
  50.2 0.0 collective-permute-done.10.got_r.mid_r
  50.2 0.7 %finish_edge.1.edge = bf16[256,128]{1,0:T(8,128)(2,1)S(1)} custom-call(s32[8]{0:T(128)S(1)} %compare_select_fusion.4.place, f32[256,128]{1,0:T(8,128)S(1)} %get-tuple-element.56.edge, bf16[256,128]{1,0:T(8,128)(2,1)S(1)} %get-tuple-element.57.edge_band, bf16[2048,128]{1,0:T(8,128)(2,1)S(1)} %collective-permute-done.10.got_r.mid_r, ...), custom_call_target="tpu_custom_call" | custom-call | tf_op jit(solution)/shard_map/finish_edge/pallas_call | solution.py:244
  50.9 0.1 collective-permute-start.13
  51.0 5.1 %collective-permute-start.12 = (bf16[256,128]{1,0:T(8,128)(2,1)S(1)}, bf16[256,128]{1,0:T(8,128)(2,1)S(1)}, u32[]{:S(2)}, u32[]{:S(2)}) collective-permute-start(bf16[256,128]{1,0:T(8,128)(2,1)S(1)} %finish_edge.1.edge), channel_id=1, source_target_pairs={{4,0},{8,4},{12,8},{16,12},{20,16},{24,20},{28,24},{32,28},{36,32}... | collective-permute-start | bytes 196616 | tf_op jit(solution)/shard_map/ppermute | solution.py:279
  56.0 1.5 %impute_near.1 = (bf16[12416,128]{1,0:T(8,128)(2,1)S(1)}, bf16[8192,128]{1,0:T(8,128)(2,1)S(1)}) custom-call(s32[8]{0:T(128)S(1)} %compare_select_fusion.4.place, s32[64]{0:T(128)S(1)} %copy-done, s32[64]{0:T(128)S(1)} %copy-done.1, s32[8]{0:T(128)S(1)} %convert_reduce_fusion.below, ...), custom_call_target="tpu_custom_call", output_to_operand_aliasing={{0}: (8, {}), {1}: (9, {})} | custom-call | tf_op jit(solution)/shard_map/impute_near/pallas_call | solution.py:244
  57.5 0.0 collective-permute-done.9.rest_l
  57.6 0.0 collective-permute-done.8.rest_r
  57.6 0.4 collective-permute-done.13.edge_l
  58.0 0.0 collective-permute-done.12.edge_r
  58.0 3.8 %impute_far.1 = (bf16[12416,128]{1,0:T(8,128)(2,1)S(1)}, bf16[8192,128]{1,0:T(8,128)(2,1)S(1)}, bf16[8192,128]{1,0:T(8,128)(2,1)}) custom-call(s32[8]{0:T(128)S(1)} %compare_select_fusion.4.place, s32[64]{0:T(128)S(1)} %copy-done, s32[64]{0:T(128)S(1)} %copy-done.1, s32[8]{0:T(128)S(1)} %convert_reduce_fusion.below, ...), custom_call_target="tpu_custom_call", output_to_operand_aliasing={{0}: (9, {}), {1}: (10, {})} | custom-call | tf_op jit(solution)/shard_map/impute_far/pallas_call | solution.py:244
  (2 shorter events, 0.0 us)
Async XLA Ops:
  2.8 8.4 %collective-permute-start.3 = (bf16[1024,128]{1,0:T(8,128)(2,1)S(1)}, bf16[1024,128]{1,0:T(8,128)(2,1)S(1)}, u32[]{:S(2)}, u32[]{:S(2)}) collective-permute-start(bf16[1024,128]{1,0:T(8,128)(2,1)S(1)} %get-tuple-element.40.w_b), channel_id=1, source_target_pairs={{0,3},{1,2},{2,1},{3,0},{4,7},{5,6},{6,5},{7,4},{8,11},{9,10},{10,... | collective-permute-start | bytes 786440 | tf_op jit(solution)/shard_map/ppermute | solution.py:276
  6.2 6.9 %collective-permute-start.2 = (bf16[1024,128]{1,0:T(8,128)(2,1)S(1)}, bf16[1024,128]{1,0:T(8,128)(2,1)S(1)}, u32[]{:S(2)}, u32[]{:S(2)}) collective-permute-start(bf16[1024,128]{1,0:T(8,128)(2,1)S(1)} %get-tuple-element.36.w_a), channel_id=1, source_target_pairs={{0,1},{1,0},{2,3},{3,2},{4,5},{5,4},{6,7},{7,6},{8,9},{9,8},{10,11... | collective-permute-start | bytes 786440 | tf_op jit(solution)/shard_map/ppermute | solution.py:276
  8.9 10.5 %collective-permute-start = (bf16[1152,128]{1,0:T(8,128)(2,1)S(1)}, bf16[1152,128]{1,0:T(8,128)(2,1)S(1)}, u32[]{:S(2)}, u32[]{:S(2)}) collective-permute-start(bf16[1152,128]{1,0:T(8,128)(2,1)S(1)} %get-tuple-element.38.w_a), channel_id=1, source_target_pairs={{0,1},{1,0},{2,3},{3,2},{4,5},{5,4},{6,7},{7,6},{8,9},{9,8},{10,11... | collective-permute-start | bytes 884744 | tf_op jit(solution)/shard_map/ppermute | solution.py:276
  10.5 8.9 %collective-permute-start.1 = (bf16[1152,128]{1,0:T(8,128)(2,1)S(1)}, bf16[1152,128]{1,0:T(8,128)(2,1)S(1)}, u32[]{:S(2)}, u32[]{:S(2)}) collective-permute-start(bf16[1152,128]{1,0:T(8,128)(2,1)S(1)} %get-tuple-element.39.w_b), channel_id=1, source_target_pairs={{0,3},{1,2},{2,1},{3,0},{4,7},{5,6},{6,5},{7,4},{8,11},{9,10},{10,... | collective-permute-start | bytes 884744 | tf_op jit(solution)/shard_map/ppermute | solution.py:276
  13.1 32.8 %copy-start = (s32[64]{0:T(128)S(1)}, s32[64]{0:T(128)}, u32[]{:S(2)}) copy-start(s32[64]{0:T(128)} %starts.5) | copy-start | bytes 772
  13.1 32.8 %copy-start.2 = (s32[8]{0:T(128)S(1)}, s32[8]{0:T(128)}, u32[]{:S(2)}) copy-start(s32[8]{0:T(128)} %constant.36.clone) | copy-start | bytes 100
  13.1 33.0 %copy-start.1 = (s32[64]{0:T(128)S(1)}, s32[64]{0:T(128)}, u32[]{:S(2)}) copy-start(s32[64]{0:T(128)} %counts.5) | copy-start | bytes 772
  13.8 11.2 %collective-permute-start.7 = (bf16[1024,128]{1,0:T(8,128)(2,1)S(1)}, bf16[1024,128]{1,0:T(8,128)(2,1)S(1)}, u32[]{:S(2)}, u32[]{:S(2)}) collective-permute-start(bf16[1024,128]{1,0:T(8,128)(2,1)S(1)} %get-tuple-element.50), channel_id=1, source_target_pairs={{0,1},{1,0},{2,3},{3,2},{4,5},{5,4},{6,7},{7,6},{8,9},{9,8},{10,11... | collective-permute-start | bytes 786440 | tf_op jit(solution)/shard_map/ppermute | solution.py:276
  14.0 11.1 %collective-permute-start.6 = (bf16[1024,128]{1,0:T(8,128)(2,1)S(1)}, bf16[1024,128]{1,0:T(8,128)(2,1)S(1)}, u32[]{:S(2)}, u32[]{:S(2)}) collective-permute-start(bf16[1024,128]{1,0:T(8,128)(2,1)S(1)} %get-tuple-element.43), channel_id=1, source_target_pairs={{0,3},{1,2},{2,1},{3,0},{4,7},{5,6},{6,5},{7,4},{8,11},{9,10},{10,... | collective-permute-start | bytes 786440 | tf_op jit(solution)/shard_map/ppermute | solution.py:276
  20.2 16.7 %collective-permute-start.5 = (bf16[1152,128]{1,0:T(8,128)(2,1)S(1)}, bf16[1152,128]{1,0:T(8,128)(2,1)S(1)}, u32[]{:S(2)}, u32[]{:S(2)}) collective-permute-start(bf16[1152,128]{1,0:T(8,128)(2,1)S(1)} %get-tuple-element.48), channel_id=1, source_target_pairs={{0,1},{1,0},{2,3},{3,2},{4,5},{5,4},{6,7},{7,6},{8,9},{9,8},{10,11... | collective-permute-start | bytes 884744 | tf_op jit(solution)/shard_map/ppermute | solution.py:276
  20.4 16.4 %collective-permute-start.4 = (bf16[1152,128]{1,0:T(8,128)(2,1)S(1)}, bf16[1152,128]{1,0:T(8,128)(2,1)S(1)}, u32[]{:S(2)}, u32[]{:S(2)}) collective-permute-start(bf16[1152,128]{1,0:T(8,128)(2,1)S(1)} %get-tuple-element.47), channel_id=1, source_target_pairs={{0,3},{1,2},{2,1},{3,0},{4,7},{5,6},{6,5},{7,4},{8,11},{9,10},{10,... | collective-permute-start | bytes 884744 | tf_op jit(solution)/shard_map/ppermute | solution.py:276
  25.1 25.0 %collective-permute-start.11 = (bf16[2048,128]{1,0:T(8,128)(2,1)S(1)}, bf16[2048,128]{1,0:T(8,128)(2,1)S(1)}, u32[]{:S(2)}, u32[]{:S(2)}) collective-permute-start(bf16[2048,128]{1,0:T(8,128)(2,1)S(1)} %combine_1.1.mid), channel_id=1, source_target_pairs={{0,4},{4,8},{8,12},{12,16},{16,20},{20,24},{24,28},{28,32},{32,36}... | collective-permute-start | bytes 1572872 | tf_op jit(solution)/shard_map/ppermute | solution.py:280
  26.9 23.3 %collective-permute-start.10 = (bf16[2048,128]{1,0:T(8,128)(2,1)S(1)}, bf16[2048,128]{1,0:T(8,128)(2,1)S(1)}, u32[]{:S(2)}, u32[]{:S(2)}) collective-permute-start(bf16[2048,128]{1,0:T(8,128)(2,1)S(1)} %combine_1.1.mid), channel_id=1, source_target_pairs={{4,0},{8,4},{12,8},{16,12},{20,16},{24,20},{28,24},{32,28},{36,32}... | collective-permute-start | bytes 1572872 | tf_op jit(solution)/shard_map/ppermute | solution.py:279
  37.0 20.6 %collective-permute-start.9 = (bf16[2048,128]{1,0:T(8,128)(2,1)S(1)}, bf16[2048,128]{1,0:T(8,128)(2,1)S(1)}, u32[]{:S(2)}, u32[]{:S(2)}) collective-permute-start(bf16[2048,128]{1,0:T(8,128)(2,1)S(1)} %get-tuple-element.55.rest), channel_id=1, source_target_pairs={{0,4},{4,8},{8,12},{12,16},{16,20},{20,24},{24,28},{28,32},{32,36}... | collective-permute-start | bytes 1572872 | tf_op jit(solution)/shard_map/ppermute | solution.py:280
  38.9 18.7 %collective-permute-start.8 = (bf16[2048,128]{1,0:T(8,128)(2,1)S(1)}, bf16[2048,128]{1,0:T(8,128)(2,1)S(1)}, u32[]{:S(2)}, u32[]{:S(2)}) collective-permute-start(bf16[2048,128]{1,0:T(8,128)(2,1)S(1)} %get-tuple-element.55.rest), channel_id=1, source_target_pairs={{4,0},{8,4},{12,8},{16,12},{20,16},{24,20},{28,24},{32,28},{36,32}... | collective-permute-start | bytes 1572872 | tf_op jit(solution)/shard_map/ppermute | solution.py:279
  50.9 7.1 %collective-permute-start.13 = (bf16[256,128]{1,0:T(8,128)(2,1)S(1)}, bf16[256,128]{1,0:T(8,128)(2,1)S(1)}, u32[]{:S(2)}, u32[]{:S(2)}) collective-permute-start(bf16[256,128]{1,0:T(8,128)(2,1)S(1)} %finish_edge.1.edge), channel_id=1, source_target_pairs={{0,4},{4,8},{8,12},{12,16},{16,20},{20,24},{24,28},{28,32},{32,36}... | collective-permute-start | bytes 196616 | tf_op jit(solution)/shard_map/ppermute | solution.py:280
  51.0 7.0 %collective-permute-start.12 = (bf16[256,128]{1,0:T(8,128)(2,1)S(1)}, bf16[256,128]{1,0:T(8,128)(2,1)S(1)}, u32[]{:S(2)}, u32[]{:S(2)}) collective-permute-start(bf16[256,128]{1,0:T(8,128)(2,1)S(1)} %finish_edge.1.edge), channel_id=1, source_target_pairs={{4,0},{8,4},{12,8},{16,12},{20,16},{24,20},{28,24},{32,28},{36,32}... | collective-permute-start | bytes 196616 | tf_op jit(solution)/shard_map/ppermute | solution.py:279

commit v10 on v9

--- a/solution.py
+++ b/solution.py
@@ -268,9 +268,8 @@
     pairs_a = [(i, i ^ 1) for i in range(4)]
     pairs_b = [(i, 3 - i) for i in range(4)]
     open_right = [(i, i + 1) for i in range(owners - 1)]
-    open_left = [(i + 1, i) for i in range(owners - 1)]
     right = open_right + [(owners - 1, 0)]
-    left = open_left + [(0, owners - 1)]
+    left = [(target, source) for source, target in right]
 
     def along_trait(x, y, pairs_x, pairs_y):
         return lax.ppermute(x, "trait", pairs_x), lax.ppermute(y, "trait", pairs_y)
@@ -323,7 +322,7 @@
     mixed2, edge_sums = call(
         combine_2, in_vmem(shaped(2 * HALF2 - 2), shaped(2, F32)), [VM] * 3, (own2, far2a, far2b)
     )
-    rest_r, rest_l = along_rows(mixed2, open_right, open_left)
+    rest_r, rest_l = along_rows(mixed2, open_right, left)
     starts_here = starts - (g * TB - TB)
     below = jnp.sum(starts_here[None, :] < jnp.array(LIMITS, jnp.int32)[:, None], axis=1, dtype=jnp.int32)
     plan = (place, starts, counts, below)

time: 61.7 us -> 61.8 us (level)
  waiting for transfers between devices: 11.4 us -> 12.5 us
  starting transfers between devices: 32.8 us -> 31.8 us
    ppermute x3, waiting for transfers between devices: 0.01 us -> 1.52 us  [along_rows(): from_right = lax.ppermute(x, ROWS, to_left)]
    ppermute x3, starting transfers between devices: 22 us -> 21 us  [along_rows(): from_right = lax.ppermute(x, ROWS, to_left)]
  transfers between devices with their start and end apart: 14 -> 14, of which waited for: 5 -> 7; matrix products, arithmetic and copies ran while one was open for 0% -> 0% of each run, Pallas kernels for 17% -> 18%
where the time goes in v10:
time: 61.8 us; the launch traced here: 61.5 us
  starting transfers between devices  31.8 us (51%)
  Pallas kernels  16.9 us (27%)
  waiting for transfers between devices  12.5 us (20%)
    ppermute x3, starting transfers between devices, along_rows(): from_right = lax.ppermute(x, ROWS, to_left)  21 us
    pallas_call x10, Pallas kernels, call(): pl.pallas_call(kernel, name=kernel.__name__, out_shape=tuple((shape for s...  16.9 us
    ppermute x4, waiting for transfers between devices, along_trait(): lax.ppermute(x, 'trait', pairs_x)  5.78 us
    ppermute x4, waiting for transfers between devices, along_trait(): lax.ppermute(y, 'trait', pairs_y)  5.17 us
    ppermute x4, starting transfers between devices, along_trait(): lax.ppermute(y, 'trait', pairs_y)  3.9 us
    ppermute x3, starting transfers between devices, along_rows(): return (from_right, lax.ppermute(x, ROWS, to_right))  3.72 us
    ppermute x4, starting transfers between devices, along_trait(): lax.ppermute(x, 'trait', pairs_x)  3.2 us
    ppermute x3, waiting for transfers between devices, along_rows(): from_right = lax.ppermute(x, ROWS, to_left)  1.52 us
  transfers between devices with their start and end apart: 14, of which 7 were waited for; matrix products, arithmetic and copies ran while one was open for 0% of the time, Pallas kernels for 18%

profile of v10, /device:TPU:1, one launch (start us, length us, event | category | flops | bytes accessed | tf_op | source)
XLA Modules:
  0.0 61.5 jit_solution(10674732009790309266)
XLA Ops:
  0.0 2.8 %whiten_1.1 = (bf16[1024,128]{1,0:T(8,128)(2,1)S(1)}, bf16[1024,128]{1,0:T(8,128)(2,1)S(1)}, bf16[256,256]{1,0:T(8,128)(2,1)S(1)}, bf16[256,256]{1,0:T(8,128)(2,1)S(1)}) custom-call(s32[8]{0:T(128)S(1)} %compare_select_fusion.4.place, bf16[4096,128]{1,0:T(8,128)(2,1)} %z.2, bf16[32,128,384]{2,1,0:T(8,128)(2,1)} %band.3, bf16[512,512]{1,0:T(8,128)(2,1)} %mix.1), custom_call_target="tpu_custom_call" | custom-call | tf_op jit(solution)/shard_map/whiten_1/pallas_call | solution.py:244
  2.8 3.4 %collective-permute-start.3 = (bf16[1024,128]{1,0:T(8,128)(2,1)S(1)}, bf16[1024,128]{1,0:T(8,128)(2,1)S(1)}, u32[]{:S(2)}, u32[]{:S(2)}) collective-permute-start(bf16[1024,128]{1,0:T(8,128)(2,1)S(1)} %get-tuple-element.40.w_b), channel_id=1, source_target_pairs={{0,3},{1,2},{2,1},{3,0},{4,7},{5,6},{6,5},{7,4},{8,11},{9,10},{10,... | collective-permute-start | bytes 786440 | tf_op jit(solution)/shard_map/ppermute | solution.py:275
  6.2 0.0 collective-permute-start.2
  6.3 2.7 %whiten_2.1 = (bf16[1152,128]{1,0:T(8,128)(2,1)S(1)}, bf16[1152,128]{1,0:T(8,128)(2,1)S(1)}, bf16[256,128]{1,0:T(8,128)(2,1)S(1)}) custom-call(bf16[4096,128]{1,0:T(8,128)(2,1)} %z.2, bf16[32,128,384]{2,1,0:T(8,128)(2,1)} %band.3), custom_call_target="tpu_custom_call" | custom-call | tf_op jit(solution)/shard_map/whiten_2/pallas_call | solution.py:244
  8.9 1.5 %collective-permute-start = (bf16[1152,128]{1,0:T(8,128)(2,1)S(1)}, bf16[1152,128]{1,0:T(8,128)(2,1)S(1)}, u32[]{:S(2)}, u32[]{:S(2)}) collective-permute-start(bf16[1152,128]{1,0:T(8,128)(2,1)S(1)} %get-tuple-element.38.w_a), channel_id=1, source_target_pairs={{0,1},{1,0},{2,3},{3,2},{4,5},{5,4},{6,7},{7,6},{8,9},{9,8},{10,11... | collective-permute-start | bytes 884744 | tf_op jit(solution)/shard_map/ppermute | solution.py:275
  10.5 0.1 collective-permute-start.1
  10.6 0.6 %collective-permute-done.3.got_b = bf16[1024,128]{1,0:T(8,128)(2,1)S(1)} collective-permute-done((bf16[1024,128]{1,0:T(8,128)(2,1)S(1)}, bf16[1024,128]{1,0:T(8,128)(2,1)S(1)}, u32[]{:S(2)}, u32[]{:S(2)}) %collective-permute-start.3) | collective-permute-done | bytes 262176 | tf_op jit(solution)/shard_map/ppermute | solution.py:275
  11.2 1.9 %collective-permute-done.2.got_a = bf16[1024,128]{1,0:T(8,128)(2,1)S(1)} collective-permute-done((bf16[1024,128]{1,0:T(8,128)(2,1)S(1)}, bf16[1024,128]{1,0:T(8,128)(2,1)S(1)}, u32[]{:S(2)}, u32[]{:S(2)}) %collective-permute-start.2) | collective-permute-done | bytes 262176 | tf_op jit(solution)/shard_map/ppermute | solution.py:275
  13.1 0.0 copy-start
  13.1 0.0 copy-start.2
  13.1 0.0 copy-start.1
  13.1 0.7 %partial.2 = (bf16[1024,128]{1,0:T(8,128)(2,1)S(1)}, bf16[1024,128]{1,0:T(8,128)(2,1)S(1)}, f32[2048,128]{1,0:T(8,128)S(1)}) custom-call(bf16[1024,128]{1,0:T(8,128)(2,1)S(1)} %get-tuple-element.36.w_a, bf16[1024,128]{1,0:T(8,128)(2,1)S(1)} %collective-permute-done.2.got_a, bf16[1024,128]{1,0:T(8,128)(2,1)S(1)} %get-tuple-element.40.w_b, ...), custom_call_target="tpu_custom_call" | custom-call | tf_op jit(solution)/shard_map/partial/pallas_call | solution.py:244
  13.8 0.2 collective-permute-start.7
  14.0 1.6 %collective-permute-start.6 = (bf16[1024,128]{1,0:T(8,128)(2,1)S(1)}, bf16[1024,128]{1,0:T(8,128)(2,1)S(1)}, u32[]{:S(2)}, u32[]{:S(2)}) collective-permute-start(bf16[1024,128]{1,0:T(8,128)(2,1)S(1)} %get-tuple-element.43), channel_id=1, source_target_pairs={{0,3},{1,2},{2,1},{3,0},{4,7},{5,6},{6,5},{7,4},{8,11},{9,10},{10,... | collective-permute-start | bytes 786440 | tf_op jit(solution)/shard_map/ppermute | solution.py:275
  15.5 3.9 %collective-permute-done.got_a = bf16[1152,128]{1,0:T(8,128)(2,1)S(1)} collective-permute-done((bf16[1152,128]{1,0:T(8,128)(2,1)S(1)}, bf16[1152,128]{1,0:T(8,128)(2,1)S(1)}, u32[]{:S(2)}, u32[]{:S(2)}) %collective-permute-start) | collective-permute-done | bytes 294944 | tf_op jit(solution)/shard_map/ppermute | solution.py:275
  19.4 0.0 collective-permute-done.1.got_b
  19.4 0.8 %partial.3 = (bf16[1152,128]{1,0:T(8,128)(2,1)S(1)}, bf16[1152,128]{1,0:T(8,128)(2,1)S(1)}, f32[2304,128]{1,0:T(8,128)S(1)}) custom-call(bf16[1152,128]{1,0:T(8,128)(2,1)S(1)} %get-tuple-element.38.w_a, bf16[1152,128]{1,0:T(8,128)(2,1)S(1)} %collective-permute-done.got_a, bf16[1152,128]{1,0:T(8,128)(2,1)S(1)} %get-tuple-element.39.w_b, ...), custom_call_target="tpu_custom_call" | custom-call | tf_op jit(solution)/shard_map/partial/pallas_call | solution.py:244
  20.2 0.2 collective-permute-start.5
  20.4 0.1 collective-permute-start.4
  20.5 4.5 %collective-permute-done.7.far_b = bf16[1024,128]{1,0:T(8,128)(2,1)S(1)} collective-permute-done((bf16[1024,128]{1,0:T(8,128)(2,1)S(1)}, bf16[1024,128]{1,0:T(8,128)(2,1)S(1)}, u32[]{:S(2)}, u32[]{:S(2)}) %collective-permute-start.7) | collective-permute-done | bytes 262176 | tf_op jit(solution)/shard_map/ppermute | solution.py:275
  25.0 0.0 collective-permute-done.6.far_a
  25.0 0.1 combine_1.1.mid
  25.1 1.7 %collective-permute-start.11 = (bf16[2048,128]{1,0:T(8,128)(2,1)S(1)}, bf16[2048,128]{1,0:T(8,128)(2,1)S(1)}, u32[]{:S(2)}, u32[]{:S(2)}) collective-permute-start(bf16[2048,128]{1,0:T(8,128)(2,1)S(1)} %combine_1.1.mid), channel_id=1, source_target_pairs={{0,4},{4,8},{8,12},{12,16},{16,20},{20,24},{24,28},{28,32},{32,36}... | collective-permute-start | bytes 1572872 | tf_op jit(solution)/shard_map/ppermute | solution.py:279
  26.9 10.0 %collective-permute-start.10 = (bf16[2048,128]{1,0:T(8,128)(2,1)S(1)}, bf16[2048,128]{1,0:T(8,128)(2,1)S(1)}, u32[]{:S(2)}, u32[]{:S(2)}) collective-permute-start(bf16[2048,128]{1,0:T(8,128)(2,1)S(1)} %combine_1.1.mid), channel_id=1, source_target_pairs={{4,0},{8,4},{12,8},{16,12},{20,16},{24,20},{28,24},{32,28},{36,32}... | collective-permute-start | bytes 1572872 | tf_op jit(solution)/shard_map/ppermute | solution.py:278
  36.8 0.0 collective-permute-done.5.far_b
  36.9 0.0 collective-permute-done.4.far_a
  36.9 0.1 combine_2.1
  37.0 1.9 %collective-permute-start.9 = (bf16[2048,128]{1,0:T(8,128)(2,1)S(1)}, bf16[2048,128]{1,0:T(8,128)(2,1)S(1)}, u32[]{:S(2)}, u32[]{:S(2)}) collective-permute-start(bf16[2048,128]{1,0:T(8,128)(2,1)S(1)} %get-tuple-element.55.rest), channel_id=1, source_target_pairs={{0,4},{4,8},{8,12},{12,16},{16,20},{20,24},{24,28},{28,32},{32,36}... | collective-permute-start | bytes 1572872 | tf_op jit(solution)/shard_map/ppermute | solution.py:279
  38.9 5.1 %collective-permute-start.8 = (bf16[2048,128]{1,0:T(8,128)(2,1)S(1)}, bf16[2048,128]{1,0:T(8,128)(2,1)S(1)}, u32[]{:S(2)}, u32[]{:S(2)}) collective-permute-start(bf16[2048,128]{1,0:T(8,128)(2,1)S(1)} %get-tuple-element.55.rest), channel_id=1, source_target_pairs={{4,0},{8,4},{12,8},{16,12},{20,16},{24,20},{28,24},{32,28},{36,32}... | collective-permute-start | bytes 1572872 | tf_op jit(solution)/shard_map/ppermute | solution.py:278
  44.0 0.0 copy-done
  44.0 0.0 copy-done.2
  44.0 0.2 convert_reduce_fusion.below
  44.2 0.0 copy-done.1
  44.2 4.1 %impute_own.1 = (bf16[12416,128]{1,0:T(8,128)(2,1)S(1)}, bf16[8192,128]{1,0:T(8,128)(2,1)S(1)}, bf16[64,128,512]{2,1,0:T(8,128)(2,1)S(1)}) custom-call(s32[8]{0:T(128)S(1)} %compare_select_fusion.4.place, s32[64]{0:T(128)S(1)} %copy-done, s32[64]{0:T(128)S(1)} %copy-done.1, s32[8]{0:T(128)S(1)} %convert_reduce_fusion.below, ...), custom_call_target="tpu_custom_call" | custom-call | tf_op jit(solution)/shard_map/impute_own/pallas_call | solution.py:244
  48.3 0.0 collective-permute-done.11.got_l.mid_l
  48.3 0.4 collective-permute-done.10.got_r.mid_r
  48.7 0.7 %finish_edge.1.edge = bf16[256,128]{1,0:T(8,128)(2,1)S(1)} custom-call(s32[8]{0:T(128)S(1)} %compare_select_fusion.4.place, f32[256,128]{1,0:T(8,128)S(1)} %get-tuple-element.56.edge, bf16[256,128]{1,0:T(8,128)(2,1)S(1)} %get-tuple-element.57.edge_band, bf16[2048,128]{1,0:T(8,128)(2,1)S(1)} %collective-permute-done.10.got_r.mid_r, ...), custom_call_target="tpu_custom_call" | custom-call | tf_op jit(solution)/shard_map/finish_edge/pallas_call | solution.py:244
  49.4 0.1 collective-permute-start.13
  49.5 5.9 %collective-permute-start.12 = (bf16[256,128]{1,0:T(8,128)(2,1)S(1)}, bf16[256,128]{1,0:T(8,128)(2,1)S(1)}, u32[]{:S(2)}, u32[]{:S(2)}) collective-permute-start(bf16[256,128]{1,0:T(8,128)(2,1)S(1)} %finish_edge.1.edge), channel_id=1, source_target_pairs={{4,0},{8,4},{12,8},{16,12},{20,16},{24,20},{28,24},{32,28},{36,32}... | collective-permute-start | bytes 196616 | tf_op jit(solution)/shard_map/ppermute | solution.py:278
  55.3 2.0 %impute_near.1 = (bf16[12416,128]{1,0:T(8,128)(2,1)S(1)}, bf16[8192,128]{1,0:T(8,128)(2,1)S(1)}) custom-call(s32[8]{0:T(128)S(1)} %compare_select_fusion.4.place, s32[64]{0:T(128)S(1)} %copy-done, s32[64]{0:T(128)S(1)} %copy-done.1, s32[8]{0:T(128)S(1)} %convert_reduce_fusion.below, ...), custom_call_target="tpu_custom_call", output_to_operand_aliasing={{0}: (8, {}), {1}: (9, {})} | custom-call | tf_op jit(solution)/shard_map/impute_near/pallas_call | solution.py:244
  57.3 0.0 collective-permute-done.9.rest_l
  57.3 0.5 collective-permute-done.8.rest_r
  57.8 0.0 collective-permute-done.13.edge_l
  57.8 0.7 %collective-permute-done.12.edge_r = bf16[256,128]{1,0:T(8,128)(2,1)S(1)} collective-permute-done((bf16[256,128]{1,0:T(8,128)(2,1)S(1)}, bf16[256,128]{1,0:T(8,128)(2,1)S(1)}, u32[]{:S(2)}, u32[]{:S(2)}) %collective-permute-start.12) | collective-permute-done | bytes 65568 | tf_op jit(solution)/shard_map/ppermute | solution.py:278
  58.5 3.0 %impute_far.1 = (bf16[12416,128]{1,0:T(8,128)(2,1)S(1)}, bf16[8192,128]{1,0:T(8,128)(2,1)S(1)}, bf16[8192,128]{1,0:T(8,128)(2,1)}) custom-call(s32[8]{0:T(128)S(1)} %compare_select_fusion.4.place, s32[64]{0:T(128)S(1)} %copy-done, s32[64]{0:T(128)S(1)} %copy-done.1, s32[8]{0:T(128)S(1)} %convert_reduce_fusion.below, ...), custom_call_target="tpu_custom_call", output_to_operand_aliasing={{0}: (9, {}), {1}: (10, {})} | custom-call | tf_op jit(solution)/shard_map/impute_far/pallas_call | solution.py:244
  (2 shorter events, 0.0 us)
Async XLA Ops:
  2.8 8.4 %collective-permute-start.3 = (bf16[1024,128]{1,0:T(8,128)(2,1)S(1)}, bf16[1024,128]{1,0:T(8,128)(2,1)S(1)}, u32[]{:S(2)}, u32[]{:S(2)}) collective-permute-start(bf16[1024,128]{1,0:T(8,128)(2,1)S(1)} %get-tuple-element.40.w_b), channel_id=1, source_target_pairs={{0,3},{1,2},{2,1},{3,0},{4,7},{5,6},{6,5},{7,4},{8,11},{9,10},{10,... | collective-permute-start | bytes 786440 | tf_op jit(solution)/shard_map/ppermute | solution.py:275
  6.2 6.9 %collective-permute-start.2 = (bf16[1024,128]{1,0:T(8,128)(2,1)S(1)}, bf16[1024,128]{1,0:T(8,128)(2,1)S(1)}, u32[]{:S(2)}, u32[]{:S(2)}) collective-permute-start(bf16[1024,128]{1,0:T(8,128)(2,1)S(1)} %get-tuple-element.36.w_a), channel_id=1, source_target_pairs={{0,1},{1,0},{2,3},{3,2},{4,5},{5,4},{6,7},{7,6},{8,9},{9,8},{10,11... | collective-permute-start | bytes 786440 | tf_op jit(solution)/shard_map/ppermute | solution.py:275
  8.9 10.5 %collective-permute-start = (bf16[1152,128]{1,0:T(8,128)(2,1)S(1)}, bf16[1152,128]{1,0:T(8,128)(2,1)S(1)}, u32[]{:S(2)}, u32[]{:S(2)}) collective-permute-start(bf16[1152,128]{1,0:T(8,128)(2,1)S(1)} %get-tuple-element.38.w_a), channel_id=1, source_target_pairs={{0,1},{1,0},{2,3},{3,2},{4,5},{5,4},{6,7},{7,6},{8,9},{9,8},{10,11... | collective-permute-start | bytes 884744 | tf_op jit(solution)/shard_map/ppermute | solution.py:275
  10.5 8.9 %collective-permute-start.1 = (bf16[1152,128]{1,0:T(8,128)(2,1)S(1)}, bf16[1152,128]{1,0:T(8,128)(2,1)S(1)}, u32[]{:S(2)}, u32[]{:S(2)}) collective-permute-start(bf16[1152,128]{1,0:T(8,128)(2,1)S(1)} %get-tuple-element.39.w_b), channel_id=1, source_target_pairs={{0,3},{1,2},{2,1},{3,0},{4,7},{5,6},{6,5},{7,4},{8,11},{9,10},{10,... | collective-permute-start | bytes 884744 | tf_op jit(solution)/shard_map/ppermute | solution.py:275
  13.1 30.9 %copy-start = (s32[64]{0:T(128)S(1)}, s32[64]{0:T(128)}, u32[]{:S(2)}) copy-start(s32[64]{0:T(128)} %starts.5) | copy-start | bytes 772
  13.1 30.9 %copy-start.2 = (s32[8]{0:T(128)S(1)}, s32[8]{0:T(128)}, u32[]{:S(2)}) copy-start(s32[8]{0:T(128)} %constant.36.clone) | copy-start | bytes 100
  13.1 31.1 %copy-start.1 = (s32[64]{0:T(128)S(1)}, s32[64]{0:T(128)}, u32[]{:S(2)}) copy-start(s32[64]{0:T(128)} %counts.5) | copy-start | bytes 772
  13.8 11.2 %collective-permute-start.7 = (bf16[1024,128]{1,0:T(8,128)(2,1)S(1)}, bf16[1024,128]{1,0:T(8,128)(2,1)S(1)}, u32[]{:S(2)}, u32[]{:S(2)}) collective-permute-start(bf16[1024,128]{1,0:T(8,128)(2,1)S(1)} %get-tuple-element.50), channel_id=1, source_target_pairs={{0,1},{1,0},{2,3},{3,2},{4,5},{5,4},{6,7},{7,6},{8,9},{9,8},{10,11... | collective-permute-start | bytes 786440 | tf_op jit(solution)/shard_map/ppermute | solution.py:275
  14.0 11.1 %collective-permute-start.6 = (bf16[1024,128]{1,0:T(8,128)(2,1)S(1)}, bf16[1024,128]{1,0:T(8,128)(2,1)S(1)}, u32[]{:S(2)}, u32[]{:S(2)}) collective-permute-start(bf16[1024,128]{1,0:T(8,128)(2,1)S(1)} %get-tuple-element.43), channel_id=1, source_target_pairs={{0,3},{1,2},{2,1},{3,0},{4,7},{5,6},{6,5},{7,4},{8,11},{9,10},{10,... | collective-permute-start | bytes 786440 | tf_op jit(solution)/shard_map/ppermute | solution.py:275
  20.2 16.7 %collective-permute-start.5 = (bf16[1152,128]{1,0:T(8,128)(2,1)S(1)}, bf16[1152,128]{1,0:T(8,128)(2,1)S(1)}, u32[]{:S(2)}, u32[]{:S(2)}) collective-permute-start(bf16[1152,128]{1,0:T(8,128)(2,1)S(1)} %get-tuple-element.48), channel_id=1, source_target_pairs={{0,1},{1,0},{2,3},{3,2},{4,5},{5,4},{6,7},{7,6},{8,9},{9,8},{10,11... | collective-permute-start | bytes 884744 | tf_op jit(solution)/shard_map/ppermute | solution.py:275
  20.4 16.4 %collective-permute-start.4 = (bf16[1152,128]{1,0:T(8,128)(2,1)S(1)}, bf16[1152,128]{1,0:T(8,128)(2,1)S(1)}, u32[]{:S(2)}, u32[]{:S(2)}) collective-permute-start(bf16[1152,128]{1,0:T(8,128)(2,1)S(1)} %get-tuple-element.47), channel_id=1, source_target_pairs={{0,3},{1,2},{2,1},{3,0},{4,7},{5,6},{6,5},{7,4},{8,11},{9,10},{10,... | collective-permute-start | bytes 884744 | tf_op jit(solution)/shard_map/ppermute | solution.py:275
  25.1 23.2 %collective-permute-start.11 = (bf16[2048,128]{1,0:T(8,128)(2,1)S(1)}, bf16[2048,128]{1,0:T(8,128)(2,1)S(1)}, u32[]{:S(2)}, u32[]{:S(2)}) collective-permute-start(bf16[2048,128]{1,0:T(8,128)(2,1)S(1)} %combine_1.1.mid), channel_id=1, source_target_pairs={{0,4},{4,8},{8,12},{12,16},{16,20},{20,24},{24,28},{28,32},{32,36}... | collective-permute-start | bytes 1572872 | tf_op jit(solution)/shard_map/ppermute | solution.py:279
  26.9 21.8 %collective-permute-start.10 = (bf16[2048,128]{1,0:T(8,128)(2,1)S(1)}, bf16[2048,128]{1,0:T(8,128)(2,1)S(1)}, u32[]{:S(2)}, u32[]{:S(2)}) collective-permute-start(bf16[2048,128]{1,0:T(8,128)(2,1)S(1)} %combine_1.1.mid), channel_id=1, source_target_pairs={{4,0},{8,4},{12,8},{16,12},{20,16},{24,20},{28,24},{32,28},{36,32}... | collective-permute-start | bytes 1572872 | tf_op jit(solution)/shard_map/ppermute | solution.py:278
  37.0 20.3 %collective-permute-start.9 = (bf16[2048,128]{1,0:T(8,128)(2,1)S(1)}, bf16[2048,128]{1,0:T(8,128)(2,1)S(1)}, u32[]{:S(2)}, u32[]{:S(2)}) collective-permute-start(bf16[2048,128]{1,0:T(8,128)(2,1)S(1)} %get-tuple-element.55.rest), channel_id=1, source_target_pairs={{0,4},{4,8},{8,12},{12,16},{16,20},{20,24},{24,28},{28,32},{32,36}... | collective-permute-start | bytes 1572872 | tf_op jit(solution)/shard_map/ppermute | solution.py:279
  38.9 18.9 %collective-permute-start.8 = (bf16[2048,128]{1,0:T(8,128)(2,1)S(1)}, bf16[2048,128]{1,0:T(8,128)(2,1)S(1)}, u32[]{:S(2)}, u32[]{:S(2)}) collective-permute-start(bf16[2048,128]{1,0:T(8,128)(2,1)S(1)} %get-tuple-element.55.rest), channel_id=1, source_target_pairs={{4,0},{8,4},{12,8},{16,12},{20,16},{24,20},{28,24},{32,28},{36,32}... | collective-permute-start | bytes 1572872 | tf_op jit(solution)/shard_map/ppermute | solution.py:278
  49.4 8.4 %collective-permute-start.13 = (bf16[256,128]{1,0:T(8,128)(2,1)S(1)}, bf16[256,128]{1,0:T(8,128)(2,1)S(1)}, u32[]{:S(2)}, u32[]{:S(2)}) collective-permute-start(bf16[256,128]{1,0:T(8,128)(2,1)S(1)} %finish_edge.1.edge), channel_id=1, source_target_pairs={{0,4},{4,8},{8,12},{12,16},{16,20},{20,24},{24,28},{28,32},{32,36}... | collective-permute-start | bytes 196616 | tf_op jit(solution)/shard_map/ppermute | solution.py:279
  49.5 9.0 %collective-permute-start.12 = (bf16[256,128]{1,0:T(8,128)(2,1)S(1)}, bf16[256,128]{1,0:T(8,128)(2,1)S(1)}, u32[]{:S(2)}, u32[]{:S(2)}) collective-permute-start(bf16[256,128]{1,0:T(8,128)(2,1)S(1)} %finish_edge.1.edge), channel_id=1, source_target_pairs={{4,0},{8,4},{12,8},{16,12},{20,16},{24,20},{28,24},{32,28},{36,32}... | collective-permute-start | bytes 196616 | tf_op jit(solution)/shard_map/ppermute | solution.py:278

commit v11 on v10

--- a/solution.py
+++ b/solution.py
@@ -270,6 +270,7 @@
     open_right = [(i, i + 1) for i in range(owners - 1)]
     right = open_right + [(owners - 1, 0)]
     left = [(target, source) for source, target in right]
+    open_left = left[:-1]
 
     def along_trait(x, y, pairs_x, pairs_y):
         return lax.ppermute(x, "trait", pairs_x), lax.ppermute(y, "trait", pairs_y)
@@ -317,7 +318,7 @@
     (own2, far2a, far2b), after = mixing(w2a, got2a, w2b, got2b)
     far1a, far1b, _ = lax.optimization_barrier((far1a, far1b, after))
     (mixed1,) = call(combine_1, in_vmem(shaped(2 * HALF1 + 2)), [VM] * 3, (own1, far1a, far1b))
-    mid_r, mid_l = along_rows(mixed1, right, left)
+    mid_r, mid_l = along_rows(mixed1, right, open_left)
     far2a, far2b, _ = lax.optimization_barrier((far2a, far2b, mixed1))
     mixed2, edge_sums = call(
         combine_2, in_vmem(shaped(2 * HALF2 - 2), shaped(2, F32)), [VM] * 3, (own2, far2a, far2b)

time: 61.8 us -> 61.5 us (level)
  waiting for transfers between devices: 12.5 us -> 11 us
  starting transfers between devices: 31.8 us -> 32.8 us
    ppermute x3, waiting for transfers between devices: 1.52 us -> 0.01 us  [along_rows(): from_right = lax.ppermute(x, ROWS, to_left)]
    ppermute x3, starting transfers between devices: 21 us -> 22 us  [along_rows(): from_right = lax.ppermute(x, ROWS, to_left)]
  transfers between devices with their start and end apart: 14 -> 14, of which waited for: 7 -> 4; matrix products, arithmetic and copies ran while one was open for 0% -> 0% of each run, Pallas kernels for 18% -> 18%
where the time goes in v11:
time: 61.5 us; the launch traced here: 61.3 us
  starting transfers between devices  32.8 us (53%)
  Pallas kernels  17.2 us (28%)
  waiting for transfers between devices  11 us (18%)
    ppermute x3, starting transfers between devices, along_rows(): from_right = lax.ppermute(x, ROWS, to_left)  22 us
    pallas_call x10, Pallas kernels, call(): pl.pallas_call(kernel, name=kernel.__name__, out_shape=tuple((shape for s...  17.2 us
    ppermute x4, waiting for transfers between devices, along_trait(): lax.ppermute(x, 'trait', pairs_x)  5.78 us
    ppermute x4, waiting for transfers between devices, along_trait(): lax.ppermute(y, 'trait', pairs_y)  5.17 us
    ppermute x4, starting transfers between devices, along_trait(): lax.ppermute(y, 'trait', pairs_y)  3.9 us
    ppermute x3, starting transfers between devices, along_rows(): return (from_right, lax.ppermute(x, ROWS, to_right))  3.72 us
    ppermute x4, starting transfers between devices, along_trait(): lax.ppermute(x, 'trait', pairs_x)  3.2 us
  transfers between devices with their start and end apart: 14, of which 4 were waited for; matrix products, arithmetic and copies ran while one was open for 0% of the time, Pallas kernels for 18%

profile of v11, /device:TPU:1, one launch (start us, length us, event | category | flops | bytes accessed | tf_op | source)
XLA Modules:
  0.0 61.3 jit_solution(307408121126284287)
XLA Ops:
  0.0 2.8 %whiten_1.1 = (bf16[1024,128]{1,0:T(8,128)(2,1)S(1)}, bf16[1024,128]{1,0:T(8,128)(2,1)S(1)}, bf16[256,256]{1,0:T(8,128)(2,1)S(1)}, bf16[256,256]{1,0:T(8,128)(2,1)S(1)}) custom-call(s32[8]{0:T(128)S(1)} %compare_select_fusion.4.place, bf16[4096,128]{1,0:T(8,128)(2,1)} %z.2, bf16[32,128,384]{2,1,0:T(8,128)(2,1)} %band.3, bf16[512,512]{1,0:T(8,128)(2,1)} %mix.1), custom_call_target="tpu_custom_call" | custom-call | tf_op jit(solution)/shard_map/whiten_1/pallas_call | solution.py:244
  2.8 3.4 %collective-permute-start.3 = (bf16[1024,128]{1,0:T(8,128)(2,1)S(1)}, bf16[1024,128]{1,0:T(8,128)(2,1)S(1)}, u32[]{:S(2)}, u32[]{:S(2)}) collective-permute-start(bf16[1024,128]{1,0:T(8,128)(2,1)S(1)} %get-tuple-element.40.w_b), channel_id=1, source_target_pairs={{0,3},{1,2},{2,1},{3,0},{4,7},{5,6},{6,5},{7,4},{8,11},{9,10},{10,... | collective-permute-start | bytes 786440 | tf_op jit(solution)/shard_map/ppermute | solution.py:276
  6.2 0.0 collective-permute-start.2
  6.3 2.7 %whiten_2.1 = (bf16[1152,128]{1,0:T(8,128)(2,1)S(1)}, bf16[1152,128]{1,0:T(8,128)(2,1)S(1)}, bf16[256,128]{1,0:T(8,128)(2,1)S(1)}) custom-call(bf16[4096,128]{1,0:T(8,128)(2,1)} %z.2, bf16[32,128,384]{2,1,0:T(8,128)(2,1)} %band.3), custom_call_target="tpu_custom_call" | custom-call | tf_op jit(solution)/shard_map/whiten_2/pallas_call | solution.py:244
  8.9 1.5 %collective-permute-start = (bf16[1152,128]{1,0:T(8,128)(2,1)S(1)}, bf16[1152,128]{1,0:T(8,128)(2,1)S(1)}, u32[]{:S(2)}, u32[]{:S(2)}) collective-permute-start(bf16[1152,128]{1,0:T(8,128)(2,1)S(1)} %get-tuple-element.38.w_a), channel_id=1, source_target_pairs={{0,1},{1,0},{2,3},{3,2},{4,5},{5,4},{6,7},{7,6},{8,9},{9,8},{10,11... | collective-permute-start | bytes 884744 | tf_op jit(solution)/shard_map/ppermute | solution.py:276
  10.5 0.1 collective-permute-start.1
  10.6 0.6 %collective-permute-done.3.got_b = bf16[1024,128]{1,0:T(8,128)(2,1)S(1)} collective-permute-done((bf16[1024,128]{1,0:T(8,128)(2,1)S(1)}, bf16[1024,128]{1,0:T(8,128)(2,1)S(1)}, u32[]{:S(2)}, u32[]{:S(2)}) %collective-permute-start.3) | collective-permute-done | bytes 262176 | tf_op jit(solution)/shard_map/ppermute | solution.py:276
  11.2 1.9 %collective-permute-done.2.got_a = bf16[1024,128]{1,0:T(8,128)(2,1)S(1)} collective-permute-done((bf16[1024,128]{1,0:T(8,128)(2,1)S(1)}, bf16[1024,128]{1,0:T(8,128)(2,1)S(1)}, u32[]{:S(2)}, u32[]{:S(2)}) %collective-permute-start.2) | collective-permute-done | bytes 262176 | tf_op jit(solution)/shard_map/ppermute | solution.py:276
  13.1 0.0 copy-start
  13.1 0.0 copy-start.2
  13.1 0.0 copy-start.1
  13.1 0.7 %partial.2 = (bf16[1024,128]{1,0:T(8,128)(2,1)S(1)}, bf16[1024,128]{1,0:T(8,128)(2,1)S(1)}, f32[2048,128]{1,0:T(8,128)S(1)}) custom-call(bf16[1024,128]{1,0:T(8,128)(2,1)S(1)} %get-tuple-element.36.w_a, bf16[1024,128]{1,0:T(8,128)(2,1)S(1)} %collective-permute-done.2.got_a, bf16[1024,128]{1,0:T(8,128)(2,1)S(1)} %get-tuple-element.40.w_b, ...), custom_call_target="tpu_custom_call" | custom-call | tf_op jit(solution)/shard_map/partial/pallas_call | solution.py:244
  13.8 0.2 collective-permute-start.7
  14.0 1.6 %collective-permute-start.6 = (bf16[1024,128]{1,0:T(8,128)(2,1)S(1)}, bf16[1024,128]{1,0:T(8,128)(2,1)S(1)}, u32[]{:S(2)}, u32[]{:S(2)}) collective-permute-start(bf16[1024,128]{1,0:T(8,128)(2,1)S(1)} %get-tuple-element.43), channel_id=1, source_target_pairs={{0,3},{1,2},{2,1},{3,0},{4,7},{5,6},{6,5},{7,4},{8,11},{9,10},{10,... | collective-permute-start | bytes 786440 | tf_op jit(solution)/shard_map/ppermute | solution.py:276
  15.5 3.9 %collective-permute-done.got_a = bf16[1152,128]{1,0:T(8,128)(2,1)S(1)} collective-permute-done((bf16[1152,128]{1,0:T(8,128)(2,1)S(1)}, bf16[1152,128]{1,0:T(8,128)(2,1)S(1)}, u32[]{:S(2)}, u32[]{:S(2)}) %collective-permute-start) | collective-permute-done | bytes 294944 | tf_op jit(solution)/shard_map/ppermute | solution.py:276
  19.4 0.0 collective-permute-done.1.got_b
  19.4 0.8 %partial.3 = (bf16[1152,128]{1,0:T(8,128)(2,1)S(1)}, bf16[1152,128]{1,0:T(8,128)(2,1)S(1)}, f32[2304,128]{1,0:T(8,128)S(1)}) custom-call(bf16[1152,128]{1,0:T(8,128)(2,1)S(1)} %get-tuple-element.38.w_a, bf16[1152,128]{1,0:T(8,128)(2,1)S(1)} %collective-permute-done.got_a, bf16[1152,128]{1,0:T(8,128)(2,1)S(1)} %get-tuple-element.39.w_b, ...), custom_call_target="tpu_custom_call" | custom-call | tf_op jit(solution)/shard_map/partial/pallas_call | solution.py:244
  20.2 0.2 collective-permute-start.5
  20.4 0.1 collective-permute-start.4
  20.5 4.5 %collective-permute-done.7.far_b = bf16[1024,128]{1,0:T(8,128)(2,1)S(1)} collective-permute-done((bf16[1024,128]{1,0:T(8,128)(2,1)S(1)}, bf16[1024,128]{1,0:T(8,128)(2,1)S(1)}, u32[]{:S(2)}, u32[]{:S(2)}) %collective-permute-start.7) | collective-permute-done | bytes 262176 | tf_op jit(solution)/shard_map/ppermute | solution.py:276
  25.0 0.0 collective-permute-done.6.far_a
  25.0 0.1 combine_1.1.mid
  25.1 1.7 %collective-permute-start.11 = (bf16[2048,128]{1,0:T(8,128)(2,1)S(1)}, bf16[2048,128]{1,0:T(8,128)(2,1)S(1)}, u32[]{:S(2)}, u32[]{:S(2)}) collective-permute-start(bf16[2048,128]{1,0:T(8,128)(2,1)S(1)} %combine_1.1.mid), channel_id=1, source_target_pairs={{0,4},{4,8},{8,12},{12,16},{16,20},{20,24},{24,28},{28,32},{32,36}... | collective-permute-start | bytes 1572872 | tf_op jit(solution)/shard_map/ppermute | solution.py:280
  26.9 11.8 %collective-permute-start.10 = (bf16[2048,128]{1,0:T(8,128)(2,1)S(1)}, bf16[2048,128]{1,0:T(8,128)(2,1)S(1)}, u32[]{:S(2)}, u32[]{:S(2)}) collective-permute-start(bf16[2048,128]{1,0:T(8,128)(2,1)S(1)} %combine_1.1.mid), channel_id=1, source_target_pairs={{4,0},{8,4},{12,8},{16,12},{20,16},{24,20},{28,24},{32,28},{36,32}... | collective-permute-start | bytes 1572872 | tf_op jit(solution)/shard_map/ppermute | solution.py:279
  38.7 0.0 collective-permute-done.5.far_b
  38.7 0.0 collective-permute-done.4.far_a
  38.7 0.1 combine_2.1
  38.8 1.9 %collective-permute-start.9 = (bf16[2048,128]{1,0:T(8,128)(2,1)S(1)}, bf16[2048,128]{1,0:T(8,128)(2,1)S(1)}, u32[]{:S(2)}, u32[]{:S(2)}) collective-permute-start(bf16[2048,128]{1,0:T(8,128)(2,1)S(1)} %get-tuple-element.55.rest), channel_id=1, source_target_pairs={{0,4},{4,8},{8,12},{12,16},{16,20},{20,24},{24,28},{28,32},{32,36}... | collective-permute-start | bytes 1572872 | tf_op jit(solution)/shard_map/ppermute | solution.py:280
  40.7 5.1 %collective-permute-start.8 = (bf16[2048,128]{1,0:T(8,128)(2,1)S(1)}, bf16[2048,128]{1,0:T(8,128)(2,1)S(1)}, u32[]{:S(2)}, u32[]{:S(2)}) collective-permute-start(bf16[2048,128]{1,0:T(8,128)(2,1)S(1)} %get-tuple-element.55.rest), channel_id=1, source_target_pairs={{4,0},{8,4},{12,8},{16,12},{20,16},{24,20},{28,24},{32,28},{36,32}... | collective-permute-start | bytes 1572872 | tf_op jit(solution)/shard_map/ppermute | solution.py:279
  45.9 0.0 copy-done
  45.9 0.0 copy-done.2
  45.9 0.2 convert_reduce_fusion.below
  46.1 0.0 copy-done.1
  46.1 4.1 %impute_own.1 = (bf16[12416,128]{1,0:T(8,128)(2,1)S(1)}, bf16[8192,128]{1,0:T(8,128)(2,1)S(1)}, bf16[64,128,512]{2,1,0:T(8,128)(2,1)S(1)}) custom-call(s32[8]{0:T(128)S(1)} %compare_select_fusion.4.place, s32[64]{0:T(128)S(1)} %copy-done, s32[64]{0:T(128)S(1)} %copy-done.1, s32[8]{0:T(128)S(1)} %convert_reduce_fusion.below, ...), custom_call_target="tpu_custom_call" | custom-call | tf_op jit(solution)/shard_map/impute_own/pallas_call | solution.py:244
  50.1 0.0 collective-permute-done.11.got_l.mid_l
  50.2 0.0 collective-permute-done.10.got_r.mid_r
  50.2 0.7 %finish_edge.1.edge = bf16[256,128]{1,0:T(8,128)(2,1)S(1)} custom-call(s32[8]{0:T(128)S(1)} %compare_select_fusion.4.place, f32[256,128]{1,0:T(8,128)S(1)} %get-tuple-element.56.edge, bf16[256,128]{1,0:T(8,128)(2,1)S(1)} %get-tuple-element.57.edge_band, bf16[2048,128]{1,0:T(8,128)(2,1)S(1)} %collective-permute-done.10.got_r.mid_r, ...), custom_call_target="tpu_custom_call" | custom-call | tf_op jit(solution)/shard_map/finish_edge/pallas_call | solution.py:244
  50.9 0.1 collective-permute-start.13
  51.0 5.1 %collective-permute-start.12 = (bf16[256,128]{1,0:T(8,128)(2,1)S(1)}, bf16[256,128]{1,0:T(8,128)(2,1)S(1)}, u32[]{:S(2)}, u32[]{:S(2)}) collective-permute-start(bf16[256,128]{1,0:T(8,128)(2,1)S(1)} %finish_edge.1.edge), channel_id=1, source_target_pairs={{4,0},{8,4},{12,8},{16,12},{20,16},{24,20},{28,24},{32,28},{36,32}... | collective-permute-start | bytes 196616 | tf_op jit(solution)/shard_map/ppermute | solution.py:279
  56.0 2.0 %impute_near.1 = (bf16[12416,128]{1,0:T(8,128)(2,1)S(1)}, bf16[8192,128]{1,0:T(8,128)(2,1)S(1)}) custom-call(s32[8]{0:T(128)S(1)} %compare_select_fusion.4.place, s32[64]{0:T(128)S(1)} %copy-done, s32[64]{0:T(128)S(1)} %copy-done.1, s32[8]{0:T(128)S(1)} %convert_reduce_fusion.below, ...), custom_call_target="tpu_custom_call", output_to_operand_aliasing={{0}: (8, {}), {1}: (9, {})} | custom-call | tf_op jit(solution)/shard_map/impute_near/pallas_call | solution.py:244
  58.0 0.0 collective-permute-done.9.rest_l
  58.0 0.0 collective-permute-done.8.rest_r
  58.0 0.0 collective-permute-done.13.edge_l
  58.0 0.0 collective-permute-done.12.edge_r
  58.0 3.3 %impute_far.1 = (bf16[12416,128]{1,0:T(8,128)(2,1)S(1)}, bf16[8192,128]{1,0:T(8,128)(2,1)S(1)}, bf16[8192,128]{1,0:T(8,128)(2,1)}) custom-call(s32[8]{0:T(128)S(1)} %compare_select_fusion.4.place, s32[64]{0:T(128)S(1)} %copy-done, s32[64]{0:T(128)S(1)} %copy-done.1, s32[8]{0:T(128)S(1)} %convert_reduce_fusion.below, ...), custom_call_target="tpu_custom_call", output_to_operand_aliasing={{0}: (9, {}), {1}: (10, {})} | custom-call | tf_op jit(solution)/shard_map/impute_far/pallas_call | solution.py:244
  (2 shorter events, 0.0 us)
Async XLA Ops:
  2.8 8.4 %collective-permute-start.3 = (bf16[1024,128]{1,0:T(8,128)(2,1)S(1)}, bf16[1024,128]{1,0:T(8,128)(2,1)S(1)}, u32[]{:S(2)}, u32[]{:S(2)}) collective-permute-start(bf16[1024,128]{1,0:T(8,128)(2,1)S(1)} %get-tuple-element.40.w_b), channel_id=1, source_target_pairs={{0,3},{1,2},{2,1},{3,0},{4,7},{5,6},{6,5},{7,4},{8,11},{9,10},{10,... | collective-permute-start | bytes 786440 | tf_op jit(solution)/shard_map/ppermute | solution.py:276
  6.2 6.9 %collective-permute-start.2 = (bf16[1024,128]{1,0:T(8,128)(2,1)S(1)}, bf16[1024,128]{1,0:T(8,128)(2,1)S(1)}, u32[]{:S(2)}, u32[]{:S(2)}) collective-permute-start(bf16[1024,128]{1,0:T(8,128)(2,1)S(1)} %get-tuple-element.36.w_a), channel_id=1, source_target_pairs={{0,1},{1,0},{2,3},{3,2},{4,5},{5,4},{6,7},{7,6},{8,9},{9,8},{10,11... | collective-permute-start | bytes 786440 | tf_op jit(solution)/shard_map/ppermute | solution.py:276
  8.9 10.5 %collective-permute-start = (bf16[1152,128]{1,0:T(8,128)(2,1)S(1)}, bf16[1152,128]{1,0:T(8,128)(2,1)S(1)}, u32[]{:S(2)}, u32[]{:S(2)}) collective-permute-start(bf16[1152,128]{1,0:T(8,128)(2,1)S(1)} %get-tuple-element.38.w_a), channel_id=1, source_target_pairs={{0,1},{1,0},{2,3},{3,2},{4,5},{5,4},{6,7},{7,6},{8,9},{9,8},{10,11... | collective-permute-start | bytes 884744 | tf_op jit(solution)/shard_map/ppermute | solution.py:276
  10.5 8.9 %collective-permute-start.1 = (bf16[1152,128]{1,0:T(8,128)(2,1)S(1)}, bf16[1152,128]{1,0:T(8,128)(2,1)S(1)}, u32[]{:S(2)}, u32[]{:S(2)}) collective-permute-start(bf16[1152,128]{1,0:T(8,128)(2,1)S(1)} %get-tuple-element.39.w_b), channel_id=1, source_target_pairs={{0,3},{1,2},{2,1},{3,0},{4,7},{5,6},{6,5},{7,4},{8,11},{9,10},{10,... | collective-permute-start | bytes 884744 | tf_op jit(solution)/shard_map/ppermute | solution.py:276
  13.1 32.8 %copy-start = (s32[64]{0:T(128)S(1)}, s32[64]{0:T(128)}, u32[]{:S(2)}) copy-start(s32[64]{0:T(128)} %starts.5) | copy-start | bytes 772
  13.1 32.8 %copy-start.2 = (s32[8]{0:T(128)S(1)}, s32[8]{0:T(128)}, u32[]{:S(2)}) copy-start(s32[8]{0:T(128)} %constant.36.clone) | copy-start | bytes 100
  13.1 33.0 %copy-start.1 = (s32[64]{0:T(128)S(1)}, s32[64]{0:T(128)}, u32[]{:S(2)}) copy-start(s32[64]{0:T(128)} %counts.5) | copy-start | bytes 772
  13.8 11.2 %collective-permute-start.7 = (bf16[1024,128]{1,0:T(8,128)(2,1)S(1)}, bf16[1024,128]{1,0:T(8,128)(2,1)S(1)}, u32[]{:S(2)}, u32[]{:S(2)}) collective-permute-start(bf16[1024,128]{1,0:T(8,128)(2,1)S(1)} %get-tuple-element.50), channel_id=1, source_target_pairs={{0,1},{1,0},{2,3},{3,2},{4,5},{5,4},{6,7},{7,6},{8,9},{9,8},{10,11... | collective-permute-start | bytes 786440 | tf_op jit(solution)/shard_map/ppermute | solution.py:276
  14.0 11.1 %collective-permute-start.6 = (bf16[1024,128]{1,0:T(8,128)(2,1)S(1)}, bf16[1024,128]{1,0:T(8,128)(2,1)S(1)}, u32[]{:S(2)}, u32[]{:S(2)}) collective-permute-start(bf16[1024,128]{1,0:T(8,128)(2,1)S(1)} %get-tuple-element.43), channel_id=1, source_target_pairs={{0,3},{1,2},{2,1},{3,0},{4,7},{5,6},{6,5},{7,4},{8,11},{9,10},{10,... | collective-permute-start | bytes 786440 | tf_op jit(solution)/shard_map/ppermute | solution.py:276
  20.2 18.5 %collective-permute-start.5 = (bf16[1152,128]{1,0:T(8,128)(2,1)S(1)}, bf16[1152,128]{1,0:T(8,128)(2,1)S(1)}, u32[]{:S(2)}, u32[]{:S(2)}) collective-permute-start(bf16[1152,128]{1,0:T(8,128)(2,1)S(1)} %get-tuple-element.48), channel_id=1, source_target_pairs={{0,1},{1,0},{2,3},{3,2},{4,5},{5,4},{6,7},{7,6},{8,9},{9,8},{10,11... | collective-permute-start | bytes 884744 | tf_op jit(solution)/shard_map/ppermute | solution.py:276
  20.4 18.3 %collective-permute-start.4 = (bf16[1152,128]{1,0:T(8,128)(2,1)S(1)}, bf16[1152,128]{1,0:T(8,128)(2,1)S(1)}, u32[]{:S(2)}, u32[]{:S(2)}) collective-permute-start(bf16[1152,128]{1,0:T(8,128)(2,1)S(1)} %get-tuple-element.47), channel_id=1, source_target_pairs={{0,3},{1,2},{2,1},{3,0},{4,7},{5,6},{6,5},{7,4},{8,11},{9,10},{10,... | collective-permute-start | bytes 884744 | tf_op jit(solution)/shard_map/ppermute | solution.py:276
  25.1 25.0 %collective-permute-start.11 = (bf16[2048,128]{1,0:T(8,128)(2,1)S(1)}, bf16[2048,128]{1,0:T(8,128)(2,1)S(1)}, u32[]{:S(2)}, u32[]{:S(2)}) collective-permute-start(bf16[2048,128]{1,0:T(8,128)(2,1)S(1)} %combine_1.1.mid), channel_id=1, source_target_pairs={{0,4},{4,8},{8,12},{12,16},{16,20},{20,24},{24,28},{28,32},{32,36}... | collective-permute-start | bytes 1572872 | tf_op jit(solution)/shard_map/ppermute | solution.py:280
  26.9 23.3 %collective-permute-start.10 = (bf16[2048,128]{1,0:T(8,128)(2,1)S(1)}, bf16[2048,128]{1,0:T(8,128)(2,1)S(1)}, u32[]{:S(2)}, u32[]{:S(2)}) collective-permute-start(bf16[2048,128]{1,0:T(8,128)(2,1)S(1)} %combine_1.1.mid), channel_id=1, source_target_pairs={{4,0},{8,4},{12,8},{16,12},{20,16},{24,20},{28,24},{32,28},{36,32}... | collective-permute-start | bytes 1572872 | tf_op jit(solution)/shard_map/ppermute | solution.py:279
  38.8 19.2 %collective-permute-start.9 = (bf16[2048,128]{1,0:T(8,128)(2,1)S(1)}, bf16[2048,128]{1,0:T(8,128)(2,1)S(1)}, u32[]{:S(2)}, u32[]{:S(2)}) collective-permute-start(bf16[2048,128]{1,0:T(8,128)(2,1)S(1)} %get-tuple-element.55.rest), channel_id=1, source_target_pairs={{0,4},{4,8},{8,12},{12,16},{16,20},{20,24},{24,28},{28,32},{32,36}... | collective-permute-start | bytes 1572872 | tf_op jit(solution)/shard_map/ppermute | solution.py:280
  40.7 17.3 %collective-permute-start.8 = (bf16[2048,128]{1,0:T(8,128)(2,1)S(1)}, bf16[2048,128]{1,0:T(8,128)(2,1)S(1)}, u32[]{:S(2)}, u32[]{:S(2)}) collective-permute-start(bf16[2048,128]{1,0:T(8,128)(2,1)S(1)} %get-tuple-element.55.rest), channel_id=1, source_target_pairs={{4,0},{8,4},{12,8},{16,12},{20,16},{24,20},{28,24},{32,28},{36,32}... | collective-permute-start | bytes 1572872 | tf_op jit(solution)/shard_map/ppermute | solution.py:279
  50.9 7.1 %collective-permute-start.13 = (bf16[256,128]{1,0:T(8,128)(2,1)S(1)}, bf16[256,128]{1,0:T(8,128)(2,1)S(1)}, u32[]{:S(2)}, u32[]{:S(2)}) collective-permute-start(bf16[256,128]{1,0:T(8,128)(2,1)S(1)} %finish_edge.1.edge), channel_id=1, source_target_pairs={{0,4},{4,8},{8,12},{12,16},{16,20},{20,24},{24,28},{28,32},{32,36}... | collective-permute-start | bytes 196616 | tf_op jit(solution)/shard_map/ppermute | solution.py:280
  51.0 7.0 %collective-permute-start.12 = (bf16[256,128]{1,0:T(8,128)(2,1)S(1)}, bf16[256,128]{1,0:T(8,128)(2,1)S(1)}, u32[]{:S(2)}, u32[]{:S(2)}) collective-permute-start(bf16[256,128]{1,0:T(8,128)(2,1)S(1)} %finish_edge.1.edge), channel_id=1, source_target_pairs={{4,0},{8,4},{12,8},{16,12},{20,16},{24,20},{28,24},{32,28},{36,32}... | collective-permute-start | bytes 196616 | tf_op jit(solution)/shard_map/ppermute | solution.py:279

commit v12 on v8

--- a/solution.py
+++ b/solution.py
@@ -46,32 +46,30 @@
     return copies
 
 
-def pieces(blocks):
-    return [(k, min(4, blocks - k)) for k in range(0, blocks, 4)]
-
-
-def whiten_1(place, z, band, mix, w_a, w_b, mix_a, mix_b, zs, bs, sems):
+def pieces(blocks, most):
+    return [(k, min(most, blocks - k)) for k in range(0, blocks, most)]
+
+
+CUTS1 = pieces(2 * HALF1, 2)
+CUTS2 = [(side, k, n) for side in range(2) for k, n in pieces(HALF2, 4)]
+
+
+def whiten_1(z, band, w_a, w_b, zs, bs, sems):
     zcopy = copy_all([(z.at[at(MID - 1, 2 * HALF1 + 2)], zs)], sems)
-    cuts = pieces(2 * HALF1)
-    bands = copy_all([(band.at[pl.ds(MID + k, n)], bs.at[pl.ds(k, n)]) for k, n in cuts], sems, 1)
-    t, a, b = place[0], place[1], place[2]
-    pairs = [(z.at[at(0)], w_a.at[at(HALF1)]), (z.at[at(TB - 1)], w_b.at[at(HALF1)])]
-    for target, near, far in ((mix_a, a, b), (mix_b, b, a)):
-        for i, row in enumerate((t, near)):
-            for j, col in enumerate((t, far)):
-                pairs.append((mix.at[at(row), at(col)], target.at[at(i), at(j)]))
-    others = copy_all(pairs, sems, 1 + len(cuts))
+    bands = copy_all([(band.at[pl.ds(MID + k, n)], bs.at[pl.ds(k, n)]) for k, n in CUTS1], sems, 1)
+    edges = [(z.at[at(0)], w_a.at[at(HALF1)]), (z.at[at(TB - 1)], w_b.at[at(HALF1)])]
+    edges = copy_all(edges, sems, 1 + len(CUTS1))
     zcopy[0].wait()
-    for (k, n), copy in zip(cuts, bands):
+    for (k, n), copy in zip(CUTS1, bands):
         copy.wait()
         for i in range(k, k + n):
             w = w_a if i < HALF1 else w_b
             w[at(i % HALF1), :] = dot(bs[i], zs[at(i, 3), :]).astype(BF)
-    for copy in others:
+    for copy in edges:
         copy.wait()
 
 
-def whiten_2(z, band, w_a, w_b, edge_band, zs, bs, sems):
+def whiten_2(place, z, band, mix, w_a, w_b, edge_band, mix_a, mix_b, zs, bs, sems):
     zcopies = copy_all(
         [
             (z.at[at(0, HALF2 + 1)], zs.at[at(1, HALF2 + 1)]),
@@ -79,13 +77,19 @@
         ],
         sems,
     )
-    cuts = [(side, k, n) for side in range(2) for k, n in pieces(HALF2)]
     bands = copy_all(
-        [(band.at[pl.ds(side * MID_END + k, n)], bs.at[pl.ds(side * HALF2 + k, n)]) for side, k, n in cuts], sems, 2
-    )
+        [(band.at[pl.ds(side * MID_END + k, n)], bs.at[pl.ds(side * HALF2 + k, n)]) for side, k, n in CUTS2], sems, 2
+    )
+    t, a, b = place[0], place[1], place[2]
+    pairs = []
+    for target, near, far in ((mix_a, a, b), (mix_b, b, a)):
+        for i, row in enumerate((t, near)):
+            for j, col in enumerate((t, far)):
+                pairs.append((mix.at[at(row), at(col)], target.at[at(i), at(j)]))
+    parts = copy_all(pairs, sems, 2 + len(CUTS2))
     zs[at(0), :] = jnp.zeros((BLK, COLS), BF)
     zs[at(2 * HALF2 + 3), :] = jnp.zeros((BLK, COLS), BF)
-    for (side, k, n), copy in zip(cuts, bands):
+    for (side, k, n), copy in zip(CUTS2, bands):
         if k == 0:
             zcopies[side].wait()
         copy.wait()
@@ -94,6 +98,8 @@
             (w_a, w_b)[side][at(i), :] = rows.astype(BF)
     edge_band[at(0), :] = bs[0, :, pl.ds(0, BLK)]
     edge_band[at(1), :] = bs[2 * HALF2 - 1, :, pl.ds(2 * BLK, BLK)]
+    for copy in parts:
+        copy.wait()
 
 
 def sums(own_rows, got_rows, mix):
@@ -284,28 +290,28 @@
 
     z, band, mix, ld = (pltpu.with_memory_space_constraint(x, pltpu.HBM) for x in (z, band, mix, ld))
     mix_part = jax.ShapeDtypeStruct((2 * COLS, 2 * COLS), BF)
-    w1a, w1b, mix_a, mix_b = call(
+    w1a, w1b = call(
         whiten_1,
-        in_vmem(shaped(HALF1 + 1), shaped(HALF1 + 1), mix_part, mix_part),
+        in_vmem(shaped(HALF1 + 1), shaped(HALF1 + 1)),
+        [HBM, HBM],
+        (z, band),
+        [
+            pltpu.VMEM(((2 * HALF1 + 2) * BLK, COLS), BF),
+            pltpu.VMEM((2 * HALF1, BLK, 3 * BLK), BF),
+            pltpu.SemaphoreType.DMA((3 + len(CUTS1),)),
+        ],
+    )
+    got1a, got1b = along_trait(w1a, w1b, pairs_a, pairs_b)
+    z, _ = lax.optimization_barrier((z, w1a))
+    w2a, w2b, edge_band, mix_a, mix_b = call(
+        whiten_2,
+        in_vmem(shaped(HALF2), shaped(HALF2), shaped(2), mix_part, mix_part),
         [SMEM, HBM, HBM, HBM],
         (place, z, band, mix),
         [
-            pltpu.VMEM(((2 * HALF1 + 2) * BLK, COLS), BF),
-            pltpu.VMEM((2 * HALF1, BLK, 3 * BLK), BF),
-            pltpu.SemaphoreType.DMA((11 + len(pieces(2 * HALF1)),)),
-        ],
-    )
-    got1a, got1b = along_trait(w1a, w1b, pairs_a, pairs_b)
-    z, _ = lax.optimization_barrier((z, w1a))
-    w2a, w2b, edge_band = call(
-        whiten_2,
-        in_vmem(shaped(HALF2), shaped(HALF2), shaped(2)),
-        [HBM, HBM],
-        (z, band),
-        [
             pltpu.VMEM(((2 * HALF2 + 4) * BLK, COLS), BF),
             pltpu.VMEM((2 * HALF2, BLK, 3 * BLK), BF),
-            pltpu.SemaphoreType.DMA((2 + 2 * len(pieces(HALF2)),)),
+            pltpu.SemaphoreType.DMA((10 + len(CUTS2),)),
         ],
     )
     got2a, got2b = along_trait(w2a, w2b, pairs_a, pairs_b)

time: 60.1 us -> 60.1 us (level)
  starting transfers between devices: 30.2 us -> 31.1 us
    ppermute x4, waiting for transfers between devices: 5.17 us -> 4.31 us  [along_trait(): lax.ppermute(y, 'trait', pairs_y)]
    ppermute x3, starting transfers between devices: 21.2 us -> 21.9 us  [along_rows(): other = lax.ppermute(x, ROWS, pairs)]
  transfers between devices with their start and end apart: 14 -> 14, of which waited for: 5 -> 4; matrix products, arithmetic and copies ran while one was open for 0% -> 0% of each run, Pallas kernels for 18% -> 19%
where the time goes in v12:
time: 60.1 us; the launch traced here: 60 us
  starting transfers between devices  31.1 us (52%)
  Pallas kernels  17.1 us (28%)
  waiting for transfers between devices  11.4 us (19%)
    ppermute x3, starting transfers between devices, along_rows(): other = lax.ppermute(x, ROWS, pairs)  21.9 us
    pallas_call x10, Pallas kernels, call(): pl.pallas_call(kernel, name=kernel.__name__, out_shape=tuple((shape for s...  17.1 us
    ppermute x4, waiting for transfers between devices, along_trait(): lax.ppermute(x, 'trait', pairs_x)  5.78 us
    ppermute x4, waiting for transfers between devices, along_trait(): lax.ppermute(y, 'trait', pairs_y)  4.31 us
    ppermute x4, starting transfers between devices, along_trait(): lax.ppermute(y, 'trait', pairs_y)  4.18 us
    ppermute x4, starting transfers between devices, along_trait(): lax.ppermute(x, 'trait', pairs_x)  3.12 us
    ppermute x3, starting transfers between devices, along_rows(): return (lax.ppermute(x, ROWS, pairs_e), other)  1.9 us
    ppermute x3, waiting for transfers between devices, along_rows(): other = lax.ppermute(x, ROWS, pairs)  1.27 us
  transfers between devices with their start and end apart: 14, of which 4 were waited for; matrix products, arithmetic and copies ran while one was open for 0% of the time, Pallas kernels for 19%

profile of v12, /device:TPU:1, one launch (start us, length us, event | category | flops | bytes accessed | tf_op | source)
XLA Modules:
  0.0 60.0 jit_solution(15894970525717447220)
XLA Ops:
  0.0 2.6 %whiten_1.1 = (bf16[1024,128]{1,0:T(8,128)(2,1)S(1)}, bf16[1024,128]{1,0:T(8,128)(2,1)S(1)}) custom-call(bf16[4096,128]{1,0:T(8,128)(2,1)} %z.2, bf16[32,128,384]{2,1,0:T(8,128)(2,1)} %band.3), custom_call_target="tpu_custom_call" | custom-call | tf_op jit(solution)/shard_map/whiten_1/pallas_call | solution.py:253
  2.6 3.4 %collective-permute-start.3 = (bf16[1024,128]{1,0:T(8,128)(2,1)S(1)}, bf16[1024,128]{1,0:T(8,128)(2,1)S(1)}, u32[]{:S(2)}, u32[]{:S(2)}) collective-permute-start(bf16[1024,128]{1,0:T(8,128)(2,1)S(1)} %get-tuple-element.40.w_b), channel_id=1, source_target_pairs={{0,3},{1,2},{2,1},{3,0},{4,7},{5,6},{6,5},{7,4},{8,11},{9,10},{10,... | collective-permute-start | bytes 786440 | tf_op jit(solution)/shard_map/ppermute | solution.py:285
  6.0 0.0 collective-permute-start.2
  6.0 3.3 %whiten_2.1 = (bf16[1152,128]{1,0:T(8,128)(2,1)S(1)}, bf16[1152,128]{1,0:T(8,128)(2,1)S(1)}, bf16[256,128]{1,0:T(8,128)(2,1)S(1)}, bf16[256,256]{1,0:T(8,128)(2,1)S(1)}, bf16[256,256]{1,0:T(8,128)(2,1)S(1)}) custom-call(s32[8]{0:T(128)S(1)} %compare_select_fusion.5.place, bf16[4096,128]{1,0:T(8,128)(2,1)} %z.2, bf16[32,128,384]{2,1,0:T(8,128)(2,1)} %band.3, ...), custom_call_target="tpu_custom_call" | custom-call | tf_op jit(solution)/shard_map/whiten_2/pallas_call | solution.py:253
  9.3 1.5 %collective-permute-start = (bf16[1152,128]{1,0:T(8,128)(2,1)S(1)}, bf16[1152,128]{1,0:T(8,128)(2,1)S(1)}, u32[]{:S(2)}, u32[]{:S(2)}) collective-permute-start(bf16[1152,128]{1,0:T(8,128)(2,1)S(1)} %get-tuple-element.38.w_a), channel_id=1, source_target_pairs={{0,1},{1,0},{2,3},{3,2},{4,5},{5,4},{6,7},{7,6},{8,9},{9,8},{10,11... | collective-permute-start | bytes 884744 | tf_op jit(solution)/shard_map/ppermute | solution.py:285
  10.9 0.1 collective-permute-start.1
  11.0 0.0 collective-permute-done.3.got_b
  11.0 1.9 %collective-permute-done.2.got_a = bf16[1024,128]{1,0:T(8,128)(2,1)S(1)} collective-permute-done((bf16[1024,128]{1,0:T(8,128)(2,1)S(1)}, bf16[1024,128]{1,0:T(8,128)(2,1)S(1)}, u32[]{:S(2)}, u32[]{:S(2)}) %collective-permute-start.2) | collective-permute-done | bytes 262176 | tf_op jit(solution)/shard_map/ppermute | solution.py:285
  12.8 0.0 copy-start
  12.8 0.0 copy-start.2
  12.8 0.0 copy-start.1
  12.9 0.7 %partial.2 = (bf16[1024,128]{1,0:T(8,128)(2,1)S(1)}, bf16[1024,128]{1,0:T(8,128)(2,1)S(1)}, f32[2048,128]{1,0:T(8,128)S(1)}) custom-call(bf16[1024,128]{1,0:T(8,128)(2,1)S(1)} %get-tuple-element.36.w_a, bf16[1024,128]{1,0:T(8,128)(2,1)S(1)} %collective-permute-done.2.got_a, bf16[1024,128]{1,0:T(8,128)(2,1)S(1)} %get-tuple-element.40.w_b, ...), custom_call_target="tpu_custom_call" | custom-call | tf_op jit(solution)/shard_map/partial/pallas_call | solution.py:253
  13.5 0.1 collective-permute-start.7
  13.7 1.6 %collective-permute-start.6 = (bf16[1024,128]{1,0:T(8,128)(2,1)S(1)}, bf16[1024,128]{1,0:T(8,128)(2,1)S(1)}, u32[]{:S(2)}, u32[]{:S(2)}) collective-permute-start(bf16[1024,128]{1,0:T(8,128)(2,1)S(1)} %get-tuple-element.43), channel_id=1, source_target_pairs={{0,3},{1,2},{2,1},{3,0},{4,7},{5,6},{6,5},{7,4},{8,11},{9,10},{10,... | collective-permute-start | bytes 786440 | tf_op jit(solution)/shard_map/ppermute | solution.py:285
  15.3 3.9 %collective-permute-done.got_a = bf16[1152,128]{1,0:T(8,128)(2,1)S(1)} collective-permute-done((bf16[1152,128]{1,0:T(8,128)(2,1)S(1)}, bf16[1152,128]{1,0:T(8,128)(2,1)S(1)}, u32[]{:S(2)}, u32[]{:S(2)}) %collective-permute-start) | collective-permute-done | bytes 294944 | tf_op jit(solution)/shard_map/ppermute | solution.py:285
  19.2 0.0 collective-permute-done.1.got_b
  19.2 0.8 %partial.3 = (bf16[1152,128]{1,0:T(8,128)(2,1)S(1)}, bf16[1152,128]{1,0:T(8,128)(2,1)S(1)}, f32[2304,128]{1,0:T(8,128)S(1)}) custom-call(bf16[1152,128]{1,0:T(8,128)(2,1)S(1)} %get-tuple-element.38.w_a, bf16[1152,128]{1,0:T(8,128)(2,1)S(1)} %collective-permute-done.got_a, bf16[1152,128]{1,0:T(8,128)(2,1)S(1)} %get-tuple-element.39.w_b, ...), custom_call_target="tpu_custom_call" | custom-call | tf_op jit(solution)/shard_map/partial/pallas_call | solution.py:253
  19.9 0.5 collective-permute-start.5
  20.5 0.0 collective-permute-start.4
  20.5 4.3 %collective-permute-done.7.far_b = bf16[1024,128]{1,0:T(8,128)(2,1)S(1)} collective-permute-done((bf16[1024,128]{1,0:T(8,128)(2,1)S(1)}, bf16[1024,128]{1,0:T(8,128)(2,1)S(1)}, u32[]{:S(2)}, u32[]{:S(2)}) %collective-permute-start.7) | collective-permute-done | bytes 262176 | tf_op jit(solution)/shard_map/ppermute | solution.py:285
  24.8 0.0 collective-permute-done.6.far_a
  24.8 0.1 combine_1.1.mid
  24.9 1.7 %collective-permute-start.11 = (bf16[2048,128]{1,0:T(8,128)(2,1)S(1)}, bf16[2048,128]{1,0:T(8,128)(2,1)S(1)}, u32[]{:S(2)}, u32[]{:S(2)}) collective-permute-start(bf16[2048,128]{1,0:T(8,128)(2,1)S(1)} %combine_1.1.mid), channel_id=1, source_target_pairs={{0,4},{4,0},{8,12},{12,8},{16,20},{20,16},{24,28},{28,24},{32,36},... | collective-permute-start | bytes 1572872 | tf_op jit(solution)/shard_map/ppermute | solution.py:289
  26.6 11.7 %collective-permute-start.10 = (bf16[2048,128]{1,0:T(8,128)(2,1)S(1)}, bf16[2048,128]{1,0:T(8,128)(2,1)S(1)}, u32[]{:S(2)}, u32[]{:S(2)}) collective-permute-start(bf16[2048,128]{1,0:T(8,128)(2,1)S(1)} %combine_1.1.mid), channel_id=1, source_target_pairs={{0,252},{4,8},{8,4},{12,16},{16,12},{20,24},{24,20},{28,32},{32,28... | collective-permute-start | bytes 1572872 | tf_op jit(solution)/shard_map/ppermute | solution.py:288
  38.3 0.0 collective-permute-done.5.far_b
  38.3 0.0 collective-permute-done.4.far_a
  38.3 0.1 combine_2.1
  38.4 0.1 collective-permute-start.9
  38.5 6.0 %collective-permute-start.8 = (bf16[2048,128]{1,0:T(8,128)(2,1)S(1)}, bf16[2048,128]{1,0:T(8,128)(2,1)S(1)}, u32[]{:S(2)}, u32[]{:S(2)}) collective-permute-start(bf16[2048,128]{1,0:T(8,128)(2,1)S(1)} %get-tuple-element.55.rest), channel_id=1, source_target_pairs={{0,0},{4,8},{8,4},{12,16},{16,12},{20,24},{24,20},{28,32},{32,28},... | collective-permute-start | bytes 1572872 | tf_op jit(solution)/shard_map/ppermute | solution.py:288
  44.4 0.0 copy-done
  44.5 0.0 copy-done.2
  44.5 0.2 convert_reduce_fusion.below
  44.7 0.0 copy-done.1
  44.7 4.1 %impute_own.1 = (bf16[12416,128]{1,0:T(8,128)(2,1)S(1)}, bf16[8192,128]{1,0:T(8,128)(2,1)S(1)}, bf16[64,128,512]{2,1,0:T(8,128)(2,1)S(1)}) custom-call(s32[8]{0:T(128)S(1)} %compare_select_fusion.5.place, s32[64]{0:T(128)S(1)} %copy-done, s32[64]{0:T(128)S(1)} %copy-done.1, s32[8]{0:T(128)S(1)} %convert_reduce_fusion.below, ...), custom_call_target="tpu_custom_call" | custom-call | tf_op jit(solution)/shard_map/impute_own/pallas_call | solution.py:253
  48.7 0.0 collective-permute-done.11.got_e.mid_e
  48.7 0.0 collective-permute-done.10.got_o.mid_o
  48.8 0.7 %finish_edge.1.edge = bf16[256,128]{1,0:T(8,128)(2,1)S(1)} custom-call(s32[8]{0:T(128)S(1)} %compare_select_fusion.5.place, f32[256,128]{1,0:T(8,128)S(1)} %get-tuple-element.56.edge, bf16[256,128]{1,0:T(8,128)(2,1)S(1)} %get-tuple-element.57.edge_band, bf16[2048,128]{1,0:T(8,128)(2,1)S(1)} %collective-permute-done.10.got_o.mid_o, ...), custom_call_target="tpu_custom_call" | custom-call | tf_op jit(solution)/shard_map/finish_edge/pallas_call | solution.py:253
  49.5 0.1 collective-permute-start.13
  49.6 4.3 %collective-permute-start.12 = (bf16[256,128]{1,0:T(8,128)(2,1)S(1)}, bf16[256,128]{1,0:T(8,128)(2,1)S(1)}, u32[]{:S(2)}, u32[]{:S(2)}) collective-permute-start(bf16[256,128]{1,0:T(8,128)(2,1)S(1)} %finish_edge.1.edge), channel_id=1, source_target_pairs={{0,252},{4,8},{8,4},{12,16},{16,12},{20,24},{24,20},{28,32},{32,28... | collective-permute-start | bytes 196616 | tf_op jit(solution)/shard_map/ppermute | solution.py:288
  53.8 1.5 %impute_near.1 = (bf16[12416,128]{1,0:T(8,128)(2,1)S(1)}, bf16[8192,128]{1,0:T(8,128)(2,1)S(1)}) custom-call(s32[8]{0:T(128)S(1)} %compare_select_fusion.5.place, s32[64]{0:T(128)S(1)} %copy-done, s32[64]{0:T(128)S(1)} %copy-done.1, s32[8]{0:T(128)S(1)} %convert_reduce_fusion.below, ...), custom_call_target="tpu_custom_call", output_to_operand_aliasing={{0}: (8, {}), {1}: (9, {})} | custom-call | tf_op jit(solution)/shard_map/impute_near/pallas_call | solution.py:253
  55.4 0.0 collective-permute-done.9.rest_e
  55.4 0.0 collective-permute-done.8.rest_o
  55.4 0.0 collective-permute-done.13.edge_e
  55.4 1.3 %collective-permute-done.12.edge_o = bf16[256,128]{1,0:T(8,128)(2,1)S(1)} collective-permute-done((bf16[256,128]{1,0:T(8,128)(2,1)S(1)}, bf16[256,128]{1,0:T(8,128)(2,1)S(1)}, u32[]{:S(2)}, u32[]{:S(2)}) %collective-permute-start.12) | collective-permute-done | bytes 65568 | tf_op jit(solution)/shard_map/ppermute | solution.py:288
  56.7 3.3 %impute_far.1 = (bf16[12416,128]{1,0:T(8,128)(2,1)S(1)}, bf16[8192,128]{1,0:T(8,128)(2,1)S(1)}, bf16[8192,128]{1,0:T(8,128)(2,1)}) custom-call(s32[8]{0:T(128)S(1)} %compare_select_fusion.5.place, s32[64]{0:T(128)S(1)} %copy-done, s32[64]{0:T(128)S(1)} %copy-done.1, s32[8]{0:T(128)S(1)} %convert_reduce_fusion.below, ...), custom_call_target="tpu_custom_call", output_to_operand_aliasing={{0}: (9, {}), {1}: (10, {})} | custom-call | tf_op jit(solution)/shard_map/impute_far/pallas_call | solution.py:253
  (2 shorter events, 0.0 us)
Async XLA Ops:
  2.6 8.4 %collective-permute-start.3 = (bf16[1024,128]{1,0:T(8,128)(2,1)S(1)}, bf16[1024,128]{1,0:T(8,128)(2,1)S(1)}, u32[]{:S(2)}, u32[]{:S(2)}) collective-permute-start(bf16[1024,128]{1,0:T(8,128)(2,1)S(1)} %get-tuple-element.40.w_b), channel_id=1, source_target_pairs={{0,3},{1,2},{2,1},{3,0},{4,7},{5,6},{6,5},{7,4},{8,11},{9,10},{10,... | collective-permute-start | bytes 786440 | tf_op jit(solution)/shard_map/ppermute | solution.py:285
  6.0 6.9 %collective-permute-start.2 = (bf16[1024,128]{1,0:T(8,128)(2,1)S(1)}, bf16[1024,128]{1,0:T(8,128)(2,1)S(1)}, u32[]{:S(2)}, u32[]{:S(2)}) collective-permute-start(bf16[1024,128]{1,0:T(8,128)(2,1)S(1)} %get-tuple-element.36.w_a), channel_id=1, source_target_pairs={{0,1},{1,0},{2,3},{3,2},{4,5},{5,4},{6,7},{7,6},{8,9},{9,8},{10,11... | collective-permute-start | bytes 786440 | tf_op jit(solution)/shard_map/ppermute | solution.py:285
  9.3 9.8 %collective-permute-start = (bf16[1152,128]{1,0:T(8,128)(2,1)S(1)}, bf16[1152,128]{1,0:T(8,128)(2,1)S(1)}, u32[]{:S(2)}, u32[]{:S(2)}) collective-permute-start(bf16[1152,128]{1,0:T(8,128)(2,1)S(1)} %get-tuple-element.38.w_a), channel_id=1, source_target_pairs={{0,1},{1,0},{2,3},{3,2},{4,5},{5,4},{6,7},{7,6},{8,9},{9,8},{10,11... | collective-permute-start | bytes 884744 | tf_op jit(solution)/shard_map/ppermute | solution.py:285
  10.9 8.3 %collective-permute-start.1 = (bf16[1152,128]{1,0:T(8,128)(2,1)S(1)}, bf16[1152,128]{1,0:T(8,128)(2,1)S(1)}, u32[]{:S(2)}, u32[]{:S(2)}) collective-permute-start(bf16[1152,128]{1,0:T(8,128)(2,1)S(1)} %get-tuple-element.39.w_b), channel_id=1, source_target_pairs={{0,3},{1,2},{2,1},{3,0},{4,7},{5,6},{6,5},{7,4},{8,11},{9,10},{10,... | collective-permute-start | bytes 884744 | tf_op jit(solution)/shard_map/ppermute | solution.py:285
  12.8 31.6 %copy-start = (s32[64]{0:T(128)S(1)}, s32[64]{0:T(128)}, u32[]{:S(2)}) copy-start(s32[64]{0:T(128)} %starts.5) | copy-start | bytes 772
  12.8 31.6 %copy-start.2 = (s32[8]{0:T(128)S(1)}, s32[8]{0:T(128)}, u32[]{:S(2)}) copy-start(s32[8]{0:T(128)} %constant.48.clone) | copy-start | bytes 100
  12.8 31.8 %copy-start.1 = (s32[64]{0:T(128)S(1)}, s32[64]{0:T(128)}, u32[]{:S(2)}) copy-start(s32[64]{0:T(128)} %counts.5) | copy-start | bytes 772
  13.5 11.2 %collective-permute-start.7 = (bf16[1024,128]{1,0:T(8,128)(2,1)S(1)}, bf16[1024,128]{1,0:T(8,128)(2,1)S(1)}, u32[]{:S(2)}, u32[]{:S(2)}) collective-permute-start(bf16[1024,128]{1,0:T(8,128)(2,1)S(1)} %get-tuple-element.50), channel_id=1, source_target_pairs={{0,1},{1,0},{2,3},{3,2},{4,5},{5,4},{6,7},{7,6},{8,9},{9,8},{10,11... | collective-permute-start | bytes 786440 | tf_op jit(solution)/shard_map/ppermute | solution.py:285
  13.7 11.1 %collective-permute-start.6 = (bf16[1024,128]{1,0:T(8,128)(2,1)S(1)}, bf16[1024,128]{1,0:T(8,128)(2,1)S(1)}, u32[]{:S(2)}, u32[]{:S(2)}) collective-permute-start(bf16[1024,128]{1,0:T(8,128)(2,1)S(1)} %get-tuple-element.43), channel_id=1, source_target_pairs={{0,3},{1,2},{2,1},{3,0},{4,7},{5,6},{6,5},{7,4},{8,11},{9,10},{10,... | collective-permute-start | bytes 786440 | tf_op jit(solution)/shard_map/ppermute | solution.py:285
  19.9 18.3 %collective-permute-start.5 = (bf16[1152,128]{1,0:T(8,128)(2,1)S(1)}, bf16[1152,128]{1,0:T(8,128)(2,1)S(1)}, u32[]{:S(2)}, u32[]{:S(2)}) collective-permute-start(bf16[1152,128]{1,0:T(8,128)(2,1)S(1)} %get-tuple-element.48), channel_id=1, source_target_pairs={{0,1},{1,0},{2,3},{3,2},{4,5},{5,4},{6,7},{7,6},{8,9},{9,8},{10,11... | collective-permute-start | bytes 884744 | tf_op jit(solution)/shard_map/ppermute | solution.py:285
  20.5 17.8 %collective-permute-start.4 = (bf16[1152,128]{1,0:T(8,128)(2,1)S(1)}, bf16[1152,128]{1,0:T(8,128)(2,1)S(1)}, u32[]{:S(2)}, u32[]{:S(2)}) collective-permute-start(bf16[1152,128]{1,0:T(8,128)(2,1)S(1)} %get-tuple-element.47), channel_id=1, source_target_pairs={{0,3},{1,2},{2,1},{3,0},{4,7},{5,6},{6,5},{7,4},{8,11},{9,10},{10,... | collective-permute-start | bytes 884744 | tf_op jit(solution)/shard_map/ppermute | solution.py:285
  24.9 23.9 %collective-permute-start.11 = (bf16[2048,128]{1,0:T(8,128)(2,1)S(1)}, bf16[2048,128]{1,0:T(8,128)(2,1)S(1)}, u32[]{:S(2)}, u32[]{:S(2)}) collective-permute-start(bf16[2048,128]{1,0:T(8,128)(2,1)S(1)} %combine_1.1.mid), channel_id=1, source_target_pairs={{0,4},{4,0},{8,12},{12,8},{16,20},{20,16},{24,28},{28,24},{32,36},... | collective-permute-start | bytes 1572872 | tf_op jit(solution)/shard_map/ppermute | solution.py:289
  26.6 22.2 %collective-permute-start.10 = (bf16[2048,128]{1,0:T(8,128)(2,1)S(1)}, bf16[2048,128]{1,0:T(8,128)(2,1)S(1)}, u32[]{:S(2)}, u32[]{:S(2)}) collective-permute-start(bf16[2048,128]{1,0:T(8,128)(2,1)S(1)} %combine_1.1.mid), channel_id=1, source_target_pairs={{0,252},{4,8},{8,4},{12,16},{16,12},{20,24},{24,20},{28,32},{32,28... | collective-permute-start | bytes 1572872 | tf_op jit(solution)/shard_map/ppermute | solution.py:288
  38.4 17.0 %collective-permute-start.9 = (bf16[2048,128]{1,0:T(8,128)(2,1)S(1)}, bf16[2048,128]{1,0:T(8,128)(2,1)S(1)}, u32[]{:S(2)}, u32[]{:S(2)}) collective-permute-start(bf16[2048,128]{1,0:T(8,128)(2,1)S(1)} %get-tuple-element.55.rest), channel_id=1, source_target_pairs={{0,4},{4,0},{8,12},{12,8},{16,20},{20,16},{24,28},{28,24},{32,36},... | collective-permute-start | bytes 1572872 | tf_op jit(solution)/shard_map/ppermute | solution.py:289
  38.5 16.9 %collective-permute-start.8 = (bf16[2048,128]{1,0:T(8,128)(2,1)S(1)}, bf16[2048,128]{1,0:T(8,128)(2,1)S(1)}, u32[]{:S(2)}, u32[]{:S(2)}) collective-permute-start(bf16[2048,128]{1,0:T(8,128)(2,1)S(1)} %get-tuple-element.55.rest), channel_id=1, source_target_pairs={{0,0},{4,8},{8,4},{12,16},{16,12},{20,24},{24,20},{28,32},{32,28},... | collective-permute-start | bytes 1572872 | tf_op jit(solution)/shard_map/ppermute | solution.py:288
  49.5 5.9 %collective-permute-start.13 = (bf16[256,128]{1,0:T(8,128)(2,1)S(1)}, bf16[256,128]{1,0:T(8,128)(2,1)S(1)}, u32[]{:S(2)}, u32[]{:S(2)}) collective-permute-start(bf16[256,128]{1,0:T(8,128)(2,1)S(1)} %finish_edge.1.edge), channel_id=1, source_target_pairs={{0,4},{4,0},{8,12},{12,8},{16,20},{20,16},{24,28},{28,24},{32,36},... | collective-permute-start | bytes 196616 | tf_op jit(solution)/shard_map/ppermute | solution.py:289
  49.6 7.1 %collective-permute-start.12 = (bf16[256,128]{1,0:T(8,128)(2,1)S(1)}, bf16[256,128]{1,0:T(8,128)(2,1)S(1)}, u32[]{:S(2)}, u32[]{:S(2)}) collective-permute-start(bf16[256,128]{1,0:T(8,128)(2,1)S(1)} %finish_edge.1.edge), channel_id=1, source_target_pairs={{0,252},{4,8},{8,4},{12,16},{16,12},{20,24},{24,20},{28,32},{32,28... | collective-permute-start | bytes 196616 | tf_op jit(solution)/shard_map/ppermute | solution.py:288

commit v13 on v12

--- a/solution.py
+++ b/solution.py
@@ -50,7 +50,7 @@
     return [(k, min(most, blocks - k)) for k in range(0, blocks, most)]
 
 
-CUTS1 = pieces(2 * HALF1, 2)
+CUTS1 = pieces(2 * HALF1, 4)
 CUTS2 = [(side, k, n) for side in range(2) for k, n in pieces(HALF2, 4)]
 
 
@@ -69,7 +69,7 @@
         copy.wait()
 
 
-def whiten_2(place, z, band, mix, w_a, w_b, edge_band, mix_a, mix_b, zs, bs, sems):
+def whiten_2(place, z, band, mix, w_a, w_b, edge_band, mix_rows, zs, bs, sems):
     zcopies = copy_all(
         [
             (z.at[at(0, HALF2 + 1)], zs.at[at(1, HALF2 + 1)]),
@@ -80,13 +80,7 @@
     bands = copy_all(
         [(band.at[pl.ds(side * MID_END + k, n)], bs.at[pl.ds(side * HALF2 + k, n)]) for side, k, n in CUTS2], sems, 2
     )
-    t, a, b = place[0], place[1], place[2]
-    pairs = []
-    for target, near, far in ((mix_a, a, b), (mix_b, b, a)):
-        for i, row in enumerate((t, near)):
-            for j, col in enumerate((t, far)):
-                pairs.append((mix.at[at(row), at(col)], target.at[at(i), at(j)]))
-    parts = copy_all(pairs, sems, 2 + len(CUTS2))
+    parts = copy_all([(mix.at[at(place[k])], mix_rows.at[at(k)]) for k in range(3)], sems, 2 + len(CUTS2))
     zs[at(0), :] = jnp.zeros((BLK, COLS), BF)
     zs[at(2 * HALF2 + 3), :] = jnp.zeros((BLK, COLS), BF)
     for (side, k, n), copy in zip(CUTS2, bands):
@@ -102,14 +96,14 @@
         copy.wait()
 
 
-def sums(own_rows, got_rows, mix):
-    return dot(own_rows, mix[pl.ds(0, COLS), :]) + dot(got_rows, mix[pl.ds(COLS, COLS), :])
-
-
-def partial(w_a, got_a, w_b, got_b, mix_a, mix_b, send_a, send_b, own):
+def partial(place, w_a, got_a, w_b, got_b, mix_rows, send_a, send_b, own):
     rows = w_a.shape[0]
-    for k, (w, got, mix, send) in enumerate(((w_a, got_a, mix_a, send_a), (w_b, got_b, mix_b, send_b))):
-        both = sums(w[...], got[...], mix)
+    for k, (w, got, send) in enumerate(((w_a, got_a, send_a), (w_b, got_b, send_b))):
+        columns = (at(place[0]), at(place[2 - k]))
+        weights = [
+            jnp.concatenate([mix_rows[at(row), column] for column in columns], axis=1) for row in (0, 1 + k)
+        ]
+        both = dot(w[...], weights[0]) + dot(got[...], weights[1])
         own[pl.ds(k * rows, rows), :] = both[:, :COLS]
         send[...] = both[:, COLS:].astype(BF)
 
@@ -289,7 +283,6 @@
         return lax.ppermute(x, ROWS, pairs_e), other
 
     z, band, mix, ld = (pltpu.with_memory_space_constraint(x, pltpu.HBM) for x in (z, band, mix, ld))
-    mix_part = jax.ShapeDtypeStruct((2 * COLS, 2 * COLS), BF)
     w1a, w1b = call(
         whiten_1,
         in_vmem(shaped(HALF1 + 1), shaped(HALF1 + 1)),
@@ -303,15 +296,15 @@
     )
     got1a, got1b = along_trait(w1a, w1b, pairs_a, pairs_b)
     z, _ = lax.optimization_barrier((z, w1a))
-    w2a, w2b, edge_band, mix_a, mix_b = call(
+    w2a, w2b, edge_band, mix_rows = call(
         whiten_2,
-        in_vmem(shaped(HALF2), shaped(HALF2), shaped(2), mix_part, mix_part),
+        in_vmem(shaped(HALF2), shaped(HALF2), shaped(2), jax.ShapeDtypeStruct((3 * COLS, mix.shape[1]), BF)),
         [SMEM, HBM, HBM, HBM],
         (place, z, band, mix),
         [
             pltpu.VMEM(((2 * HALF2 + 4) * BLK, COLS), BF),
             pltpu.VMEM((2 * HALF2, BLK, 3 * BLK), BF),
-            pltpu.SemaphoreType.DMA((10 + len(CUTS2),)),
+            pltpu.SemaphoreType.DMA((5 + len(CUTS2),)),
         ],
     )
     got2a, got2b = along_trait(w2a, w2b, pairs_a, pairs_b)
@@ -319,7 +312,9 @@
     def mixing(w_a, got_a, w_b, got_b):
         blocks = w_a.shape[0] // BLK
         outs = in_vmem(shaped(blocks), shaped(blocks), shaped(2 * blocks, F32))
-        send_a, send_b, own = call(partial, outs, [VM] * 6, (w_a, got_a, w_b, got_b, mix_a, mix_b))
+        send_a, send_b, own = call(
+            partial, outs, [SMEM] + [VM] * 5, (place, w_a, got_a, w_b, got_b, mix_rows)
+        )
         return (own, *along_trait(send_a, send_b, pairs_b, pairs_a)), send_a
 
     (own1, far1a, far1b), after = mixing(w1a, got1a, w1b, got1b)

time: 60.1 us -> 60.1 us (level)
  Pallas kernels: 17.1 us -> 18.7 us
  waiting for transfers between devices: 11.4 us -> 10.2 us
    pallas_call x10, Pallas kernels: 17.1 us -> 18.7 us  [call(): pl.pallas_call(kernel, name=kernel.__name__, out_shape=tuple((shape for s...]
  transfers between devices with their start and end apart: 14 -> 14, of which waited for: 4 -> 5; matrix products, arithmetic and copies ran while one was open for 0% -> 0% of each run, Pallas kernels for 19% -> 21%
where the time goes in v13:
time: 60.1 us; the launch traced here: 60 us
  starting transfers between devices  30.7 us (51%)
  Pallas kernels  18.7 us (31%)
  waiting for transfers between devices  10.2 us (17%)
    ppermute x3, starting transfers between devices, along_rows(): other = lax.ppermute(x, ROWS, pairs)  21.5 us
    pallas_call x10, Pallas kernels, call(): pl.pallas_call(kernel, name=kernel.__name__, out_shape=tuple((shape for s...  18.7 us
    ppermute x4, waiting for transfers between devices, along_trait(): lax.ppermute(x, 'trait', pairs_x)  5.23 us
    ppermute x4, starting transfers between devices, along_trait(): lax.ppermute(y, 'trait', pairs_y)  4.25 us
    ppermute x4, waiting for transfers between devices, along_trait(): lax.ppermute(y, 'trait', pairs_y)  3.75 us
    ppermute x4, starting transfers between devices, along_trait(): lax.ppermute(x, 'trait', pairs_x)  3.12 us
    ppermute x3, starting transfers between devices, along_rows(): return (lax.ppermute(x, ROWS, pairs_e), other)  1.9 us
  transfers between devices with their start and end apart: 14, of which 5 were waited for; matrix products, arithmetic and copies ran while one was open for 0% of the time, Pallas kernels for 21%

profile of v13, /device:TPU:1, one launch (start us, length us, event | category | flops | bytes accessed | tf_op | source)
XLA Modules:
  0.0 60.0 jit_solution(9216414131701246489)
XLA Ops:
  0.0 2.2 %whiten_1.1 = (bf16[1024,128]{1,0:T(8,128)(2,1)S(1)}, bf16[1024,128]{1,0:T(8,128)(2,1)S(1)}) custom-call(bf16[4096,128]{1,0:T(8,128)(2,1)} %z.2, bf16[32,128,384]{2,1,0:T(8,128)(2,1)} %band.3), custom_call_target="tpu_custom_call" | custom-call | tf_op jit(solution)/shard_map/whiten_1/pallas_call | solution.py:247
  2.2 3.4 %collective-permute-start.3 = (bf16[1024,128]{1,0:T(8,128)(2,1)S(1)}, bf16[1024,128]{1,0:T(8,128)(2,1)S(1)}, u32[]{:S(2)}, u32[]{:S(2)}) collective-permute-start(bf16[1024,128]{1,0:T(8,128)(2,1)S(1)} %get-tuple-element.39.w_b), channel_id=1, source_target_pairs={{0,3},{1,2},{2,1},{3,0},{4,7},{5,6},{6,5},{7,4},{8,11},{9,10},{10,... | collective-permute-start | bytes 786440 | tf_op jit(solution)/shard_map/ppermute | solution.py:279
  5.6 0.0 collective-permute-start.2
  5.6 3.3 %whiten_2.1 = (bf16[1152,128]{1,0:T(8,128)(2,1)S(1)}, bf16[1152,128]{1,0:T(8,128)(2,1)S(1)}, bf16[256,128]{1,0:T(8,128)(2,1)S(1)}, bf16[384,512]{1,0:T(8,128)(2,1)S(1)}) custom-call(s32[8]{0:T(128)S(1)} %compare_select_fusion.5.place, bf16[4096,128]{1,0:T(8,128)(2,1)} %z.2, bf16[32,128,384]{2,1,0:T(8,128)(2,1)} %band.3, bf16[512,512]{1,0:T(8,128)(2,1)} %mix.1), custom_call_target="tpu_custom_call" | custom-call | tf_op jit(solution)/shard_map/whiten_2/pallas_call | solution.py:247
  8.9 1.5 %collective-permute-start = (bf16[1152,128]{1,0:T(8,128)(2,1)S(1)}, bf16[1152,128]{1,0:T(8,128)(2,1)S(1)}, u32[]{:S(2)}, u32[]{:S(2)}) collective-permute-start(bf16[1152,128]{1,0:T(8,128)(2,1)S(1)} %get-tuple-element.37.w_a), channel_id=1, source_target_pairs={{0,1},{1,0},{2,3},{3,2},{4,5},{5,4},{6,7},{7,6},{8,9},{9,8},{10,11... | collective-permute-start | bytes 884744 | tf_op jit(solution)/shard_map/ppermute | solution.py:279
  10.4 0.1 collective-permute-start.1
  10.5 0.1 collective-permute-done.3.got_b
  10.6 1.9 %collective-permute-done.2.got_a = bf16[1024,128]{1,0:T(8,128)(2,1)S(1)} collective-permute-done((bf16[1024,128]{1,0:T(8,128)(2,1)S(1)}, bf16[1024,128]{1,0:T(8,128)(2,1)S(1)}, u32[]{:S(2)}, u32[]{:S(2)}) %collective-permute-start.2) | collective-permute-done | bytes 262176 | tf_op jit(solution)/shard_map/ppermute | solution.py:279
  12.5 0.0 copy-start
  12.5 0.0 copy-start.2
  12.5 0.0 copy-start.1
  12.5 1.2 %partial.2 = (bf16[1024,128]{1,0:T(8,128)(2,1)S(1)}, bf16[1024,128]{1,0:T(8,128)(2,1)S(1)}, f32[2048,128]{1,0:T(8,128)S(1)}) custom-call(s32[8]{0:T(128)S(1)} %compare_select_fusion.5.place, bf16[1024,128]{1,0:T(8,128)(2,1)S(1)} %get-tuple-element.35.w_a, bf16[1024,128]{1,0:T(8,128)(2,1)S(1)} %collective-permute-done.2.got_a, ...), custom_call_target="tpu_custom_call" | custom-call | tf_op jit(solution)/shard_map/partial/pallas_call | solution.py:247
  13.7 0.1 collective-permute-start.7
  13.9 1.6 %collective-permute-start.6 = (bf16[1024,128]{1,0:T(8,128)(2,1)S(1)}, bf16[1024,128]{1,0:T(8,128)(2,1)S(1)}, u32[]{:S(2)}, u32[]{:S(2)}) collective-permute-start(bf16[1024,128]{1,0:T(8,128)(2,1)S(1)} %get-tuple-element.41), channel_id=1, source_target_pairs={{0,3},{1,2},{2,1},{3,0},{4,7},{5,6},{6,5},{7,4},{8,11},{9,10},{10,... | collective-permute-start | bytes 786440 | tf_op jit(solution)/shard_map/ppermute | solution.py:279
  15.4 3.3 %collective-permute-done.got_a = bf16[1152,128]{1,0:T(8,128)(2,1)S(1)} collective-permute-done((bf16[1152,128]{1,0:T(8,128)(2,1)S(1)}, bf16[1152,128]{1,0:T(8,128)(2,1)S(1)}, u32[]{:S(2)}, u32[]{:S(2)}) %collective-permute-start) | collective-permute-done | bytes 294944 | tf_op jit(solution)/shard_map/ppermute | solution.py:279
  18.8 0.0 collective-permute-done.1.got_b
  18.8 1.3 %partial.3 = (bf16[1152,128]{1,0:T(8,128)(2,1)S(1)}, bf16[1152,128]{1,0:T(8,128)(2,1)S(1)}, f32[2304,128]{1,0:T(8,128)S(1)}) custom-call(s32[8]{0:T(128)S(1)} %compare_select_fusion.5.place, bf16[1152,128]{1,0:T(8,128)(2,1)S(1)} %get-tuple-element.37.w_a, bf16[1152,128]{1,0:T(8,128)(2,1)S(1)} %collective-permute-done.got_a, ...), custom_call_target="tpu_custom_call" | custom-call | tf_op jit(solution)/shard_map/partial/pallas_call | solution.py:247
  20.1 0.6 %collective-permute-start.5 = (bf16[1152,128]{1,0:T(8,128)(2,1)S(1)}, bf16[1152,128]{1,0:T(8,128)(2,1)S(1)}, u32[]{:S(2)}, u32[]{:S(2)}) collective-permute-start(bf16[1152,128]{1,0:T(8,128)(2,1)S(1)} %get-tuple-element.46), channel_id=1, source_target_pairs={{0,1},{1,0},{2,3},{3,2},{4,5},{5,4},{6,7},{7,6},{8,9},{9,8},{10,11... | collective-permute-start | bytes 884744 | tf_op jit(solution)/shard_map/ppermute | solution.py:279
  20.7 0.0 collective-permute-start.4
  20.7 3.7 %collective-permute-done.7.far_b = bf16[1024,128]{1,0:T(8,128)(2,1)S(1)} collective-permute-done((bf16[1024,128]{1,0:T(8,128)(2,1)S(1)}, bf16[1024,128]{1,0:T(8,128)(2,1)S(1)}, u32[]{:S(2)}, u32[]{:S(2)}) %collective-permute-start.7) | collective-permute-done | bytes 262176 | tf_op jit(solution)/shard_map/ppermute | solution.py:279
  24.4 0.0 collective-permute-done.6.far_a
  24.4 0.1 combine_1.1.mid
  24.5 1.7 %collective-permute-start.11 = (bf16[2048,128]{1,0:T(8,128)(2,1)S(1)}, bf16[2048,128]{1,0:T(8,128)(2,1)S(1)}, u32[]{:S(2)}, u32[]{:S(2)}) collective-permute-start(bf16[2048,128]{1,0:T(8,128)(2,1)S(1)} %combine_1.1.mid), channel_id=1, source_target_pairs={{0,4},{4,0},{8,12},{12,8},{16,20},{20,16},{24,28},{28,24},{32,36},... | collective-permute-start | bytes 1572872 | tf_op jit(solution)/shard_map/ppermute | solution.py:283
  26.2 11.2 %collective-permute-start.10 = (bf16[2048,128]{1,0:T(8,128)(2,1)S(1)}, bf16[2048,128]{1,0:T(8,128)(2,1)S(1)}, u32[]{:S(2)}, u32[]{:S(2)}) collective-permute-start(bf16[2048,128]{1,0:T(8,128)(2,1)S(1)} %combine_1.1.mid), channel_id=1, source_target_pairs={{0,252},{4,8},{8,4},{12,16},{16,12},{20,24},{24,20},{28,32},{32,28... | collective-permute-start | bytes 1572872 | tf_op jit(solution)/shard_map/ppermute | solution.py:282
  37.4 0.0 collective-permute-done.5.far_b
  37.4 0.0 collective-permute-done.4.far_a
  37.4 0.1 combine_2.1
  37.5 0.1 collective-permute-start.9
  37.6 6.4 %collective-permute-start.8 = (bf16[2048,128]{1,0:T(8,128)(2,1)S(1)}, bf16[2048,128]{1,0:T(8,128)(2,1)S(1)}, u32[]{:S(2)}, u32[]{:S(2)}) collective-permute-start(bf16[2048,128]{1,0:T(8,128)(2,1)S(1)} %get-tuple-element.53.rest), channel_id=1, source_target_pairs={{0,0},{4,8},{8,4},{12,16},{16,12},{20,24},{24,20},{28,32},{32,28},... | collective-permute-start | bytes 1572872 | tf_op jit(solution)/shard_map/ppermute | solution.py:282
  44.0 0.0 copy-done
  44.0 0.0 copy-done.2
  44.1 0.2 convert_reduce_fusion.below
  44.2 0.0 copy-done.1
  44.2 4.1 %impute_own.1 = (bf16[12416,128]{1,0:T(8,128)(2,1)S(1)}, bf16[8192,128]{1,0:T(8,128)(2,1)S(1)}, bf16[64,128,512]{2,1,0:T(8,128)(2,1)S(1)}) custom-call(s32[8]{0:T(128)S(1)} %compare_select_fusion.5.place, s32[64]{0:T(128)S(1)} %copy-done, s32[64]{0:T(128)S(1)} %copy-done.1, s32[8]{0:T(128)S(1)} %convert_reduce_fusion.below, ...), custom_call_target="tpu_custom_call" | custom-call | tf_op jit(solution)/shard_map/impute_own/pallas_call | solution.py:247
  48.3 0.0 collective-permute-done.11.got_e.mid_e
  48.3 0.0 collective-permute-done.10.got_o.mid_o
  48.3 0.7 %finish_edge.1.edge = bf16[256,128]{1,0:T(8,128)(2,1)S(1)} custom-call(s32[8]{0:T(128)S(1)} %compare_select_fusion.5.place, f32[256,128]{1,0:T(8,128)S(1)} %get-tuple-element.54.edge, bf16[256,128]{1,0:T(8,128)(2,1)S(1)} %get-tuple-element.55.edge_band, bf16[2048,128]{1,0:T(8,128)(2,1)S(1)} %collective-permute-done.10.got_o.mid_o, ...), custom_call_target="tpu_custom_call" | custom-call | tf_op jit(solution)/shard_map/finish_edge/pallas_call | solution.py:247
  49.0 0.1 collective-permute-start.13
  49.1 3.9 %collective-permute-start.12 = (bf16[256,128]{1,0:T(8,128)(2,1)S(1)}, bf16[256,128]{1,0:T(8,128)(2,1)S(1)}, u32[]{:S(2)}, u32[]{:S(2)}) collective-permute-start(bf16[256,128]{1,0:T(8,128)(2,1)S(1)} %finish_edge.1.edge), channel_id=1, source_target_pairs={{0,252},{4,8},{8,4},{12,16},{16,12},{20,24},{24,20},{28,32},{32,28... | collective-permute-start | bytes 196616 | tf_op jit(solution)/shard_map/ppermute | solution.py:282
  53.1 2.0 %impute_near.1 = (bf16[12416,128]{1,0:T(8,128)(2,1)S(1)}, bf16[8192,128]{1,0:T(8,128)(2,1)S(1)}) custom-call(s32[8]{0:T(128)S(1)} %compare_select_fusion.5.place, s32[64]{0:T(128)S(1)} %copy-done, s32[64]{0:T(128)S(1)} %copy-done.1, s32[8]{0:T(128)S(1)} %convert_reduce_fusion.below, ...), custom_call_target="tpu_custom_call", output_to_operand_aliasing={{0}: (8, {}), {1}: (9, {})} | custom-call | tf_op jit(solution)/shard_map/impute_near/pallas_call | solution.py:247
  55.0 0.0 collective-permute-done.9.rest_e
  55.0 0.0 collective-permute-done.8.rest_o
  55.0 0.0 collective-permute-done.13.edge_e
  55.0 1.2 %collective-permute-done.12.edge_o = bf16[256,128]{1,0:T(8,128)(2,1)S(1)} collective-permute-done((bf16[256,128]{1,0:T(8,128)(2,1)S(1)}, bf16[256,128]{1,0:T(8,128)(2,1)S(1)}, u32[]{:S(2)}, u32[]{:S(2)}) %collective-permute-start.12) | collective-permute-done | bytes 65568 | tf_op jit(solution)/shard_map/ppermute | solution.py:282
  56.2 3.8 %impute_far.1 = (bf16[12416,128]{1,0:T(8,128)(2,1)S(1)}, bf16[8192,128]{1,0:T(8,128)(2,1)S(1)}, bf16[8192,128]{1,0:T(8,128)(2,1)}) custom-call(s32[8]{0:T(128)S(1)} %compare_select_fusion.5.place, s32[64]{0:T(128)S(1)} %copy-done, s32[64]{0:T(128)S(1)} %copy-done.1, s32[8]{0:T(128)S(1)} %convert_reduce_fusion.below, ...), custom_call_target="tpu_custom_call", output_to_operand_aliasing={{0}: (9, {}), {1}: (10, {})} | custom-call | tf_op jit(solution)/shard_map/impute_far/pallas_call | solution.py:247
  (2 shorter events, 0.0 us)
Async XLA Ops:
  2.2 8.4 %collective-permute-start.3 = (bf16[1024,128]{1,0:T(8,128)(2,1)S(1)}, bf16[1024,128]{1,0:T(8,128)(2,1)S(1)}, u32[]{:S(2)}, u32[]{:S(2)}) collective-permute-start(bf16[1024,128]{1,0:T(8,128)(2,1)S(1)} %get-tuple-element.39.w_b), channel_id=1, source_target_pairs={{0,3},{1,2},{2,1},{3,0},{4,7},{5,6},{6,5},{7,4},{8,11},{9,10},{10,... | collective-permute-start | bytes 786440 | tf_op jit(solution)/shard_map/ppermute | solution.py:279
  5.6 6.9 %collective-permute-start.2 = (bf16[1024,128]{1,0:T(8,128)(2,1)S(1)}, bf16[1024,128]{1,0:T(8,128)(2,1)S(1)}, u32[]{:S(2)}, u32[]{:S(2)}) collective-permute-start(bf16[1024,128]{1,0:T(8,128)(2,1)S(1)} %get-tuple-element.35.w_a), channel_id=1, source_target_pairs={{0,1},{1,0},{2,3},{3,2},{4,5},{5,4},{6,7},{7,6},{8,9},{9,8},{10,11... | collective-permute-start | bytes 786440 | tf_op jit(solution)/shard_map/ppermute | solution.py:279
  8.9 9.9 %collective-permute-start = (bf16[1152,128]{1,0:T(8,128)(2,1)S(1)}, bf16[1152,128]{1,0:T(8,128)(2,1)S(1)}, u32[]{:S(2)}, u32[]{:S(2)}) collective-permute-start(bf16[1152,128]{1,0:T(8,128)(2,1)S(1)} %get-tuple-element.37.w_a), channel_id=1, source_target_pairs={{0,1},{1,0},{2,3},{3,2},{4,5},{5,4},{6,7},{7,6},{8,9},{9,8},{10,11... | collective-permute-start | bytes 884744 | tf_op jit(solution)/shard_map/ppermute | solution.py:279
  10.4 8.4 %collective-permute-start.1 = (bf16[1152,128]{1,0:T(8,128)(2,1)S(1)}, bf16[1152,128]{1,0:T(8,128)(2,1)S(1)}, u32[]{:S(2)}, u32[]{:S(2)}) collective-permute-start(bf16[1152,128]{1,0:T(8,128)(2,1)S(1)} %get-tuple-element.38.w_b), channel_id=1, source_target_pairs={{0,3},{1,2},{2,1},{3,0},{4,7},{5,6},{6,5},{7,4},{8,11},{9,10},{10,... | collective-permute-start | bytes 884744 | tf_op jit(solution)/shard_map/ppermute | solution.py:279
  12.5 31.6 %copy-start = (s32[64]{0:T(128)S(1)}, s32[64]{0:T(128)}, u32[]{:S(2)}) copy-start(s32[64]{0:T(128)} %starts.5) | copy-start | bytes 772
  12.5 31.6 %copy-start.2 = (s32[8]{0:T(128)S(1)}, s32[8]{0:T(128)}, u32[]{:S(2)}) copy-start(s32[8]{0:T(128)} %constant.48.clone) | copy-start | bytes 100
  12.5 31.8 %copy-start.1 = (s32[64]{0:T(128)S(1)}, s32[64]{0:T(128)}, u32[]{:S(2)}) copy-start(s32[64]{0:T(128)} %counts.5) | copy-start | bytes 772
  13.7 10.7 %collective-permute-start.7 = (bf16[1024,128]{1,0:T(8,128)(2,1)S(1)}, bf16[1024,128]{1,0:T(8,128)(2,1)S(1)}, u32[]{:S(2)}, u32[]{:S(2)}) collective-permute-start(bf16[1024,128]{1,0:T(8,128)(2,1)S(1)} %get-tuple-element.48), channel_id=1, source_target_pairs={{0,1},{1,0},{2,3},{3,2},{4,5},{5,4},{6,7},{7,6},{8,9},{9,8},{10,11... | collective-permute-start | bytes 786440 | tf_op jit(solution)/shard_map/ppermute | solution.py:279
  13.9 10.5 %collective-permute-start.6 = (bf16[1024,128]{1,0:T(8,128)(2,1)S(1)}, bf16[1024,128]{1,0:T(8,128)(2,1)S(1)}, u32[]{:S(2)}, u32[]{:S(2)}) collective-permute-start(bf16[1024,128]{1,0:T(8,128)(2,1)S(1)} %get-tuple-element.41), channel_id=1, source_target_pairs={{0,3},{1,2},{2,1},{3,0},{4,7},{5,6},{6,5},{7,4},{8,11},{9,10},{10,... | collective-permute-start | bytes 786440 | tf_op jit(solution)/shard_map/ppermute | solution.py:279
  20.1 17.3 %collective-permute-start.5 = (bf16[1152,128]{1,0:T(8,128)(2,1)S(1)}, bf16[1152,128]{1,0:T(8,128)(2,1)S(1)}, u32[]{:S(2)}, u32[]{:S(2)}) collective-permute-start(bf16[1152,128]{1,0:T(8,128)(2,1)S(1)} %get-tuple-element.46), channel_id=1, source_target_pairs={{0,1},{1,0},{2,3},{3,2},{4,5},{5,4},{6,7},{7,6},{8,9},{9,8},{10,11... | collective-permute-start | bytes 884744 | tf_op jit(solution)/shard_map/ppermute | solution.py:279
  20.7 16.7 %collective-permute-start.4 = (bf16[1152,128]{1,0:T(8,128)(2,1)S(1)}, bf16[1152,128]{1,0:T(8,128)(2,1)S(1)}, u32[]{:S(2)}, u32[]{:S(2)}) collective-permute-start(bf16[1152,128]{1,0:T(8,128)(2,1)S(1)} %get-tuple-element.45), channel_id=1, source_target_pairs={{0,3},{1,2},{2,1},{3,0},{4,7},{5,6},{6,5},{7,4},{8,11},{9,10},{10,... | collective-permute-start | bytes 884744 | tf_op jit(solution)/shard_map/ppermute | solution.py:279
  24.5 23.8 %collective-permute-start.11 = (bf16[2048,128]{1,0:T(8,128)(2,1)S(1)}, bf16[2048,128]{1,0:T(8,128)(2,1)S(1)}, u32[]{:S(2)}, u32[]{:S(2)}) collective-permute-start(bf16[2048,128]{1,0:T(8,128)(2,1)S(1)} %combine_1.1.mid), channel_id=1, source_target_pairs={{0,4},{4,0},{8,12},{12,8},{16,20},{20,16},{24,28},{28,24},{32,36},... | collective-permute-start | bytes 1572872 | tf_op jit(solution)/shard_map/ppermute | solution.py:283
  26.2 22.1 %collective-permute-start.10 = (bf16[2048,128]{1,0:T(8,128)(2,1)S(1)}, bf16[2048,128]{1,0:T(8,128)(2,1)S(1)}, u32[]{:S(2)}, u32[]{:S(2)}) collective-permute-start(bf16[2048,128]{1,0:T(8,128)(2,1)S(1)} %combine_1.1.mid), channel_id=1, source_target_pairs={{0,252},{4,8},{8,4},{12,16},{16,12},{20,24},{24,20},{28,32},{32,28... | collective-permute-start | bytes 1572872 | tf_op jit(solution)/shard_map/ppermute | solution.py:282
  37.5 17.5 %collective-permute-start.9 = (bf16[2048,128]{1,0:T(8,128)(2,1)S(1)}, bf16[2048,128]{1,0:T(8,128)(2,1)S(1)}, u32[]{:S(2)}, u32[]{:S(2)}) collective-permute-start(bf16[2048,128]{1,0:T(8,128)(2,1)S(1)} %get-tuple-element.53.rest), channel_id=1, source_target_pairs={{0,4},{4,0},{8,12},{12,8},{16,20},{20,16},{24,28},{28,24},{32,36},... | collective-permute-start | bytes 1572872 | tf_op jit(solution)/shard_map/ppermute | solution.py:283
  37.6 17.4 %collective-permute-start.8 = (bf16[2048,128]{1,0:T(8,128)(2,1)S(1)}, bf16[2048,128]{1,0:T(8,128)(2,1)S(1)}, u32[]{:S(2)}, u32[]{:S(2)}) collective-permute-start(bf16[2048,128]{1,0:T(8,128)(2,1)S(1)} %get-tuple-element.53.rest), channel_id=1, source_target_pairs={{0,0},{4,8},{8,4},{12,16},{16,12},{20,24},{24,20},{28,32},{32,28},... | collective-permute-start | bytes 1572872 | tf_op jit(solution)/shard_map/ppermute | solution.py:282
  49.0 6.0 %collective-permute-start.13 = (bf16[256,128]{1,0:T(8,128)(2,1)S(1)}, bf16[256,128]{1,0:T(8,128)(2,1)S(1)}, u32[]{:S(2)}, u32[]{:S(2)}) collective-permute-start(bf16[256,128]{1,0:T(8,128)(2,1)S(1)} %finish_edge.1.edge), channel_id=1, source_target_pairs={{0,4},{4,0},{8,12},{12,8},{16,20},{20,16},{24,28},{28,24},{32,36},... | collective-permute-start | bytes 196616 | tf_op jit(solution)/shard_map/ppermute | solution.py:283
  49.1 7.1 %collective-permute-start.12 = (bf16[256,128]{1,0:T(8,128)(2,1)S(1)}, bf16[256,128]{1,0:T(8,128)(2,1)S(1)}, u32[]{:S(2)}, u32[]{:S(2)}) collective-permute-start(bf16[256,128]{1,0:T(8,128)(2,1)S(1)} %finish_edge.1.edge), channel_id=1, source_target_pairs={{0,252},{4,8},{8,4},{12,16},{16,12},{20,24},{24,20},{28,32},{32,28... | collective-permute-start | bytes 196616 | tf_op jit(solution)/shard_map/ppermute | solution.py:282

commit v14 on v13

--- a/solution.py
+++ b/solution.py
@@ -54,6 +54,11 @@
 CUTS2 = [(side, k, n) for side in range(2) for k, n in pieces(HALF2, 4)]
 
 
+def place():
+    t = lax.axis_index("trait")
+    return t, t ^ 1, 3 - t
+
+
 def whiten_1(z, band, w_a, w_b, zs, bs, sems):
     zcopy = copy_all([(z.at[at(MID - 1, 2 * HALF1 + 2)], zs)], sems)
     bands = copy_all([(band.at[pl.ds(MID + k, n)], bs.at[pl.ds(k, n)]) for k, n in CUTS1], sems, 1)
@@ -69,7 +74,7 @@
         copy.wait()
 
 
-def whiten_2(place, z, band, mix, w_a, w_b, edge_band, mix_rows, zs, bs, sems):
+def whiten_2(z, band, mix, w_a, w_b, edge_band, mix_rows, zs, bs, sems):
     zcopies = copy_all(
         [
             (z.at[at(0, HALF2 + 1)], zs.at[at(1, HALF2 + 1)]),
@@ -80,7 +85,7 @@
     bands = copy_all(
         [(band.at[pl.ds(side * MID_END + k, n)], bs.at[pl.ds(side * HALF2 + k, n)]) for side, k, n in CUTS2], sems, 2
     )
-    parts = copy_all([(mix.at[at(place[k])], mix_rows.at[at(k)]) for k in range(3)], sems, 2 + len(CUTS2))
+    parts = copy_all([(mix.at[at(row)], mix_rows.at[at(k)]) for k, row in enumerate(place())], sems, 2 + len(CUTS2))
     zs[at(0), :] = jnp.zeros((BLK, COLS), BF)
     zs[at(2 * HALF2 + 3), :] = jnp.zeros((BLK, COLS), BF)
     for (side, k, n), copy in zip(CUTS2, bands):
@@ -96,10 +101,11 @@
         copy.wait()
 
 
-def partial(place, w_a, got_a, w_b, got_b, mix_rows, send_a, send_b, own):
+def partial(w_a, got_a, w_b, got_b, mix_rows, send_a, send_b, own):
+    here = place()
     rows = w_a.shape[0]
     for k, (w, got, send) in enumerate(((w_a, got_a, send_a), (w_b, got_b, send_b))):
-        columns = (at(place[0]), at(place[2 - k]))
+        columns = (at(here[0]), at(here[2 - k]))
         weights = [
             jnp.concatenate([mix_rows[at(row), column] for column in columns], axis=1) for row in (0, 1 + k)
         ]
@@ -123,18 +129,19 @@
     edge[at(1), :] = own[at(2 * HALF2 - 1), :] + far_b[at(inner), :].astype(F32)
 
 
-def finish_edge(place, edge, edge_band, got_o, got_e, out):
-    odd = place[5] == 1
+def finish_edge(edge, edge_band, got_o, got_e, out):
+    g = lax.axis_index(ROWS)
+    odd = g % 2 == 1
     nothing = jnp.zeros((BLK, COLS), BF)
     from_left = jnp.where(odd, got_e[at(2 * HALF1 + 1), :], got_o[at(2 * HALF1 + 1), :])
     from_right = jnp.where(odd, got_o[at(2 * HALF1), :], got_e[at(2 * HALF1), :])
-    from_left = jnp.where(place[3] == 0, nothing, from_left)
-    from_right = jnp.where(place[3] == place[4] - 1, nothing, from_right)
+    from_left = jnp.where(g == 0, nothing, from_left)
+    from_right = jnp.where(g == lax.axis_size(ROWS) - 1, nothing, from_right)
     for k, rows in enumerate((from_left, from_right)):
         out[at(k), :] = (edge[at(k), :] + dot(edge_band[at(k), :], rows)).astype(BF)
 
 
-def on_ranges(ranges, starts, counts, lowest, ld, ext, out, ready=None, send=None):
+def on_ranges(ranges, plan, ld, ext, out, ready=None, send=None):
     total = 0
     parts = []
     for low, high in ranges:
@@ -152,8 +159,8 @@
             ready(k)
         for i in range(UNROLL):
             u = window_of(jnp.minimum(UNROLL * k + i, total - 1))
-            first = jnp.clip(starts[u] - lowest, 0, 3 * TB - 1)
-            have = counts[u]
+            first = jnp.clip(plan[u], 0, 3 * TB - 1)
+            have = plan[UB + u]
             window = [ext[at(jnp.where(s < have, jnp.minimum(first + s, ZERO), ZERO)), :] for s in range(WIN)]
             out[at(u), :] = dot(ld[u], jnp.concatenate(window, axis=0)).astype(BF)
         if send is None:
@@ -182,9 +189,9 @@
 )
 
 
-def impute_own(place, starts, counts, below, mid, rest, ld, ext, out, ld_here, sems):
+def impute_own(plan, mid, rest, ld, ext, out, ld_here, sems):
     inner = HALF2 - 1
-    low, high = below[3], below[4]
+    low, high = plan[2 * UB + 3], plan[2 * UB + 4]
     groups = (high - low + UNROLL - 1) // UNROLL
 
     def load(k):
@@ -207,27 +214,27 @@
     move(ext, TB + MID_END, rest, inner, inner)
     ext[at(ZERO), :] = jnp.zeros((BLK, COLS), BF)
     load(0).wait()
-    on_ranges([(low, high)], starts, counts, place[3] * TB - TB, ld_here, ext, out, ready)
+    on_ranges([(low, high)], plan, ld_here, ext, out, ready)
     lax.fori_loop(groups + 1, UB // UNROLL, rest_ready, 0)
 
 
-def impute_near(place, starts, counts, below, edge, mid_o, mid_e, ld, before, done, ext, out):
+def impute_near(plan, edge, mid_o, mid_e, ld, before, done, ext, out):
     move(ext, TB, edge, 0, 1)
     move(ext, 2 * TB - 1, edge, 1, 1)
-    move(ext, 2 * TB * (1 - place[5]) + MID, mid_e, 0, 2 * HALF1)
-    move(ext, 2 * TB * place[5] + MID, mid_o, 0, 2 * HALF1)
-    ranges = [(below[k], below[k + 1]) for k in (0, 2, 4, 6)]
-    on_ranges(ranges, starts, counts, place[3] * TB - TB, ld, ext, out)
-
-
-def impute_far(place, starts, counts, below, rest_o, rest_e, edge_o, edge_e, ld, before, done, ext, rows, out, sems):
+    move(ext, 2 * TB * (1 - lax.axis_index(ROWS) % 2) + MID, mid_e, 0, 2 * HALF1)
+    move(ext, 2 * TB * (lax.axis_index(ROWS) % 2) + MID, mid_o, 0, 2 * HALF1)
+    ranges = [(plan[2 * UB + k], plan[2 * UB + k + 1]) for k in (0, 2, 4, 6)]
+    on_ranges(ranges, plan, ld, ext, out)
+
+
+def impute_far(plan, rest_o, rest_e, edge_o, edge_e, ld, before, done, ext, rows, out, sems):
     inner = HALF2 - 1
-    for base, rest, edge in ((2 * TB * (1 - place[5]), rest_e, edge_e), (2 * TB * place[5], rest_o, edge_o)):
+    for base, rest, edge in ((2 * TB * (1 - lax.axis_index(ROWS) % 2), rest_e, edge_e), (2 * TB * (lax.axis_index(ROWS) % 2), rest_o, edge_o)):
         move(ext, base, edge, 0, 1)
         move(ext, base + 1, rest, 0, inner)
         move(ext, base + MID_END, rest, inner, inner)
         move(ext, base + TB - 1, edge, 1, 1)
-    ranges = [(0, below[0]), (below[1], below[2]), (below[5], below[6]), (below[7], UB)]
+    ranges = [(0, plan[2 * UB + 0]), (plan[2 * UB + 1], plan[2 * UB + 2]), (plan[2 * UB + 5], plan[2 * UB + 6]), (plan[2 * UB + 7], UB)]
 
     def leave(k):
         part = at(k * UNROLL, UNROLL)
@@ -237,7 +244,7 @@
         leave(k).start()
         return carry
 
-    sent = on_ranges(ranges, starts, counts, place[3] * TB - TB, ld, ext, rows, send=send)
+    sent = on_ranges(ranges, plan, ld, ext, rows, send=send)
     lax.fori_loop(sent, UB // UNROLL, send, 0)
     for k in range(UB // UNROLL):
         leave(k).wait()
@@ -261,13 +268,8 @@
 
 
 def on_device(z, band, ld, mix, starts, counts):
-    t = lax.axis_index("trait")
     g = lax.axis_index(ROWS)
     owners = lax.axis_size(ROWS)
-    lane = lax.iota(jnp.int32, 8)
-    place = jnp.zeros((8,), jnp.int32)
-    for k, value in enumerate((t, t ^ 1, 3 - t, g, owners, g % 2)):
-        place = jnp.where(lane == k, value, place)
     pairs_a = [(i, i ^ 1) for i in range(4)]
     pairs_b = [(i, 3 - i) for i in range(4)]
     pairs_e = [(i, i ^ 1) for i in range(owners)]
@@ -299,8 +301,8 @@
     w2a, w2b, edge_band, mix_rows = call(
         whiten_2,
         in_vmem(shaped(HALF2), shaped(HALF2), shaped(2), jax.ShapeDtypeStruct((3 * COLS, mix.shape[1]), BF)),
-        [SMEM, HBM, HBM, HBM],
-        (place, z, band, mix),
+        [HBM, HBM, HBM],
+        (z, band, mix),
         [
             pltpu.VMEM(((2 * HALF2 + 4) * BLK, COLS), BF),
             pltpu.VMEM((2 * HALF2, BLK, 3 * BLK), BF),
@@ -312,9 +314,7 @@
     def mixing(w_a, got_a, w_b, got_b):
         blocks = w_a.shape[0] // BLK
         outs = in_vmem(shaped(blocks), shaped(blocks), shaped(2 * blocks, F32))
-        send_a, send_b, own = call(
-            partial, outs, [SMEM] + [VM] * 5, (place, w_a, got_a, w_b, got_b, mix_rows)
-        )
+        send_a, send_b, own = call(partial, outs, [VM] * 5, (w_a, got_a, w_b, got_b, mix_rows))
         return (own, *along_trait(send_a, send_b, pairs_b, pairs_a)), send_a
 
     (own1, far1a, far1b), after = mixing(w1a, got1a, w1b, got1b)
@@ -330,34 +330,34 @@
     rest_e, rest_o = along_rows(mixed2, pairs_open)
     starts_here = starts - (g * TB - TB)
     below = jnp.sum(starts_here[None, :] < jnp.array(LIMITS, jnp.int32)[:, None], axis=1, dtype=jnp.int32)
-    plan = (place, starts, counts, below)
+    plan = jnp.concatenate([starts_here, counts, below])
     ext, done, ld = call(
         impute_own,
         in_vmem(shaped(EXT), shaped(UB), jax.ShapeDtypeStruct(ld.shape, BF)),
-        [SMEM] * 4 + [VM] * 2 + [HBM],
-        (*plan, mixed1, mixed2, ld),
+        [SMEM] + [VM] * 2 + [HBM],
+        (plan, mixed1, mixed2, ld),
         [pltpu.SemaphoreType.DMA((UB // UNROLL,))],
     )
     mid_o, mid_e, ext = lax.optimization_barrier((mid_o, mid_e, ext))
     (mixed3,) = call(
-        finish_edge, in_vmem(shaped(2)), [SMEM] + [VM] * 4, (place, edge_sums, edge_band, mid_o, mid_e)
+        finish_edge, in_vmem(shaped(2)), [VM] * 4, (edge_sums, edge_band, mid_o, mid_e)
     )
     edge_e, edge_o = along_rows(mixed3, pairs_o)
     ext, done = call(
         impute_near,
         in_vmem(shaped(EXT), shaped(UB)),
-        [SMEM] * 4 + [VM] * 6,
-        (*plan, mixed3, mid_o, mid_e, ld, ext, done),
+        [SMEM] + [VM] * 6,
+        (plan, mixed3, mid_o, mid_e, ld, ext, done),
         (),
-        {8: 0, 9: 1},
+        {5: 0, 6: 1},
     )
     _, _, out = call(
         impute_far,
         in_vmem(shaped(EXT), shaped(UB)) + [(shaped(UB), HBM)],
-        [SMEM] * 4 + [VM] * 7,
-        (*plan, rest_o, rest_e, edge_o, edge_e, ld, ext, done),
+        [SMEM] + [VM] * 7,
+        (plan, rest_o, rest_e, edge_o, edge_e, ld, ext, done),
         [pltpu.SemaphoreType.DMA((UB // UNROLL,))],
-        {9: 0, 10: 1},
+        {6: 0, 7: 1},
     )
     return out
 

time: 60.1 us -> 59.1 us (0.983)
  Pallas kernels: 18.7 us -> 16.1 us
  waiting for transfers between devices: 10.2 us -> 11.9 us
    pallas_call x10, Pallas kernels: 18.7 us -> 16.1 us  [call(): pl.pallas_call(kernel, name=kernel.__name__, out_shape=tuple((shape for s...]
    ppermute x4, waiting for transfers between devices: 3.75 us -> 5.09 us  [along_trait(): lax.ppermute(y, 'trait', pairs_y)]
  transfers between devices with their start and end apart: 14 -> 14, of which waited for: 5 -> 5; matrix products, arithmetic and copies ran while one was open for 0% -> 0% of each run, Pallas kernels for 21% -> 18%
where the time goes in v14:
time: 59.1 us; the launch traced here: 58.7 us
  starting transfers between devices  30.2 us (51%)
  Pallas kernels  16.1 us (27%)
  waiting for transfers between devices  11.9 us (20%)
    ppermute x3, starting transfers between devices, along_rows(): other = lax.ppermute(x, ROWS, pairs)  21.2 us
    pallas_call x10, Pallas kernels, call(): pl.pallas_call(kernel, name=kernel.__name__, out_shape=tuple((shape for s...  16.1 us
    ppermute x4, waiting for transfers between devices, along_trait(): lax.ppermute(x, 'trait', pairs_x)  5.76 us
    ppermute x4, waiting for transfers between devices, along_trait(): lax.ppermute(y, 'trait', pairs_y)  5.09 us
    ppermute x4, starting transfers between devices, along_trait(): lax.ppermute(y, 'trait', pairs_y)  3.92 us
    ppermute x4, starting transfers between devices, along_trait(): lax.ppermute(x, 'trait', pairs_x)  3.21 us
    ppermute x3, starting transfers between devices, along_rows(): return (lax.ppermute(x, ROWS, pairs_e), other)  1.9 us
  transfers between devices with their start and end apart: 14, of which 5 were waited for; matrix products, arithmetic and copies ran while one was open for 0% of the time, Pallas kernels for 18%

profile of v14, /device:TPU:1, one launch (start us, length us, event | category | flops | bytes accessed | tf_op | source)
XLA Modules:
  0.0 58.7 jit_solution(15680648046048379042)
XLA Ops:
  0.0 2.2 %whiten_1.1 = (bf16[1024,128]{1,0:T(8,128)(2,1)S(1)}, bf16[1024,128]{1,0:T(8,128)(2,1)S(1)}) custom-call(bf16[4096,128]{1,0:T(8,128)(2,1)} %z.2, bf16[32,128,384]{2,1,0:T(8,128)(2,1)} %band.3), custom_call_target="tpu_custom_call" | custom-call | tf_op jit(solution)/shard_map/whiten_1/pallas_call | solution.py:254
  2.2 3.4 %collective-permute-start.3 = (bf16[1024,128]{1,0:T(8,128)(2,1)S(1)}, bf16[1024,128]{1,0:T(8,128)(2,1)S(1)}, u32[]{:S(2)}, u32[]{:S(2)}) collective-permute-start(bf16[1024,128]{1,0:T(8,128)(2,1)S(1)} %get-tuple-element.39.w_b), channel_id=1, source_target_pairs={{0,3},{1,2},{2,1},{3,0},{4,7},{5,6},{6,5},{7,4},{8,11},{9,10},{10,... | collective-permute-start | bytes 786440 | tf_op jit(solution)/shard_map/ppermute | solution.py:281
  5.6 0.0 collective-permute-start.2
  5.6 2.7 %whiten_2.1 = (bf16[1152,128]{1,0:T(8,128)(2,1)S(1)}, bf16[1152,128]{1,0:T(8,128)(2,1)S(1)}, bf16[256,128]{1,0:T(8,128)(2,1)S(1)}, bf16[384,512]{1,0:T(8,128)(2,1)S(1)}) custom-call(bf16[4096,128]{1,0:T(8,128)(2,1)} %z.2, bf16[32,128,384]{2,1,0:T(8,128)(2,1)} %band.3, bf16[512,512]{1,0:T(8,128)(2,1)} %mix.1), custom_call_target="tpu_custom_call" | custom-call | tf_op jit(solution)/shard_map/whiten_2/pallas_call | solution.py:254
  8.3 1.5 %collective-permute-start = (bf16[1152,128]{1,0:T(8,128)(2,1)S(1)}, bf16[1152,128]{1,0:T(8,128)(2,1)S(1)}, u32[]{:S(2)}, u32[]{:S(2)}) collective-permute-start(bf16[1152,128]{1,0:T(8,128)(2,1)S(1)} %get-tuple-element.37.w_a), channel_id=1, source_target_pairs={{0,1},{1,0},{2,3},{3,2},{4,5},{5,4},{6,7},{7,6},{8,9},{9,8},{10,11... | collective-permute-start | bytes 884744 | tf_op jit(solution)/shard_map/ppermute | solution.py:281
  9.9 0.1 collective-permute-start.1
  10.0 0.6 %collective-permute-done.3.got_b = bf16[1024,128]{1,0:T(8,128)(2,1)S(1)} collective-permute-done((bf16[1024,128]{1,0:T(8,128)(2,1)S(1)}, bf16[1024,128]{1,0:T(8,128)(2,1)S(1)}, u32[]{:S(2)}, u32[]{:S(2)}) %collective-permute-start.3) | collective-permute-done | bytes 262176 | tf_op jit(solution)/shard_map/ppermute | solution.py:281
  10.6 1.9 %collective-permute-done.2.got_a = bf16[1024,128]{1,0:T(8,128)(2,1)S(1)} collective-permute-done((bf16[1024,128]{1,0:T(8,128)(2,1)S(1)}, bf16[1024,128]{1,0:T(8,128)(2,1)S(1)}, u32[]{:S(2)}, u32[]{:S(2)}) %collective-permute-start.2) | collective-permute-done | bytes 262176 | tf_op jit(solution)/shard_map/ppermute | solution.py:281
  12.5 0.0 copy-start.1
  12.5 0.0 copy-start.2
  12.5 0.0 copy-start
  12.5 0.7 %partial.2 = (bf16[1024,128]{1,0:T(8,128)(2,1)S(1)}, bf16[1024,128]{1,0:T(8,128)(2,1)S(1)}, f32[2048,128]{1,0:T(8,128)S(1)}) custom-call(bf16[1024,128]{1,0:T(8,128)(2,1)S(1)} %get-tuple-element.35.w_a, bf16[1024,128]{1,0:T(8,128)(2,1)S(1)} %collective-permute-done.2.got_a, bf16[1024,128]{1,0:T(8,128)(2,1)S(1)} %get-tuple-element.39.w_b, ...), custom_call_target="tpu_custom_call" | custom-call | tf_op jit(solution)/shard_map/partial/pallas_call | solution.py:254
  13.2 0.1 collective-permute-start.7
  13.3 1.6 %collective-permute-start.6 = (bf16[1024,128]{1,0:T(8,128)(2,1)S(1)}, bf16[1024,128]{1,0:T(8,128)(2,1)S(1)}, u32[]{:S(2)}, u32[]{:S(2)}) collective-permute-start(bf16[1024,128]{1,0:T(8,128)(2,1)S(1)} %get-tuple-element.41), channel_id=1, source_target_pairs={{0,3},{1,2},{2,1},{3,0},{4,7},{5,6},{6,5},{7,4},{8,11},{9,10},{10,... | collective-permute-start | bytes 786440 | tf_op jit(solution)/shard_map/ppermute | solution.py:281
  14.9 3.9 %collective-permute-done.got_a = bf16[1152,128]{1,0:T(8,128)(2,1)S(1)} collective-permute-done((bf16[1152,128]{1,0:T(8,128)(2,1)S(1)}, bf16[1152,128]{1,0:T(8,128)(2,1)S(1)}, u32[]{:S(2)}, u32[]{:S(2)}) %collective-permute-start) | collective-permute-done | bytes 294944 | tf_op jit(solution)/shard_map/ppermute | solution.py:281
  18.8 0.0 collective-permute-done.1.got_b
  18.8 0.8 %partial.3 = (bf16[1152,128]{1,0:T(8,128)(2,1)S(1)}, bf16[1152,128]{1,0:T(8,128)(2,1)S(1)}, f32[2304,128]{1,0:T(8,128)S(1)}) custom-call(bf16[1152,128]{1,0:T(8,128)(2,1)S(1)} %get-tuple-element.37.w_a, bf16[1152,128]{1,0:T(8,128)(2,1)S(1)} %collective-permute-done.got_a, bf16[1152,128]{1,0:T(8,128)(2,1)S(1)} %get-tuple-element.38.w_b, ...), custom_call_target="tpu_custom_call" | custom-call | tf_op jit(solution)/shard_map/partial/pallas_call | solution.py:254
  19.6 0.3 collective-permute-start.5
  19.8 0.1 collective-permute-start.4
  19.9 4.5 %collective-permute-done.7.far_b = bf16[1024,128]{1,0:T(8,128)(2,1)S(1)} collective-permute-done((bf16[1024,128]{1,0:T(8,128)(2,1)S(1)}, bf16[1024,128]{1,0:T(8,128)(2,1)S(1)}, u32[]{:S(2)}, u32[]{:S(2)}) %collective-permute-start.7) | collective-permute-done | bytes 262176 | tf_op jit(solution)/shard_map/ppermute | solution.py:281
  24.4 0.0 collective-permute-done.6.far_a
  24.4 0.1 combine_1.1.mid
  24.5 1.7 %collective-permute-start.11 = (bf16[2048,128]{1,0:T(8,128)(2,1)S(1)}, bf16[2048,128]{1,0:T(8,128)(2,1)S(1)}, u32[]{:S(2)}, u32[]{:S(2)}) collective-permute-start(bf16[2048,128]{1,0:T(8,128)(2,1)S(1)} %combine_1.1.mid), channel_id=1, source_target_pairs={{0,4},{4,0},{8,12},{12,8},{16,20},{20,16},{24,28},{28,24},{32,36},... | collective-permute-start | bytes 1572872 | tf_op jit(solution)/shard_map/ppermute | solution.py:285
  26.2 10.9 %collective-permute-start.10 = (bf16[2048,128]{1,0:T(8,128)(2,1)S(1)}, bf16[2048,128]{1,0:T(8,128)(2,1)S(1)}, u32[]{:S(2)}, u32[]{:S(2)}) collective-permute-start(bf16[2048,128]{1,0:T(8,128)(2,1)S(1)} %combine_1.1.mid), channel_id=1, source_target_pairs={{0,252},{4,8},{8,4},{12,16},{16,12},{20,24},{24,20},{28,32},{32,28... | collective-permute-start | bytes 1572872 | tf_op jit(solution)/shard_map/ppermute | solution.py:284
  37.1 0.0 collective-permute-done.5.far_b
  37.1 0.0 collective-permute-done.4.far_a
  37.2 0.1 combine_2.1
  37.3 0.1 collective-permute-start.9
  37.4 6.2 %collective-permute-start.8 = (bf16[2048,128]{1,0:T(8,128)(2,1)S(1)}, bf16[2048,128]{1,0:T(8,128)(2,1)S(1)}, u32[]{:S(2)}, u32[]{:S(2)}) collective-permute-start(bf16[2048,128]{1,0:T(8,128)(2,1)S(1)} %get-tuple-element.53.rest), channel_id=1, source_target_pairs={{0,0},{4,8},{8,4},{12,16},{16,12},{20,24},{24,20},{28,32},{32,28},... | collective-permute-start | bytes 1572872 | tf_op jit(solution)/shard_map/ppermute | solution.py:284
  43.6 0.0 copy-done.1
  43.6 0.0 copy-done.2
  43.6 0.2 convert_reduce_fusion
  43.8 0.0 copy-done
  43.8 0.1 pad_add_fusion.plan
  43.9 4.1 %impute_own.1 = (bf16[12416,128]{1,0:T(8,128)(2,1)S(1)}, bf16[8192,128]{1,0:T(8,128)(2,1)S(1)}, bf16[64,128,512]{2,1,0:T(8,128)(2,1)S(1)}) custom-call(s32[136]{0:T(256)S(1)} %pad_add_fusion.plan, bf16[2048,128]{1,0:T(8,128)(2,1)S(1)} %combine_1.1.mid, bf16[2048,128]{1,0:T(8,128)(2,1)S(1)} %get-tuple-element.53.rest, bf16[64,128,512]{2,1,0:T(8,128)(2,1)} %ld.1), custom_call_target="tpu_custom_call" | custom-call | tf_op jit(solution)/shard_map/impute_own/pallas_call | solution.py:254
  48.0 0.0 collective-permute-done.11.got_e.mid_e
  48.0 0.0 collective-permute-done.10.got_o.mid_o
  48.0 0.2 finish_edge.1.edge
  48.2 0.1 collective-permute-start.13
  48.3 4.0 %collective-permute-start.12 = (bf16[256,128]{1,0:T(8,128)(2,1)S(1)}, bf16[256,128]{1,0:T(8,128)(2,1)S(1)}, u32[]{:S(2)}, u32[]{:S(2)}) collective-permute-start(bf16[256,128]{1,0:T(8,128)(2,1)S(1)} %finish_edge.1.edge), channel_id=1, source_target_pairs={{0,252},{4,8},{8,4},{12,16},{16,12},{20,24},{24,20},{28,32},{32,28... | collective-permute-start | bytes 196616 | tf_op jit(solution)/shard_map/ppermute | solution.py:284
  52.3 2.0 %impute_near.1 = (bf16[12416,128]{1,0:T(8,128)(2,1)S(1)}, bf16[8192,128]{1,0:T(8,128)(2,1)S(1)}) custom-call(s32[136]{0:T(256)S(1)} %pad_add_fusion.plan, bf16[256,128]{1,0:T(8,128)(2,1)S(1)} %finish_edge.1.edge, bf16[2048,128]{1,0:T(8,128)(2,1)S(1)} %collective-permute-done.10.got_o.mid_o, ...), custom_call_target="tpu_custom_call", output_to_operand_aliasing={{0}: (5, {}), {1}: (6, {})} | custom-call | tf_op jit(solution)/shard_map/impute_near/pallas_call | solution.py:254
  54.2 0.0 collective-permute-done.9.rest_e
  54.3 0.0 collective-permute-done.8.rest_o
  54.3 0.0 collective-permute-done.13.edge_e
  54.3 1.1 %collective-permute-done.12.edge_o = bf16[256,128]{1,0:T(8,128)(2,1)S(1)} collective-permute-done((bf16[256,128]{1,0:T(8,128)(2,1)S(1)}, bf16[256,128]{1,0:T(8,128)(2,1)S(1)}, u32[]{:S(2)}, u32[]{:S(2)}) %collective-permute-start.12) | collective-permute-done | bytes 65568 | tf_op jit(solution)/shard_map/ppermute | solution.py:284
  55.4 3.3 %impute_far.1 = (bf16[12416,128]{1,0:T(8,128)(2,1)S(1)}, bf16[8192,128]{1,0:T(8,128)(2,1)S(1)}, bf16[8192,128]{1,0:T(8,128)(2,1)}) custom-call(s32[136]{0:T(256)S(1)} %pad_add_fusion.plan, bf16[2048,128]{1,0:T(8,128)(2,1)S(1)} %collective-permute-done.8.rest_o, ...), custom_call_target="tpu_custom_call", output_to_operand_aliasing={{0}: (6, {}), {1}: (7, {})} | custom-call | tf_op jit(solution)/shard_map/impute_far/pallas_call | solution.py:254
  (1 shorter events, 0.0 us)
Async XLA Ops:
  2.2 8.4 %collective-permute-start.3 = (bf16[1024,128]{1,0:T(8,128)(2,1)S(1)}, bf16[1024,128]{1,0:T(8,128)(2,1)S(1)}, u32[]{:S(2)}, u32[]{:S(2)}) collective-permute-start(bf16[1024,128]{1,0:T(8,128)(2,1)S(1)} %get-tuple-element.39.w_b), channel_id=1, source_target_pairs={{0,3},{1,2},{2,1},{3,0},{4,7},{5,6},{6,5},{7,4},{8,11},{9,10},{10,... | collective-permute-start | bytes 786440 | tf_op jit(solution)/shard_map/ppermute | solution.py:281
  5.6 6.9 %collective-permute-start.2 = (bf16[1024,128]{1,0:T(8,128)(2,1)S(1)}, bf16[1024,128]{1,0:T(8,128)(2,1)S(1)}, u32[]{:S(2)}, u32[]{:S(2)}) collective-permute-start(bf16[1024,128]{1,0:T(8,128)(2,1)S(1)} %get-tuple-element.35.w_a), channel_id=1, source_target_pairs={{0,1},{1,0},{2,3},{3,2},{4,5},{5,4},{6,7},{7,6},{8,9},{9,8},{10,11... | collective-permute-start | bytes 786440 | tf_op jit(solution)/shard_map/ppermute | solution.py:281
  8.3 10.5 %collective-permute-start = (bf16[1152,128]{1,0:T(8,128)(2,1)S(1)}, bf16[1152,128]{1,0:T(8,128)(2,1)S(1)}, u32[]{:S(2)}, u32[]{:S(2)}) collective-permute-start(bf16[1152,128]{1,0:T(8,128)(2,1)S(1)} %get-tuple-element.37.w_a), channel_id=1, source_target_pairs={{0,1},{1,0},{2,3},{3,2},{4,5},{5,4},{6,7},{7,6},{8,9},{9,8},{10,11... | collective-permute-start | bytes 884744 | tf_op jit(solution)/shard_map/ppermute | solution.py:281
  9.9 8.9 %collective-permute-start.1 = (bf16[1152,128]{1,0:T(8,128)(2,1)S(1)}, bf16[1152,128]{1,0:T(8,128)(2,1)S(1)}, u32[]{:S(2)}, u32[]{:S(2)}) collective-permute-start(bf16[1152,128]{1,0:T(8,128)(2,1)S(1)} %get-tuple-element.38.w_b), channel_id=1, source_target_pairs={{0,3},{1,2},{2,1},{3,0},{4,7},{5,6},{6,5},{7,4},{8,11},{9,10},{10,... | collective-permute-start | bytes 884744 | tf_op jit(solution)/shard_map/ppermute | solution.py:281
  12.5 31.1 %copy-start.1 = (s32[64]{0:T(128)S(1)}, s32[64]{0:T(128)}, u32[]{:S(2)}) copy-start(s32[64]{0:T(128)} %param.11) | copy-start | bytes 772
  12.5 31.2 %copy-start.2 = (s32[8]{0:T(128)S(1)}, s32[8]{0:T(128)}, u32[]{:S(2)}) copy-start(s32[8]{0:T(128)} %constant.20.clone) | copy-start | bytes 100
  12.5 31.4 %copy-start = (s32[64]{0:T(128)S(1)}, s32[64]{0:T(128)}, u32[]{:S(2)}) copy-start(s32[64]{0:T(128)} %param.12) | copy-start | bytes 772
  13.2 11.2 %collective-permute-start.7 = (bf16[1024,128]{1,0:T(8,128)(2,1)S(1)}, bf16[1024,128]{1,0:T(8,128)(2,1)S(1)}, u32[]{:S(2)}, u32[]{:S(2)}) collective-permute-start(bf16[1024,128]{1,0:T(8,128)(2,1)S(1)} %get-tuple-element.48), channel_id=1, source_target_pairs={{0,1},{1,0},{2,3},{3,2},{4,5},{5,4},{6,7},{7,6},{8,9},{9,8},{10,11... | collective-permute-start | bytes 786440 | tf_op jit(solution)/shard_map/ppermute | solution.py:281
  13.3 11.1 %collective-permute-start.6 = (bf16[1024,128]{1,0:T(8,128)(2,1)S(1)}, bf16[1024,128]{1,0:T(8,128)(2,1)S(1)}, u32[]{:S(2)}, u32[]{:S(2)}) collective-permute-start(bf16[1024,128]{1,0:T(8,128)(2,1)S(1)} %get-tuple-element.41), channel_id=1, source_target_pairs={{0,3},{1,2},{2,1},{3,0},{4,7},{5,6},{6,5},{7,4},{8,11},{9,10},{10,... | collective-permute-start | bytes 786440 | tf_op jit(solution)/shard_map/ppermute | solution.py:281
  19.6 17.6 %collective-permute-start.5 = (bf16[1152,128]{1,0:T(8,128)(2,1)S(1)}, bf16[1152,128]{1,0:T(8,128)(2,1)S(1)}, u32[]{:S(2)}, u32[]{:S(2)}) collective-permute-start(bf16[1152,128]{1,0:T(8,128)(2,1)S(1)} %get-tuple-element.46), channel_id=1, source_target_pairs={{0,1},{1,0},{2,3},{3,2},{4,5},{5,4},{6,7},{7,6},{8,9},{9,8},{10,11... | collective-permute-start | bytes 884744 | tf_op jit(solution)/shard_map/ppermute | solution.py:281
  19.8 17.3 %collective-permute-start.4 = (bf16[1152,128]{1,0:T(8,128)(2,1)S(1)}, bf16[1152,128]{1,0:T(8,128)(2,1)S(1)}, u32[]{:S(2)}, u32[]{:S(2)}) collective-permute-start(bf16[1152,128]{1,0:T(8,128)(2,1)S(1)} %get-tuple-element.45), channel_id=1, source_target_pairs={{0,3},{1,2},{2,1},{3,0},{4,7},{5,6},{6,5},{7,4},{8,11},{9,10},{10,... | collective-permute-start | bytes 884744 | tf_op jit(solution)/shard_map/ppermute | solution.py:281
  24.5 23.5 %collective-permute-start.11 = (bf16[2048,128]{1,0:T(8,128)(2,1)S(1)}, bf16[2048,128]{1,0:T(8,128)(2,1)S(1)}, u32[]{:S(2)}, u32[]{:S(2)}) collective-permute-start(bf16[2048,128]{1,0:T(8,128)(2,1)S(1)} %combine_1.1.mid), channel_id=1, source_target_pairs={{0,4},{4,0},{8,12},{12,8},{16,20},{20,16},{24,28},{28,24},{32,36},... | collective-permute-start | bytes 1572872 | tf_op jit(solution)/shard_map/ppermute | solution.py:285
  26.2 21.8 %collective-permute-start.10 = (bf16[2048,128]{1,0:T(8,128)(2,1)S(1)}, bf16[2048,128]{1,0:T(8,128)(2,1)S(1)}, u32[]{:S(2)}, u32[]{:S(2)}) collective-permute-start(bf16[2048,128]{1,0:T(8,128)(2,1)S(1)} %combine_1.1.mid), channel_id=1, source_target_pairs={{0,252},{4,8},{8,4},{12,16},{16,12},{20,24},{24,20},{28,32},{32,28... | collective-permute-start | bytes 1572872 | tf_op jit(solution)/shard_map/ppermute | solution.py:284
  37.3 17.0 %collective-permute-start.9 = (bf16[2048,128]{1,0:T(8,128)(2,1)S(1)}, bf16[2048,128]{1,0:T(8,128)(2,1)S(1)}, u32[]{:S(2)}, u32[]{:S(2)}) collective-permute-start(bf16[2048,128]{1,0:T(8,128)(2,1)S(1)} %get-tuple-element.53.rest), channel_id=1, source_target_pairs={{0,4},{4,0},{8,12},{12,8},{16,20},{20,16},{24,28},{28,24},{32,36},... | collective-permute-start | bytes 1572872 | tf_op jit(solution)/shard_map/ppermute | solution.py:285
  37.4 16.9 %collective-permute-start.8 = (bf16[2048,128]{1,0:T(8,128)(2,1)S(1)}, bf16[2048,128]{1,0:T(8,128)(2,1)S(1)}, u32[]{:S(2)}, u32[]{:S(2)}) collective-permute-start(bf16[2048,128]{1,0:T(8,128)(2,1)S(1)} %get-tuple-element.53.rest), channel_id=1, source_target_pairs={{0,0},{4,8},{8,4},{12,16},{16,12},{20,24},{24,20},{28,32},{32,28},... | collective-permute-start | bytes 1572872 | tf_op jit(solution)/shard_map/ppermute | solution.py:284
  48.2 6.1 %collective-permute-start.13 = (bf16[256,128]{1,0:T(8,128)(2,1)S(1)}, bf16[256,128]{1,0:T(8,128)(2,1)S(1)}, u32[]{:S(2)}, u32[]{:S(2)}) collective-permute-start(bf16[256,128]{1,0:T(8,128)(2,1)S(1)} %finish_edge.1.edge), channel_id=1, source_target_pairs={{0,4},{4,0},{8,12},{12,8},{16,20},{20,16},{24,28},{28,24},{32,36},... | collective-permute-start | bytes 196616 | tf_op jit(solution)/shard_map/ppermute | solution.py:285
  48.3 7.1 %collective-permute-start.12 = (bf16[256,128]{1,0:T(8,128)(2,1)S(1)}, bf16[256,128]{1,0:T(8,128)(2,1)S(1)}, u32[]{:S(2)}, u32[]{:S(2)}) collective-permute-start(bf16[256,128]{1,0:T(8,128)(2,1)S(1)} %finish_edge.1.edge), channel_id=1, source_target_pairs={{0,252},{4,8},{8,4},{12,16},{16,12},{20,24},{24,20},{28,32},{32,28... | collective-permute-start | bytes 196616 | tf_op jit(solution)/shard_map/ppermute | solution.py:284

commit v15 on v14

--- a/solution.py
+++ b/solution.py
@@ -50,8 +50,8 @@
     return [(k, min(most, blocks - k)) for k in range(0, blocks, most)]
 
 
-CUTS1 = pieces(2 * HALF1, 4)
-CUTS2 = [(side, k, n) for side in range(2) for k, n in pieces(HALF2, 4)]
+CUTS1 = pieces(2 * HALF1, 7)
+CUTS2 = [(side, k, n) for side in range(2) for k, n in pieces(HALF2, 5)]
 
 
 def place():

time: 59.1 us -> 58.7 us (level)
  Pallas kernels: 16.1 us -> 15.2 us
  waiting for transfers between devices: 11.9 us -> 12.8 us
    pallas_call x10, Pallas kernels: 16.1 us -> 15.2 us  [call(): pl.pallas_call(kernel, name=kernel.__name__, out_shape=tuple((shape for s...]
    ppermute x3, waiting for transfers between devices: 1.09 us -> 1.85 us  [along_rows(): other = lax.ppermute(x, ROWS, pairs)]
  transfers between devices with their start and end apart: 14 -> 14, of which waited for: 5 -> 5; matrix products, arithmetic and copies ran while one was open for 0% -> 0% of each run, Pallas kernels for 18% -> 17%
where the time goes in v15:
time: 58.7 us; the launch traced here: 58.5 us
  starting transfers between devices  30 us (51%)
  Pallas kernels  15.2 us (26%)
  waiting for transfers between devices  12.8 us (22%)
    ppermute x3, starting transfers between devices, along_rows(): other = lax.ppermute(x, ROWS, pairs)  20.9 us
    pallas_call x10, Pallas kernels, call(): pl.pallas_call(kernel, name=kernel.__name__, out_shape=tuple((shape for s...  15.2 us
    ppermute x4, waiting for transfers between devices, along_trait(): lax.ppermute(x, 'trait', pairs_x)  5.76 us
    ppermute x4, waiting for transfers between devices, along_trait(): lax.ppermute(y, 'trait', pairs_y)  5.21 us
    ppermute x4, starting transfers between devices, along_trait(): lax.ppermute(y, 'trait', pairs_y)  3.83 us
    ppermute x4, starting transfers between devices, along_trait(): lax.ppermute(x, 'trait', pairs_x)  3.45 us
    ppermute x3, starting transfers between devices, along_rows(): return (lax.ppermute(x, ROWS, pairs_e), other)  1.91 us
    ppermute x3, waiting for transfers between devices, along_rows(): other = lax.ppermute(x, ROWS, pairs)  1.85 us
  transfers between devices with their start and end apart: 14, of which 5 were waited for; matrix products, arithmetic and copies ran while one was open for 0% of the time, Pallas kernels for 17%

profile of v15, /device:TPU:1, one launch (start us, length us, event | category | flops | bytes accessed | tf_op | source)
XLA Modules:
  0.0 58.5 jit_solution(4291459505632706373)
XLA Ops:
  0.0 2.0 %whiten_1.1 = (bf16[1024,128]{1,0:T(8,128)(2,1)S(1)}, bf16[1024,128]{1,0:T(8,128)(2,1)S(1)}) custom-call(bf16[4096,128]{1,0:T(8,128)(2,1)} %z.2, bf16[32,128,384]{2,1,0:T(8,128)(2,1)} %band.3), custom_call_target="tpu_custom_call" | custom-call | tf_op jit(solution)/shard_map/whiten_1/pallas_call | solution.py:254
  2.0 3.4 %collective-permute-start.3 = (bf16[1024,128]{1,0:T(8,128)(2,1)S(1)}, bf16[1024,128]{1,0:T(8,128)(2,1)S(1)}, u32[]{:S(2)}, u32[]{:S(2)}) collective-permute-start(bf16[1024,128]{1,0:T(8,128)(2,1)S(1)} %get-tuple-element.39.w_b), channel_id=1, source_target_pairs={{0,3},{1,2},{2,1},{3,0},{4,7},{5,6},{6,5},{7,4},{8,11},{9,10},{10,... | collective-permute-start | bytes 786440 | tf_op jit(solution)/shard_map/ppermute | solution.py:281
  5.4 0.0 collective-permute-start.2
  5.4 2.4 %whiten_2.1 = (bf16[1152,128]{1,0:T(8,128)(2,1)S(1)}, bf16[1152,128]{1,0:T(8,128)(2,1)S(1)}, bf16[256,128]{1,0:T(8,128)(2,1)S(1)}, bf16[384,512]{1,0:T(8,128)(2,1)S(1)}) custom-call(bf16[4096,128]{1,0:T(8,128)(2,1)} %z.2, bf16[32,128,384]{2,1,0:T(8,128)(2,1)} %band.3, bf16[512,512]{1,0:T(8,128)(2,1)} %mix.1), custom_call_target="tpu_custom_call" | custom-call | tf_op jit(solution)/shard_map/whiten_2/pallas_call | solution.py:254
  7.9 1.6 %collective-permute-start = (bf16[1152,128]{1,0:T(8,128)(2,1)S(1)}, bf16[1152,128]{1,0:T(8,128)(2,1)S(1)}, u32[]{:S(2)}, u32[]{:S(2)}) collective-permute-start(bf16[1152,128]{1,0:T(8,128)(2,1)S(1)} %get-tuple-element.37.w_a), channel_id=1, source_target_pairs={{0,1},{1,0},{2,3},{3,2},{4,5},{5,4},{6,7},{7,6},{8,9},{9,8},{10,11... | collective-permute-start | bytes 884744 | tf_op jit(solution)/shard_map/ppermute | solution.py:281
  9.4 0.1 collective-permute-start.1
  9.5 0.9 %collective-permute-done.3.got_b = bf16[1024,128]{1,0:T(8,128)(2,1)S(1)} collective-permute-done((bf16[1024,128]{1,0:T(8,128)(2,1)S(1)}, bf16[1024,128]{1,0:T(8,128)(2,1)S(1)}, u32[]{:S(2)}, u32[]{:S(2)}) %collective-permute-start.3) | collective-permute-done | bytes 262176 | tf_op jit(solution)/shard_map/ppermute | solution.py:281
  10.4 1.9 %collective-permute-done.2.got_a = bf16[1024,128]{1,0:T(8,128)(2,1)S(1)} collective-permute-done((bf16[1024,128]{1,0:T(8,128)(2,1)S(1)}, bf16[1024,128]{1,0:T(8,128)(2,1)S(1)}, u32[]{:S(2)}, u32[]{:S(2)}) %collective-permute-start.2) | collective-permute-done | bytes 262176 | tf_op jit(solution)/shard_map/ppermute | solution.py:281
  12.3 0.0 copy-start.1
  12.3 0.0 copy-start.2
  12.3 0.0 copy-start
  12.3 0.7 %partial.2 = (bf16[1024,128]{1,0:T(8,128)(2,1)S(1)}, bf16[1024,128]{1,0:T(8,128)(2,1)S(1)}, f32[2048,128]{1,0:T(8,128)S(1)}) custom-call(bf16[1024,128]{1,0:T(8,128)(2,1)S(1)} %get-tuple-element.35.w_a, bf16[1024,128]{1,0:T(8,128)(2,1)S(1)} %collective-permute-done.2.got_a, bf16[1024,128]{1,0:T(8,128)(2,1)S(1)} %get-tuple-element.39.w_b, ...), custom_call_target="tpu_custom_call" | custom-call | tf_op jit(solution)/shard_map/partial/pallas_call | solution.py:254
  13.0 0.2 collective-permute-start.7
  13.2 1.6 %collective-permute-start.6 = (bf16[1024,128]{1,0:T(8,128)(2,1)S(1)}, bf16[1024,128]{1,0:T(8,128)(2,1)S(1)}, u32[]{:S(2)}, u32[]{:S(2)}) collective-permute-start(bf16[1024,128]{1,0:T(8,128)(2,1)S(1)} %get-tuple-element.41), channel_id=1, source_target_pairs={{0,3},{1,2},{2,1},{3,0},{4,7},{5,6},{6,5},{7,4},{8,11},{9,10},{10,... | collective-permute-start | bytes 786440 | tf_op jit(solution)/shard_map/ppermute | solution.py:281
  14.7 3.9 %collective-permute-done.got_a = bf16[1152,128]{1,0:T(8,128)(2,1)S(1)} collective-permute-done((bf16[1152,128]{1,0:T(8,128)(2,1)S(1)}, bf16[1152,128]{1,0:T(8,128)(2,1)S(1)}, u32[]{:S(2)}, u32[]{:S(2)}) %collective-permute-start) | collective-permute-done | bytes 294944 | tf_op jit(solution)/shard_map/ppermute | solution.py:281
  18.6 0.0 collective-permute-done.1.got_b
  18.6 0.8 %partial.3 = (bf16[1152,128]{1,0:T(8,128)(2,1)S(1)}, bf16[1152,128]{1,0:T(8,128)(2,1)S(1)}, f32[2304,128]{1,0:T(8,128)S(1)}) custom-call(bf16[1152,128]{1,0:T(8,128)(2,1)S(1)} %get-tuple-element.37.w_a, bf16[1152,128]{1,0:T(8,128)(2,1)S(1)} %collective-permute-done.got_a, bf16[1152,128]{1,0:T(8,128)(2,1)S(1)} %get-tuple-element.38.w_b, ...), custom_call_target="tpu_custom_call" | custom-call | tf_op jit(solution)/shard_map/partial/pallas_call | solution.py:254
  19.4 0.2 collective-permute-start.5
  19.5 0.3 collective-permute-start.4
  19.9 4.3 %collective-permute-done.7.far_b = bf16[1024,128]{1,0:T(8,128)(2,1)S(1)} collective-permute-done((bf16[1024,128]{1,0:T(8,128)(2,1)S(1)}, bf16[1024,128]{1,0:T(8,128)(2,1)S(1)}, u32[]{:S(2)}, u32[]{:S(2)}) %collective-permute-start.7) | collective-permute-done | bytes 262176 | tf_op jit(solution)/shard_map/ppermute | solution.py:281
  24.2 0.0 collective-permute-done.6.far_a
  24.2 0.1 combine_1.1.mid
  24.3 1.7 %collective-permute-start.11 = (bf16[2048,128]{1,0:T(8,128)(2,1)S(1)}, bf16[2048,128]{1,0:T(8,128)(2,1)S(1)}, u32[]{:S(2)}, u32[]{:S(2)}) collective-permute-start(bf16[2048,128]{1,0:T(8,128)(2,1)S(1)} %combine_1.1.mid), channel_id=1, source_target_pairs={{0,4},{4,0},{8,12},{12,8},{16,20},{20,16},{24,28},{28,24},{32,36},... | collective-permute-start | bytes 1572872 | tf_op jit(solution)/shard_map/ppermute | solution.py:285
  26.0 10.6 %collective-permute-start.10 = (bf16[2048,128]{1,0:T(8,128)(2,1)S(1)}, bf16[2048,128]{1,0:T(8,128)(2,1)S(1)}, u32[]{:S(2)}, u32[]{:S(2)}) collective-permute-start(bf16[2048,128]{1,0:T(8,128)(2,1)S(1)} %combine_1.1.mid), channel_id=1, source_target_pairs={{0,252},{4,8},{8,4},{12,16},{16,12},{20,24},{24,20},{28,32},{32,28... | collective-permute-start | bytes 1572872 | tf_op jit(solution)/shard_map/ppermute | solution.py:284
  36.6 0.0 collective-permute-done.5.far_b
  36.6 0.0 collective-permute-done.4.far_a
  36.6 0.1 combine_2.1
  36.8 0.1 collective-permute-start.9
  36.9 6.5 %collective-permute-start.8 = (bf16[2048,128]{1,0:T(8,128)(2,1)S(1)}, bf16[2048,128]{1,0:T(8,128)(2,1)S(1)}, u32[]{:S(2)}, u32[]{:S(2)}) collective-permute-start(bf16[2048,128]{1,0:T(8,128)(2,1)S(1)} %get-tuple-element.53.rest), channel_id=1, source_target_pairs={{0,0},{4,8},{8,4},{12,16},{16,12},{20,24},{24,20},{28,32},{32,28},... | collective-permute-start | bytes 1572872 | tf_op jit(solution)/shard_map/ppermute | solution.py:284
  43.4 0.0 copy-done.1
  43.4 0.0 copy-done.2
  43.4 0.2 convert_reduce_fusion
  43.6 0.0 copy-done
  43.6 0.1 pad_add_fusion.plan
  43.7 4.1 %impute_own.1 = (bf16[12416,128]{1,0:T(8,128)(2,1)S(1)}, bf16[8192,128]{1,0:T(8,128)(2,1)S(1)}, bf16[64,128,512]{2,1,0:T(8,128)(2,1)S(1)}) custom-call(s32[136]{0:T(256)S(1)} %pad_add_fusion.plan, bf16[2048,128]{1,0:T(8,128)(2,1)S(1)} %combine_1.1.mid, bf16[2048,128]{1,0:T(8,128)(2,1)S(1)} %get-tuple-element.53.rest, bf16[64,128,512]{2,1,0:T(8,128)(2,1)} %ld.1), custom_call_target="tpu_custom_call" | custom-call | tf_op jit(solution)/shard_map/impute_own/pallas_call | solution.py:254
  47.8 0.0 collective-permute-done.11.got_e.mid_e
  47.8 0.0 collective-permute-done.10.got_o.mid_o
  47.8 0.2 finish_edge.1.edge
  48.0 0.1 collective-permute-start.13
  48.1 3.7 %collective-permute-start.12 = (bf16[256,128]{1,0:T(8,128)(2,1)S(1)}, bf16[256,128]{1,0:T(8,128)(2,1)S(1)}, u32[]{:S(2)}, u32[]{:S(2)}) collective-permute-start(bf16[256,128]{1,0:T(8,128)(2,1)S(1)} %finish_edge.1.edge), channel_id=1, source_target_pairs={{0,252},{4,8},{8,4},{12,16},{16,12},{20,24},{24,20},{28,32},{32,28... | collective-permute-start | bytes 196616 | tf_op jit(solution)/shard_map/ppermute | solution.py:284
  51.8 1.5 %impute_near.1 = (bf16[12416,128]{1,0:T(8,128)(2,1)S(1)}, bf16[8192,128]{1,0:T(8,128)(2,1)S(1)}) custom-call(s32[136]{0:T(256)S(1)} %pad_add_fusion.plan, bf16[256,128]{1,0:T(8,128)(2,1)S(1)} %finish_edge.1.edge, bf16[2048,128]{1,0:T(8,128)(2,1)S(1)} %collective-permute-done.10.got_o.mid_o, ...), custom_call_target="tpu_custom_call", output_to_operand_aliasing={{0}: (5, {}), {1}: (6, {})} | custom-call | tf_op jit(solution)/shard_map/impute_near/pallas_call | solution.py:254
  53.3 0.0 collective-permute-done.9.rest_e
  53.3 0.0 collective-permute-done.8.rest_o
  53.3 0.0 collective-permute-done.13.edge_e
  53.3 1.8 %collective-permute-done.12.edge_o = bf16[256,128]{1,0:T(8,128)(2,1)S(1)} collective-permute-done((bf16[256,128]{1,0:T(8,128)(2,1)S(1)}, bf16[256,128]{1,0:T(8,128)(2,1)S(1)}, u32[]{:S(2)}, u32[]{:S(2)}) %collective-permute-start.12) | collective-permute-done | bytes 65568 | tf_op jit(solution)/shard_map/ppermute | solution.py:284
  55.2 3.3 %impute_far.1 = (bf16[12416,128]{1,0:T(8,128)(2,1)S(1)}, bf16[8192,128]{1,0:T(8,128)(2,1)S(1)}, bf16[8192,128]{1,0:T(8,128)(2,1)}) custom-call(s32[136]{0:T(256)S(1)} %pad_add_fusion.plan, bf16[2048,128]{1,0:T(8,128)(2,1)S(1)} %collective-permute-done.8.rest_o, ...), custom_call_target="tpu_custom_call", output_to_operand_aliasing={{0}: (6, {}), {1}: (7, {})} | custom-call | tf_op jit(solution)/shard_map/impute_far/pallas_call | solution.py:254
  (1 shorter events, 0.0 us)
Async XLA Ops:
  2.0 8.4 %collective-permute-start.3 = (bf16[1024,128]{1,0:T(8,128)(2,1)S(1)}, bf16[1024,128]{1,0:T(8,128)(2,1)S(1)}, u32[]{:S(2)}, u32[]{:S(2)}) collective-permute-start(bf16[1024,128]{1,0:T(8,128)(2,1)S(1)} %get-tuple-element.39.w_b), channel_id=1, source_target_pairs={{0,3},{1,2},{2,1},{3,0},{4,7},{5,6},{6,5},{7,4},{8,11},{9,10},{10,... | collective-permute-start | bytes 786440 | tf_op jit(solution)/shard_map/ppermute | solution.py:281
  5.4 6.9 %collective-permute-start.2 = (bf16[1024,128]{1,0:T(8,128)(2,1)S(1)}, bf16[1024,128]{1,0:T(8,128)(2,1)S(1)}, u32[]{:S(2)}, u32[]{:S(2)}) collective-permute-start(bf16[1024,128]{1,0:T(8,128)(2,1)S(1)} %get-tuple-element.35.w_a), channel_id=1, source_target_pairs={{0,1},{1,0},{2,3},{3,2},{4,5},{5,4},{6,7},{7,6},{8,9},{9,8},{10,11... | collective-permute-start | bytes 786440 | tf_op jit(solution)/shard_map/ppermute | solution.py:281
  7.9 10.7 %collective-permute-start = (bf16[1152,128]{1,0:T(8,128)(2,1)S(1)}, bf16[1152,128]{1,0:T(8,128)(2,1)S(1)}, u32[]{:S(2)}, u32[]{:S(2)}) collective-permute-start(bf16[1152,128]{1,0:T(8,128)(2,1)S(1)} %get-tuple-element.37.w_a), channel_id=1, source_target_pairs={{0,1},{1,0},{2,3},{3,2},{4,5},{5,4},{6,7},{7,6},{8,9},{9,8},{10,11... | collective-permute-start | bytes 884744 | tf_op jit(solution)/shard_map/ppermute | solution.py:281
  9.4 9.2 %collective-permute-start.1 = (bf16[1152,128]{1,0:T(8,128)(2,1)S(1)}, bf16[1152,128]{1,0:T(8,128)(2,1)S(1)}, u32[]{:S(2)}, u32[]{:S(2)}) collective-permute-start(bf16[1152,128]{1,0:T(8,128)(2,1)S(1)} %get-tuple-element.38.w_b), channel_id=1, source_target_pairs={{0,3},{1,2},{2,1},{3,0},{4,7},{5,6},{6,5},{7,4},{8,11},{9,10},{10,... | collective-permute-start | bytes 884744 | tf_op jit(solution)/shard_map/ppermute | solution.py:281
  12.3 31.1 %copy-start.1 = (s32[64]{0:T(128)S(1)}, s32[64]{0:T(128)}, u32[]{:S(2)}) copy-start(s32[64]{0:T(128)} %param.11) | copy-start | bytes 772
  12.3 31.2 %copy-start.2 = (s32[8]{0:T(128)S(1)}, s32[8]{0:T(128)}, u32[]{:S(2)}) copy-start(s32[8]{0:T(128)} %constant.20.clone) | copy-start | bytes 100
  12.3 31.4 %copy-start = (s32[64]{0:T(128)S(1)}, s32[64]{0:T(128)}, u32[]{:S(2)}) copy-start(s32[64]{0:T(128)} %param.12) | copy-start | bytes 772
  13.0 11.2 %collective-permute-start.7 = (bf16[1024,128]{1,0:T(8,128)(2,1)S(1)}, bf16[1024,128]{1,0:T(8,128)(2,1)S(1)}, u32[]{:S(2)}, u32[]{:S(2)}) collective-permute-start(bf16[1024,128]{1,0:T(8,128)(2,1)S(1)} %get-tuple-element.48), channel_id=1, source_target_pairs={{0,1},{1,0},{2,3},{3,2},{4,5},{5,4},{6,7},{7,6},{8,9},{9,8},{10,11... | collective-permute-start | bytes 786440 | tf_op jit(solution)/shard_map/ppermute | solution.py:281
  13.2 11.1 %collective-permute-start.6 = (bf16[1024,128]{1,0:T(8,128)(2,1)S(1)}, bf16[1024,128]{1,0:T(8,128)(2,1)S(1)}, u32[]{:S(2)}, u32[]{:S(2)}) collective-permute-start(bf16[1024,128]{1,0:T(8,128)(2,1)S(1)} %get-tuple-element.41), channel_id=1, source_target_pairs={{0,3},{1,2},{2,1},{3,0},{4,7},{5,6},{6,5},{7,4},{8,11},{9,10},{10,... | collective-permute-start | bytes 786440 | tf_op jit(solution)/shard_map/ppermute | solution.py:281
  19.4 17.3 %collective-permute-start.5 = (bf16[1152,128]{1,0:T(8,128)(2,1)S(1)}, bf16[1152,128]{1,0:T(8,128)(2,1)S(1)}, u32[]{:S(2)}, u32[]{:S(2)}) collective-permute-start(bf16[1152,128]{1,0:T(8,128)(2,1)S(1)} %get-tuple-element.46), channel_id=1, source_target_pairs={{0,1},{1,0},{2,3},{3,2},{4,5},{5,4},{6,7},{7,6},{8,9},{9,8},{10,11... | collective-permute-start | bytes 884744 | tf_op jit(solution)/shard_map/ppermute | solution.py:281
  19.5 17.1 %collective-permute-start.4 = (bf16[1152,128]{1,0:T(8,128)(2,1)S(1)}, bf16[1152,128]{1,0:T(8,128)(2,1)S(1)}, u32[]{:S(2)}, u32[]{:S(2)}) collective-permute-start(bf16[1152,128]{1,0:T(8,128)(2,1)S(1)} %get-tuple-element.45), channel_id=1, source_target_pairs={{0,3},{1,2},{2,1},{3,0},{4,7},{5,6},{6,5},{7,4},{8,11},{9,10},{10,... | collective-permute-start | bytes 884744 | tf_op jit(solution)/shard_map/ppermute | solution.py:281
  24.3 23.5 %collective-permute-start.11 = (bf16[2048,128]{1,0:T(8,128)(2,1)S(1)}, bf16[2048,128]{1,0:T(8,128)(2,1)S(1)}, u32[]{:S(2)}, u32[]{:S(2)}) collective-permute-start(bf16[2048,128]{1,0:T(8,128)(2,1)S(1)} %combine_1.1.mid), channel_id=1, source_target_pairs={{0,4},{4,0},{8,12},{12,8},{16,20},{20,16},{24,28},{28,24},{32,36},... | collective-permute-start | bytes 1572872 | tf_op jit(solution)/shard_map/ppermute | solution.py:285
  26.0 21.8 %collective-permute-start.10 = (bf16[2048,128]{1,0:T(8,128)(2,1)S(1)}, bf16[2048,128]{1,0:T(8,128)(2,1)S(1)}, u32[]{:S(2)}, u32[]{:S(2)}) collective-permute-start(bf16[2048,128]{1,0:T(8,128)(2,1)S(1)} %combine_1.1.mid), channel_id=1, source_target_pairs={{0,252},{4,8},{8,4},{12,16},{16,12},{20,24},{24,20},{28,32},{32,28... | collective-permute-start | bytes 1572872 | tf_op jit(solution)/shard_map/ppermute | solution.py:284
  36.8 16.5 %collective-permute-start.9 = (bf16[2048,128]{1,0:T(8,128)(2,1)S(1)}, bf16[2048,128]{1,0:T(8,128)(2,1)S(1)}, u32[]{:S(2)}, u32[]{:S(2)}) collective-permute-start(bf16[2048,128]{1,0:T(8,128)(2,1)S(1)} %get-tuple-element.53.rest), channel_id=1, source_target_pairs={{0,4},{4,0},{8,12},{12,8},{16,20},{20,16},{24,28},{28,24},{32,36},... | collective-permute-start | bytes 1572872 | tf_op jit(solution)/shard_map/ppermute | solution.py:285
  36.9 16.5 %collective-permute-start.8 = (bf16[2048,128]{1,0:T(8,128)(2,1)S(1)}, bf16[2048,128]{1,0:T(8,128)(2,1)S(1)}, u32[]{:S(2)}, u32[]{:S(2)}) collective-permute-start(bf16[2048,128]{1,0:T(8,128)(2,1)S(1)} %get-tuple-element.53.rest), channel_id=1, source_target_pairs={{0,0},{4,8},{8,4},{12,16},{16,12},{20,24},{24,20},{28,32},{32,28},... | collective-permute-start | bytes 1572872 | tf_op jit(solution)/shard_map/ppermute | solution.py:284
  48.0 5.3 %collective-permute-start.13 = (bf16[256,128]{1,0:T(8,128)(2,1)S(1)}, bf16[256,128]{1,0:T(8,128)(2,1)S(1)}, u32[]{:S(2)}, u32[]{:S(2)}) collective-permute-start(bf16[256,128]{1,0:T(8,128)(2,1)S(1)} %finish_edge.1.edge), channel_id=1, source_target_pairs={{0,4},{4,0},{8,12},{12,8},{16,20},{20,16},{24,28},{28,24},{32,36},... | collective-permute-start | bytes 196616 | tf_op jit(solution)/shard_map/ppermute | solution.py:285
  48.1 7.1 %collective-permute-start.12 = (bf16[256,128]{1,0:T(8,128)(2,1)S(1)}, bf16[256,128]{1,0:T(8,128)(2,1)S(1)}, u32[]{:S(2)}, u32[]{:S(2)}) collective-permute-start(bf16[256,128]{1,0:T(8,128)(2,1)S(1)} %finish_edge.1.edge), channel_id=1, source_target_pairs={{0,252},{4,8},{8,4},{12,16},{16,12},{20,24},{24,20},{28,32},{32,28... | collective-permute-start | bytes 196616 | tf_op jit(solution)/shard_map/ppermute | solution.py:284
